TPU v7x, 128 devices: a whole 4x4x4 slice. The times are simulated.
128 devices in a mesh: front: 2 (over core), row: 8 (over y, x_hi), col: 8 (over z, x_lo).
Axes of the slice: x: 4 (x_hi: 2, x_lo: 2; x = x_hi * 2 + x_lo), y: 4, z: 4, core: 2. Of those that a mesh axis runs over, the one named last changes fastest.
Arguments:
- front_matrix: bfloat16 [2, 3, 8, 256, 3, 8, 256], P('front', None, 'row', None, None, 'col'), as said below
- contributions: bfloat16 [2, 8, 8, 32, 256, 256], P('front', 'row', 'col'), may hold values from -3 to 3
- target_front: int32 [2, 8, 8, 32], P('front', 'row', 'col'), may hold values from 0 to 1, as said below
- target_row: int32 [2, 8, 8, 32], P('front', 'row', 'col'), may hold values from 8 to 23, as said below
- target_col: int32 [2, 8, 8, 32], P('front', 'row', 'col'), may hold values from 0 to 22, as said below
- live_count: int32 [2, 8, 8], P('front', 'row', 'col'), may hold values from 24 to 32
Outputs:
- factor: float32 [2, 3, 8, 256, 3, 8, 256], P('front', None, 'row', None, None, 'col')
Inputs may be any that keep to these rules, and one draw needn't show every extreme that they name: `front_matrix`: Symmetric; its leading 2 * 2 * 256 rows and columns form a strictly diagonally dominant block with a positive diagonal. `target_front`: among one device's live slots at most 2 aim at one pair of parent front and target_row modulo the number of row devices, and on every device one such pair takes exactly 2. `target_row`: never one of the first 4 tile rows, nor one of the first tile rows as many as the col devices. `target_col`: below the slot's target_row, and congruent to the holding device's col index modulo the number of col devices.
All inputs are finite; a program needn't handle non-finite values.
Results may differ from a plain program's by a relative error of at most 0.0003.
Values may be sent and summed in bfloat16 or wider, within the bound.
No kernel may reach another device: no remote copies, remote signals or barrier semaphores. Data moves between devices by JAX's collectives and lax.ppermute only.
A program may use at most 128 MiB of HBM per device.

v0:
```python
import jax
import jax.numpy as jnp
import numpy as np
from jax import lax
from jax.sharding import PartitionSpec as P

PANEL_TILES = 2
PANELS = 2


def broadcast(array, axis, root):
    mine = lax.axis_index(axis) == root
    return lax.psum(jnp.where(mine, array, jnp.zeros_like(array)), axis)


def mirror_tiles(square, tile_size):
    tile_ids = jnp.arange(square.shape[0]) // tile_size
    return jnp.where(tile_ids[:, None] >= tile_ids[None, :], square, square.T)


def panel_factor(square, tile_size):
    return jnp.linalg.cholesky(mirror_tiles(square, tile_size))


def below_solve(lead_factor, row_block):
    return lax.linalg.triangular_solve(
        lead_factor, row_block, left_side=False, lower=True, transpose_a=True
    )


def pack_buckets(
    contrib_tiles, destination, live_slots, slot_ids, bucket_total, capacity, local_tile
):
    earlier = (
        (destination[:, None] == destination[None, :])
        & live_slots[None, :]
        & (slot_ids[None, :] < slot_ids[:, None])
    )
    position = jnp.sum(earlier.astype(jnp.int32), axis=1)
    bucket = destination * capacity + position
    matches = (bucket[None, :] == jnp.arange(bucket_total, dtype=jnp.int32)[:, None]) & live_slots[
        None, :
    ]
    source = jnp.sum(jnp.where(matches, slot_ids[None, :], 0), axis=1)
    filled = jnp.any(matches, axis=1)
    packed = jnp.where(filled[:, None, None], contrib_tiles[source], jnp.zeros((), jnp.bfloat16))
    targets = jnp.where(filled, local_tile[source], -1)
    return (packed, targets)


def route_tiles(
    contributions,
    target_front,
    target_row,
    target_col,
    live_count,
    tile_cols,
    n_front,
    n_row,
    n_col,
):
    slot_total = contributions.shape[3]
    tile_size = contributions.shape[4]
    contrib_tiles = contributions.reshape(slot_total, tile_size, tile_size)
    fronts_to = target_front.reshape(slot_total)
    rows_to = target_row.reshape(slot_total)
    cols_to = target_col.reshape(slot_total)
    slot_ids = jnp.arange(slot_total, dtype=jnp.int32)
    live_slots = slot_ids < live_count.reshape(())
    capacity = max(2, -(-slot_total // (n_front * n_row)))
    local_tile = rows_to // n_row * tile_cols + cols_to // n_col
    destination = fronts_to * n_row + rows_to % n_row
    bucket_total = n_front * n_row * capacity
    packed, targets = pack_buckets(
        contrib_tiles, destination, live_slots, slot_ids, bucket_total, capacity, local_tile
    )
    received, arrived = (
        lax.all_to_all(packed, ("front", "row"), split_axis=0, concat_axis=0, tiled=True),
        lax.all_to_all(targets, ("front", "row"), split_axis=0, concat_axis=0, tiled=True),
    )
    return (received, arrived)


def per_device(front_matrix, contributions, target_front, target_row, target_col, live_count):
    tile_rows = front_matrix.shape[1]
    tile_size = front_matrix.shape[3]
    tile_cols = front_matrix.shape[4]
    n_front = lax.axis_size("front")
    n_row = lax.axis_size("row")
    n_col = lax.axis_size("col")
    row_index = lax.axis_index("row")
    col_index = lax.axis_index("col")
    work = front_matrix.reshape(tile_rows, tile_size, tile_cols, tile_size).astype(jnp.float32)
    received, arrived = route_tiles(
        contributions,
        target_front,
        target_row,
        target_col,
        live_count,
        tile_cols,
        n_front,
        n_row,
        n_col,
    )
    local_total = tile_rows * tile_cols
    selector = (arrived[None, :] == jnp.arange(local_total, dtype=jnp.int32)[:, None]).astype(
        jnp.bfloat16
    )
    assembled = jnp.dot(
        selector,
        received.reshape(received.shape[0], tile_size * tile_size),
        preferred_element_type=jnp.float32,
    )
    work = work + assembled.reshape(tile_rows, tile_cols, tile_size, tile_size).transpose(
        0, 2, 1, 3
    )
    global_rows = jnp.arange(tile_rows, dtype=jnp.int32) * n_row + row_index
    global_cols = jnp.arange(tile_cols, dtype=jnp.int32) * n_col + col_index
    panel_width = PANEL_TILES * tile_size
    for panel_number in range(PANELS):
        first_tile = panel_number * PANEL_TILES
        after_tile = first_tile + PANEL_TILES
        pieces = []
        for member in range(PANEL_TILES):
            tile_index = first_tile + member
            pieces.append(broadcast(work[:, :, tile_index // n_col, :], "col", tile_index % n_col))
        rows_panel = jnp.concatenate(pieces, axis=2)
        diagonal_part = jnp.stack(
            [
                jnp.where(
                    row_index == (first_tile + member) % n_row,
                    rows_panel[(first_tile + member) // n_row],
                    0.0,
                )
                for member in range(PANEL_TILES)
            ]
        )
        lead_block = (
            lax.psum(diagonal_part.astype(jnp.bfloat16), "row")
            .astype(jnp.float32)
            .reshape(panel_width, panel_width)
        )
        lead_factor = panel_factor(lead_block, tile_size)
        solved = below_solve(
            lead_factor, rows_panel.reshape(tile_rows * tile_size, panel_width)
        ).reshape(tile_rows, tile_size, panel_width)
        offset = global_rows - first_tile
        in_panel = (offset >= 0) & (offset < PANEL_TILES)
        picked = lead_factor.reshape(PANEL_TILES, tile_size, panel_width)[
            jnp.clip(offset, 0, PANEL_TILES - 1)
        ]
        row_mask = global_rows >= after_tile
        factor_rows = jnp.where(
            row_mask[:, None, None], solved, jnp.where(in_panel[:, None, None], picked, 0.0)
        )
        grouped = factor_rows.reshape(tile_cols, n_col // n_row, tile_size, panel_width)
        own_piece = lax.dynamic_index_in_dim(grouped, col_index // n_row, axis=1, keepdims=False)
        cols_panel = broadcast(own_piece, "row", col_index % n_row)
        col_mask = global_cols >= after_tile
        for member in range(PANEL_TILES):
            tile_index = first_tile + member
            local_col = tile_index // n_col
            owner = col_index == tile_index % n_col
            stored = jnp.where(
                owner,
                factor_rows[:, :, member * tile_size : (member + 1) * tile_size],
                work[:, :, local_col, :],
            )
            work = work.at[:, :, local_col, :].set(stored)
        early_slots = []
        late_slots = [
            slot_number for slot_number in range(tile_cols) if slot_number not in early_slots
        ]
        for group_slots in (early_slots, late_slots):
            if group_slots:
                indices = np.array(group_slots, dtype=np.int32)
                update = jnp.einsum(
                    "atk,bsk->atbs",
                    factor_rows,
                    cols_panel[indices],
                    precision=lax.Precision.HIGHEST,
                    preferred_element_type=jnp.float32,
                )
                trailing_mask = (
                    row_mask[:, None, None, None] & col_mask[indices][None, None, :, None]
                )
                work = work.at[:, :, indices, :].add(-jnp.where(trailing_mask, update, 0.0))
    lower = global_rows[:, None] >= global_cols[None, :]
    factor = jnp.where(lower[:, None, :, None], work, 0.0)
    return factor.reshape(1, tile_rows, 1, tile_size, tile_cols, 1, tile_size)


def solution(mesh):
    in_specs = (
        P("front", None, "row", None, None, "col", None),
        P("front", "row", "col", None, None, None),
        P("front", "row", "col", None),
        P("front", "row", "col", None),
        P("front", "row", "col", None),
        P("front", "row", "col"),
    )
    out_specs = P("front", None, "row", None, None, "col", None)
    return jax.shard_map(
        per_device, mesh=mesh, in_specs=in_specs, out_specs=out_specs, check_vma=False
    )
```

profile of v0, /device:TPU:6, one launch (start us, length us, event | category | flops | bytes accessed | tf_op | source)
XLA Modules:
  0.0 1015.9 jit_solution(2382640748277828764)
XLA Ops:
  9.8 7.4 all-to-all-start
  17.2 5.0 gather_fusion.1
  22.2 4.5 broadcast_select_fusion
  26.7 7.4 all-to-all-start.1
  35.4 47.2 %all-to-all-done.1 = bf16[32,256,256]{2,1,0:T(8,128)(2,1)} async-done(((bf16[32,256,256]{2,1,0:T(8,128)(2,1)}), bf16[32,256,256]{2,1,0:T(8,128)(2,1)}, u32[]{:S(2)}, u32[]{:S(2)}) %all-to-all-start.1) | async-done | bytes 4194336 | tf_op jit(solution)/shard_map/all_to_all | solution.py:78
  82.5 5.6 convert_add_fusion
  88.7 1.6 fusion.29
  90.5 88.1 %all-reduce.20.cloned.1.call-done = (f32[3,256,256]{2,1,0:T(8,128)}, f32[3,256,256]{2,1,0:T(8,128)}) async-done(((f32[3,256,256]{2,1,0:T(8,128)}, f32[3,256,256]{2,1,0:T(8,128)}), (f32[3,256,256]{2,1,0:T(8,128)}, f32[3,256,256]{2,1,0:T(8,128)})) %all-reduce.20.cloned.1.call-update) | async-done | bytes 1572880 | tf_op jit(solution)/shard_map/psum | solution.py:13
  183.6 83.0 %all-reduce.10.cloned.1.call-done = bf16[512,512]{1,0:T(8,128)(2,1)} async-done(((bf16[512,512]{1,0:T(8,128)(2,1)}), bf16[512,512]{1,0:T(8,128)(2,1)}) %all-reduce.10.cloned.1.call-update) | async-done | bytes 524304 | tf_op jit(solution)/shard_map/psum | solution.py:139
  270.6 11.7 %cholesky.286 = f32[128,128]{1,0:T(8,128)S(1)} custom-call(f32[128,128]{1,0:T(8,128)S(1)} %cholesky.426), custom_call_target="Cholesky" | custom-call | tf_op jit(solution)/shard_map/jit(cholesky)/cholesky | solution.py:22
  282.5 9.8 custom-call.27
  294.8 11.7 %cholesky.305 = f32[128,128]{1,0:T(8,128)S(1)} custom-call(f32[128,128]{1,0:T(8,128)S(1)} %cholesky.430), custom_call_target="Cholesky" | custom-call | tf_op jit(solution)/shard_map/jit(cholesky)/cholesky | solution.py:22
  306.6 10.2 %custom-call.28 = f32[1,128,128]{1,2,0:T(8,128)S(1)} custom-call(f32[1,128,128]{2,1,0:T(8,128)S(1)} %get-tuple-element.129), custom_call_target="InvertDiagBlocksLowerTriangular" | custom-call | tf_op jit(solution)/shard_map/jit(cholesky)/cholesky | solution.py:22
  318.3 11.7 %cholesky.326 = f32[128,128]{1,0:T(8,128)S(1)} custom-call(f32[128,128]{1,0:T(8,128)S(1)} %cholesky.435), custom_call_target="Cholesky" | custom-call | tf_op jit(solution)/shard_map/jit(cholesky)/cholesky | solution.py:22
  330.8 9.8 custom-call.29
  342.1 11.8 %cholesky.343 = f32[128,128]{1,0:T(8,128)S(1)} custom-call(f32[128,128]{1,0:T(8,128)S(1)} %convolution_subtract_fusion.11), custom_call_target="Cholesky" | custom-call | tf_op jit(solution)/shard_map/jit(cholesky)/cholesky | solution.py:22
  359.3 12.2 %while.8 = (s32[]{:T(128)}, f32[512,512]{1,0:T(8,128)}, s32[4,2]{0,1:T(2,128)S(1)}, f32[4,128,128]{2,1,0:T(8,128)S(1)}, s32[]{:T(128)}) while((s32[]{:T(128)}, f32[512,512]{1,0:T(8,128)}, s32[4,2]{0,1:T(2,128)S(1)}, f32[4,128,128]{2,1,0:T(8,128)S(1)}, s32[]{:T(128)}) %tuple.82), condition=%wide.while_cond.4, body=%wide.while_body.4.sunk | while | flops 2 | bytes 131181 | solution.py:26
  360.0 2.4 bitcast_dynamic-update-slice_fusion.5
  363.1 2.4 bitcast_dynamic-update-slice_fusion.5
  366.1 2.4 bitcast_dynamic-update-slice_fusion.5
  369.2 2.3 bitcast_dynamic-update-slice_fusion.5
  371.5 39.3 %custom-call.30 = f32[4,128,128]{1,2,0:T(8,128)S(1)} custom-call(f32[4,128,128]{2,1,0:T(8,128)S(1)} %get-tuple-element.69), custom_call_target="InvertDiagBlocksLowerTriangular" | custom-call | tf_op jit(solution)/shard_map/triangular_solve/custom-call.3 | solution.py:26
  412.4 1.8 convolution_subtract_fusion.3
  414.8 2.5 convolution_subtract_fusion.5
  417.8 3.2 convolution_subtract_fusion.2
  422.8 3.0 copy.72
  425.8 1.8 gather_fusion.2
  427.6 3.5 broadcast_select_fusion.2
  434.0 17.9 %scatter.14 = f32[3,256,3,256]{3,2,1,0:T(4,128)} dynamic-update-slice(f32[3,256,3,256]{3,2,1,0:T(4,128)} %copy-done.3, f32[3,256,1,256]{3,2,1,0:T(1,128)S(1)} %copy.73, s32[]{:T(128)} %copy.158, s32[]{:T(128)} %copy.158, s32[]{:T(128)} %copy.158, s32[]{:T(128)} %copy.158) | dynamic-update-slice | bytes 1572868 | tf_op jit(solution)/shard_map/scatter | solution.py:169
  452.4 17.9 %scatter.15 = f32[3,256,3,256]{3,2,1,0:T(4,128)} dynamic-update-slice(f32[3,256,3,256]{3,2,1,0:T(4,128)} %scatter.14, f32[3,256,1,256]{3,2,1,0:T(1,128)S(1)} %reshape.562, s32[]{:T(128)} %copy.158, s32[]{:T(128)} %copy.158, s32[]{:T(128)} %copy.158, s32[]{:T(128)} %copy.158) | dynamic-update-slice | bytes 1572868 | tf_op jit(solution)/shard_map/scatter | solution.py:169
  470.3 2.3 copy.74
  472.6 53.2 %all-reduce.12.cloned.1.call-done = f32[3,256,512]{2,1,0:T(8,128)} async-done(((f32[3,256,512]{2,1,0:T(8,128)}), f32[3,256,512]{2,1,0:T(8,128)}) %all-reduce.12.cloned.1.call-update) | async-done | bytes 1572880 | tf_op jit(solution)/shard_map/psum | solution.py:13
  525.8 3.2 gather_fusion.4
  529.0 6.0 negate_bitcast_fusion.1
  536.6 4.3 scatter_fusion
  542.2 86.8 %all-reduce.18.cloned.1.call-done = (f32[3,256,256]{2,1,0:T(8,128)}, f32[3,256,256]{2,1,0:T(8,128)}) async-done(((f32[3,256,256]{2,1,0:T(8,128)}, f32[3,256,256]{2,1,0:T(8,128)}), (f32[3,256,256]{2,1,0:T(8,128)}, f32[3,256,256]{2,1,0:T(8,128)})) %all-reduce.18.cloned.1.call-update) | async-done | bytes 1572880 | tf_op jit(solution)/shard_map/psum | solution.py:13
  633.1 83.9 %all-reduce.14.cloned.1.call-done = bf16[512,512]{1,0:T(8,128)(2,1)} async-done(((bf16[512,512]{1,0:T(8,128)(2,1)}), bf16[512,512]{1,0:T(8,128)(2,1)}) %all-reduce.14.cloned.1.call-update) | async-done | bytes 524304 | tf_op jit(solution)/shard_map/psum | solution.py:139
  717.0 2.2 copy.77
  724.6 11.7 %cholesky.358 = f32[128,128]{1,0:T(8,128)S(1)} custom-call(f32[128,128]{1,0:T(8,128)S(1)} %cholesky.439), custom_call_target="Cholesky" | custom-call | tf_op jit(solution)/shard_map/jit(cholesky)/cholesky | solution.py:22
  737.0 9.8 custom-call.31
  750.0 11.7 %cholesky.377 = f32[128,128]{1,0:T(8,128)S(1)} custom-call(f32[128,128]{1,0:T(8,128)S(1)} %cholesky.443), custom_call_target="Cholesky" | custom-call | tf_op jit(solution)/shard_map/jit(cholesky)/cholesky | solution.py:22
  763.8 9.9 custom-call.32
  776.9 13.2 %cholesky.398 = f32[128,128]{1,0:T(8,128)} custom-call(f32[128,128]{1,0:T(8,128)} %cholesky.448), custom_call_target="Cholesky" | custom-call | tf_op jit(solution)/shard_map/jit(cholesky)/cholesky | solution.py:22
  792.2 11.3 %custom-call.33 = f32[1,128,128]{1,2,0:T(8,128)} custom-call(f32[1,128,128]{2,1,0:T(8,128)} %get-tuple-element.116), custom_call_target="InvertDiagBlocksLowerTriangular" | custom-call | tf_op jit(solution)/shard_map/jit(cholesky)/cholesky | solution.py:22
  805.8 11.9 %cholesky.415 = f32[128,128]{1,0:T(8,128)S(1)} custom-call(f32[128,128]{1,0:T(8,128)S(1)} %convolution_subtract_fusion.10), custom_call_target="Cholesky" | custom-call | tf_op jit(solution)/shard_map/jit(cholesky)/cholesky | solution.py:22
  821.1 1.6 fusion.18
  822.7 11.7 %while.9 = (s32[]{:T(128)}, f32[512,512]{1,0:T(8,128)}, s32[4,2]{0,1:T(2,128)S(1)}, f32[4,128,128]{2,1,0:T(8,128)S(1)}, s32[]{:T(128)}) while((s32[]{:T(128)}, f32[512,512]{1,0:T(8,128)}, s32[4,2]{0,1:T(2,128)S(1)}, f32[4,128,128]{2,1,0:T(8,128)S(1)}, s32[]{:T(128)}) %tuple.102), condition=%wide.while_cond.4.clone, body=%wide.while_body.4.clone.sunk | while | flops 2 | bytes 131181 | solution.py:26
  823.4 2.3 bitcast_dynamic-update-slice_fusion.6
  826.3 2.3 bitcast_dynamic-update-slice_fusion.6
  829.3 2.3 bitcast_dynamic-update-slice_fusion.6
  832.2 2.2 bitcast_dynamic-update-slice_fusion.6
  834.4 39.3 %custom-call.34 = f32[4,128,128]{1,2,0:T(8,128)S(1)} custom-call(f32[4,128,128]{2,1,0:T(8,128)S(1)} %get-tuple-element.70), custom_call_target="InvertDiagBlocksLowerTriangular" | custom-call | tf_op jit(solution)/shard_map/triangular_solve/custom-call.3 | solution.py:26
  873.7 1.6 fusion.33
  875.4 1.8 convolution_subtract_fusion.1
  877.8 2.3 convolution_subtract_fusion.4
  880.6 3.1 convolution_subtract_fusion
  885.5 3.1 copy.79
  888.6 1.8 gather_fusion.5
  890.4 4.2 broadcast_select_fusion.1
  897.2 92.0 %all-reduce.16.cloned.1.call-done = f32[3,256,512]{2,1,0:T(8,128)} async-done(((f32[3,256,512]{2,1,0:T(8,128)}), f32[3,256,512]{2,1,0:T(8,128)}) %all-reduce.16.cloned.1.call-update) | async-done | bytes 1572880 | tf_op jit(solution)/shard_map/psum | solution.py:13
  989.2 3.2 gather_fusion.7
  992.4 6.0 negate_bitcast_fusion
  1000.0 4.5 scatter_fusion.1
  1004.8 3.8 copy.83
  (168 shorter events, 69.4 us)
Async XLA Ops:
  9.8 16.9 %all-to-all-start = ((s32[16,2,1]{1,2,0:T(1,128)}), s32[16,2,1]{1,2,0:T(1,128)S(1)}, u32[]{:S(2)}, u32[]{:S(2)}) async-start(s32[16,2,1]{1,2,0:T(1,128)} %bitcast.7), calls=%async_computation | async-start | bytes 16384 | tf_op jit(solution)/shard_map/all_to_all | solution.py:79
  26.7 55.9 %copy-start.15 = (bf16[1,3,1,256,3,1,256]{6,3,5,4,2,1,0:T(8,128)(2,1)S(1)}, bf16[1,3,1,256,3,1,256]{6,3,5,4,2,1,0:T(8,128)(2,1)}, u32[]{:S(2)}) copy-start(bf16[1,3,1,256,3,1,256]{6,3,5,4,2,1,0:T(8,128)(2,1)} %param.25) | copy-start | bytes 3538948
  26.7 55.9 %all-to-all-start.1 = ((bf16[32,256,256]{2,1,0:T(8,128)(2,1)}), bf16[32,256,256]{2,1,0:T(8,128)(2,1)}, u32[]{:S(2)}, u32[]{:S(2)}) async-start(bf16[32,256,256]{2,1,0:T(8,128)(2,1)} %broadcast_select_fusion), calls=%async_computation.1 | async-start | bytes 8388608 | tf_op jit(solution)/shard_map/all_to_all | solution.py:78
  34.0 144.6 %all-reduce.20.cloned.1.call-start = ((), (), s32[]{:S(2)}) async-start(), calls=%async_computation.7 | async-start | bytes 3145728 | tf_op jit(solution)/shard_map/psum | solution.py:13
  88.2 2.2 copy-start.3
  90.4 176.2 %all-reduce.10.cloned.1.call-start = ((), (), s32[]{:S(2)}) async-start(), calls=%async_computation.2 | async-start | bytes 1048576 | tf_op jit(solution)/shard_map/psum | solution.py:139
  178.6 1.4 copy-start.10
  180.1 1.2 copy-start.4
  182.2 343.6 %all-reduce.12.cloned.1.call-start = ((), (), s32[]{:S(2)}) async-start(), calls=%async_computation.3 | async-start | bytes 3145728 | tf_op jit(solution)/shard_map/psum | solution.py:13
  269.6 1.0 copy-start.9
  431.1 2.1 copy-start.1
  431.1 197.9 %all-reduce.18.cloned.1.call-start = ((), (), s32[]{:S(2)}) async-start(), calls=%async_computation.6 | async-start | bytes 3145728 | tf_op jit(solution)/shard_map/psum | solution.py:13
  433.2 18.7 %copy-start.7 = (f32[3,256,256]{2,1,0:T(8,128)S(1)}, f32[3,256,256]{2,1,0:T(8,128)}, u32[]{:S(2)}) copy-start(f32[3,256,256]{2,1,0:T(8,128)} %get-tuple-element.105) | copy-start | bytes 2359300
  542.1 174.9 %all-reduce.14.cloned.1.call-start = ((), (), s32[]{:S(2)}) async-start(), calls=%async_computation.4 | async-start | bytes 1048576 | tf_op jit(solution)/shard_map/psum | solution.py:139
  629.1 1.4 copy-start.11
  630.5 1.2 copy-start.5
  632.6 356.6 %all-reduce.16.cloned.1.call-start = ((), (), s32[]{:S(2)}) async-start(), calls=%async_computation.5 | async-start | bytes 3145728 | tf_op jit(solution)/shard_map/psum | solution.py:13
  723.6 1.0 copy-start.8
  749.4 0.7 copy-start.12
  873.7 4.0 copy-start.6
  885.5 3.1 copy-start.2
  888.6 1.8 copy-start.13
  888.6 1.8 copy-start.14
  895.4 1.6 copy-start
Sparse Core Ops, SparseCore 0:
  90.5 88.0 all-reduce.19
  182.3 84.2 all-reduce.9
  431.2 94.5 all-reduce.11
  542.3 86.7 all-reduce.17
  632.7 84.2 all-reduce.13
  894.8 94.4 all-reduce.15
where the time goes:
time: 1030 us; the launch traced here: 1020 us
  waiting for transfers between devices  534 us (52%)
  other arithmetic  284 us (28%)
  local copies, waits for them, and re-layouts  109 us (11%)
  matrix products  51.3 us (5%)
  between operations  20.6 us (2%)
  starting transfers between devices  15.9 us (2%)
    psum x4, waiting for transfers between devices, broadcast(): return lax.psum(jnp.where(mine, array, jnp.zeros_like(array)), axis)  320 us
    psum x2, waiting for transfers between devices, per_device(): lax.psum(diagonal_part.astype(jnp.bfloat16), 'row').astype(jnp.float32)  167 us
    another operation x29, other arithmetic, panel_factor(): return jnp.linalg.cholesky(mirror_tiles(square, tile_size))  164 us
    another operation x7, other arithmetic, below_solve(): lax.linalg.triangular_solve(lead_factor, row_block, left_side=False, lowe...  84 us
    all_to_all x1, waiting for transfers between devices, route_tiles(): lax.all_to_all(packed, ('front', 'row'), split_axis=0, concat_axis=0, til...  47.2 us
    scatter x4, local copies, waits for them, and re-layouts, per_device(): work = work.at[:, :, local_col, :].set(stored)  38.2 us
    another operation x29, local copies, waits for them, and re-layouts, below_solve(): lax.linalg.triangular_solve(lead_factor, row_block, left_side=False, lowe...  30 us
    another operation x14, matrix products, below_solve(): lax.linalg.triangular_solve(lead_factor, row_block, left_side=False, lowe...  21 us
  transfers between devices with their start and end apart: 8, of which 7 were waited for; matrix products, arithmetic and copies ran while one was open for 5% of the time, Pallas kernels for 0%

commit v1 on v0

v1 whole, which is shorter than its diff:
```python
import jax
import jax.numpy as jnp
from jax import lax
from jax.experimental import pallas as pl
from jax.experimental.pallas import tpu as pltpu
from jax.sharding import PartitionSpec as P

LEAD_TILES = 4
BLOCK = 128
STRIP = 8
VMEM_BYTES = 56 * 1024 * 1024


def vmem():
    return pl.BlockSpec(memory_space=pltpu.VMEM)


def smem():
    return pl.BlockSpec(memory_space=pltpu.SMEM)


def hbm():
    return pl.BlockSpec(memory_space=pl.ANY)


def nt(left, right, precision=None):
    return lax.dot_general(
        left, right, (((1,), (1,)), ((), ())), precision=precision, preferred_element_type=jnp.float32
    )


def split(value):
    high = value.astype(jnp.bfloat16)
    return high, (value - high.astype(jnp.float32)).astype(jnp.bfloat16)


def nt3(left, right):
    return nt(left[0], right[0]) + (nt(left[0], right[1]) + nt(left[1], right[0]))


def pack(contributions, target_front, target_row, target_col, live_count, n_front, n_row, n_col, tile_cols):
    slots, size, _ = contributions.shape
    capacity = max(2, -(-slots // (n_front * n_row)))
    buckets = n_front * n_row * capacity

    def kernel(front_ref, row_ref, col_ref, live_ref, tiles_ref, packed_ref, targets_ref, counts, sems):
        live = live_ref[0]

        def clear(i, carry):
            targets_ref[i] = -1
            return carry

        lax.fori_loop(0, buckets, clear, 0)

        def clear_counts(i, carry):
            counts[i] = 0
            return carry

        lax.fori_loop(0, n_front * n_row, clear_counts, 0)

        def copy(slot, bucket):
            return pltpu.make_async_copy(tiles_ref.at[slot], packed_ref.at[bucket], sems.at[slot])

        def send(slot, carry):
            row, col = row_ref[slot], col_ref[slot]
            destination = front_ref[slot] * n_row + lax.rem(row, n_row)
            position = counts[destination]
            counts[destination] = position + 1
            bucket = destination * capacity + position
            targets_ref[bucket] = lax.div(row, n_row) * tile_cols + lax.div(col, n_col)
            copy(slot, bucket).start()
            return carry

        lax.fori_loop(0, live, send, 0)

        def finish(slot, carry):
            copy(slot, 0).wait()
            return carry

        lax.fori_loop(0, live, finish, 0)

    return pl.pallas_call(
        kernel,
        name="pack",
        out_shape=(
            jax.ShapeDtypeStruct((buckets, size, size), contributions.dtype),
            jax.ShapeDtypeStruct((buckets,), jnp.int32),
        ),
        in_specs=[smem()] * 4 + [hbm()],
        out_specs=(hbm(), smem()),
        scratch_shapes=[pltpu.SMEM((n_front * n_row,), jnp.int32), pltpu.SemaphoreType.DMA((slots,))],
    )(target_front, target_row, target_col, live_count, contributions)


EXTENDED = ((1, 0), (1, 1), (2, 0), (2, 1), (2, 2))


def assemble(received, arrived, front):
    total, size, _ = received.shape

    def kernel(arrived_ref, received_ref, front_ref, ext_ref, panel_ref, landed, sems):
        def copy(i):
            return pltpu.make_async_copy(received_ref.at[i], landed.at[i], sems.at[i])

        def fetch(i, carry):
            @pl.when(arrived_ref[i] >= 0)
            def _():
                copy(i).start()

            return carry

        lax.fori_loop(0, total, fetch, 0)
        for slot, (a, b) in enumerate(EXTENDED):
            ext_ref[slot] = front_ref[a, b].astype(jnp.float32)

        def add(i, carry):
            target = arrived_ref[i]

            @pl.when(target >= 0)
            def _():
                copy(i).wait()
                slot = jnp.where(target >= 6, target - 4, target - 3)
                ext_ref[slot] = ext_ref[slot] + landed[i].astype(jnp.float32)

            return carry

        lax.fori_loop(0, total, add, 0)
        panel_ref[0:size] = ext_ref[0]
        panel_ref[size : 2 * size] = ext_ref[2]

    return pl.pallas_call(
        kernel,
        name="assemble",
        out_shape=(
            jax.ShapeDtypeStruct((len(EXTENDED), size, size), jnp.float32),
            jax.ShapeDtypeStruct((2 * size, size), jnp.float32),
        ),
        in_specs=[smem(), hbm(), vmem()],
        out_specs=(vmem(), vmem()),
        scratch_shapes=[pltpu.VMEM((total, size, size), jnp.bfloat16), pltpu.SemaphoreType.DMA((total,))],
        compiler_params=pltpu.CompilerParams(vmem_limit_bytes=VMEM_BYTES),
    )(arrived, received, front)


def pick_lane(value, lane):
    index = jnp.full(value.shape, lane, jnp.int32)
    return jnp.take_along_axis(value, index, axis=1, mode="promise_in_bounds")


def factor_block(work):
    rows = lax.broadcasted_iota(jnp.int32, (BLOCK, BLOCK), 0)
    lanes = lax.broadcasted_iota(jnp.int32, (STRIP, BLOCK), 1)
    strip_rows = lax.broadcasted_iota(jnp.int32, (STRIP, BLOCK), 0)

    def spread(value, i):
        return jnp.broadcast_to(value[i : i + 1, :], value.shape)

    def step(number, carry):
        base = pl.multiple_of(number * STRIP, STRIP)
        strip = work[pl.ds(base, STRIP), :]
        own = [pick_lane(strip, base + i) for i in range(STRIP)]
        whole = work[...]
        below = rows >= base + STRIP
        columns = [jnp.where(below, pick_lane(whole, base + i), 0.0) for i in range(STRIP)]
        for i in range(STRIP):
            pivot = spread(own[i], i)
            inverse = 1.0 / pivot
            factors = jnp.where(strip_rows > i, own[i] * inverse, 0.0)
            line = jnp.where(lanes == base + i, pivot + pivot, spread(strip, i))
            strip = strip - factors * line
            lower = columns[i] * jnp.broadcast_to(inverse[0:1], whole.shape)
            for j in range(i + 1, STRIP):
                entry = spread(own[j], i)
                own[j] = own[j] - factors * entry
                columns[j] = columns[j] - lower * jnp.broadcast_to(entry[0:1], whole.shape)
            whole = whole - lower * jnp.broadcast_to(line[0:1], whole.shape)
        work[...] = whole
        work[pl.ds(base, STRIP), :] = strip
        return carry

    lax.fori_loop(0, BLOCK // STRIP, step, 0)


HIGHEST = lax.Precision.HIGHEST


def factorize(lead, ids, size):
    order = LEAD_TILES * size
    pairs = [(i, j) for i in range(LEAD_TILES) for j in range(i + 1)]
    blocks = order // BLOCK

    def kernel(ids_ref, lead_ref, high_ref, low_ref, inv_high_ref, inv_low_ref, own_ref, full, inverses, work):
        r = lax.broadcasted_iota(jnp.int32, (BLOCK, BLOCK), 0)
        c = lax.broadcasted_iota(jnp.int32, (BLOCK, BLOCK), 1)
        for number, (i, j) in enumerate(pairs):
            full[i * size : (i + 1) * size, j * size : (j + 1) * size] = (
                lead_ref[:, number].astype(jnp.float32).reshape(size, size)
            )
        for k in range(blocks):
            s, e = k * BLOCK, (k + 1) * BLOCK
            work[...] = full[s:e, s:e]
            factor_block(work)
            done = work[...]
            diagonal = jnp.where(r == c, done, 0.0)
            root = lax.rsqrt(jnp.sum(diagonal, axis=1, keepdims=True))
            inverse = jnp.where(r >= c, done, 0.0) * root * (1.0 / jnp.sum(diagonal, axis=0, keepdims=True))
            inverses[k] = inverse
            full[s:e, s:e] = (jnp.where(r <= c, done, 0.0) * root).T
            if e < order:
                panel = nt(full[e:order, s:e], inverse, HIGHEST)
                full[e:order, s:e] = panel
                for j in range(k + 1, blocks):
                    o = j * BLOCK
                    full[o:order, o : o + BLOCK] = full[o:order, o : o + BLOCK] - nt(
                        panel[o - e :], panel[o - e : o - e + BLOCK], HIGHEST
                    )
        half = size // BLOCK
        for q in range(LEAD_TILES):
            s = q * size
            full[s : s + BLOCK, s + BLOCK : s + size] = jnp.zeros((BLOCK, size - BLOCK), jnp.float32)
            first, second = inverses[q * half], inverses[q * half + 1]
            corner = -jnp.dot(
                second,
                jnp.dot(
                    full[s + BLOCK : s + size, s : s + BLOCK], first,
                    precision=HIGHEST, preferred_element_type=jnp.float32,
                ),
                precision=HIGHEST, preferred_element_type=jnp.float32,
            )
            for (y, x, part) in ((0, 0, first), (0, 1, jnp.zeros_like(first)), (1, 0, corner), (1, 1, second)):
                high, low = split(part)
                inv_high_ref[q, y * BLOCK : (y + 1) * BLOCK, x * BLOCK : (x + 1) * BLOCK] = high
                inv_low_ref[q, y * BLOCK : (y + 1) * BLOCK, x * BLOCK : (x + 1) * BLOCK] = low
        for number, (i, j) in enumerate(pairs):
            tile = full[i * size : (i + 1) * size, j * size : (j + 1) * size]
            high, low = split(tile)
            high_ref[i * size : (i + 1) * size, j * size : (j + 1) * size] = high
            low_ref[i * size : (i + 1) * size, j * size : (j + 1) * size] = low

            @pl.when((ids_ref[0] == i) & (ids_ref[1] == j))
            def _():
                own_ref[...] = tile

    wide = jax.ShapeDtypeStruct((order, order), jnp.bfloat16)
    inv = jax.ShapeDtypeStruct((LEAD_TILES, size, size), jnp.bfloat16)
    return pl.pallas_call(
        kernel,
        name="factorize",
        out_shape=(wide, wide, inv, inv, jax.ShapeDtypeStruct((size, size), jnp.float32)),
        in_specs=[smem(), vmem()],
        out_specs=(vmem(),) * 5,
        scratch_shapes=[
            pltpu.VMEM((order, order), jnp.float32),
            pltpu.VMEM((blocks, BLOCK, BLOCK), jnp.float32),
            pltpu.VMEM((BLOCK, BLOCK), jnp.float32),
        ],
        compiler_params=pltpu.CompilerParams(vmem_limit_bytes=VMEM_BYTES),
    )(ids, lead)


def finish(ids, rows, cols, early, factors, own, extended, front):
    size = own.shape[0]
    order = LEAD_TILES * size
    tile_rows, tile_cols = front.shape[:2]
    lanes = 128
    parts = size // lanes
    total = 6 * size

    def kernel(
        ids_ref, rows_ref, cols_ref, early_ref, high_ref, low_ref, ih_ref, il_ref, own_ref, ext_ref, front_ref,
        out_ref, xh, xl, panel,
    ):
        row, col = ids_ref[0], ids_ref[1]

        def put(a, b, tile):
            for part in range(parts):
                start = (a * size * tile_cols + b) * parts + part
                out_ref[pl.ds(start, size, stride=tile_cols * parts), :] = tile[:, part * lanes : (part + 1) * lanes]

        for q in range(LEAD_TILES):
            s, e = q * size, (q + 1) * size
            acc = jnp.concatenate(
                [
                    rows_ref[:, q].reshape(2 * size, size),
                    cols_ref[:, q].reshape(2 * size, size),
                    early_ref[:, q].astype(jnp.float32).reshape(size, size),
                    early_ref[:, LEAD_TILES + q].astype(jnp.float32).reshape(size, size),
                ],
                axis=0,
            )
            if q:
                acc = acc - nt3((xh[:, 0:s], xl[:, 0:s]), (high_ref[s:e, 0:s], low_ref[s:e, 0:s]))
            x = nt3(split(acc), (ih_ref[q], il_ref[q]))
            high, low = split(x)
            xh[:, s:e] = high
            xl[:, s:e] = low

            @pl.when(col == q)
            def _():
                panel[0 : 2 * size] = x[0 : 2 * size]
                panel[2 * size :] = x[4 * size : 5 * size]

        zero = jnp.zeros((size, size), jnp.float32)
        for a, b in ((0, 1), (0, 2), (1, 2)):
            put(a, b, zero)

        def update(a, b, base, x, y):
            def take(ref, n):
                return ref[n * size : (n + 1) * size, :]

            put(a, b, base - nt3((take(xh, x), take(xl, x)), (take(xh, y), take(xl, y))))

        in_panel = col < LEAD_TILES

        @pl.when(in_panel)
        def _():
            put(1, 0, panel[0:size])
            put(2, 0, panel[size : 2 * size])

        @pl.when(jnp.logical_not(in_panel))
        def _():
            update(1, 0, ext_ref[0], 0, 5)
            update(2, 0, ext_ref[2], 1, 5)

        lead_row = row < LEAD_TILES

        @pl.when(row < col)
        def _():
            put(0, 0, zero)
            put(1, 1, zero)
            put(2, 2, zero)

        @pl.when(row >= col)
        def _():
            @pl.when(lead_row)
            def _():
                put(0, 0, own_ref[...])

            @pl.when(jnp.logical_not(lead_row) & in_panel)
            def _():
                put(0, 0, panel[2 * size :])

            @pl.when(jnp.logical_not(in_panel))
            def _():
                update(0, 0, front_ref[0, 0].astype(jnp.float32), 4, 5)

            update(1, 1, ext_ref[1], 0, 2)
            update(2, 2, ext_ref[4], 1, 3)

        update(2, 1, ext_ref[3], 1, 2)

    return pl.pallas_call(
        kernel,
        name="finish",
        out_shape=jax.ShapeDtypeStruct((tile_rows * size * tile_cols * parts, lanes), jnp.float32),
        in_specs=[smem()] + [vmem()] * 10,
        out_specs=vmem(),
        scratch_shapes=[
            pltpu.VMEM((total, order), jnp.bfloat16),
            pltpu.VMEM((total, order), jnp.bfloat16),
            pltpu.VMEM((3 * size, size), jnp.float32),
        ],
        compiler_params=pltpu.CompilerParams(vmem_limit_bytes=VMEM_BYTES),
    )(ids, rows, cols, early, *factors, own, extended, front)


def exchange(value, axis):
    return lax.all_to_all(value, axis, split_axis=0, concat_axis=0, tiled=True)


def gather(value, axis):
    count = lax.axis_size(axis)
    return exchange(jnp.broadcast_to(value[None], (count,) + value.shape), axis)


def per_device(front_matrix, contributions, target_front, target_row, target_col, live_count):
    _, tile_rows, _, size, tile_cols, _, _ = front_matrix.shape
    n_front, n_row, n_col = (lax.axis_size(name) for name in ("front", "row", "col"))
    slots = contributions.shape[3]
    front = front_matrix.reshape(tile_rows, size, tile_cols, size).transpose(0, 2, 1, 3)
    ids = jnp.stack([lax.axis_index("row"), lax.axis_index("col")]).astype(jnp.int32)

    packed, targets = pack(
        contributions.reshape(slots, size, size),
        target_front.reshape(slots), target_row.reshape(slots), target_col.reshape(slots),
        live_count.reshape(1), n_front, n_row, n_col, tile_cols,
    )
    arrived = exchange(targets, ("front", "row"))
    received = exchange(packed, ("front", "row"))

    thin = size // n_col
    chunk = exchange(front[0, 0].reshape(n_col, thin, size), "col")[:LEAD_TILES]
    leading = gather(chunk, "row")
    lower = jnp.stack([leading[i, j] for i in range(LEAD_TILES) for j in range(i + 1)])
    lead = gather(lower, "col")
    aimed = jnp.concatenate([jnp.broadcast_to(chunk[None], leading.shape), leading], axis=1)
    early = exchange(aimed, "col")
    *factors, own = factorize(lead, ids, size)

    extended, panel = assemble(received, arrived, front)
    mine = exchange(panel.reshape(n_col, 2 * size // n_col, size), "col")[:LEAD_TILES]
    rows = gather(mine, "col")
    turned = lax.ppermute(
        mine, ("row", "col"), [(r * n_col + c, c * n_col + r) for r in range(n_row) for c in range(n_col)]
    )
    cols = gather(turned, "row")
    factor = finish(ids, rows, cols, early, factors, own, extended, front)
    return factor.reshape(1, tile_rows, 1, size, tile_cols, 1, size)


def solution(mesh):
    in_specs = (
        P("front", None, "row", None, None, "col", None),
        P("front", "row", "col", None, None, None),
        P("front", "row", "col", None),
        P("front", "row", "col", None),
        P("front", "row", "col", None),
        P("front", "row", "col"),
    )
    out_specs = P("front", None, "row", None, None, "col", None)
    return jax.shard_map(per_device, mesh=mesh, in_specs=in_specs, out_specs=out_specs, check_vma=False)
```

time: 1030 us -> 407 us (0.40); the launches traced: 1020 us -> 406 us
  waiting for transfers between devices: 534 us -> 115 us
  other arithmetic: 284 us -> 2.38 us
  Pallas kernels: 0 us -> 212 us
  local copies, waits for them, and re-layouts: 109 us -> 9.09 us
  matrix products: 51.3 us -> 0 us
  starting transfers between devices: 15.9 us -> 51.9 us
  between operations: 20.6 us -> 0.76 us
  blocking collectives: 0 us -> 14.5 us
    psum x6 -> x0, waiting for transfers between devices: 487 us -> none  [the longest x4 320 us: broadcast(): return lax.psum(jnp.where(mine, array, jnp.zeros_like(array)), axis)]
    another operation x40 -> x1, other arithmetic: 250 us -> 0.65 us  [per_device(): jnp.stack([lax.axis_index('row'), lax.axis_index('col')]).astype(jnp.int32)]
    pallas_call x0 -> x4, Pallas kernels: none -> 212 us  [the longest x1 130 us: pack(): pl.pallas_call(kernel, name='pack', out_shape=(jax.ShapeDtypeStruct((buck...]
    all_to_all x2 -> x8, waiting for transfers between devices: 47.2 us -> 115 us  [exchange(): return lax.all_to_all(value, axis, split_axis=0, concat_axis=0, tiled=True)]
    scatter x4 -> x0, local copies, waits for them, and re-layouts: 38.2 us -> none  [per_device(): work = work.at[:, :, local_col, :].set(stored)]
    all_to_all x2 -> x8, starting transfers between devices: 14.8 us -> 50.3 us  [exchange(): return lax.all_to_all(value, axis, split_axis=0, concat_axis=0, tiled=True)]
    another operation x26 -> x0, matrix products: 33.7 us -> none  [the longest x14 21 us: below_solve(): lax.linalg.triangular_solve(lead_factor, row_block, left_side=False, lowe...]
    another operation x41 -> x1, local copies, waits for them, and re-layouts: 31.4 us -> 0.01 us  [per_device(): jnp.stack([leading[i, j] for i in range(LEAD_TILES) for j in range(i + 1)])]
  transfers between devices with their start and end apart: 8 -> 9, of which waited for: 7 -> 6; matrix products, arithmetic and copies ran while one was open for 5% -> 1% of each run, Pallas kernels for 0% -> 47%
where the time goes in v1:
time: 407 us; the launch traced here: 406 us
  Pallas kernels  212 us (52%)
  waiting for transfers between devices  115 us (28%)
  starting transfers between devices  51.9 us (13%)
  blocking collectives  14.5 us (4%)
  local copies, waits for them, and re-layouts  9.09 us (2%)
    pallas_call x1, Pallas kernels, pack(): pl.pallas_call(kernel, name='pack', out_shape=(jax.ShapeDtypeStruct((buck...  130 us
    all_to_all x8, waiting for transfers between devices, exchange(): return lax.all_to_all(value, axis, split_axis=0, concat_axis=0, tiled=True)  115 us
    pallas_call x1, Pallas kernels, factorize(): pl.pallas_call(kernel, name='factorize', out_shape=(wide, wide, inv, inv,...  57.4 us
    all_to_all x8, starting transfers between devices, exchange(): return lax.all_to_all(value, axis, split_axis=0, concat_axis=0, tiled=True)  50.3 us
    pallas_call x1, Pallas kernels, finish(): pl.pallas_call(kernel, name='finish', out_shape=jax.ShapeDtypeStruct((til...  20.1 us
    all_to_all x1, blocking collectives, exchange(): return lax.all_to_all(value, axis, split_axis=0, concat_axis=0, tiled=True)  14.5 us
  transfers between devices with their start and end apart: 9, of which 6 were waited for; matrix products, arithmetic and copies ran while one was open for 1% of the time, Pallas kernels for 47%

profile of v1, /device:TPU:6, one launch (start us, length us, event | category | flops | bytes accessed | tf_op | source)
XLA Modules:
  0.0 406.4 jit_solution(10232359013550994116)
XLA Ops:
  0.0 1.6 slice.53
  1.6 6.8 %all-to-all-start.5 = ((bf16[8,32,256]{2,1,0:T(8,128)(2,1)}), bf16[8,32,256]{2,1,0:T(8,128)(2,1)S(1)}, u32[]{:S(2)}, u32[]{:S(2)}) async-start(bf16[8,32,256]{2,1,0:T(8,128)(2,1)} %bitcast.12), calls=%async_computation.5 | async-start | bytes 262144 | tf_op jit(solution)/shard_map/all_to_all | solution.py:368
  9.0 130.0 %pack.1 = (bf16[32,256,256]{2,1,0:T(8,128)(2,1)}, s32[32]{0:T(128)}) custom-call(s32[32]{0:T(128)} %bitcast.61, s32[32]{0:T(128)} %bitcast.62, s32[32]{0:T(128)} %bitcast.63, s32[1]{0:T(128)} %bitcast.55.live_ref, bf16[32,256,256]{2,1,0:T(8,128)(2,1)} %bitcast.59), custom_call_target="tpu_custom_call" | custom-call | tf_op jit(solution)/shard_map/pack/pallas_call | solution.py:82
  139.0 1.4 all_to_all.31
  140.3 0.0 all-to-all-done.5
  140.3 4.8 %all-to-all-start = ((s32[16,2,1]{1,2,0:T(1,128)}), s32[16,2,1]{1,2,0:T(1,128)S(1)}, u32[]{:S(2)}, u32[]{:S(2)}) async-start(s32[16,2,1]{1,2,0:T(1,128)} %bitcast.7), calls=%async_computation | async-start | bytes 16384 | tf_op jit(solution)/shard_map/all_to_all | solution.py:368
  145.1 4.7 %all-to-all-done = s32[16,2,1]{1,2,0:T(1,128)S(1)} async-done(((s32[16,2,1]{1,2,0:T(1,128)}), s32[16,2,1]{1,2,0:T(1,128)S(1)}, u32[]{:S(2)}, u32[]{:S(2)}) %all-to-all-start) | async-done | bytes 160 | tf_op jit(solution)/shard_map/all_to_all | solution.py:368
  149.9 14.5 %all_to_all.51 = bf16[8,4,32,256]{3,2,1,0:T(8,128)(2,1)S(1)} all-to-all(bf16[8,4,32,256]{3,2,1,0:T(8,128)(2,1)S(1)} %broadcast_in_dim.10), channel_id=1, replica_groups=mesh['front'=2,'row'=8,'col'=8] {'row'}, dimensions={0} | all-to-all | bytes 1048576 | tf_op jit(solution)/shard_map/all_to_all | solution.py:368
  164.5 7.0 %all-to-all-start.1 = ((bf16[32,256,256]{2,1,0:T(8,128)(2,1)}), bf16[32,256,256]{2,1,0:T(8,128)(2,1)}, u32[]{:S(2)}, u32[]{:S(2)}) async-start(bf16[32,256,256]{2,1,0:T(8,128)(2,1)} %get-tuple-element.15), calls=%async_computation.1 | async-start | bytes 8388608 | tf_op jit(solution)/shard_map/all_to_all | solution.py:368
  171.4 0.5 broadcast.7
  171.9 0.7 reduce.3
  172.6 0.6 all_to_all.33.arrived_ref
  173.2 1.1 pad_maximum_fusion
  174.3 45.7 %all-to-all-done.1.received_ref = bf16[32,256,256]{2,1,0:T(8,128)(2,1)} async-done(((bf16[32,256,256]{2,1,0:T(8,128)(2,1)}), bf16[32,256,256]{2,1,0:T(8,128)(2,1)}, u32[]{:S(2)}, u32[]{:S(2)}) %all-to-all-start.1) | async-done | bytes 4194336 | tf_op jit(solution)/shard_map/all_to_all | solution.py:368
  220.0 8.3 %all-to-all-start.7 = ((bf16[8,8,32,256]{3,2,1,0:T(8,128)(2,1)}), bf16[8,8,32,256]{3,2,1,0:T(8,128)(2,1)S(1)}, u32[]{:S(2)}, u32[]{:S(2)}) async-start(bf16[8,8,32,256]{3,2,1,0:T(8,128)(2,1)} %pad_maximum_fusion), calls=%async_computation.7 | async-start | bytes 2097152 | tf_op jit(solution)/shard_map/all_to_all | solution.py:368
  228.4 5.0 %assemble.1 = (f32[5,256,256]{2,1,0:T(8,128)}, f32[512,256]{1,0:T(8,128)}) custom-call(s32[32]{0:T(128)} %all_to_all.33.arrived_ref, bf16[32,256,256]{2,1,0:T(8,128)(2,1)} %all-to-all-done.1.received_ref, bf16[3,3,256,256]{3,2,1,0:T(8,128)(2,1)} %bitcast.57), custom_call_target="tpu_custom_call" | custom-call | tf_op jit(solution)/shard_map/assemble/pallas_call | solution.py:131
  233.4 9.8 %all-to-all-done.7.early_ref = bf16[8,8,32,256]{3,2,1,0:T(8,128)(2,1)S(1)} async-done(((bf16[8,8,32,256]{3,2,1,0:T(8,128)(2,1)}), bf16[8,8,32,256]{3,2,1,0:T(8,128)(2,1)S(1)}, u32[]{:S(2)}, u32[]{:S(2)}) %all-to-all-start.7) | async-done | bytes 1048608 | tf_op jit(solution)/shard_map/all_to_all | solution.py:368
  243.3 0.0 copy-start.2
  243.3 4.6 %all-to-all-start.2 = ((f32[8,64,256]{2,1,0:T(8,128)}), f32[8,64,256]{2,1,0:T(8,128)S(1)}, u32[]{:S(2)}, u32[]{:S(2)}) async-start(f32[8,64,256]{2,1,0:T(8,128)} %bitcast.60), calls=%async_computation.2 | async-start | bytes 1048576 | tf_op jit(solution)/shard_map/all_to_all | solution.py:368
  247.9 8.4 %all-to-all-done.2 = f32[8,64,256]{2,1,0:T(8,128)S(1)} async-done(((f32[8,64,256]{2,1,0:T(8,128)}), f32[8,64,256]{2,1,0:T(8,128)S(1)}, u32[]{:S(2)}, u32[]{:S(2)}) %all-to-all-start.2) | async-done | bytes 524320 | tf_op jit(solution)/shard_map/all_to_all | solution.py:368
  256.3 1.2 broadcast_in_dim.11
  257.6 0.0 copy-done.2
  257.6 4.7 %all-to-all-start.8 = ((bf16[8,10,32,256]{3,2,1,0:T(8,128)(2,1)}), bf16[8,10,32,256]{3,2,1,0:T(8,128)(2,1)S(1)}, u32[]{:S(2)}, u32[]{:S(2)}) async-start(bf16[8,10,32,256]{3,2,1,0:T(8,128)(2,1)} %broadcast_in_dim.11), calls=%async_computation.8 | async-start | bytes 2621440 | tf_op jit(solution)/shard_map/all_to_all | solution.py:368
  262.2 0.0 copy-start.3
  262.2 16.0 %all-to-all-done.8.lead_ref = bf16[8,10,32,256]{3,2,1,0:T(8,128)(2,1)S(1)} async-done(((bf16[8,10,32,256]{3,2,1,0:T(8,128)(2,1)}), bf16[8,10,32,256]{3,2,1,0:T(8,128)(2,1)S(1)}, u32[]{:S(2)}, u32[]{:S(2)}) %all-to-all-start.8) | async-done | bytes 1310752 | tf_op jit(solution)/shard_map/all_to_all | solution.py:368
  278.2 0.0 copy-start.1
  278.2 1.7 broadcast_in_dim.8
  280.0 0.0 copy-done.3
  280.0 0.0 copy-done.1
  280.0 4.7 %all-to-all-start.3 = ((f32[8,4,64,256]{3,2,1,0:T(8,128)}), f32[8,4,64,256]{3,2,1,0:T(8,128)S(1)}, u32[]{:S(2)}, u32[]{:S(2)}) async-start(f32[8,4,64,256]{3,2,1,0:T(8,128)} %broadcast_in_dim.8), calls=%async_computation.3 | async-start | bytes 4194304 | tf_op jit(solution)/shard_map/all_to_all | solution.py:368
  284.7 1.6 collective-permute-start
  286.3 0.0 collective-permute-done
  286.3 30.5 %all-to-all-done.3.rows_ref = f32[8,4,64,256]{3,2,1,0:T(8,128)S(1)} async-done(((f32[8,4,64,256]{3,2,1,0:T(8,128)}), f32[8,4,64,256]{3,2,1,0:T(8,128)S(1)}, u32[]{:S(2)}, u32[]{:S(2)}) %all-to-all-start.3) | async-done | bytes 2097184 | tf_op jit(solution)/shard_map/all_to_all | solution.py:368
  316.8 0.0 copy-start
  316.8 1.7 broadcast_in_dim.9
  318.5 0.2 copy-done
  318.8 9.5 %all-to-all-start.4 = ((f32[8,4,64,256]{3,2,1,0:T(8,128)}), f32[8,4,64,256]{3,2,1,0:T(8,128)}, u32[]{:S(2)}, u32[]{:S(2)}) async-start(f32[8,4,64,256]{3,2,1,0:T(8,128)} %broadcast_in_dim.9), calls=%async_computation.4 | async-start | bytes 4194304 | tf_op jit(solution)/shard_map/all_to_all | solution.py:368
  328.3 0.7 pad_add_fusion.ids_ref
  328.9 57.4 %factorize.1 = (bf16[1024,1024]{1,0:T(8,128)(2,1)}, bf16[1024,1024]{1,0:T(8,128)(2,1)}, bf16[4,256,256]{2,1,0:T(8,128)(2,1)}, bf16[4,256,256]{2,1,0:T(8,128)(2,1)}, f32[256,256]{1,0:T(8,128)}) custom-call(s32[2]{0:T(128)} %pad_add_fusion.ids_ref, bf16[8,10,32,256]{3,2,1,0:T(8,128)(2,1)} %copy-done.1), custom_call_target="tpu_custom_call" | custom-call | tf_op jit(solution)/shard_map/factorize/pallas_call | solution.py:246
  386.3 0.0 all-to-all-done.4.cols_ref
  386.3 20.1 %finish.1 = f32[4608,128]{1,0:T(8,128)} custom-call(s32[2]{0:T(128)} %pad_add_fusion.ids_ref, f32[8,4,64,256]{3,2,1,0:T(8,128)} %copy-done, f32[8,4,64,256]{3,2,1,0:T(8,128)} %all-to-all-done.4.cols_ref, bf16[8,8,32,256]{3,2,1,0:T(8,128)(2,1)} %copy-done.2, bf16[1024,1024]{1,0:T(8,128)(2,1)} %get-tuple-element.17.high_ref, ...), custom_call_target="tpu_custom_call" | custom-call | tf_op jit(solution)/shard_map/finish/pallas_call | solution.py:352
  (13 shorter events, 0.1 us)
Async XLA Ops:
  1.6 138.8 %all-to-all-start.5 = ((bf16[8,32,256]{2,1,0:T(8,128)(2,1)}), bf16[8,32,256]{2,1,0:T(8,128)(2,1)S(1)}, u32[]{:S(2)}, u32[]{:S(2)}) async-start(bf16[8,32,256]{2,1,0:T(8,128)(2,1)} %bitcast.12), calls=%async_computation.5 | async-start | bytes 262144 | tf_op jit(solution)/shard_map/all_to_all | solution.py:368
  140.3 9.6 %all-to-all-start = ((s32[16,2,1]{1,2,0:T(1,128)}), s32[16,2,1]{1,2,0:T(1,128)S(1)}, u32[]{:S(2)}, u32[]{:S(2)}) async-start(s32[16,2,1]{1,2,0:T(1,128)} %bitcast.7), calls=%async_computation | async-start | bytes 16384 | tf_op jit(solution)/shard_map/all_to_all | solution.py:368
  164.5 55.6 %all-to-all-start.1 = ((bf16[32,256,256]{2,1,0:T(8,128)(2,1)}), bf16[32,256,256]{2,1,0:T(8,128)(2,1)}, u32[]{:S(2)}, u32[]{:S(2)}) async-start(bf16[32,256,256]{2,1,0:T(8,128)(2,1)} %get-tuple-element.15), calls=%async_computation.1 | async-start | bytes 8388608 | tf_op jit(solution)/shard_map/all_to_all | solution.py:368
  220.0 23.2 %all-to-all-start.7 = ((bf16[8,8,32,256]{3,2,1,0:T(8,128)(2,1)}), bf16[8,8,32,256]{3,2,1,0:T(8,128)(2,1)S(1)}, u32[]{:S(2)}, u32[]{:S(2)}) async-start(bf16[8,8,32,256]{3,2,1,0:T(8,128)(2,1)} %pad_maximum_fusion), calls=%async_computation.7 | async-start | bytes 2097152 | tf_op jit(solution)/shard_map/all_to_all | solution.py:368
  243.3 14.3 %copy-start.2 = (bf16[8,8,32,256]{3,2,1,0:T(8,128)(2,1)}, bf16[8,8,32,256]{3,2,1,0:T(8,128)(2,1)S(1)}, u32[]{:S(2)}) copy-start(bf16[8,8,32,256]{3,2,1,0:T(8,128)(2,1)S(1)} %all-to-all-done.7.early_ref) | copy-start | bytes 3145732
  243.3 13.1 %all-to-all-start.2 = ((f32[8,64,256]{2,1,0:T(8,128)}), f32[8,64,256]{2,1,0:T(8,128)S(1)}, u32[]{:S(2)}, u32[]{:S(2)}) async-start(f32[8,64,256]{2,1,0:T(8,128)} %bitcast.60), calls=%async_computation.2 | async-start | bytes 1048576 | tf_op jit(solution)/shard_map/all_to_all | solution.py:368
  257.6 20.7 %all-to-all-start.8 = ((bf16[8,10,32,256]{3,2,1,0:T(8,128)(2,1)}), bf16[8,10,32,256]{3,2,1,0:T(8,128)(2,1)S(1)}, u32[]{:S(2)}, u32[]{:S(2)}) async-start(bf16[8,10,32,256]{3,2,1,0:T(8,128)(2,1)} %broadcast_in_dim.11), calls=%async_computation.8 | async-start | bytes 2621440 | tf_op jit(solution)/shard_map/all_to_all | solution.py:368
  262.2 17.8 %copy-start.3 = (f32[4,64,256]{2,1,0:T(8,128)}, f32[4,64,256]{2,1,0:T(8,128)S(1)}, u32[]{:S(2)}) copy-start(f32[4,64,256]{2,1,0:T(8,128)S(1)} %slice.52) | copy-start | bytes 786436
  278.2 1.8 copy-start.1
  280.0 36.8 %all-to-all-start.3 = ((f32[8,4,64,256]{3,2,1,0:T(8,128)}), f32[8,4,64,256]{3,2,1,0:T(8,128)S(1)}, u32[]{:S(2)}, u32[]{:S(2)}) async-start(f32[8,4,64,256]{3,2,1,0:T(8,128)} %broadcast_in_dim.8), calls=%async_computation.3 | async-start | bytes 4194304 | tf_op jit(solution)/shard_map/all_to_all | solution.py:368
  284.7 1.6 collective-permute-start
  316.8 2.0 copy-start
  318.8 67.5 %all-to-all-start.4 = ((f32[8,4,64,256]{3,2,1,0:T(8,128)}), f32[8,4,64,256]{3,2,1,0:T(8,128)}, u32[]{:S(2)}, u32[]{:S(2)}) async-start(f32[8,4,64,256]{3,2,1,0:T(8,128)} %broadcast_in_dim.9), calls=%async_computation.4 | async-start | bytes 4194304 | tf_op jit(solution)/shard_map/all_to_all | solution.py:368

commit v2 on v1

--- a/solution.py
+++ b/solution.py
@@ -8,6 +8,7 @@
 LEAD_TILES = 4
 BLOCK = 128
 STRIP = 8
+FIRST_STEPS = 4
 VMEM_BYTES = 56 * 1024 * 1024
 
 
@@ -43,7 +44,9 @@
     capacity = max(2, -(-slots // (n_front * n_row)))
     buckets = n_front * n_row * capacity
 
-    def kernel(front_ref, row_ref, col_ref, live_ref, tiles_ref, packed_ref, targets_ref, counts, sems):
+    def kernel(
+        front_ref, row_ref, col_ref, live_ref, tiles_ref, packed_ref, targets_ref, counts, bucket_of, stage, sems_in, sems_out
+    ):
         live = live_ref[0]
 
         def clear(i, carry):
@@ -58,8 +61,11 @@
 
         lax.fori_loop(0, n_front * n_row, clear_counts, 0)
 
-        def copy(slot, bucket):
-            return pltpu.make_async_copy(tiles_ref.at[slot], packed_ref.at[bucket], sems.at[slot])
+        def fetch(slot, bucket):
+            return pltpu.make_async_copy(tiles_ref.at[slot], stage.at[bucket], sems_in.at[slot])
+
+        def store(slot, bucket):
+            return pltpu.make_async_copy(stage.at[bucket], packed_ref.at[bucket], sems_out.at[slot])
 
         def send(slot, carry):
             row, col = row_ref[slot], col_ref[slot]
@@ -68,16 +74,25 @@
             counts[destination] = position + 1
             bucket = destination * capacity + position
             targets_ref[bucket] = lax.div(row, n_row) * tile_cols + lax.div(col, n_col)
-            copy(slot, bucket).start()
+            bucket_of[slot] = bucket
+            fetch(slot, bucket).start()
             return carry
 
         lax.fori_loop(0, live, send, 0)
 
-        def finish(slot, carry):
-            copy(slot, 0).wait()
-            return carry
-
-        lax.fori_loop(0, live, finish, 0)
+        def forward(slot, carry):
+            bucket = bucket_of[slot]
+            fetch(slot, bucket).wait()
+            store(slot, bucket).start()
+            return carry
+
+        lax.fori_loop(0, live, forward, 0)
+
+        def drain(slot, carry):
+            store(slot, bucket_of[slot]).wait()
+            return carry
+
+        lax.fori_loop(0, live, drain, 0)
 
     return pl.pallas_call(
         kernel,
@@ -88,15 +103,47 @@
         ),
         in_specs=[smem()] * 4 + [hbm()],
         out_specs=(hbm(), smem()),
-        scratch_shapes=[pltpu.SMEM((n_front * n_row,), jnp.int32), pltpu.SemaphoreType.DMA((slots,))],
+        scratch_shapes=[
+            pltpu.SMEM((n_front * n_row,), jnp.int32),
+            pltpu.SMEM((slots,), jnp.int32),
+            pltpu.VMEM((buckets, size, size), contributions.dtype),
+            pltpu.SemaphoreType.DMA((slots,)),
+            pltpu.SemaphoreType.DMA((slots,)),
+        ],
+        compiler_params=pltpu.CompilerParams(vmem_limit_bytes=VMEM_BYTES),
     )(target_front, target_row, target_col, live_count, contributions)
 
 
+SCALE_ROWS = 8
+SCALE_STEPS = 64
+
+
+def encode(values):
+    n, m = values.shape
+    top = jnp.max(jnp.abs(values), axis=1, keepdims=True)
+    code = jnp.floor(jnp.log2(jnp.maximum(top, 2.0**-110)) * SCALE_STEPS) + 1.0
+    coded = jnp.round(values * jnp.exp2(15.0 - 1e-3 - code / SCALE_STEPS))
+    picked = lax.broadcasted_iota(jnp.int32, (n, m), 0) == lax.broadcasted_iota(jnp.int32, (n, m), 1)
+    line = jnp.sum(jnp.where(picked, code, 0.0), axis=0, keepdims=True)
+    lines = jnp.broadcast_to(line, (SCALE_ROWS, m))
+    return jnp.concatenate([coded, lines], axis=0).astype(jnp.int32).astype(jnp.int16)
+
+
+def decode(coded):
+    wide = coded.astype(jnp.int32).astype(jnp.float32)
+    n, m = wide.shape[0] - SCALE_ROWS, wide.shape[1]
+    values, line = wide[:n], wide[n : n + 1]
+    picked = lax.broadcasted_iota(jnp.int32, (n, m), 0) == lax.broadcasted_iota(jnp.int32, (n, m), 1)
+    code = jnp.sum(jnp.where(picked, jnp.broadcast_to(line, (n, m)), 0.0), axis=1, keepdims=True)
+    return values * jnp.exp2(code / SCALE_STEPS - 15.0 + 1e-3)
+
+
 EXTENDED = ((1, 0), (1, 1), (2, 0), (2, 1), (2, 2))
 
 
-def assemble(received, arrived, front):
+def assemble(received, arrived, front, chunks):
     total, size, _ = received.shape
+    thin = 2 * size // chunks
 
     def kernel(arrived_ref, received_ref, front_ref, ext_ref, panel_ref, landed, sems):
         def copy(i):
@@ -125,15 +172,16 @@
             return carry
 
         lax.fori_loop(0, total, add, 0)
-        panel_ref[0:size] = ext_ref[0]
-        panel_ref[size : 2 * size] = ext_ref[2]
+        for chunk in range(chunks):
+            start = chunk * thin
+            panel_ref[chunk] = encode(ext_ref[2 * (start // size), pl.ds(start % size, thin), :])
 
     return pl.pallas_call(
         kernel,
         name="assemble",
         out_shape=(
             jax.ShapeDtypeStruct((len(EXTENDED), size, size), jnp.float32),
-            jax.ShapeDtypeStruct((2 * size, size), jnp.float32),
+            jax.ShapeDtypeStruct((chunks, thin + SCALE_ROWS, size), jnp.int16),
         ),
         in_specs=[smem(), hbm(), vmem()],
         out_specs=(vmem(), vmem()),
@@ -184,36 +232,63 @@
 HIGHEST = lax.Precision.HIGHEST
 
 
-def factorize(lead, ids, size):
+def eliminate(full, inverses, work, blocks):
+    order = full.shape[0]
+    r = lax.broadcasted_iota(jnp.int32, (BLOCK, BLOCK), 0)
+    c = lax.broadcasted_iota(jnp.int32, (BLOCK, BLOCK), 1)
+    for k in blocks:
+        s, e = k * BLOCK, (k + 1) * BLOCK
+        work[...] = full[s:e, s:e]
+        factor_block(work)
+        done = work[...]
+        diagonal = jnp.where(r == c, done, 0.0)
+        root = lax.rsqrt(jnp.sum(diagonal, axis=1, keepdims=True))
+        inverse = jnp.where(r >= c, done, 0.0) * root * (1.0 / jnp.sum(diagonal, axis=0, keepdims=True))
+        inverses[k] = inverse
+        full[s:e, s:e] = (jnp.where(r <= c, done, 0.0) * root).T
+        if e < order:
+            panel = nt(full[e:order, s:e], inverse, HIGHEST)
+            full[e:order, s:e] = panel
+            for o in range(e, order, BLOCK):
+                full[o:order, o : o + BLOCK] = full[o:order, o : o + BLOCK] - nt(
+                    panel[o - e :], panel[o - e : o - e + BLOCK], HIGHEST
+                )
+
+
+PAIRS = tuple((i, j) for i in range(LEAD_TILES) for j in range(i + 1))
+
+
+def factorize_first(lead, size, blocks):
     order = LEAD_TILES * size
-    pairs = [(i, j) for i in range(LEAD_TILES) for j in range(i + 1)]
-    blocks = order // BLOCK
-
-    def kernel(ids_ref, lead_ref, high_ref, low_ref, inv_high_ref, inv_low_ref, own_ref, full, inverses, work):
-        r = lax.broadcasted_iota(jnp.int32, (BLOCK, BLOCK), 0)
-        c = lax.broadcasted_iota(jnp.int32, (BLOCK, BLOCK), 1)
-        for number, (i, j) in enumerate(pairs):
+
+    def kernel(lead_ref, full, inverses, work):
+        for number, (i, j) in enumerate(PAIRS):
             full[i * size : (i + 1) * size, j * size : (j + 1) * size] = (
                 lead_ref[:, number].astype(jnp.float32).reshape(size, size)
             )
-        for k in range(blocks):
-            s, e = k * BLOCK, (k + 1) * BLOCK
-            work[...] = full[s:e, s:e]
-            factor_block(work)
-            done = work[...]
-            diagonal = jnp.where(r == c, done, 0.0)
-            root = lax.rsqrt(jnp.sum(diagonal, axis=1, keepdims=True))
-            inverse = jnp.where(r >= c, done, 0.0) * root * (1.0 / jnp.sum(diagonal, axis=0, keepdims=True))
-            inverses[k] = inverse
-            full[s:e, s:e] = (jnp.where(r <= c, done, 0.0) * root).T
-            if e < order:
-                panel = nt(full[e:order, s:e], inverse, HIGHEST)
-                full[e:order, s:e] = panel
-                for j in range(k + 1, blocks):
-                    o = j * BLOCK
-                    full[o:order, o : o + BLOCK] = full[o:order, o : o + BLOCK] - nt(
-                        panel[o - e :], panel[o - e : o - e + BLOCK], HIGHEST
-                    )
+        eliminate(full, inverses, work, blocks)
+
+    return pl.pallas_call(
+        kernel,
+        name="factorize_first",
+        out_shape=(
+            jax.ShapeDtypeStruct((order, order), jnp.float32),
+            jax.ShapeDtypeStruct((order // BLOCK, BLOCK, BLOCK), jnp.float32),
+        ),
+        in_specs=[vmem()],
+        out_specs=(vmem(),) * 2,
+        scratch_shapes=[pltpu.VMEM((BLOCK, BLOCK), jnp.float32)],
+        compiler_params=pltpu.CompilerParams(vmem_limit_bytes=VMEM_BYTES),
+    )(lead)
+
+
+def factorize_last(begun, begun_inverses, ids, size, blocks):
+    order = LEAD_TILES * size
+
+    def kernel(ids_ref, begun_ref, begun_inv_ref, high_ref, low_ref, inv_high_ref, inv_low_ref, own_ref, full, inverses, work):
+        full[...] = begun_ref[...]
+        inverses[...] = begun_inv_ref[...]
+        eliminate(full, inverses, work, blocks)
         half = size // BLOCK
         for q in range(LEAD_TILES):
             s = q * size
@@ -231,7 +306,7 @@
                 high, low = split(part)
                 inv_high_ref[q, y * BLOCK : (y + 1) * BLOCK, x * BLOCK : (x + 1) * BLOCK] = high
                 inv_low_ref[q, y * BLOCK : (y + 1) * BLOCK, x * BLOCK : (x + 1) * BLOCK] = low
-        for number, (i, j) in enumerate(pairs):
+        for i, j in PAIRS:
             tile = full[i * size : (i + 1) * size, j * size : (j + 1) * size]
             high, low = split(tile)
             high_ref[i * size : (i + 1) * size, j * size : (j + 1) * size] = high
@@ -245,17 +320,17 @@
     inv = jax.ShapeDtypeStruct((LEAD_TILES, size, size), jnp.bfloat16)
     return pl.pallas_call(
         kernel,
-        name="factorize",
+        name="factorize_last",
         out_shape=(wide, wide, inv, inv, jax.ShapeDtypeStruct((size, size), jnp.float32)),
-        in_specs=[smem(), vmem()],
+        in_specs=[smem(), vmem(), vmem()],
         out_specs=(vmem(),) * 5,
         scratch_shapes=[
             pltpu.VMEM((order, order), jnp.float32),
-            pltpu.VMEM((blocks, BLOCK, BLOCK), jnp.float32),
+            pltpu.VMEM((order // BLOCK, BLOCK, BLOCK), jnp.float32),
             pltpu.VMEM((BLOCK, BLOCK), jnp.float32),
         ],
         compiler_params=pltpu.CompilerParams(vmem_limit_bytes=VMEM_BYTES),
-    )(ids, lead)
+    )(ids, begun, begun_inverses)
 
 
 def finish(ids, rows, cols, early, factors, own, extended, front):
@@ -281,8 +356,8 @@
             s, e = q * size, (q + 1) * size
             acc = jnp.concatenate(
                 [
-                    rows_ref[:, q].reshape(2 * size, size),
-                    cols_ref[:, q].reshape(2 * size, size),
+                    *[decode(rows_ref[k, q]) for k in range(rows_ref.shape[0])],
+                    *[decode(cols_ref[k, q]) for k in range(cols_ref.shape[0])],
                     early_ref[:, q].astype(jnp.float32).reshape(size, size),
                     early_ref[:, LEAD_TILES + q].astype(jnp.float32).reshape(size, size),
                 ],
@@ -395,15 +470,19 @@
     lead = gather(lower, "col")
     aimed = jnp.concatenate([jnp.broadcast_to(chunk[None], leading.shape), leading], axis=1)
     early = exchange(aimed, "col")
-    *factors, own = factorize(lead, ids, size)
-
-    extended, panel = assemble(received, arrived, front)
-    mine = exchange(panel.reshape(n_col, 2 * size // n_col, size), "col")[:LEAD_TILES]
+    steps = LEAD_TILES * size // BLOCK
+    begun, inverses = factorize_first(lead, size, range(FIRST_STEPS))
+    arrived, begun = lax.optimization_barrier((arrived, begun))
+
+    extended, panel = assemble(received, arrived, front, n_col)
+    mine = exchange(panel, "col")[:LEAD_TILES]
     rows = gather(mine, "col")
     turned = lax.ppermute(
         mine, ("row", "col"), [(r * n_col + c, c * n_col + r) for r in range(n_row) for c in range(n_col)]
     )
+    turned, begun = lax.optimization_barrier((turned, begun))
     cols = gather(turned, "row")
+    *factors, own = factorize_last(begun, inverses, ids, size, range(FIRST_STEPS, steps))
     factor = finish(ids, rows, cols, early, factors, own, extended, front)
     return factor.reshape(1, tile_rows, 1, size, tile_cols, 1, size)
 

time: 407 us -> 241 us (0.59)
  Pallas kernels: 212 us -> 91.7 us
  waiting for transfers between devices: 115 us -> 56.3 us
  blocking collectives: 14.5 us -> 34.4 us
  starting transfers between devices: 51.9 us -> 45.9 us
    pallas_call x1, Pallas kernels: 130 us -> 5.38 us  [pack(): pl.pallas_call(kernel, name='pack', out_shape=(jax.ShapeDtypeStruct((buck...]
    all_to_all x8 -> x7, waiting for transfers between devices: 115 us -> 56.3 us  [exchange(): return lax.all_to_all(value, axis, split_axis=0, concat_axis=0, tiled=True)]
    all_to_all x1 -> x2, blocking collectives: 14.5 us -> 34.4 us  [exchange(): return lax.all_to_all(value, axis, split_axis=0, concat_axis=0, tiled=True)]
    all_to_all x8 -> x7, starting transfers between devices: 50.3 us -> 45.2 us  [exchange(): return lax.all_to_all(value, axis, split_axis=0, concat_axis=0, tiled=True)]
    pallas_call x1 -> x2, Pallas kernels: 57.4 us -> 61.5 us  [the longest x1 32.2 us: factorize_first(): pl.pallas_call(kernel, name='factorize_first', out_shape=(jax.ShapeDtypeS...]
  transfers between devices with their start and end apart: 9 -> 8, of which waited for: 6 -> 6; matrix products, arithmetic and copies ran while one was open for 1% -> 2% of each run, Pallas kernels for 47% -> 28%
where the time goes in v2:
time: 241 us
  Pallas kernels  91.7 us (38%)
  waiting for transfers between devices  56.3 us (23%)
  starting transfers between devices  45.9 us (19%)
  blocking collectives  34.4 us (14%)
  local copies, waits for them, and re-layouts  8.28 us (3%)
  other arithmetic  3.35 us (1%)
    all_to_all x7, waiting for transfers between devices, exchange(): return lax.all_to_all(value, axis, split_axis=0, concat_axis=0, tiled=True)  56.3 us
    all_to_all x7, starting transfers between devices, exchange(): return lax.all_to_all(value, axis, split_axis=0, concat_axis=0, tiled=True)  45.2 us
    all_to_all x2, blocking collectives, exchange(): return lax.all_to_all(value, axis, split_axis=0, concat_axis=0, tiled=True)  34.4 us
    pallas_call x1, Pallas kernels, factorize_first(): pl.pallas_call(kernel, name='factorize_first', out_shape=(jax.ShapeDtypeS...  32.2 us
    pallas_call x1, Pallas kernels, factorize_last(): pl.pallas_call(kernel, name='factorize_last', out_shape=(wide, wide, inv,...  29.3 us
    pallas_call x1, Pallas kernels, finish(): pl.pallas_call(kernel, name='finish', out_shape=jax.ShapeDtypeStruct((til...  20 us
    pallas_call x1, Pallas kernels, pack(): pl.pallas_call(kernel, name='pack', out_shape=(jax.ShapeDtypeStruct((buck...  5.38 us
    pallas_call x1, Pallas kernels, assemble(): pl.pallas_call(kernel, name='assemble', out_shape=(jax.ShapeDtypeStruct((...  4.84 us
  transfers between devices with their start and end apart: 8, of which 6 were waited for; matrix products, arithmetic and copies ran while one was open for 2% of the time, Pallas kernels for 28%

profile of v2, /device:TPU:6, one launch (start us, length us, event | category | flops | bytes accessed | tf_op | source)
XLA Modules:
  0.0 240.7 jit_solution(15480655623655401390)
XLA Ops:
  0.0 0.9 slice.52
  0.9 12.0 %all_to_all.52 = bf16[8,32,256]{2,1,0:T(8,128)(2,1)S(1)} all-to-all(bf16[8,32,256]{2,1,0:T(8,128)(2,1)S(1)} %bitcast.59), channel_id=1, replica_groups=mesh['front'=2,'row'=8,'col'=8] {'col'}, dimensions={0} | all-to-all | bytes 262144 | tf_op jit(solution)/shard_map/all_to_all | solution.py:443
  12.9 0.9 broadcast_in_dim.8
  13.8 7.4 %all-to-all-start.2 = ((bf16[8,4,32,256]{3,2,1,0:T(8,128)(2,1)}), bf16[8,4,32,256]{3,2,1,0:T(8,128)(2,1)S(1)}, u32[]{:S(2)}, u32[]{:S(2)}) async-start(bf16[8,4,32,256]{3,2,1,0:T(8,128)(2,1)} %broadcast_in_dim.8), calls=%async_computation.2 | async-start | bytes 1048576 | tf_op jit(solution)/shard_map/all_to_all | solution.py:443
  21.9 5.4 %pack.1 = (bf16[32,256,256]{2,1,0:T(8,128)(2,1)}, s32[32]{0:T(128)}) custom-call(s32[32]{0:T(128)} %bitcast.60, s32[32]{0:T(128)} %bitcast.61, s32[32]{0:T(128)} %bitcast.62, s32[1]{0:T(128)} %bitcast.54.live_ref, bf16[32,256,256]{2,1,0:T(8,128)(2,1)} %bitcast.58), custom_call_target="tpu_custom_call" | custom-call | tf_op jit(solution)/shard_map/pack/pallas_call | solution.py:97
  27.3 1.4 all_to_all.32
  28.6 0.1 all-to-all-done.2
  28.7 6.8 %all-to-all-start = ((s32[16,2,1]{1,2,0:T(1,128)}), s32[16,2,1]{1,2,0:T(1,128)S(1)}, u32[]{:S(2)}, u32[]{:S(2)}) async-start(s32[16,2,1]{1,2,0:T(1,128)} %bitcast.7), calls=%async_computation | async-start | bytes 16384 | tf_op jit(solution)/shard_map/all_to_all | solution.py:443
  35.7 4.6 %all-to-all-done = s32[16,2,1]{1,2,0:T(1,128)S(1)} async-done(((s32[16,2,1]{1,2,0:T(1,128)}), s32[16,2,1]{1,2,0:T(1,128)S(1)}, u32[]{:S(2)}, u32[]{:S(2)}) %all-to-all-start) | async-done | bytes 160 | tf_op jit(solution)/shard_map/all_to_all | solution.py:443
  40.3 0.1 broadcast_in_dim.9
  40.4 22.4 %all_to_all.53.lead_ref = bf16[8,10,32,256]{3,2,1,0:T(8,128)(2,1)} all-to-all(bf16[8,10,32,256]{3,2,1,0:T(8,128)(2,1)S(1)} %broadcast_in_dim.9), channel_id=1, replica_groups=mesh['front'=2,'row'=8,'col'=8] {'col'}, dimensions={0} | all-to-all | bytes 2621440 | tf_op jit(solution)/shard_map/all_to_all | solution.py:443
  62.8 7.8 %all-to-all-start.4 = ((bf16[32,256,256]{2,1,0:T(8,128)(2,1)}), bf16[32,256,256]{2,1,0:T(8,128)(2,1)}, u32[]{:S(2)}, u32[]{:S(2)}) async-start(bf16[32,256,256]{2,1,0:T(8,128)(2,1)} %get-tuple-element.23), calls=%async_computation.4 | async-start | bytes 8388608 | tf_op jit(solution)/shard_map/all_to_all | solution.py:443
  70.7 0.5 broadcast.7
  71.2 0.7 reduce.3
  71.9 0.6 all_to_all.34.arrived_ref
  72.5 32.2 %factorize_first.1 = (f32[1024,1024]{1,0:T(8,128)}, f32[8,128,128]{2,1,0:T(8,128)}) custom-call(bf16[8,10,32,256]{3,2,1,0:T(8,128)(2,1)} %all_to_all.53.lead_ref), custom_call_target="tpu_custom_call" | custom-call | tf_op jit(solution)/shard_map/factorize_first/pallas_call | solution.py:271
  104.7 14.6 %all-to-all-done.4.received_ref = bf16[32,256,256]{2,1,0:T(8,128)(2,1)} async-done(((bf16[32,256,256]{2,1,0:T(8,128)(2,1)}), bf16[32,256,256]{2,1,0:T(8,128)(2,1)}, u32[]{:S(2)}, u32[]{:S(2)}) %all-to-all-start.4) | async-done | bytes 4194336 | tf_op jit(solution)/shard_map/all_to_all | solution.py:443
  119.3 4.8 %assemble.1 = (f32[5,256,256]{2,1,0:T(8,128)}, s16[8,72,256]{2,1,0:T(8,128)(2,1)}) custom-call(s32[32]{0:T(128)} %all_to_all.34.arrived_ref, bf16[32,256,256]{2,1,0:T(8,128)(2,1)} %all-to-all-done.4.received_ref, bf16[3,3,256,256]{3,2,1,0:T(8,128)(2,1)} %bitcast.56), custom_call_target="tpu_custom_call" | custom-call | tf_op jit(solution)/shard_map/assemble/pallas_call | solution.py:179
  124.1 4.0 %all-to-all-start.5 = ((s16[8,72,256]{2,1,0:T(8,128)(2,1)}), s16[8,72,256]{2,1,0:T(8,128)(2,1)S(1)}, u32[]{:S(2)}, u32[]{:S(2)}) async-start(s16[8,72,256]{2,1,0:T(8,128)(2,1)} %get-tuple-element.24), calls=%async_computation.5 | async-start | bytes 589824 | tf_op jit(solution)/shard_map/all_to_all | solution.py:443
  128.2 2.1 pad_maximum_fusion
  130.3 5.1 %all-to-all-done.5 = s16[8,72,256]{2,1,0:T(8,128)(2,1)S(1)} async-done(((s16[8,72,256]{2,1,0:T(8,128)(2,1)}), s16[8,72,256]{2,1,0:T(8,128)(2,1)S(1)}, u32[]{:S(2)}, u32[]{:S(2)}) %all-to-all-start.5) | async-done | bytes 294944 | tf_op jit(solution)/shard_map/all_to_all | solution.py:443
  135.3 4.6 %all-to-all-start.8 = ((bf16[8,8,32,256]{3,2,1,0:T(8,128)(2,1)}), bf16[8,8,32,256]{3,2,1,0:T(8,128)(2,1)S(1)}, u32[]{:S(2)}, u32[]{:S(2)}) async-start(bf16[8,8,32,256]{3,2,1,0:T(8,128)(2,1)} %pad_maximum_fusion), calls=%async_computation.8 | async-start | bytes 2097152 | tf_op jit(solution)/shard_map/all_to_all | solution.py:443
  140.0 14.4 %all-to-all-done.8.early_ref = bf16[8,8,32,256]{3,2,1,0:T(8,128)(2,1)S(1)} async-done(((bf16[8,8,32,256]{3,2,1,0:T(8,128)(2,1)}), bf16[8,8,32,256]{3,2,1,0:T(8,128)(2,1)S(1)}, u32[]{:S(2)}, u32[]{:S(2)}) %all-to-all-start.8) | async-done | bytes 1048608 | tf_op jit(solution)/shard_map/all_to_all | solution.py:443
  154.3 0.0 copy-start.2
  154.3 1.2 broadcast_in_dim.10
  155.5 0.2 copy-done.2
  155.7 4.6 %all-to-all-start.6 = ((s16[8,4,72,256]{3,2,1,0:T(8,128)(2,1)}), s16[8,4,72,256]{3,2,1,0:T(8,128)(2,1)S(1)}, u32[]{:S(2)}, u32[]{:S(2)}) async-start(s16[8,4,72,256]{3,2,1,0:T(8,128)(2,1)} %broadcast_in_dim.10), calls=%async_computation.6 | async-start | bytes 2359296 | tf_op jit(solution)/shard_map/all_to_all | solution.py:443
  160.4 0.7 collective-permute-start
  161.0 0.0 collective-permute-done
  161.0 17.6 %all-to-all-done.6.rows_ref = s16[8,4,72,256]{3,2,1,0:T(8,128)(2,1)S(1)} async-done(((s16[8,4,72,256]{3,2,1,0:T(8,128)(2,1)}), s16[8,4,72,256]{3,2,1,0:T(8,128)(2,1)S(1)}, u32[]{:S(2)}, u32[]{:S(2)}) %all-to-all-start.6) | async-done | bytes 1179680 | tf_op jit(solution)/shard_map/all_to_all | solution.py:443
  178.6 0.0 copy-start
  178.6 1.2 broadcast_in_dim.11
  179.8 0.2 copy-done
  180.0 9.8 %all-to-all-start.7 = ((s16[8,4,72,256]{3,2,1,0:T(8,128)(2,1)}), s16[8,4,72,256]{3,2,1,0:T(8,128)(2,1)S(1)}, u32[]{:S(2)}, u32[]{:S(2)}) async-start(s16[8,4,72,256]{3,2,1,0:T(8,128)(2,1)} %broadcast_in_dim.11), calls=%async_computation.7 | async-start | bytes 2359296 | tf_op jit(solution)/shard_map/all_to_all | solution.py:443
  189.8 0.6 pad_add_fusion.ids_ref
  190.4 29.3 %factorize_last.1 = (bf16[1024,1024]{1,0:T(8,128)(2,1)}, bf16[1024,1024]{1,0:T(8,128)(2,1)}, bf16[4,256,256]{2,1,0:T(8,128)(2,1)}, bf16[4,256,256]{2,1,0:T(8,128)(2,1)}, f32[256,256]{1,0:T(8,128)}) custom-call(s32[2]{0:T(128)} %pad_add_fusion.ids_ref, f32[1024,1024]{1,0:T(8,128)} %get-tuple-element.27.begun_ref, f32[8,128,128]{2,1,0:T(8,128)} %get-tuple-element.28.begun_inv_ref), custom_call_target="tpu_custom_call" | custom-call | tf_op jit(solution)/shard_map/factorize_last/pallas_call | solution.py:321
  219.6 0.0 all-to-all-done.7.cols_ref
  219.7 0.0 copy-start.1
  219.7 1.1 copy-done.1
  220.7 20.0 %finish.1 = f32[4608,128]{1,0:T(8,128)} custom-call(s32[2]{0:T(128)} %pad_add_fusion.ids_ref, s16[8,4,72,256]{3,2,1,0:T(8,128)(2,1)} %copy-done, s16[8,4,72,256]{3,2,1,0:T(8,128)(2,1)} %copy-done.1, bf16[8,8,32,256]{3,2,1,0:T(8,128)(2,1)} %copy-done.2, bf16[1024,1024]{1,0:T(8,128)(2,1)} %get-tuple-element.29.high_ref, ...), custom_call_target="tpu_custom_call" | custom-call | tf_op jit(solution)/shard_map/finish/pallas_call | solution.py:427
  (12 shorter events, 0.1 us)
Async XLA Ops:
  13.8 15.0 %all-to-all-start.2 = ((bf16[8,4,32,256]{3,2,1,0:T(8,128)(2,1)}), bf16[8,4,32,256]{3,2,1,0:T(8,128)(2,1)S(1)}, u32[]{:S(2)}, u32[]{:S(2)}) async-start(bf16[8,4,32,256]{3,2,1,0:T(8,128)(2,1)} %broadcast_in_dim.8), calls=%async_computation.2 | async-start | bytes 1048576 | tf_op jit(solution)/shard_map/all_to_all | solution.py:443
  28.7 11.5 %all-to-all-start = ((s32[16,2,1]{1,2,0:T(1,128)}), s32[16,2,1]{1,2,0:T(1,128)S(1)}, u32[]{:S(2)}, u32[]{:S(2)}) async-start(s32[16,2,1]{1,2,0:T(1,128)} %bitcast.7), calls=%async_computation | async-start | bytes 16384 | tf_op jit(solution)/shard_map/all_to_all | solution.py:443
  62.8 56.5 %all-to-all-start.4 = ((bf16[32,256,256]{2,1,0:T(8,128)(2,1)}), bf16[32,256,256]{2,1,0:T(8,128)(2,1)}, u32[]{:S(2)}, u32[]{:S(2)}) async-start(bf16[32,256,256]{2,1,0:T(8,128)(2,1)} %get-tuple-element.23), calls=%async_computation.4 | async-start | bytes 8388608 | tf_op jit(solution)/shard_map/all_to_all | solution.py:443
  124.1 11.2 %all-to-all-start.5 = ((s16[8,72,256]{2,1,0:T(8,128)(2,1)}), s16[8,72,256]{2,1,0:T(8,128)(2,1)S(1)}, u32[]{:S(2)}, u32[]{:S(2)}) async-start(s16[8,72,256]{2,1,0:T(8,128)(2,1)} %get-tuple-element.24), calls=%async_computation.5 | async-start | bytes 589824 | tf_op jit(solution)/shard_map/all_to_all | solution.py:443
  135.3 19.0 %all-to-all-start.8 = ((bf16[8,8,32,256]{3,2,1,0:T(8,128)(2,1)}), bf16[8,8,32,256]{3,2,1,0:T(8,128)(2,1)S(1)}, u32[]{:S(2)}, u32[]{:S(2)}) async-start(bf16[8,8,32,256]{3,2,1,0:T(8,128)(2,1)} %pad_maximum_fusion), calls=%async_computation.8 | async-start | bytes 2097152 | tf_op jit(solution)/shard_map/all_to_all | solution.py:443
  154.3 1.4 copy-start.2
  155.7 22.9 %all-to-all-start.6 = ((s16[8,4,72,256]{3,2,1,0:T(8,128)(2,1)}), s16[8,4,72,256]{3,2,1,0:T(8,128)(2,1)S(1)}, u32[]{:S(2)}, u32[]{:S(2)}) async-start(s16[8,4,72,256]{3,2,1,0:T(8,128)(2,1)} %broadcast_in_dim.10), calls=%async_computation.6 | async-start | bytes 2359296 | tf_op jit(solution)/shard_map/all_to_all | solution.py:443
  160.4 0.7 collective-permute-start
  178.6 1.4 copy-start
  180.0 39.6 %all-to-all-start.7 = ((s16[8,4,72,256]{3,2,1,0:T(8,128)(2,1)}), s16[8,4,72,256]{3,2,1,0:T(8,128)(2,1)S(1)}, u32[]{:S(2)}, u32[]{:S(2)}) async-start(s16[8,4,72,256]{3,2,1,0:T(8,128)(2,1)} %broadcast_in_dim.11), calls=%async_computation.7 | async-start | bytes 2359296 | tf_op jit(solution)/shard_map/all_to_all | solution.py:443
  219.7 1.1 copy-start.1

commit v3 on v2

--- a/solution.py
+++ b/solution.py
@@ -5,10 +5,12 @@
 from jax.experimental.pallas import tpu as pltpu
 from jax.sharding import PartitionSpec as P
 
+
 LEAD_TILES = 4
 BLOCK = 128
+RUN = 32
 STRIP = 8
-FIRST_STEPS = 4
+FIRST_STEPS = 6
 VMEM_BYTES = 56 * 1024 * 1024
 
 
@@ -39,79 +41,101 @@
     return nt(left[0], right[0]) + (nt(left[0], right[1]) + nt(left[1], right[0]))
 
 
-def pack(contributions, target_front, target_row, target_col, live_count, n_front, n_row, n_col, tile_cols):
-    slots, size, _ = contributions.shape
+def plan(target_front, target_row, target_col, live_count, n_front, n_row, n_col, tile_cols):
+    slots = target_front.shape[0]
     capacity = max(2, -(-slots // (n_front * n_row)))
     buckets = n_front * n_row * capacity
 
-    def kernel(
-        front_ref, row_ref, col_ref, live_ref, tiles_ref, packed_ref, targets_ref, counts, bucket_of, stage, sems_in, sems_out
-    ):
-        live = live_ref[0]
-
+    def kernel(front_ref, row_ref, col_ref, live_ref, targets_ref, bucket_ref, counts):
         def clear(i, carry):
             targets_ref[i] = -1
             return carry
 
         lax.fori_loop(0, buckets, clear, 0)
 
+        def clear_slots(i, carry):
+            bucket_ref[i] = -1
+            return carry
+
+        lax.fori_loop(0, slots, clear_slots, 0)
+
         def clear_counts(i, carry):
             counts[i] = 0
             return carry
 
         lax.fori_loop(0, n_front * n_row, clear_counts, 0)
 
-        def fetch(slot, bucket):
-            return pltpu.make_async_copy(tiles_ref.at[slot], stage.at[bucket], sems_in.at[slot])
-
-        def store(slot, bucket):
-            return pltpu.make_async_copy(stage.at[bucket], packed_ref.at[bucket], sems_out.at[slot])
-
-        def send(slot, carry):
+        def assign(slot, carry):
             row, col = row_ref[slot], col_ref[slot]
             destination = front_ref[slot] * n_row + lax.rem(row, n_row)
             position = counts[destination]
             counts[destination] = position + 1
             bucket = destination * capacity + position
             targets_ref[bucket] = lax.div(row, n_row) * tile_cols + lax.div(col, n_col)
-            bucket_of[slot] = bucket
-            fetch(slot, bucket).start()
-            return carry
-
-        lax.fori_loop(0, live, send, 0)
+            bucket_ref[slot] = bucket
+            return carry
+
+        lax.fori_loop(0, live_ref[0], assign, 0)
+
+    return pl.pallas_call(
+        kernel,
+        name="plan",
+        out_shape=(jax.ShapeDtypeStruct((buckets,), jnp.int32), jax.ShapeDtypeStruct((slots,), jnp.int32)),
+        in_specs=[smem()] * 4,
+        out_specs=(smem(), smem()),
+        scratch_shapes=[pltpu.SMEM((n_front * n_row,), jnp.int32)],
+    )(target_front, target_row, target_col, live_count)
+
+
+def move(contributions, bucket_of, buckets):
+    slots, size, _ = contributions.shape
+
+    def kernel(bucket_ref, tiles_ref, packed_ref, stage, sems_in, sems_out):
+        def fetch(slot):
+            return pltpu.make_async_copy(tiles_ref.at[slot], stage.at[slot], sems_in.at[slot])
+
+        def store(slot, bucket):
+            return pltpu.make_async_copy(stage.at[slot], packed_ref.at[bucket], sems_out.at[slot])
+
+        for slot in range(slots):
+            fetch(slot).start()
 
         def forward(slot, carry):
-            bucket = bucket_of[slot]
-            fetch(slot, bucket).wait()
-            store(slot, bucket).start()
-            return carry
-
-        lax.fori_loop(0, live, forward, 0)
+            fetch(slot).wait()
+            bucket = bucket_ref[slot]
+
+            @pl.when(bucket >= 0)
+            def _():
+                store(slot, bucket).start()
+
+            return carry
+
+        lax.fori_loop(0, slots, forward, 0)
 
         def drain(slot, carry):
-            store(slot, bucket_of[slot]).wait()
-            return carry
-
-        lax.fori_loop(0, live, drain, 0)
-
-    return pl.pallas_call(
-        kernel,
-        name="pack",
-        out_shape=(
-            jax.ShapeDtypeStruct((buckets, size, size), contributions.dtype),
-            jax.ShapeDtypeStruct((buckets,), jnp.int32),
-        ),
-        in_specs=[smem()] * 4 + [hbm()],
-        out_specs=(hbm(), smem()),
+            bucket = bucket_ref[slot]
+
+            @pl.when(bucket >= 0)
+            def _():
+                store(slot, bucket).wait()
+
+            return carry
+
+        lax.fori_loop(0, slots, drain, 0)
+
+    return pl.pallas_call(
+        kernel,
+        name="move",
+        out_shape=jax.ShapeDtypeStruct((buckets, size, size), contributions.dtype),
+        in_specs=[smem(), hbm()],
+        out_specs=hbm(),
         scratch_shapes=[
-            pltpu.SMEM((n_front * n_row,), jnp.int32),
-            pltpu.SMEM((slots,), jnp.int32),
-            pltpu.VMEM((buckets, size, size), contributions.dtype),
+            pltpu.VMEM((slots, size, size), contributions.dtype),
             pltpu.SemaphoreType.DMA((slots,)),
             pltpu.SemaphoreType.DMA((slots,)),
         ],
         compiler_params=pltpu.CompilerParams(vmem_limit_bytes=VMEM_BYTES),
-    )(target_front, target_row, target_col, live_count, contributions)
+    )(bucket_of, contributions)
 
 
 SCALE_ROWS = 8
@@ -143,9 +167,9 @@
 
 def assemble(received, arrived, front, chunks):
     total, size, _ = received.shape
-    thin = 2 * size // chunks
-
-    def kernel(arrived_ref, received_ref, front_ref, ext_ref, panel_ref, landed, sems):
+    thin = front.shape[0] * size // chunks
+
+    def kernel(arrived_ref, received_ref, front_ref, ext_ref, panel_ref, landed, column, sems):
         def copy(i):
             return pltpu.make_async_copy(received_ref.at[i], landed.at[i], sems.at[i])
 
@@ -172,9 +196,11 @@
             return carry
 
         lax.fori_loop(0, total, add, 0)
+        column[0:size] = front_ref[0, 0].astype(jnp.float32)
+        column[size : 2 * size] = ext_ref[0]
+        column[2 * size : 3 * size] = ext_ref[2]
         for chunk in range(chunks):
-            start = chunk * thin
-            panel_ref[chunk] = encode(ext_ref[2 * (start // size), pl.ds(start % size, thin), :])
+            panel_ref[chunk] = encode(column[chunk * thin : (chunk + 1) * thin, :])
 
     return pl.pallas_call(
         kernel,
@@ -185,7 +211,11 @@
         ),
         in_specs=[smem(), hbm(), vmem()],
         out_specs=(vmem(), vmem()),
-        scratch_shapes=[pltpu.VMEM((total, size, size), jnp.bfloat16), pltpu.SemaphoreType.DMA((total,))],
+        scratch_shapes=[
+            pltpu.VMEM((total, size, size), jnp.bfloat16),
+            pltpu.VMEM((3 * size, size), jnp.float32),
+            pltpu.SemaphoreType.DMA((total,)),
+        ],
         compiler_params=pltpu.CompilerParams(vmem_limit_bytes=VMEM_BYTES),
     )(arrived, received, front)
 
@@ -196,19 +226,18 @@
 
 
 def factor_block(work):
-    rows = lax.broadcasted_iota(jnp.int32, (BLOCK, BLOCK), 0)
     lanes = lax.broadcasted_iota(jnp.int32, (STRIP, BLOCK), 1)
     strip_rows = lax.broadcasted_iota(jnp.int32, (STRIP, BLOCK), 0)
 
     def spread(value, i):
         return jnp.broadcast_to(value[i : i + 1, :], value.shape)
 
-    def step(number, carry):
+    def step(number, top):
         base = pl.multiple_of(number * STRIP, STRIP)
         strip = work[pl.ds(base, STRIP), :]
         own = [pick_lane(strip, base + i) for i in range(STRIP)]
-        whole = work[...]
-        below = rows >= base + STRIP
+        whole = work[top:BLOCK, :]
+        below = lax.broadcasted_iota(jnp.int32, whole.shape, 0) + top >= base + STRIP
         columns = [jnp.where(below, pick_lane(whole, base + i), 0.0) for i in range(STRIP)]
         for i in range(STRIP):
             pivot = spread(own[i], i)
@@ -222,11 +251,12 @@
                 own[j] = own[j] - factors * entry
                 columns[j] = columns[j] - lower * jnp.broadcast_to(entry[0:1], whole.shape)
             whole = whole - lower * jnp.broadcast_to(line[0:1], whole.shape)
-        work[...] = whole
+        work[top:BLOCK, :] = whole
         work[pl.ds(base, STRIP), :] = strip
-        return carry
-
-    lax.fori_loop(0, BLOCK // STRIP, step, 0)
+        return top
+
+    for top in range(0, BLOCK, RUN):
+        lax.fori_loop(top // STRIP, (top + RUN) // STRIP, lambda number, carry: step(number, top) * 0 + carry, 0)
 
 
 HIGHEST = lax.Precision.HIGHEST
@@ -258,14 +288,17 @@
 PAIRS = tuple((i, j) for i in range(LEAD_TILES) for j in range(i + 1))
 
 
-def factorize_first(lead, size, blocks):
+def factorize_first(ids, lead, size, blocks):
     order = LEAD_TILES * size
 
-    def kernel(lead_ref, full, inverses, work):
-        for number, (i, j) in enumerate(PAIRS):
-            full[i * size : (i + 1) * size, j * size : (j + 1) * size] = (
-                lead_ref[:, number].astype(jnp.float32).reshape(size, size)
-            )
+    def kernel(place_ref, *refs):
+        *pieces, full, inverses, work = refs
+        for ref, inner, chunk in pair_pieces(pieces, place_ref[1]):
+            for number, (i, j) in enumerate(PAIRS):
+                tile = ref[inner, number].astype(jnp.float32)
+                thin = tile.shape[0]
+                start = pl.multiple_of(i * size + chunk * thin, thin)
+                full[pl.ds(start, thin), j * size : (j + 1) * size] = tile
         eliminate(full, inverses, work, blocks)
 
     return pl.pallas_call(
@@ -275,11 +308,11 @@
             jax.ShapeDtypeStruct((order, order), jnp.float32),
             jax.ShapeDtypeStruct((order // BLOCK, BLOCK, BLOCK), jnp.float32),
         ),
-        in_specs=[vmem()],
+        in_specs=[smem()] + [vmem()] * len(lead),
         out_specs=(vmem(),) * 2,
         scratch_shapes=[pltpu.VMEM((BLOCK, BLOCK), jnp.float32)],
         compiler_params=pltpu.CompilerParams(vmem_limit_bytes=VMEM_BYTES),
-    )(lead)
+    )(ids, *lead)
 
 
 def factorize_last(begun, begun_inverses, ids, size, blocks):
@@ -333,18 +366,42 @@
     )(ids, begun, begun_inverses)
 
 
-def finish(ids, rows, cols, early, factors, own, extended, front):
+def solve(panel, factors):
+    _, coded_rows, size = panel.shape
+    thin, order = coded_rows - SCALE_ROWS, LEAD_TILES * size
+
+    def kernel(panel_ref, high_ref, low_ref, ih_ref, il_ref, out_ref, xh, xl):
+        for q in range(LEAD_TILES):
+            s, e = q * size, (q + 1) * size
+            acc = decode(panel_ref[q])
+            if q:
+                acc = acc - nt3((xh[:, 0:s], xl[:, 0:s]), (high_ref[s:e, 0:s], low_ref[s:e, 0:s]))
+            x = nt3(split(acc), (ih_ref[q], il_ref[q]))
+            xh[:, s:e], xl[:, s:e] = split(x)
+            out_ref[q] = encode(x)
+
+    return pl.pallas_call(
+        kernel,
+        name="solve",
+        out_shape=jax.ShapeDtypeStruct((LEAD_TILES, coded_rows, size), jnp.int16),
+        in_specs=[vmem()] * 5,
+        out_specs=vmem(),
+        scratch_shapes=[pltpu.VMEM((thin, order), jnp.bfloat16)] * 2,
+        compiler_params=pltpu.CompilerParams(vmem_limit_bytes=VMEM_BYTES),
+    )(panel, *factors)
+
+
+def finish(ids, rows, cols, own, extended, front):
     size = own.shape[0]
     order = LEAD_TILES * size
     tile_rows, tile_cols = front.shape[:2]
     lanes = 128
     parts = size // lanes
-    total = 6 * size
-
-    def kernel(
-        ids_ref, rows_ref, cols_ref, early_ref, high_ref, low_ref, ih_ref, il_ref, own_ref, ext_ref, front_ref,
-        out_ref, xh, xl, panel,
-    ):
+    half = len(rows)
+
+    def kernel(ids_ref, *refs):
+        row_pieces, col_pieces = refs[:half], refs[half : 2 * half]
+        own_ref, ext_ref, front_ref, out_ref, xh, xl = refs[2 * half :]
         row, col = ids_ref[0], ids_ref[1]
 
         def put(a, b, tile):
@@ -352,52 +409,44 @@
                 start = (a * size * tile_cols + b) * parts + part
                 out_ref[pl.ds(start, size, stride=tile_cols * parts), :] = tile[:, part * lanes : (part + 1) * lanes]
 
-        for q in range(LEAD_TILES):
-            s, e = q * size, (q + 1) * size
-            acc = jnp.concatenate(
-                [
-                    *[decode(rows_ref[k, q]) for k in range(rows_ref.shape[0])],
-                    *[decode(cols_ref[k, q]) for k in range(cols_ref.shape[0])],
-                    early_ref[:, q].astype(jnp.float32).reshape(size, size),
-                    early_ref[:, LEAD_TILES + q].astype(jnp.float32).reshape(size, size),
-                ],
-                axis=0,
-            )
-            if q:
-                acc = acc - nt3((xh[:, 0:s], xl[:, 0:s]), (high_ref[s:e, 0:s], low_ref[s:e, 0:s]))
-            x = nt3(split(acc), (ih_ref[q], il_ref[q]))
-            high, low = split(x)
-            xh[:, s:e] = high
-            xl[:, s:e] = low
-
-            @pl.when(col == q)
-            def _():
-                panel[0 : 2 * size] = x[0 : 2 * size]
-                panel[2 * size :] = x[4 * size : 5 * size]
+        for pieces, place, first in ((row_pieces, col, 0), (col_pieces, row, tile_rows * size)):
+            for ref, inner, chunk in pair_pieces(pieces, place):
+                for q in range(LEAD_TILES):
+                    value = decode(ref[inner, q])
+                    thin = value.shape[0]
+                    start = pl.multiple_of(first + chunk * thin, 32)
+                    high, low = split(value)
+                    xh[pl.ds(start, thin), q * size : (q + 1) * size] = high
+                    xl[pl.ds(start, thin), q * size : (q + 1) * size] = low
+
+        def take(ref, n):
+            return ref[n * size : (n + 1) * size, :]
+
+        def update(a, b, base):
+            x, y = a, tile_rows + b
+            put(a, b, base - nt3((take(xh, x), take(xl, x)), (take(xh, y), take(xl, y))))
+
+        def put_panel(a):
+            for q in range(LEAD_TILES):
+
+                @pl.when(col == q)
+                def _():
+                    high = xh[a * size : (a + 1) * size, q * size : (q + 1) * size].astype(jnp.float32)
+                    low = xl[a * size : (a + 1) * size, q * size : (q + 1) * size].astype(jnp.float32)
+                    put(a, 0, high + low)
 
         zero = jnp.zeros((size, size), jnp.float32)
         for a, b in ((0, 1), (0, 2), (1, 2)):
             put(a, b, zero)
-
-        def update(a, b, base, x, y):
-            def take(ref, n):
-                return ref[n * size : (n + 1) * size, :]
-
-            put(a, b, base - nt3((take(xh, x), take(xl, x)), (take(xh, y), take(xl, y))))
-
         in_panel = col < LEAD_TILES
-
-        @pl.when(in_panel)
-        def _():
-            put(1, 0, panel[0:size])
-            put(2, 0, panel[size : 2 * size])
+        lead_row = row < LEAD_TILES
+        put_panel(1)
+        put_panel(2)
 
         @pl.when(jnp.logical_not(in_panel))
         def _():
-            update(1, 0, ext_ref[0], 0, 5)
-            update(2, 0, ext_ref[2], 1, 5)
-
-        lead_row = row < LEAD_TILES
+            update(1, 0, ext_ref[0])
+            update(2, 0, ext_ref[2])
 
         @pl.when(row < col)
         def _():
@@ -411,41 +460,56 @@
             def _():
                 put(0, 0, own_ref[...])
 
-            @pl.when(jnp.logical_not(lead_row) & in_panel)
-            def _():
-                put(0, 0, panel[2 * size :])
+            @pl.when(jnp.logical_not(lead_row))
+            def _():
+                put_panel(0)
 
             @pl.when(jnp.logical_not(in_panel))
             def _():
-                update(0, 0, front_ref[0, 0].astype(jnp.float32), 4, 5)
-
-            update(1, 1, ext_ref[1], 0, 2)
-            update(2, 2, ext_ref[4], 1, 3)
-
-        update(2, 1, ext_ref[3], 1, 2)
+                update(0, 0, front_ref[0, 0].astype(jnp.float32))
+
+            update(1, 1, ext_ref[1])
+            update(2, 2, ext_ref[4])
+
+        update(2, 1, ext_ref[3])
 
     return pl.pallas_call(
         kernel,
         name="finish",
         out_shape=jax.ShapeDtypeStruct((tile_rows * size * tile_cols * parts, lanes), jnp.float32),
-        in_specs=[smem()] + [vmem()] * 10,
+        in_specs=[smem()] + [vmem()] * (2 * half + 3),
         out_specs=vmem(),
-        scratch_shapes=[
-            pltpu.VMEM((total, order), jnp.bfloat16),
-            pltpu.VMEM((total, order), jnp.bfloat16),
-            pltpu.VMEM((3 * size, size), jnp.float32),
-        ],
+        scratch_shapes=[pltpu.VMEM((2 * tile_rows * size, order), jnp.bfloat16)] * 2,
         compiler_params=pltpu.CompilerParams(vmem_limit_bytes=VMEM_BYTES),
-    )(ids, rows, cols, early, *factors, own, extended, front)
+    )(ids, *rows, *cols, own, extended, front)
+
+
+SHIFTS = (1, 3, 2)
 
 
 def exchange(value, axis):
     return lax.all_to_all(value, axis, split_axis=0, concat_axis=0, tiled=True)
 
 
-def gather(value, axis):
-    count = lax.axis_size(axis)
-    return exchange(jnp.broadcast_to(value[None], (count,) + value.shape), axis)
+def permute(value, axis, target):
+    return lax.ppermute(value, axis, [(i, target(i)) for i in range(lax.axis_size(axis))])
+
+
+def pair_gather(value, axis):
+    ring = lax.axis_size(axis) // 2
+    partner = permute(value, axis, lambda i: i ^ 1)
+    pair = jnp.stack([value, partner])
+    shifted = [permute(pair, axis, lambda i: (i // 2 + shift) % ring * 2 + i % 2) for shift in SHIFTS]
+    return (pair, *shifted)
+
+
+def pair_pieces(pieces, place):
+    ring = len(SHIFTS) + 1
+    for ref, shift in zip(pieces, (0,) + SHIFTS, strict=True):
+        source = lax.rem(lax.div(place, 2) + (ring - shift), ring) * 2
+        side = lax.rem(place, 2)
+        yield ref, 0, source + side
+        yield ref, 1, source + 1 - side
 
 
 def per_device(front_matrix, contributions, target_front, target_row, target_col, live_count):
@@ -455,35 +519,48 @@
     front = front_matrix.reshape(tile_rows, size, tile_cols, size).transpose(0, 2, 1, 3)
     ids = jnp.stack([lax.axis_index("row"), lax.axis_index("col")]).astype(jnp.int32)
 
-    packed, targets = pack(
-        contributions.reshape(slots, size, size),
+    thin = size // n_col
+    chunk = exchange(front[0, 0].reshape(n_col, thin, size), "col")[:LEAD_TILES]
+
+    targets, bucket_of = plan(
         target_front.reshape(slots), target_row.reshape(slots), target_col.reshape(slots),
         live_count.reshape(1), n_front, n_row, n_col, tile_cols,
     )
-    arrived = exchange(targets, ("front", "row"))
+    packed = move(contributions.reshape(slots, size, size), bucket_of, targets.shape[0])
     received = exchange(packed, ("front", "row"))
 
-    thin = size // n_col
-    chunk = exchange(front[0, 0].reshape(n_col, thin, size), "col")[:LEAD_TILES]
-    leading = gather(chunk, "row")
-    lower = jnp.stack([leading[i, j] for i in range(LEAD_TILES) for j in range(i + 1)])
-    lead = gather(lower, "col")
-    aimed = jnp.concatenate([jnp.broadcast_to(chunk[None], leading.shape), leading], axis=1)
-    early = exchange(aimed, "col")
+    capacity = targets.shape[0] // (n_front * n_row)
+    other = permute(targets, "front", lambda i: 1 - i)
+    front_index = lax.axis_index("front")
+    by_source = [jnp.where(front_index == source, targets, other) for source in range(n_front)]
+    aimed = lax.dynamic_index_in_dim(
+        jnp.stack(by_source).reshape(n_front, n_front, n_row, capacity), front_index, axis=1, keepdims=False
+    )
+    notes = aimed.transpose(1, 0, 2).reshape(n_row, 1, n_front * capacity).astype(jnp.bfloat16)
+    notes = jnp.pad(notes, ((0, 0), (0, 7), (0, size - n_front * capacity)))
+    flat = chunk.reshape(LEAD_TILES * thin, size)
+    sent = jnp.concatenate([jnp.broadcast_to(flat[None], (n_row,) + flat.shape), notes], axis=1)
+    got = exchange(sent, "row")
+    leading = got[:, : LEAD_TILES * thin].reshape(n_row, LEAD_TILES, thin, size)
+    arrived = got[:, LEAD_TILES * thin, : n_front * capacity].astype(jnp.int32)
+    arrived = arrived.reshape(n_row, n_front, capacity).transpose(1, 0, 2).reshape(targets.shape)
+
+    lower = jnp.concatenate([leading[i, : i + 1] for i in range(LEAD_TILES)], axis=0)
+    lead = pair_gather(lower, "col")
     steps = LEAD_TILES * size // BLOCK
-    begun, inverses = factorize_first(lead, size, range(FIRST_STEPS))
+    begun, inverses = factorize_first(ids, lead, size, range(FIRST_STEPS))
     arrived, begun = lax.optimization_barrier((arrived, begun))
 
     extended, panel = assemble(received, arrived, front, n_col)
-    mine = exchange(panel, "col")[:LEAD_TILES]
-    rows = gather(mine, "col")
+    mine = exchange(panel, "col")
+    *factors, own = factorize_last(begun, inverses, ids, size, range(FIRST_STEPS, steps))
+    solved = solve(mine, factors)
     turned = lax.ppermute(
-        mine, ("row", "col"), [(r * n_col + c, c * n_col + r) for r in range(n_row) for c in range(n_col)]
+        solved, ("row", "col"), [(r * n_col + c, c * n_col + r) for r in range(n_row) for c in range(n_col)]
     )
-    turned, begun = lax.optimization_barrier((turned, begun))
-    cols = gather(turned, "row")
-    *factors, own = factorize_last(begun, inverses, ids, size, range(FIRST_STEPS, steps))
-    factor = finish(ids, rows, cols, early, factors, own, extended, front)
+    rows = pair_gather(solved, "col")
+    cols = pair_gather(turned, "row")
+    factor = finish(ids, rows, cols, own, extended, front)
     return factor.reshape(1, tile_rows, 1, size, tile_cols, 1, size)
 
 

time: 241 us -> 235 us (0.975)
  waiting for transfers between devices: 56.3 us -> 93 us
  blocking collectives: 34.4 us -> 0 us
  Pallas kernels: 91.7 us -> 77.6 us
  starting transfers between devices: 45.9 us -> 53.4 us
  local copies, waits for them, and re-layouts: 8.28 us -> 5.35 us
    ppermute x1 -> x14, waiting for transfers between devices: 0.01 us -> 85 us  [the longest x13 85 us: permute(): lax.ppermute(value, axis, [(i, target(i)) for i in range(lax.axis_size(ax...]
    all_to_all x7 -> x4, waiting for transfers between devices: 56.3 us -> 8.04 us  [exchange(): return lax.all_to_all(value, axis, split_axis=0, concat_axis=0, tiled=True)]
    all_to_all x2 -> x0, blocking collectives: 34.4 us -> none  [exchange(): return lax.all_to_all(value, axis, split_axis=0, concat_axis=0, tiled=True)]
    ppermute x1 -> x14, starting transfers between devices: 0.66 us -> 27.5 us  [the longest x13 25.9 us: permute(): lax.ppermute(value, axis, [(i, target(i)) for i in range(lax.axis_size(ax...]
    all_to_all x7 -> x4, starting transfers between devices: 45.2 us -> 25.9 us  [exchange(): return lax.all_to_all(value, axis, split_axis=0, concat_axis=0, tiled=True)]
    pallas_call x1, Pallas kernels: 29.3 us -> 14.6 us  [factorize_last(): pl.pallas_call(kernel, name='factorize_last', out_shape=(wide, wide, inv,...]
    pallas_call x1, Pallas kernels: 20 us -> 7.9 us  [finish(): pl.pallas_call(kernel, name='finish', out_shape=jax.ShapeDtypeStruct((til...]
    pallas_call x1 -> x3, Pallas kernels: 5.38 us -> 13 us  [the longest x1 5.84 us: solve(): pl.pallas_call(kernel, name='solve', out_shape=jax.ShapeDtypeStruct((LEAD...]
  transfers between devices with their start and end apart: 8 -> 18, of which waited for: 6 -> 11; matrix products, arithmetic and copies ran while one was open for 2% -> 2% of each run, Pallas kernels for 28% -> 24%
where the time goes in v3:
time: 235 us; the launch traced here: 233 us
  waiting for transfers between devices  93 us (40%)
  Pallas kernels  77.6 us (33%)
  starting transfers between devices  53.4 us (23%)
  local copies, waits for them, and re-layouts  5.35 us (2%)
  other arithmetic  3.19 us (1%)
    ppermute x13, waiting for transfers between devices, permute(): lax.ppermute(value, axis, [(i, target(i)) for i in range(lax.axis_size(ax...  85 us
    pallas_call x1, Pallas kernels, factorize_first(): pl.pallas_call(kernel, name='factorize_first', out_shape=(jax.ShapeDtypeS...  37.2 us
    all_to_all x4, starting transfers between devices, exchange(): return lax.all_to_all(value, axis, split_axis=0, concat_axis=0, tiled=True)  25.9 us
    ppermute x13, starting transfers between devices, permute(): lax.ppermute(value, axis, [(i, target(i)) for i in range(lax.axis_size(ax...  25.9 us
    pallas_call x1, Pallas kernels, factorize_last(): pl.pallas_call(kernel, name='factorize_last', out_shape=(wide, wide, inv,...  14.6 us
    all_to_all x4, waiting for transfers between devices, exchange(): return lax.all_to_all(value, axis, split_axis=0, concat_axis=0, tiled=True)  8.04 us
    pallas_call x1, Pallas kernels, finish(): pl.pallas_call(kernel, name='finish', out_shape=jax.ShapeDtypeStruct((til...  7.9 us
    pallas_call x1, Pallas kernels, solve(): pl.pallas_call(kernel, name='solve', out_shape=jax.ShapeDtypeStruct((LEAD...  5.84 us
  transfers between devices with their start and end apart: 18, of which 11 were waited for; matrix products, arithmetic and copies ran while one was open for 2% of the time, Pallas kernels for 24%

profile of v3, /device:TPU:6, one launch (start us, length us, event | category | flops | bytes accessed | tf_op | source)
XLA Modules:
  0.0 233.3 jit_solution(16872746104029963673)
XLA Ops:
  0.7 2.1 plan.1
  2.7 0.1 collective-permute-start
  2.8 1.6 slice.34
  4.4 6.8 %all-to-all-start = ((bf16[8,32,256]{2,1,0:T(8,128)(2,1)}), bf16[8,32,256]{2,1,0:T(8,128)(2,1)S(1)}, u32[]{:S(2)}, u32[]{:S(2)}) async-start(bf16[8,32,256]{2,1,0:T(8,128)(2,1)} %bitcast.4), calls=%async_computation | async-start | bytes 262144 | tf_op jit(solution)/shard_map/all_to_all | solution.py:491
  11.2 0.0 collective-permute-done
  11.2 0.6 broadcast_select_fusion.1
  11.8 0.1 stack.48
  11.9 0.1 copy.27
  12.0 0.1 stack.49
  12.1 0.1 copy.28
  12.2 0.1 copy.34
  12.3 4.3 %all-to-all-done = bf16[8,32,256]{2,1,0:T(8,128)(2,1)S(1)} async-done(((bf16[8,32,256]{2,1,0:T(8,128)(2,1)}), bf16[8,32,256]{2,1,0:T(8,128)(2,1)S(1)}, u32[]{:S(2)}, u32[]{:S(2)}) %all-to-all-start) | async-done | bytes 131104 | tf_op jit(solution)/shard_map/all_to_all | solution.py:491
  16.6 0.8 fusion.1
  17.5 7.4 %all-to-all-start.1 = ((bf16[8,136,256]{2,1,0:T(8,128)(2,1)}), bf16[8,136,256]{2,1,0:T(8,128)(2,1)S(1)}, u32[]{:S(2)}, u32[]{:S(2)}) async-start(bf16[8,136,256]{2,1,0:T(8,128)(2,1)} %fusion.1), calls=%async_computation.1 | async-start | bytes 1114112 | tf_op jit(solution)/shard_map/all_to_all | solution.py:491
  24.9 5.1 %move.1 = bf16[32,256,256]{2,1,0:T(8,128)(2,1)} custom-call(s32[32]{0:T(128)} %get-tuple-element.21.bucket_ref, bf16[32,256,256]{2,1,0:T(8,128)(2,1)} %bitcast.41), custom_call_target="tpu_custom_call" | custom-call | tf_op jit(solution)/shard_map/move/pallas_call | solution.py:126
  30.0 3.7 %all-to-all-done.1 = bf16[8,136,256]{2,1,0:T(8,128)(2,1)S(1)} async-done(((bf16[8,136,256]{2,1,0:T(8,128)(2,1)}), bf16[8,136,256]{2,1,0:T(8,128)(2,1)S(1)}, u32[]{:S(2)}, u32[]{:S(2)}) %all-to-all-start.1) | async-done | bytes 557088 | tf_op jit(solution)/shard_map/all_to_all | solution.py:491
  33.7 7.0 %all-to-all-start.2 = ((bf16[32,256,256]{2,1,0:T(8,128)(2,1)}), bf16[32,256,256]{2,1,0:T(8,128)(2,1)}, u32[]{:S(2)}, u32[]{:S(2)}) async-start(bf16[32,256,256]{2,1,0:T(8,128)(2,1)} %move.1), calls=%async_computation.2 | async-start | bytes 8388608 | tf_op jit(solution)/shard_map/all_to_all | solution.py:491
  40.8 1.1 collective-permute-start.1
  41.9 51.5 %collective-permute-done.1 = bf16[10,32,256]{2,1,0:T(8,128)(2,1)S(1)} collective-permute-done((bf16[10,32,256]{2,1,0:T(8,128)(2,1)S(1)}, bf16[10,32,256]{2,1,0:T(8,128)(2,1)S(1)}, u32[]{:S(2)}, u32[]{:S(2)}) %collective-permute-start.1) | collective-permute-done | bytes 163872 | tf_op jit(solution)/shard_map/ppermute | solution.py:495
  93.4 0.0 copy-start.3
  93.4 1.5 collective-permute-start.4
  94.9 1.7 collective-permute-start.3
  96.5 0.4 collective-permute-start.2
  96.9 0.6 pad_add_fusion.2.place_ref.ids_ref
  97.6 0.1 copy.33
  97.7 0.1 copy.31
  97.8 0.7 reshape.68.arrived_ref
  98.4 7.2 %collective-permute-done.4.refs_3_ = bf16[2,10,32,256]{3,2,1,0:T(8,128)(2,1)S(1)} collective-permute-done((bf16[2,10,32,256]{3,2,1,0:T(8,128)(2,1)S(1)}, bf16[2,10,32,256]{3,2,1,0:T(8,128)(2,1)S(1)}, u32[]{:S(2)}, u32[]{:S(2)}) %collective-permute-start.4) | collective-permute-done | bytes 327712 | tf_op jit(solution)/shard_map/ppermute | solution.py:495
  105.6 4.1 %collective-permute-done.3.refs_2_ = bf16[2,10,32,256]{3,2,1,0:T(8,128)(2,1)S(1)} collective-permute-done((bf16[2,10,32,256]{3,2,1,0:T(8,128)(2,1)S(1)}, bf16[2,10,32,256]{3,2,1,0:T(8,128)(2,1)S(1)}, u32[]{:S(2)}, u32[]{:S(2)}) %collective-permute-start.3) | collective-permute-done | bytes 327712 | tf_op jit(solution)/shard_map/ppermute | solution.py:495
  109.7 1.5 collective-permute-done.2.refs_1_
  111.2 0.0 copy-done.3
  111.2 0.0 copy-start.12
  111.2 0.7 copy-done.12
  111.9 37.2 %factorize_first.1 = (f32[1024,1024]{1,0:T(8,128)}, f32[8,128,128]{2,1,0:T(8,128)}) custom-call(s32[2]{0:T(128)} %pad_add_fusion.2.place_ref.ids_ref, bf16[2,10,32,256]{3,2,1,0:T(8,128)(2,1)} %copy-done.3, bf16[2,10,32,256]{3,2,1,0:T(8,128)(2,1)} %copy-done.12, bf16[2,10,32,256]{3,2,1,0:T(8,128)(2,1)} %copy-done.11, bf16[2,10,32,256]{3,2,1,0:T(8,128)(2,1)} %copy-done.10), custom_call_target="tpu_custom_call" | custom-call | tf_op jit(solution)/shard_map/factorize_first/pallas_call | solution.py:304
  149.1 0.0 all-to-all-done.2.received_ref
  149.1 4.9 %assemble.1 = (f32[5,256,256]{2,1,0:T(8,128)}, s16[8,104,256]{2,1,0:T(8,128)(2,1)}) custom-call(s32[32]{0:T(128)} %reshape.68.arrived_ref, bf16[32,256,256]{2,1,0:T(8,128)(2,1)} %all-to-all-done.2.received_ref, bf16[3,3,256,256]{3,2,1,0:T(8,128)(2,1)} %bitcast.39), custom_call_target="tpu_custom_call" | custom-call | tf_op jit(solution)/shard_map/assemble/pallas_call | solution.py:205
  154.0 4.8 %all-to-all-start.3 = ((s16[8,104,256]{2,1,0:T(8,128)(2,1)}), s16[8,104,256]{2,1,0:T(8,128)(2,1)S(1)}, u32[]{:S(2)}, u32[]{:S(2)}) async-start(s16[8,104,256]{2,1,0:T(8,128)(2,1)} %get-tuple-element.22), calls=%async_computation.3 | async-start | bytes 851968 | tf_op jit(solution)/shard_map/all_to_all | solution.py:491
  158.8 14.6 %factorize_last.1 = (bf16[1024,1024]{1,0:T(8,128)(2,1)}, bf16[1024,1024]{1,0:T(8,128)(2,1)}, bf16[4,256,256]{2,1,0:T(8,128)(2,1)}, bf16[4,256,256]{2,1,0:T(8,128)(2,1)}, f32[256,256]{1,0:T(8,128)}) custom-call(s32[2]{0:T(128)} %pad_add_fusion.2.place_ref.ids_ref, f32[1024,1024]{1,0:T(8,128)} %get-tuple-element.23.begun_ref, ...), custom_call_target="tpu_custom_call" | custom-call | tf_op jit(solution)/shard_map/factorize_last/pallas_call | solution.py:354
  173.4 0.0 all-to-all-done.3.panel_ref
  173.4 0.8 copy-done
  174.1 5.8 %solve.1 = s16[4,104,256]{2,1,0:T(8,128)(2,1)} custom-call(s16[8,104,256]{2,1,0:T(8,128)(2,1)} %copy-done, bf16[1024,1024]{1,0:T(8,128)(2,1)} %get-tuple-element.25.high_ref, bf16[1024,1024]{1,0:T(8,128)(2,1)} %get-tuple-element.26.low_ref, bf16[4,256,256]{2,1,0:T(8,128)(2,1)} %get-tuple-element.27.ih_ref, bf16[4,256,256]{2,1,0:T(8,128)(2,1)} %get-tuple-element.28.il_ref), custom_call_target="tpu_custom_call" | custom-call | tf_op jit(solution)/shard_map/solve/pallas_call | solution.py:383
  180.0 0.0 collective-permute-start.5
  180.0 1.6 collective-permute-start.9
  181.6 5.3 %collective-permute-done.5 = s16[4,104,256]{2,1,0:T(8,128)(2,1)S(1)} collective-permute-done((s16[4,104,256]{2,1,0:T(8,128)(2,1)}, s16[4,104,256]{2,1,0:T(8,128)(2,1)S(1)}, u32[]{:S(2)}, u32[]{:S(2)}) %collective-permute-start.5) | collective-permute-done | bytes 213024 | tf_op jit(solution)/shard_map/ppermute | solution.py:495
  186.9 1.0 pad_add_fusion.refs_0_
  187.8 3.1 %collective-permute-start.8 = (s16[2,4,104,256]{3,2,1,0:T(8,128)(2,1)S(1)}, s16[2,4,104,256]{3,2,1,0:T(8,128)(2,1)S(1)}, u32[]{:S(2)}, u32[]{:S(2)}) collective-permute-start(s16[2,4,104,256]{3,2,1,0:T(8,128)(2,1)S(1)} %pad_add_fusion.refs_0_), channel_id=1, source_target_pairs={{0,4},{1,5},{2,6},{3,7},{4,0},{5,1},{6,2},{7,3},{8,12},{9,13},{10,... | collective-permute-start | bytes 1277960 | tf_op jit(solution)/shard_map/ppermute | solution.py:495
  190.9 0.0 collective-permute-done.9
  190.9 1.4 collective-permute-start.10
  192.3 9.3 %collective-permute-start.7 = (s16[2,4,104,256]{3,2,1,0:T(8,128)(2,1)S(1)}, s16[2,4,104,256]{3,2,1,0:T(8,128)(2,1)S(1)}, u32[]{:S(2)}, u32[]{:S(2)}) collective-permute-start(s16[2,4,104,256]{3,2,1,0:T(8,128)(2,1)S(1)} %pad_add_fusion.refs_0_), channel_id=1, source_target_pairs={{0,6},{1,7},{2,0},{3,1},{4,2},{5,3},{6,4},{7,5},{8,14},{9,15},{10,... | collective-permute-start | bytes 1277960 | tf_op jit(solution)/shard_map/ppermute | solution.py:495
  201.7 0.0 collective-permute-start.6
  201.7 0.0 collective-permute-done.10
  201.7 5.4 %collective-permute-start.13 = (s16[2,4,104,256]{3,2,1,0:T(8,128)(2,1)S(1)}, s16[2,4,104,256]{3,2,1,0:T(8,128)(2,1)S(1)}, u32[]{:S(2)}, u32[]{:S(2)}) collective-permute-start(s16[2,4,104,256]{3,2,1,0:T(8,128)(2,1)S(1)} %pad_add_fusion.1.refs_4_), channel_id=1, source_target_pairs={{0,32},{8,40},{16,48},{24,56},{32,0},{40,8},{48,16},{56,24},{1,33}... | collective-permute-start | bytes 1277960 | tf_op jit(solution)/shard_map/ppermute | solution.py:495
  207.1 0.9 collective-permute-start.12
  208.0 0.0 collective-permute-done.8.refs_3_
  208.0 1.2 collective-permute-start.11
  209.1 3.7 %collective-permute-done.7.refs_2_ = s16[2,4,104,256]{3,2,1,0:T(8,128)(2,1)S(1)} collective-permute-done((s16[2,4,104,256]{3,2,1,0:T(8,128)(2,1)S(1)}, s16[2,4,104,256]{3,2,1,0:T(8,128)(2,1)S(1)}, u32[]{:S(2)}, u32[]{:S(2)}) %collective-permute-start.7) | collective-permute-done | bytes 426016 | tf_op jit(solution)/shard_map/ppermute | solution.py:495
  212.9 0.1 collective-permute-done.6.refs_1_
  213.0 4.8 %collective-permute-done.13.refs_7_ = s16[2,4,104,256]{3,2,1,0:T(8,128)(2,1)S(1)} collective-permute-done((s16[2,4,104,256]{3,2,1,0:T(8,128)(2,1)S(1)}, s16[2,4,104,256]{3,2,1,0:T(8,128)(2,1)S(1)}, u32[]{:S(2)}, u32[]{:S(2)}) %collective-permute-start.13) | collective-permute-done | bytes 426016 | tf_op jit(solution)/shard_map/ppermute | solution.py:495
  217.8 6.7 %collective-permute-done.12.refs_6_ = s16[2,4,104,256]{3,2,1,0:T(8,128)(2,1)S(1)} collective-permute-done((s16[2,4,104,256]{3,2,1,0:T(8,128)(2,1)S(1)}, s16[2,4,104,256]{3,2,1,0:T(8,128)(2,1)S(1)}, u32[]{:S(2)}, u32[]{:S(2)}) %collective-permute-start.12) | collective-permute-done | bytes 426016 | tf_op jit(solution)/shard_map/ppermute | solution.py:495
  224.5 0.0 collective-permute-done.11.refs_5_
  224.5 0.0 copy-done.1
  224.6 0.7 copy-done.8
  225.2 0.2 copy-done.9
  225.4 7.9 %finish.1 = f32[4608,128]{1,0:T(8,128)} custom-call(s32[2]{0:T(128)} %pad_add_fusion.2.place_ref.ids_ref, s16[2,4,104,256]{3,2,1,0:T(8,128)(2,1)} %copy-done.1, s16[2,4,104,256]{3,2,1,0:T(8,128)(2,1)} %copy-done.6, s16[2,4,104,256]{3,2,1,0:T(8,128)(2,1)} %copy-done.5, s16[2,4,104,256]{3,2,1,0:T(8,128)(2,1)} %copy-done.4, s16[2,4,104,256]{3,2,1,0:T(8,128)(2,1)} %copy-done.2, ...), custom_call_target="tpu_custom_call" | custom-call | tf_op jit(solution)/shard_map/finish/pallas_call | solution.py:476
  (31 shorter events, 0.2 us)
Async XLA Ops:
  2.7 8.4 %collective-permute-start = (s32[32]{0:T(128)}, s32[32]{0:T(128)S(1)}, u32[]{:S(2)}, u32[]{:S(2)}) collective-permute-start(s32[32]{0:T(128)} %get-tuple-element.18), channel_id=1, source_target_pairs={{0,64},{64,0},{1,65},{65,1},{2,66},{66,2},{3,67},{67,3},{4,68},{68... | collective-permute-start | bytes 392 | tf_op jit(solution)/shard_map/ppermute | solution.py:495
  4.4 12.2 %all-to-all-start = ((bf16[8,32,256]{2,1,0:T(8,128)(2,1)}), bf16[8,32,256]{2,1,0:T(8,128)(2,1)S(1)}, u32[]{:S(2)}, u32[]{:S(2)}) async-start(bf16[8,32,256]{2,1,0:T(8,128)(2,1)} %bitcast.4), calls=%async_computation | async-start | bytes 262144 | tf_op jit(solution)/shard_map/all_to_all | solution.py:491
  17.5 16.2 %all-to-all-start.1 = ((bf16[8,136,256]{2,1,0:T(8,128)(2,1)}), bf16[8,136,256]{2,1,0:T(8,128)(2,1)S(1)}, u32[]{:S(2)}, u32[]{:S(2)}) async-start(bf16[8,136,256]{2,1,0:T(8,128)(2,1)} %fusion.1), calls=%async_computation.1 | async-start | bytes 1114112 | tf_op jit(solution)/shard_map/all_to_all | solution.py:491
  33.7 115.4 %all-to-all-start.2 = ((bf16[32,256,256]{2,1,0:T(8,128)(2,1)}), bf16[32,256,256]{2,1,0:T(8,128)(2,1)}, u32[]{:S(2)}, u32[]{:S(2)}) async-start(bf16[32,256,256]{2,1,0:T(8,128)(2,1)} %move.1), calls=%async_computation.2 | async-start | bytes 8388608 | tf_op jit(solution)/shard_map/all_to_all | solution.py:491
  40.8 52.6 %collective-permute-start.1 = (bf16[10,32,256]{2,1,0:T(8,128)(2,1)S(1)}, bf16[10,32,256]{2,1,0:T(8,128)(2,1)S(1)}, u32[]{:S(2)}, u32[]{:S(2)}) collective-permute-start(bf16[10,32,256]{2,1,0:T(8,128)(2,1)S(1)} %get-tuple-element.32), channel_id=1, source_target_pairs={{0,1},{1,0},{2,3},{3,2},{4,5},{5,4},{6,7},{7,6},{8,9},{9,8},{10,11... | collective-permute-start | bytes 491528 | tf_op jit(solution)/shard_map/ppermute | solution.py:495
  93.4 17.8 %copy-start.3 = (bf16[2,10,32,256]{3,2,1,0:T(8,128)(2,1)}, bf16[2,10,32,256]{3,2,1,0:T(8,128)(2,1)S(1)}, u32[]{:S(2)}) copy-start(bf16[2,10,32,256]{3,2,1,0:T(8,128)(2,1)S(1)} %pad_maximum_fusion.refs_0_) | copy-start | bytes 983044
  93.4 12.2 %collective-permute-start.4 = (bf16[2,10,32,256]{3,2,1,0:T(8,128)(2,1)S(1)}, bf16[2,10,32,256]{3,2,1,0:T(8,128)(2,1)S(1)}, u32[]{:S(2)}, u32[]{:S(2)}) collective-permute-start(bf16[2,10,32,256]{3,2,1,0:T(8,128)(2,1)S(1)} %pad_maximum_fusion.refs_0_), channel_id=1, source_target_pairs={{0,4},{1,5},{2,6},{3,7},{4,0},{5,1},{6,2},{7,3},{8,12},{9,13},{10,... | collective-permute-start | bytes 983048 | tf_op jit(solution)/shard_map/ppermute | solution.py:495
  94.9 14.9 %collective-permute-start.3 = (bf16[2,10,32,256]{3,2,1,0:T(8,128)(2,1)S(1)}, bf16[2,10,32,256]{3,2,1,0:T(8,128)(2,1)S(1)}, u32[]{:S(2)}, u32[]{:S(2)}) collective-permute-start(bf16[2,10,32,256]{3,2,1,0:T(8,128)(2,1)S(1)} %pad_maximum_fusion.refs_0_), channel_id=1, source_target_pairs={{0,6},{1,7},{2,0},{3,1},{4,2},{5,3},{6,4},{7,5},{8,14},{9,15},{10,... | collective-permute-start | bytes 983048 | tf_op jit(solution)/shard_map/ppermute | solution.py:495
  96.5 14.7 %collective-permute-start.2 = (bf16[2,10,32,256]{3,2,1,0:T(8,128)(2,1)S(1)}, bf16[2,10,32,256]{3,2,1,0:T(8,128)(2,1)S(1)}, u32[]{:S(2)}, u32[]{:S(2)}) collective-permute-start(bf16[2,10,32,256]{3,2,1,0:T(8,128)(2,1)S(1)} %pad_maximum_fusion.refs_0_), channel_id=1, source_target_pairs={{0,2},{1,3},{2,4},{3,5},{4,6},{5,7},{6,0},{7,1},{8,10},{9,11},{10,... | collective-permute-start | bytes 983048 | tf_op jit(solution)/shard_map/ppermute | solution.py:495
  105.6 5.6 %copy-start.10 = (bf16[2,10,32,256]{3,2,1,0:T(8,128)(2,1)}, bf16[2,10,32,256]{3,2,1,0:T(8,128)(2,1)S(1)}, u32[]{:S(2)}) copy-start(bf16[2,10,32,256]{3,2,1,0:T(8,128)(2,1)S(1)} %collective-permute-done.4.refs_3_) | copy-start | bytes 983044
  109.7 1.5 copy-start.11
  111.2 0.7 copy-start.12
  154.0 19.3 %all-to-all-start.3 = ((s16[8,104,256]{2,1,0:T(8,128)(2,1)}), s16[8,104,256]{2,1,0:T(8,128)(2,1)S(1)}, u32[]{:S(2)}, u32[]{:S(2)}) async-start(s16[8,104,256]{2,1,0:T(8,128)(2,1)} %get-tuple-element.22), calls=%async_computation.3 | async-start | bytes 851968 | tf_op jit(solution)/shard_map/all_to_all | solution.py:491
  173.4 0.8 copy-start
  180.0 6.9 %collective-permute-start.5 = (s16[4,104,256]{2,1,0:T(8,128)(2,1)}, s16[4,104,256]{2,1,0:T(8,128)(2,1)S(1)}, u32[]{:S(2)}, u32[]{:S(2)}) collective-permute-start(s16[4,104,256]{2,1,0:T(8,128)(2,1)} %solve.1), channel_id=1, source_target_pairs={{0,1},{1,0},{2,3},{3,2},{4,5},{5,4},{6,7},{7,6},{8,9},{9,8},{10,11... | collective-permute-start | bytes 638984 | tf_op jit(solution)/shard_map/ppermute | solution.py:495
  180.0 10.9 %collective-permute-start.9 = (s16[4,104,256]{2,1,0:T(8,128)(2,1)}, s16[4,104,256]{2,1,0:T(8,128)(2,1)S(1)}, u32[]{:S(2)}, u32[]{:S(2)}) collective-permute-start(s16[4,104,256]{2,1,0:T(8,128)(2,1)} %solve.1), channel_id=1, source_target_pairs={{0,0},{1,8},{2,16},{3,24},{4,32},{5,40},{6,48},{7,56},{8,1},{9,9},... | collective-permute-start | bytes 638984 | tf_op jit(solution)/shard_map/ppermute | solution.py:558
  187.8 36.7 %copy-start.1 = (s16[2,4,104,256]{3,2,1,0:T(8,128)(2,1)}, s16[2,4,104,256]{3,2,1,0:T(8,128)(2,1)S(1)}, u32[]{:S(2)}) copy-start(s16[2,4,104,256]{3,2,1,0:T(8,128)(2,1)S(1)} %pad_add_fusion.refs_0_) | copy-start | bytes 1277956
  187.8 20.1 %collective-permute-start.8 = (s16[2,4,104,256]{3,2,1,0:T(8,128)(2,1)S(1)}, s16[2,4,104,256]{3,2,1,0:T(8,128)(2,1)S(1)}, u32[]{:S(2)}, u32[]{:S(2)}) collective-permute-start(s16[2,4,104,256]{3,2,1,0:T(8,128)(2,1)S(1)} %pad_add_fusion.refs_0_), channel_id=1, source_target_pairs={{0,4},{1,5},{2,6},{3,7},{4,0},{5,1},{6,2},{7,3},{8,12},{9,13},{10,... | collective-permute-start | bytes 1277960 | tf_op jit(solution)/shard_map/ppermute | solution.py:495
  190.9 10.8 %collective-permute-start.10 = (s16[4,104,256]{2,1,0:T(8,128)(2,1)S(1)}, s16[4,104,256]{2,1,0:T(8,128)(2,1)S(1)}, u32[]{:S(2)}, u32[]{:S(2)}) collective-permute-start(s16[4,104,256]{2,1,0:T(8,128)(2,1)S(1)} %collective-permute-done.9), channel_id=1, source_target_pairs={{0,8},{8,0},{16,24},{24,16},{32,40},{40,32},{48,56},{56,48},{1,9},... | collective-permute-start | bytes 638984 | tf_op jit(solution)/shard_map/ppermute | solution.py:495
  192.3 20.5 %collective-permute-start.7 = (s16[2,4,104,256]{3,2,1,0:T(8,128)(2,1)S(1)}, s16[2,4,104,256]{3,2,1,0:T(8,128)(2,1)S(1)}, u32[]{:S(2)}, u32[]{:S(2)}) collective-permute-start(s16[2,4,104,256]{3,2,1,0:T(8,128)(2,1)S(1)} %pad_add_fusion.refs_0_), channel_id=1, source_target_pairs={{0,6},{1,7},{2,0},{3,1},{4,2},{5,3},{6,4},{7,5},{8,14},{9,15},{10,... | collective-permute-start | bytes 1277960 | tf_op jit(solution)/shard_map/ppermute | solution.py:495
  201.7 11.3 %collective-permute-start.6 = (s16[2,4,104,256]{3,2,1,0:T(8,128)(2,1)S(1)}, s16[2,4,104,256]{3,2,1,0:T(8,128)(2,1)S(1)}, u32[]{:S(2)}, u32[]{:S(2)}) collective-permute-start(s16[2,4,104,256]{3,2,1,0:T(8,128)(2,1)S(1)} %pad_add_fusion.refs_0_), channel_id=1, source_target_pairs={{0,2},{1,3},{2,4},{3,5},{4,6},{5,7},{6,0},{7,1},{8,10},{9,11},{10,... | collective-permute-start | bytes 1277960 | tf_op jit(solution)/shard_map/ppermute | solution.py:495
  201.7 22.8 %copy-start.2 = (s16[2,4,104,256]{3,2,1,0:T(8,128)(2,1)}, s16[2,4,104,256]{3,2,1,0:T(8,128)(2,1)S(1)}, u32[]{:S(2)}) copy-start(s16[2,4,104,256]{3,2,1,0:T(8,128)(2,1)S(1)} %pad_add_fusion.1.refs_4_) | copy-start | bytes 1277956
  201.7 16.0 %collective-permute-start.13 = (s16[2,4,104,256]{3,2,1,0:T(8,128)(2,1)S(1)}, s16[2,4,104,256]{3,2,1,0:T(8,128)(2,1)S(1)}, u32[]{:S(2)}, u32[]{:S(2)}) collective-permute-start(s16[2,4,104,256]{3,2,1,0:T(8,128)(2,1)S(1)} %pad_add_fusion.1.refs_4_), channel_id=1, source_target_pairs={{0,32},{8,40},{16,48},{24,56},{32,0},{40,8},{48,16},{56,24},{1,33}... | collective-permute-start | bytes 1277960 | tf_op jit(solution)/shard_map/ppermute | solution.py:495
  207.1 17.4 %collective-permute-start.12 = (s16[2,4,104,256]{3,2,1,0:T(8,128)(2,1)S(1)}, s16[2,4,104,256]{3,2,1,0:T(8,128)(2,1)S(1)}, u32[]{:S(2)}, u32[]{:S(2)}) collective-permute-start(s16[2,4,104,256]{3,2,1,0:T(8,128)(2,1)S(1)} %pad_add_fusion.1.refs_4_), channel_id=1, source_target_pairs={{0,48},{8,56},{16,0},{24,8},{32,16},{40,24},{48,32},{56,40},{1,49}... | collective-permute-start | bytes 1277960 | tf_op jit(solution)/shard_map/ppermute | solution.py:495
  208.0 16.6 %copy-start.4 = (s16[2,4,104,256]{3,2,1,0:T(8,128)(2,1)}, s16[2,4,104,256]{3,2,1,0:T(8,128)(2,1)S(1)}, u32[]{:S(2)}) copy-start(s16[2,4,104,256]{3,2,1,0:T(8,128)(2,1)S(1)} %collective-permute-done.8.refs_3_) | copy-start | bytes 1277956
  208.0 16.5 %collective-permute-start.11 = (s16[2,4,104,256]{3,2,1,0:T(8,128)(2,1)S(1)}, s16[2,4,104,256]{3,2,1,0:T(8,128)(2,1)S(1)}, u32[]{:S(2)}, u32[]{:S(2)}) collective-permute-start(s16[2,4,104,256]{3,2,1,0:T(8,128)(2,1)S(1)} %pad_add_fusion.1.refs_4_), channel_id=1, source_target_pairs={{0,16},{8,24},{16,32},{24,40},{32,48},{40,56},{48,0},{56,8},{1,17}... | collective-permute-start | bytes 1277960 | tf_op jit(solution)/shard_map/ppermute | solution.py:495
  212.9 11.7 %copy-start.5 = (s16[2,4,104,256]{3,2,1,0:T(8,128)(2,1)}, s16[2,4,104,256]{3,2,1,0:T(8,128)(2,1)S(1)}, u32[]{:S(2)}) copy-start(s16[2,4,104,256]{3,2,1,0:T(8,128)(2,1)S(1)} %collective-permute-done.7.refs_2_) | copy-start | bytes 1277956
  213.0 11.5 %copy-start.6 = (s16[2,4,104,256]{3,2,1,0:T(8,128)(2,1)}, s16[2,4,104,256]{3,2,1,0:T(8,128)(2,1)S(1)}, u32[]{:S(2)}) copy-start(s16[2,4,104,256]{3,2,1,0:T(8,128)(2,1)S(1)} %collective-permute-done.6.refs_1_) | copy-start | bytes 1277956
  217.8 6.8 %copy-start.7 = (s16[2,4,104,256]{3,2,1,0:T(8,128)(2,1)}, s16[2,4,104,256]{3,2,1,0:T(8,128)(2,1)S(1)}, u32[]{:S(2)}) copy-start(s16[2,4,104,256]{3,2,1,0:T(8,128)(2,1)S(1)} %collective-permute-done.13.refs_7_) | copy-start | bytes 1277956
  224.5 0.7 copy-start.8
  224.5 0.9 copy-start.9

commit v4 on v3

--- a/solution.py
+++ b/solution.py
@@ -8,9 +8,10 @@
 
 LEAD_TILES = 4
 BLOCK = 128
+HALF = 64
 RUN = 32
 STRIP = 8
-FIRST_STEPS = 6
+FIRST_STEPS = 7
 VMEM_BYTES = 56 * 1024 * 1024
 
 
@@ -232,11 +233,11 @@
     def spread(value, i):
         return jnp.broadcast_to(value[i : i + 1, :], value.shape)
 
-    def step(number, top):
+    def step(number, top, bottom):
         base = pl.multiple_of(number * STRIP, STRIP)
         strip = work[pl.ds(base, STRIP), :]
         own = [pick_lane(strip, base + i) for i in range(STRIP)]
-        whole = work[top:BLOCK, :]
+        whole = work[top:bottom, :]
         below = lax.broadcasted_iota(jnp.int32, whole.shape, 0) + top >= base + STRIP
         columns = [jnp.where(below, pick_lane(whole, base + i), 0.0) for i in range(STRIP)]
         for i in range(STRIP):
@@ -251,12 +252,30 @@
                 own[j] = own[j] - factors * entry
                 columns[j] = columns[j] - lower * jnp.broadcast_to(entry[0:1], whole.shape)
             whole = whole - lower * jnp.broadcast_to(line[0:1], whole.shape)
-        work[top:BLOCK, :] = whole
+        work[top:bottom, :] = whole
         work[pl.ds(base, STRIP), :] = strip
-        return top
-
-    for top in range(0, BLOCK, RUN):
-        lax.fori_loop(top // STRIP, (top + RUN) // STRIP, lambda number, carry: step(number, top) * 0 + carry, 0)
+
+    for first in range(0, BLOCK, HALF):
+        last = first + HALF
+        for top in range(first, last, RUN):
+
+            def run(number, carry, top=top):
+                step(number, top, last)
+                return carry
+
+            lax.fori_loop(top // STRIP, (top + RUN) // STRIP, run, 0)
+        if last < BLOCK:
+            done = work[first:last, :]
+            at_pivot = lax.broadcasted_iota(jnp.int32, done.shape, 0) + first == lax.broadcasted_iota(
+                jnp.int32, done.shape, 1
+            )
+            pivots = jnp.where(at_pivot, done, 0.0)
+            scaled = done / jnp.sum(pivots, axis=1, keepdims=True)
+            change = lax.dot_general(
+                scaled, done + pivots, (((0,), (0,)), ((), ())),
+                precision=lax.Precision.HIGHEST, preferred_element_type=jnp.float32,
+            )
+            work[last:BLOCK, :] = work[last:BLOCK, :] - change[last:BLOCK, :]
 
 
 HIGHEST = lax.Precision.HIGHEST
@@ -366,29 +385,33 @@
     )(ids, begun, begun_inverses)
 
 
-def solve(panel, factors):
-    _, coded_rows, size = panel.shape
+def solve(panels, factors):
+    _, coded_rows, size = panels[0].shape
     thin, order = coded_rows - SCALE_ROWS, LEAD_TILES * size
-
-    def kernel(panel_ref, high_ref, low_ref, ih_ref, il_ref, out_ref, xh, xl):
+    count = len(panels)
+
+    def kernel(*refs):
+        panel_refs, (high_ref, low_ref, ih_ref, il_ref) = refs[:count], refs[count : count + 4]
+        *out_refs, xh, xl = refs[count + 4 :]
         for q in range(LEAD_TILES):
             s, e = q * size, (q + 1) * size
-            acc = decode(panel_ref[q])
+            acc = jnp.concatenate([decode(ref[q]) for ref in panel_refs], axis=0)
             if q:
                 acc = acc - nt3((xh[:, 0:s], xl[:, 0:s]), (high_ref[s:e, 0:s], low_ref[s:e, 0:s]))
             x = nt3(split(acc), (ih_ref[q], il_ref[q]))
             xh[:, s:e], xl[:, s:e] = split(x)
-            out_ref[q] = encode(x)
+            for number, ref in enumerate(out_refs):
+                ref[q] = encode(x[number * thin : (number + 1) * thin])
 
     return pl.pallas_call(
         kernel,
         name="solve",
-        out_shape=jax.ShapeDtypeStruct((LEAD_TILES, coded_rows, size), jnp.int16),
-        in_specs=[vmem()] * 5,
-        out_specs=vmem(),
-        scratch_shapes=[pltpu.VMEM((thin, order), jnp.bfloat16)] * 2,
+        out_shape=(jax.ShapeDtypeStruct((LEAD_TILES, coded_rows, size), jnp.int16),) * count,
+        in_specs=[vmem()] * (count + 4),
+        out_specs=(vmem(),) * count,
+        scratch_shapes=[pltpu.VMEM((count * thin, order), jnp.bfloat16)] * 2,
         compiler_params=pltpu.CompilerParams(vmem_limit_bytes=VMEM_BYTES),
-    )(panel, *factors)
+    )(*panels, *factors)
 
 
 def finish(ids, rows, cols, own, extended, front):
@@ -552,12 +575,12 @@
     arrived, begun = lax.optimization_barrier((arrived, begun))
 
     extended, panel = assemble(received, arrived, front, n_col)
-    mine = exchange(panel, "col")
+    mine = exchange(panel, "col")[:LEAD_TILES]
     *factors, own = factorize_last(begun, inverses, ids, size, range(FIRST_STEPS, steps))
-    solved = solve(mine, factors)
     turned = lax.ppermute(
-        solved, ("row", "col"), [(r * n_col + c, c * n_col + r) for r in range(n_row) for c in range(n_col)]
+        mine, ("row", "col"), [(r * n_col + c, c * n_col + r) for r in range(n_row) for c in range(n_col)]
     )
+    solved, turned = solve((mine, turned), factors)
     rows = pair_gather(solved, "col")
     cols = pair_gather(turned, "row")
     factor = finish(ids, rows, cols, own, extended, front)

time: 235 us -> 239 us (1.017)
  blocking collectives: 0 us -> 12.9 us
  starting transfers between devices: 53.4 us -> 44.3 us
  Pallas kernels: 77.6 us -> 74.7 us
    all_to_all x0 -> x1, blocking collectives: none -> 12.9 us  [exchange(): return lax.all_to_all(value, axis, split_axis=0, concat_axis=0, tiled=True)]
    pallas_call x1, Pallas kernels: 14.6 us -> 9.56 us  [factorize_last(): pl.pallas_call(kernel, name='factorize_last', out_shape=(wide, wide, inv,...]
    all_to_all x4 -> x3, starting transfers between devices: 25.9 us -> 21.2 us  [exchange(): return lax.all_to_all(value, axis, split_axis=0, concat_axis=0, tiled=True)]
    ppermute x13, starting transfers between devices: 25.9 us -> 22.5 us  [permute(): lax.ppermute(value, axis, [(i, target(i)) for i in range(lax.axis_size(ax...]
    all_to_all x4 -> x3, waiting for transfers between devices: 8.04 us -> 8.03 us  [exchange(): return lax.all_to_all(value, axis, split_axis=0, concat_axis=0, tiled=True)]
  transfers between devices with their start and end apart: 18 -> 17, of which waited for: 11 -> 11; matrix products, arithmetic and copies ran while one was open for 2% -> 2% of each run, Pallas kernels for 24% -> 23%
where the time goes in v4:
time: 239 us; the launch traced here: 237 us
  waiting for transfers between devices  95.1 us (40%)
  Pallas kernels  74.7 us (31%)
  starting transfers between devices  44.3 us (19%)
  blocking collectives  12.9 us (5%)
  local copies, waits for them, and re-layouts  5.28 us (2%)
  other arithmetic  4.12 us (2%)
    ppermute x13, waiting for transfers between devices, permute(): lax.ppermute(value, axis, [(i, target(i)) for i in range(lax.axis_size(ax...  87 us
    pallas_call x1, Pallas kernels, factorize_first(): pl.pallas_call(kernel, name='factorize_first', out_shape=(jax.ShapeDtypeS...  39.2 us
    ppermute x13, starting transfers between devices, permute(): lax.ppermute(value, axis, [(i, target(i)) for i in range(lax.axis_size(ax...  22.5 us
    all_to_all x3, starting transfers between devices, exchange(): return lax.all_to_all(value, axis, split_axis=0, concat_axis=0, tiled=True)  21.2 us
    all_to_all x1, blocking collectives, exchange(): return lax.all_to_all(value, axis, split_axis=0, concat_axis=0, tiled=True)  12.9 us
    pallas_call x1, Pallas kernels, factorize_last(): pl.pallas_call(kernel, name='factorize_last', out_shape=(wide, wide, inv,...  9.56 us
    all_to_all x3, waiting for transfers between devices, exchange(): return lax.all_to_all(value, axis, split_axis=0, concat_axis=0, tiled=True)  8.03 us
    pallas_call x1, Pallas kernels, finish(): pl.pallas_call(kernel, name='finish', out_shape=jax.ShapeDtypeStruct((til...  7.91 us
  transfers between devices with their start and end apart: 17, of which 11 were waited for; matrix products, arithmetic and copies ran while one was open for 2% of the time, Pallas kernels for 23%

profile of v4, /device:TPU:6, one launch (start us, length us, event | category | flops | bytes accessed | tf_op | source)
XLA Modules:
  0.0 237.2 jit_solution(6134046211034435054)
XLA Ops:
  0.7 2.1 plan.1
  2.7 0.1 collective-permute-start
  2.8 1.6 slice.38
  4.4 6.8 %all-to-all-start = ((bf16[8,32,256]{2,1,0:T(8,128)(2,1)}), bf16[8,32,256]{2,1,0:T(8,128)(2,1)S(1)}, u32[]{:S(2)}, u32[]{:S(2)}) async-start(bf16[8,32,256]{2,1,0:T(8,128)(2,1)} %bitcast.4), calls=%async_computation | async-start | bytes 262144 | tf_op jit(solution)/shard_map/all_to_all | solution.py:514
  11.2 0.0 collective-permute-done
  11.2 0.6 broadcast_select_fusion.1
  11.8 0.1 stack.48
  11.9 0.1 copy.27
  12.0 0.1 stack.49
  12.1 0.1 copy.28
  12.2 0.1 copy.34
  12.3 4.3 %all-to-all-done = bf16[8,32,256]{2,1,0:T(8,128)(2,1)S(1)} async-done(((bf16[8,32,256]{2,1,0:T(8,128)(2,1)}), bf16[8,32,256]{2,1,0:T(8,128)(2,1)S(1)}, u32[]{:S(2)}, u32[]{:S(2)}) %all-to-all-start) | async-done | bytes 131104 | tf_op jit(solution)/shard_map/all_to_all | solution.py:514
  16.6 0.8 fusion.1
  17.5 7.4 %all-to-all-start.1 = ((bf16[8,136,256]{2,1,0:T(8,128)(2,1)}), bf16[8,136,256]{2,1,0:T(8,128)(2,1)S(1)}, u32[]{:S(2)}, u32[]{:S(2)}) async-start(bf16[8,136,256]{2,1,0:T(8,128)(2,1)} %fusion.1), calls=%async_computation.1 | async-start | bytes 1114112 | tf_op jit(solution)/shard_map/all_to_all | solution.py:514
  24.9 5.1 %move.1 = bf16[32,256,256]{2,1,0:T(8,128)(2,1)} custom-call(s32[32]{0:T(128)} %get-tuple-element.23.bucket_ref, bf16[32,256,256]{2,1,0:T(8,128)(2,1)} %bitcast.41), custom_call_target="tpu_custom_call" | custom-call | tf_op jit(solution)/shard_map/move/pallas_call | solution.py:127
  30.0 3.7 %all-to-all-done.1 = bf16[8,136,256]{2,1,0:T(8,128)(2,1)S(1)} async-done(((bf16[8,136,256]{2,1,0:T(8,128)(2,1)}), bf16[8,136,256]{2,1,0:T(8,128)(2,1)S(1)}, u32[]{:S(2)}, u32[]{:S(2)}) %all-to-all-start.1) | async-done | bytes 557088 | tf_op jit(solution)/shard_map/all_to_all | solution.py:514
  33.7 7.0 %all-to-all-start.2 = ((bf16[32,256,256]{2,1,0:T(8,128)(2,1)}), bf16[32,256,256]{2,1,0:T(8,128)(2,1)}, u32[]{:S(2)}, u32[]{:S(2)}) async-start(bf16[32,256,256]{2,1,0:T(8,128)(2,1)} %move.1), calls=%async_computation.2 | async-start | bytes 8388608 | tf_op jit(solution)/shard_map/all_to_all | solution.py:514
  40.8 1.1 collective-permute-start.1
  41.9 51.5 %collective-permute-done.1 = bf16[10,32,256]{2,1,0:T(8,128)(2,1)S(1)} collective-permute-done((bf16[10,32,256]{2,1,0:T(8,128)(2,1)S(1)}, bf16[10,32,256]{2,1,0:T(8,128)(2,1)S(1)}, u32[]{:S(2)}, u32[]{:S(2)}) %collective-permute-start.1) | collective-permute-done | bytes 163872 | tf_op jit(solution)/shard_map/ppermute | solution.py:518
  93.4 0.0 copy-start.2
  93.4 1.5 collective-permute-start.4
  94.9 1.7 collective-permute-start.3
  96.5 0.4 collective-permute-start.2
  96.9 0.6 pad_add_fusion.2.place_ref.ids_ref
  97.6 0.1 copy.33
  97.7 0.1 copy.31
  97.8 0.7 reshape.68.arrived_ref
  98.4 7.2 %collective-permute-done.4.refs_3_ = bf16[2,10,32,256]{3,2,1,0:T(8,128)(2,1)S(1)} collective-permute-done((bf16[2,10,32,256]{3,2,1,0:T(8,128)(2,1)S(1)}, bf16[2,10,32,256]{3,2,1,0:T(8,128)(2,1)S(1)}, u32[]{:S(2)}, u32[]{:S(2)}) %collective-permute-start.4) | collective-permute-done | bytes 327712 | tf_op jit(solution)/shard_map/ppermute | solution.py:518
  105.6 4.1 %collective-permute-done.3.refs_2_ = bf16[2,10,32,256]{3,2,1,0:T(8,128)(2,1)S(1)} collective-permute-done((bf16[2,10,32,256]{3,2,1,0:T(8,128)(2,1)S(1)}, bf16[2,10,32,256]{3,2,1,0:T(8,128)(2,1)S(1)}, u32[]{:S(2)}, u32[]{:S(2)}) %collective-permute-start.3) | collective-permute-done | bytes 327712 | tf_op jit(solution)/shard_map/ppermute | solution.py:518
  109.7 1.5 collective-permute-done.2.refs_1_
  111.2 0.0 copy-start.12
  111.2 0.7 copy-done.12
  111.9 39.2 %factorize_first.1 = (f32[1024,1024]{1,0:T(8,128)}, f32[8,128,128]{2,1,0:T(8,128)}) custom-call(s32[2]{0:T(128)} %pad_add_fusion.2.place_ref.ids_ref, bf16[2,10,32,256]{3,2,1,0:T(8,128)(2,1)} %copy-done.2, bf16[2,10,32,256]{3,2,1,0:T(8,128)(2,1)} %copy-done.12, bf16[2,10,32,256]{3,2,1,0:T(8,128)(2,1)} %copy-done.11, bf16[2,10,32,256]{3,2,1,0:T(8,128)(2,1)} %copy-done.10), custom_call_target="tpu_custom_call" | custom-call | tf_op jit(solution)/shard_map/factorize_first/pallas_call | solution.py:323
  151.2 0.0 all-to-all-done.2.received_ref
  151.2 4.9 %assemble.1 = (f32[5,256,256]{2,1,0:T(8,128)}, s16[8,104,256]{2,1,0:T(8,128)(2,1)}) custom-call(s32[32]{0:T(128)} %reshape.68.arrived_ref, bf16[32,256,256]{2,1,0:T(8,128)(2,1)} %all-to-all-done.2.received_ref, bf16[3,3,256,256]{3,2,1,0:T(8,128)(2,1)} %bitcast.39), custom_call_target="tpu_custom_call" | custom-call | tf_op jit(solution)/shard_map/assemble/pallas_call | solution.py:206
  156.0 12.9 %all_to_all.20 = s16[8,104,256]{2,1,0:T(8,128)(2,1)S(1)} all-to-all(s16[8,104,256]{2,1,0:T(8,128)(2,1)} %get-tuple-element.24), channel_id=1, replica_groups=mesh['front'=2,'row'=8,'col'=8] {'col'}, dimensions={0} | all-to-all | bytes 851968 | tf_op jit(solution)/shard_map/all_to_all | solution.py:514
  168.9 0.7 collective-permute-start.5
  169.6 9.6 %factorize_last.1 = (bf16[1024,1024]{1,0:T(8,128)(2,1)}, bf16[1024,1024]{1,0:T(8,128)(2,1)}, bf16[4,256,256]{2,1,0:T(8,128)(2,1)}, bf16[4,256,256]{2,1,0:T(8,128)(2,1)}, f32[256,256]{1,0:T(8,128)}) custom-call(s32[2]{0:T(128)} %pad_add_fusion.2.place_ref.ids_ref, f32[1024,1024]{1,0:T(8,128)} %get-tuple-element.25.begun_ref, ...), custom_call_target="tpu_custom_call" | custom-call | tf_op jit(solution)/shard_map/factorize_last/pallas_call | solution.py:373
  179.2 0.0 collective-permute-done.5.refs_1_
  179.2 0.7 copy-done.13
  179.9 6.0 %solve.1 = (s16[4,104,256]{2,1,0:T(8,128)(2,1)}, s16[4,104,256]{2,1,0:T(8,128)(2,1)}) custom-call(s16[4,104,256]{2,1,0:T(8,128)(2,1)} %copy-done.3, s16[4,104,256]{2,1,0:T(8,128)(2,1)} %copy-done.13, bf16[1024,1024]{1,0:T(8,128)(2,1)} %get-tuple-element.27.refs_2_, bf16[1024,1024]{1,0:T(8,128)(2,1)} %get-tuple-element.28.refs_3_, ...), custom_call_target="tpu_custom_call" | custom-call | tf_op jit(solution)/shard_map/solve/pallas_call | solution.py:406
  185.9 4.5 %collective-permute-start.10 = (s16[4,104,256]{2,1,0:T(8,128)(2,1)}, s16[4,104,256]{2,1,0:T(8,128)(2,1)S(1)}, u32[]{:S(2)}, u32[]{:S(2)}) collective-permute-start(s16[4,104,256]{2,1,0:T(8,128)(2,1)} %get-tuple-element.32), channel_id=1, source_target_pairs={{0,8},{8,0},{16,24},{24,16},{32,40},{40,32},{48,56},{56,48},{1,9},... | collective-permute-start | bytes 638984 | tf_op jit(solution)/shard_map/ppermute | solution.py:518
  190.4 4.2 %collective-permute-done.10 = s16[4,104,256]{2,1,0:T(8,128)(2,1)S(1)} collective-permute-done((s16[4,104,256]{2,1,0:T(8,128)(2,1)}, s16[4,104,256]{2,1,0:T(8,128)(2,1)S(1)}, u32[]{:S(2)}, u32[]{:S(2)}) %collective-permute-start.10) | collective-permute-done | bytes 213024 | tf_op jit(solution)/shard_map/ppermute | solution.py:518
  194.6 1.0 pad_add_fusion.1.refs_4_
  195.6 5.8 %collective-permute-start.13 = (s16[2,4,104,256]{3,2,1,0:T(8,128)(2,1)S(1)}, s16[2,4,104,256]{3,2,1,0:T(8,128)(2,1)S(1)}, u32[]{:S(2)}, u32[]{:S(2)}) collective-permute-start(s16[2,4,104,256]{3,2,1,0:T(8,128)(2,1)S(1)} %pad_add_fusion.1.refs_4_), channel_id=1, source_target_pairs={{0,32},{8,40},{16,48},{24,56},{32,0},{40,8},{48,16},{56,24},{1,33}... | collective-permute-start | bytes 1277960 | tf_op jit(solution)/shard_map/ppermute | solution.py:518
  201.4 1.5 collective-permute-start.6
  203.0 1.6 collective-permute-start.12
  204.5 0.8 collective-permute-start.11
  205.3 2.2 collective-permute-done.6
  207.5 1.0 pad_add_fusion.refs_0_
  208.5 0.5 collective-permute-start.9
  209.0 2.2 collective-permute-start.8
  211.2 0.5 collective-permute-done.13.refs_7_
  211.7 0.9 collective-permute-start.7
  212.5 9.8 %collective-permute-done.12.refs_6_ = s16[2,4,104,256]{3,2,1,0:T(8,128)(2,1)S(1)} collective-permute-done((s16[2,4,104,256]{3,2,1,0:T(8,128)(2,1)S(1)}, s16[2,4,104,256]{3,2,1,0:T(8,128)(2,1)S(1)}, u32[]{:S(2)}, u32[]{:S(2)}) %collective-permute-start.12) | collective-permute-done | bytes 426016 | tf_op jit(solution)/shard_map/ppermute | solution.py:518
  222.3 0.0 collective-permute-done.11.refs_5_
  222.3 0.0 collective-permute-done.9.refs_3_
  222.3 6.1 %collective-permute-done.8.refs_2_ = s16[2,4,104,256]{3,2,1,0:T(8,128)(2,1)S(1)} collective-permute-done((s16[2,4,104,256]{3,2,1,0:T(8,128)(2,1)S(1)}, s16[2,4,104,256]{3,2,1,0:T(8,128)(2,1)S(1)}, u32[]{:S(2)}, u32[]{:S(2)}) %collective-permute-start.8) | collective-permute-done | bytes 426016 | tf_op jit(solution)/shard_map/ppermute | solution.py:518
  228.4 0.0 collective-permute-done.7.refs_1_
  228.4 0.0 copy-done.1
  228.4 0.0 copy-done.4
  228.5 0.7 copy-done.8
  229.2 0.1 copy-done.9
  229.3 7.9 %finish.1 = f32[4608,128]{1,0:T(8,128)} custom-call(s32[2]{0:T(128)} %pad_add_fusion.2.place_ref.ids_ref, s16[2,4,104,256]{3,2,1,0:T(8,128)(2,1)} %copy-done.1, s16[2,4,104,256]{3,2,1,0:T(8,128)(2,1)} %copy-done.9, s16[2,4,104,256]{3,2,1,0:T(8,128)(2,1)} %copy-done.8, s16[2,4,104,256]{3,2,1,0:T(8,128)(2,1)} %copy-done.7, s16[2,4,104,256]{3,2,1,0:T(8,128)(2,1)} %copy-done, ...), custom_call_target="tpu_custom_call" | custom-call | tf_op jit(solution)/shard_map/finish/pallas_call | solution.py:499
  (33 shorter events, 0.2 us)
Async XLA Ops:
  2.7 8.4 %collective-permute-start = (s32[32]{0:T(128)}, s32[32]{0:T(128)S(1)}, u32[]{:S(2)}, u32[]{:S(2)}) collective-permute-start(s32[32]{0:T(128)} %get-tuple-element.20), channel_id=1, source_target_pairs={{0,64},{64,0},{1,65},{65,1},{2,66},{66,2},{3,67},{67,3},{4,68},{68... | collective-permute-start | bytes 392 | tf_op jit(solution)/shard_map/ppermute | solution.py:518
  4.4 12.2 %all-to-all-start = ((bf16[8,32,256]{2,1,0:T(8,128)(2,1)}), bf16[8,32,256]{2,1,0:T(8,128)(2,1)S(1)}, u32[]{:S(2)}, u32[]{:S(2)}) async-start(bf16[8,32,256]{2,1,0:T(8,128)(2,1)} %bitcast.4), calls=%async_computation | async-start | bytes 262144 | tf_op jit(solution)/shard_map/all_to_all | solution.py:514
  17.5 16.2 %all-to-all-start.1 = ((bf16[8,136,256]{2,1,0:T(8,128)(2,1)}), bf16[8,136,256]{2,1,0:T(8,128)(2,1)S(1)}, u32[]{:S(2)}, u32[]{:S(2)}) async-start(bf16[8,136,256]{2,1,0:T(8,128)(2,1)} %fusion.1), calls=%async_computation.1 | async-start | bytes 1114112 | tf_op jit(solution)/shard_map/all_to_all | solution.py:514
  33.7 117.5 %all-to-all-start.2 = ((bf16[32,256,256]{2,1,0:T(8,128)(2,1)}), bf16[32,256,256]{2,1,0:T(8,128)(2,1)}, u32[]{:S(2)}, u32[]{:S(2)}) async-start(bf16[32,256,256]{2,1,0:T(8,128)(2,1)} %move.1), calls=%async_computation.2 | async-start | bytes 8388608 | tf_op jit(solution)/shard_map/all_to_all | solution.py:514
  40.8 52.6 %collective-permute-start.1 = (bf16[10,32,256]{2,1,0:T(8,128)(2,1)S(1)}, bf16[10,32,256]{2,1,0:T(8,128)(2,1)S(1)}, u32[]{:S(2)}, u32[]{:S(2)}) collective-permute-start(bf16[10,32,256]{2,1,0:T(8,128)(2,1)S(1)} %get-tuple-element.36), channel_id=1, source_target_pairs={{0,1},{1,0},{2,3},{3,2},{4,5},{5,4},{6,7},{7,6},{8,9},{9,8},{10,11... | collective-permute-start | bytes 491528 | tf_op jit(solution)/shard_map/ppermute | solution.py:518
  93.4 17.8 %copy-start.2 = (bf16[2,10,32,256]{3,2,1,0:T(8,128)(2,1)}, bf16[2,10,32,256]{3,2,1,0:T(8,128)(2,1)S(1)}, u32[]{:S(2)}) copy-start(bf16[2,10,32,256]{3,2,1,0:T(8,128)(2,1)S(1)} %pad_maximum_fusion.refs_0_) | copy-start | bytes 983044
  93.4 12.2 %collective-permute-start.4 = (bf16[2,10,32,256]{3,2,1,0:T(8,128)(2,1)S(1)}, bf16[2,10,32,256]{3,2,1,0:T(8,128)(2,1)S(1)}, u32[]{:S(2)}, u32[]{:S(2)}) collective-permute-start(bf16[2,10,32,256]{3,2,1,0:T(8,128)(2,1)S(1)} %pad_maximum_fusion.refs_0_), channel_id=1, source_target_pairs={{0,4},{1,5},{2,6},{3,7},{4,0},{5,1},{6,2},{7,3},{8,12},{9,13},{10,... | collective-permute-start | bytes 983048 | tf_op jit(solution)/shard_map/ppermute | solution.py:518
  94.9 14.9 %collective-permute-start.3 = (bf16[2,10,32,256]{3,2,1,0:T(8,128)(2,1)S(1)}, bf16[2,10,32,256]{3,2,1,0:T(8,128)(2,1)S(1)}, u32[]{:S(2)}, u32[]{:S(2)}) collective-permute-start(bf16[2,10,32,256]{3,2,1,0:T(8,128)(2,1)S(1)} %pad_maximum_fusion.refs_0_), channel_id=1, source_target_pairs={{0,6},{1,7},{2,0},{3,1},{4,2},{5,3},{6,4},{7,5},{8,14},{9,15},{10,... | collective-permute-start | bytes 983048 | tf_op jit(solution)/shard_map/ppermute | solution.py:518
  96.5 14.7 %collective-permute-start.2 = (bf16[2,10,32,256]{3,2,1,0:T(8,128)(2,1)S(1)}, bf16[2,10,32,256]{3,2,1,0:T(8,128)(2,1)S(1)}, u32[]{:S(2)}, u32[]{:S(2)}) collective-permute-start(bf16[2,10,32,256]{3,2,1,0:T(8,128)(2,1)S(1)} %pad_maximum_fusion.refs_0_), channel_id=1, source_target_pairs={{0,2},{1,3},{2,4},{3,5},{4,6},{5,7},{6,0},{7,1},{8,10},{9,11},{10,... | collective-permute-start | bytes 983048 | tf_op jit(solution)/shard_map/ppermute | solution.py:518
  105.6 5.6 %copy-start.10 = (bf16[2,10,32,256]{3,2,1,0:T(8,128)(2,1)}, bf16[2,10,32,256]{3,2,1,0:T(8,128)(2,1)S(1)}, u32[]{:S(2)}) copy-start(bf16[2,10,32,256]{3,2,1,0:T(8,128)(2,1)S(1)} %collective-permute-done.4.refs_3_) | copy-start | bytes 983044
  109.7 1.5 copy-start.11
  111.2 0.7 copy-start.12
  168.9 10.3 %copy-start.3 = (s16[4,104,256]{2,1,0:T(8,128)(2,1)}, s16[4,104,256]{2,1,0:T(8,128)(2,1)S(1)}, u32[]{:S(2)}) copy-start(s16[4,104,256]{2,1,0:T(8,128)(2,1)S(1)} %slice.46.refs_0_) | copy-start | bytes 638980
  168.9 10.2 %collective-permute-start.5 = (s16[4,104,256]{2,1,0:T(8,128)(2,1)S(1)}, s16[4,104,256]{2,1,0:T(8,128)(2,1)S(1)}, u32[]{:S(2)}, u32[]{:S(2)}) collective-permute-start(s16[4,104,256]{2,1,0:T(8,128)(2,1)S(1)} %slice.46.refs_0_), channel_id=1, source_target_pairs={{0,0},{1,8},{2,16},{3,24},{4,32},{5,40},{6,48},{7,56},{8,1},{9,9},... | collective-permute-start | bytes 638984 | tf_op jit(solution)/shard_map/ppermute | solution.py:580
  179.2 0.7 copy-start.13
  185.9 8.8 %collective-permute-start.10 = (s16[4,104,256]{2,1,0:T(8,128)(2,1)}, s16[4,104,256]{2,1,0:T(8,128)(2,1)S(1)}, u32[]{:S(2)}, u32[]{:S(2)}) collective-permute-start(s16[4,104,256]{2,1,0:T(8,128)(2,1)} %get-tuple-element.32), channel_id=1, source_target_pairs={{0,8},{8,0},{16,24},{24,16},{32,40},{40,32},{48,56},{56,48},{1,9},... | collective-permute-start | bytes 638984 | tf_op jit(solution)/shard_map/ppermute | solution.py:518
  195.6 32.8 %copy-start = (s16[2,4,104,256]{3,2,1,0:T(8,128)(2,1)}, s16[2,4,104,256]{3,2,1,0:T(8,128)(2,1)S(1)}, u32[]{:S(2)}) copy-start(s16[2,4,104,256]{3,2,1,0:T(8,128)(2,1)S(1)} %pad_add_fusion.1.refs_4_) | copy-start | bytes 1277956
  195.6 16.0 %collective-permute-start.13 = (s16[2,4,104,256]{3,2,1,0:T(8,128)(2,1)S(1)}, s16[2,4,104,256]{3,2,1,0:T(8,128)(2,1)S(1)}, u32[]{:S(2)}, u32[]{:S(2)}) collective-permute-start(s16[2,4,104,256]{3,2,1,0:T(8,128)(2,1)S(1)} %pad_add_fusion.1.refs_4_), channel_id=1, source_target_pairs={{0,32},{8,40},{16,48},{24,56},{32,0},{40,8},{48,16},{56,24},{1,33}... | collective-permute-start | bytes 1277960 | tf_op jit(solution)/shard_map/ppermute | solution.py:518
  201.4 6.1 %collective-permute-start.6 = (s16[4,104,256]{2,1,0:T(8,128)(2,1)}, s16[4,104,256]{2,1,0:T(8,128)(2,1)S(1)}, u32[]{:S(2)}, u32[]{:S(2)}) collective-permute-start(s16[4,104,256]{2,1,0:T(8,128)(2,1)} %get-tuple-element.31), channel_id=1, source_target_pairs={{0,1},{1,0},{2,3},{3,2},{4,5},{5,4},{6,7},{7,6},{8,9},{9,8},{10,11... | collective-permute-start | bytes 638984 | tf_op jit(solution)/shard_map/ppermute | solution.py:518
  203.0 19.3 %collective-permute-start.12 = (s16[2,4,104,256]{3,2,1,0:T(8,128)(2,1)S(1)}, s16[2,4,104,256]{3,2,1,0:T(8,128)(2,1)S(1)}, u32[]{:S(2)}, u32[]{:S(2)}) collective-permute-start(s16[2,4,104,256]{3,2,1,0:T(8,128)(2,1)S(1)} %pad_add_fusion.1.refs_4_), channel_id=1, source_target_pairs={{0,48},{8,56},{16,0},{24,8},{32,16},{40,24},{48,32},{56,40},{1,49}... | collective-permute-start | bytes 1277960 | tf_op jit(solution)/shard_map/ppermute | solution.py:518
  204.5 17.8 %collective-permute-start.11 = (s16[2,4,104,256]{3,2,1,0:T(8,128)(2,1)S(1)}, s16[2,4,104,256]{3,2,1,0:T(8,128)(2,1)S(1)}, u32[]{:S(2)}, u32[]{:S(2)}) collective-permute-start(s16[2,4,104,256]{3,2,1,0:T(8,128)(2,1)S(1)} %pad_add_fusion.1.refs_4_), channel_id=1, source_target_pairs={{0,16},{8,24},{16,32},{24,40},{32,48},{40,56},{48,0},{56,8},{1,17}... | collective-permute-start | bytes 1277960 | tf_op jit(solution)/shard_map/ppermute | solution.py:518
  208.5 19.9 %copy-start.1 = (s16[2,4,104,256]{3,2,1,0:T(8,128)(2,1)}, s16[2,4,104,256]{3,2,1,0:T(8,128)(2,1)S(1)}, u32[]{:S(2)}) copy-start(s16[2,4,104,256]{3,2,1,0:T(8,128)(2,1)S(1)} %pad_add_fusion.refs_0_) | copy-start | bytes 1277956
  208.5 13.9 %collective-permute-start.9 = (s16[2,4,104,256]{3,2,1,0:T(8,128)(2,1)S(1)}, s16[2,4,104,256]{3,2,1,0:T(8,128)(2,1)S(1)}, u32[]{:S(2)}, u32[]{:S(2)}) collective-permute-start(s16[2,4,104,256]{3,2,1,0:T(8,128)(2,1)S(1)} %pad_add_fusion.refs_0_), channel_id=1, source_target_pairs={{0,4},{1,5},{2,6},{3,7},{4,0},{5,1},{6,2},{7,3},{8,12},{9,13},{10,... | collective-permute-start | bytes 1277960 | tf_op jit(solution)/shard_map/ppermute | solution.py:518
  209.0 19.4 %collective-permute-start.8 = (s16[2,4,104,256]{3,2,1,0:T(8,128)(2,1)S(1)}, s16[2,4,104,256]{3,2,1,0:T(8,128)(2,1)S(1)}, u32[]{:S(2)}, u32[]{:S(2)}) collective-permute-start(s16[2,4,104,256]{3,2,1,0:T(8,128)(2,1)S(1)} %pad_add_fusion.refs_0_), channel_id=1, source_target_pairs={{0,6},{1,7},{2,0},{3,1},{4,2},{5,3},{6,4},{7,5},{8,14},{9,15},{10,... | collective-permute-start | bytes 1277960 | tf_op jit(solution)/shard_map/ppermute | solution.py:518
  211.7 16.8 %copy-start.4 = (s16[2,4,104,256]{3,2,1,0:T(8,128)(2,1)}, s16[2,4,104,256]{3,2,1,0:T(8,128)(2,1)S(1)}, u32[]{:S(2)}) copy-start(s16[2,4,104,256]{3,2,1,0:T(8,128)(2,1)S(1)} %collective-permute-done.13.refs_7_) | copy-start | bytes 1277956
  211.7 16.7 %collective-permute-start.7 = (s16[2,4,104,256]{3,2,1,0:T(8,128)(2,1)S(1)}, s16[2,4,104,256]{3,2,1,0:T(8,128)(2,1)S(1)}, u32[]{:S(2)}, u32[]{:S(2)}) collective-permute-start(s16[2,4,104,256]{3,2,1,0:T(8,128)(2,1)S(1)} %pad_add_fusion.refs_0_), channel_id=1, source_target_pairs={{0,2},{1,3},{2,4},{3,5},{4,6},{5,7},{6,0},{7,1},{8,10},{9,11},{10,... | collective-permute-start | bytes 1277960 | tf_op jit(solution)/shard_map/ppermute | solution.py:518
  222.3 6.1 %copy-start.5 = (s16[2,4,104,256]{3,2,1,0:T(8,128)(2,1)}, s16[2,4,104,256]{3,2,1,0:T(8,128)(2,1)S(1)}, u32[]{:S(2)}) copy-start(s16[2,4,104,256]{3,2,1,0:T(8,128)(2,1)S(1)} %collective-permute-done.12.refs_6_) | copy-start | bytes 1277956
  222.3 6.1 %copy-start.6 = (s16[2,4,104,256]{3,2,1,0:T(8,128)(2,1)}, s16[2,4,104,256]{3,2,1,0:T(8,128)(2,1)S(1)}, u32[]{:S(2)}) copy-start(s16[2,4,104,256]{3,2,1,0:T(8,128)(2,1)S(1)} %collective-permute-done.11.refs_5_) | copy-start | bytes 1277956
  222.3 6.1 %copy-start.7 = (s16[2,4,104,256]{3,2,1,0:T(8,128)(2,1)}, s16[2,4,104,256]{3,2,1,0:T(8,128)(2,1)S(1)}, u32[]{:S(2)}) copy-start(s16[2,4,104,256]{3,2,1,0:T(8,128)(2,1)S(1)} %collective-permute-done.9.refs_3_) | copy-start | bytes 1277956
  228.4 0.8 copy-start.8
  228.4 0.9 copy-start.9

commit v5 on v4

--- a/solution.py
+++ b/solution.py
@@ -11,7 +11,6 @@
 HALF = 64
 RUN = 32
 STRIP = 8
-FIRST_STEPS = 7
 VMEM_BYTES = 56 * 1024 * 1024
 
 
@@ -42,29 +41,39 @@
     return nt(left[0], right[0]) + (nt(left[0], right[1]) + nt(left[1], right[0]))
 
 
-def plan(target_front, target_row, target_col, live_count, n_front, n_row, n_col, tile_cols):
-    slots = target_front.shape[0]
+NOTE_ROWS = 8
+
+
+def pack(contributions, target_front, target_row, target_col, live_count, n_front, n_row, n_col, tile_cols):
+    slots, size, _ = contributions.shape
     capacity = max(2, -(-slots // (n_front * n_row)))
     buckets = n_front * n_row * capacity
-
-    def kernel(front_ref, row_ref, col_ref, live_ref, targets_ref, bucket_ref, counts):
+    kind = contributions.dtype
+
+    def kernel(
+        front_ref, row_ref, col_ref, live_ref, tiles_ref, packed_ref,
+        counts, bucket_of, stage, notes, sems_in, sems_out, note_sem,
+    ):
+        live = live_ref[0]
+
+        def fetch(slot):
+            return pltpu.make_async_copy(tiles_ref.at[slot], stage.at[slot], sems_in.at[slot])
+
+        def store(slot, bucket):
+            return pltpu.make_async_copy(stage.at[slot], packed_ref.at[bucket, pl.ds(0, size)], sems_out.at[slot])
+
+        def start(slot, carry):
+            fetch(slot).start()
+            return carry
+
+        lax.fori_loop(0, live, start, 0)
+        notes[...] = jnp.full(notes.shape, -1.0, kind)
+
         def clear(i, carry):
-            targets_ref[i] = -1
-            return carry
-
-        lax.fori_loop(0, buckets, clear, 0)
-
-        def clear_slots(i, carry):
-            bucket_ref[i] = -1
-            return carry
-
-        lax.fori_loop(0, slots, clear_slots, 0)
-
-        def clear_counts(i, carry):
             counts[i] = 0
             return carry
 
-        lax.fori_loop(0, n_front * n_row, clear_counts, 0)
+        lax.fori_loop(0, n_front * n_row, clear, 0)
 
         def assign(slot, carry):
             row, col = row_ref[slot], col_ref[slot]
@@ -72,71 +81,46 @@
             position = counts[destination]
             counts[destination] = position + 1
             bucket = destination * capacity + position
-            targets_ref[bucket] = lax.div(row, n_row) * tile_cols + lax.div(col, n_col)
-            bucket_ref[slot] = bucket
+            bucket_of[slot] = bucket
+            target = lax.div(row, n_row) * tile_cols + lax.div(col, n_col)
+            notes[bucket] = jnp.full(notes.shape[1:], target, jnp.int32).astype(jnp.float32).astype(kind)
             return carry
 
-        lax.fori_loop(0, live_ref[0], assign, 0)
+        lax.fori_loop(0, live, assign, 0)
+        note_copy = pltpu.make_async_copy(notes, packed_ref.at[:, pl.ds(size, NOTE_ROWS)], note_sem)
+        note_copy.start()
+
+        def forward(slot, carry):
+            fetch(slot).wait()
+            store(slot, bucket_of[slot]).start()
+            return carry
+
+        lax.fori_loop(0, live, forward, 0)
+
+        def drain(slot, carry):
+            store(slot, bucket_of[slot]).wait()
+            return carry
+
+        lax.fori_loop(0, live, drain, 0)
+        note_copy.wait()
 
     return pl.pallas_call(
         kernel,
-        name="plan",
-        out_shape=(jax.ShapeDtypeStruct((buckets,), jnp.int32), jax.ShapeDtypeStruct((slots,), jnp.int32)),
-        in_specs=[smem()] * 4,
-        out_specs=(smem(), smem()),
-        scratch_shapes=[pltpu.SMEM((n_front * n_row,), jnp.int32)],
-    )(target_front, target_row, target_col, live_count)
-
-
-def move(contributions, bucket_of, buckets):
-    slots, size, _ = contributions.shape
-
-    def kernel(bucket_ref, tiles_ref, packed_ref, stage, sems_in, sems_out):
-        def fetch(slot):
-            return pltpu.make_async_copy(tiles_ref.at[slot], stage.at[slot], sems_in.at[slot])
-
-        def store(slot, bucket):
-            return pltpu.make_async_copy(stage.at[slot], packed_ref.at[bucket], sems_out.at[slot])
-
-        for slot in range(slots):
-            fetch(slot).start()
-
-        def forward(slot, carry):
-            fetch(slot).wait()
-            bucket = bucket_ref[slot]
-
-            @pl.when(bucket >= 0)
-            def _():
-                store(slot, bucket).start()
-
-            return carry
-
-        lax.fori_loop(0, slots, forward, 0)
-
-        def drain(slot, carry):
-            bucket = bucket_ref[slot]
-
-            @pl.when(bucket >= 0)
-            def _():
-                store(slot, bucket).wait()
-
-            return carry
-
-        lax.fori_loop(0, slots, drain, 0)
-
-    return pl.pallas_call(
-        kernel,
-        name="move",
-        out_shape=jax.ShapeDtypeStruct((buckets, size, size), contributions.dtype),
-        in_specs=[smem(), hbm()],
+        name="pack",
+        out_shape=jax.ShapeDtypeStruct((buckets, size + NOTE_ROWS, size), kind),
+        in_specs=[smem()] * 4 + [hbm()],
         out_specs=hbm(),
         scratch_shapes=[
-            pltpu.VMEM((slots, size, size), contributions.dtype),
+            pltpu.SMEM((n_front * n_row,), jnp.int32),
+            pltpu.SMEM((slots,), jnp.int32),
+            pltpu.VMEM((slots, size, size), kind),
+            pltpu.VMEM((buckets, NOTE_ROWS, size), kind),
             pltpu.SemaphoreType.DMA((slots,)),
             pltpu.SemaphoreType.DMA((slots,)),
+            pltpu.SemaphoreType.DMA,
         ],
         compiler_params=pltpu.CompilerParams(vmem_limit_bytes=VMEM_BYTES),
-    )(bucket_of, contributions)
+    )(target_front, target_row, target_col, live_count, contributions)
 
 
 SCALE_ROWS = 8
@@ -167,12 +151,12 @@
 
 
 def assemble(received, arrived, front, chunks):
-    total, size, _ = received.shape
+    total, _, size = received.shape
     thin = front.shape[0] * size // chunks
 
     def kernel(arrived_ref, received_ref, front_ref, ext_ref, panel_ref, landed, column, sems):
         def copy(i):
-            return pltpu.make_async_copy(received_ref.at[i], landed.at[i], sems.at[i])
+            return pltpu.make_async_copy(received_ref.at[i, pl.ds(0, size)], landed.at[i], sems.at[i])
 
         def fetch(i, carry):
             @pl.when(arrived_ref[i] >= 0)
@@ -278,9 +262,6 @@
             work[last:BLOCK, :] = work[last:BLOCK, :] - change[last:BLOCK, :]
 
 
-HIGHEST = lax.Precision.HIGHEST
-
-
 def eliminate(full, inverses, work, blocks):
     order = full.shape[0]
     r = lax.broadcasted_iota(jnp.int32, (BLOCK, BLOCK), 0)
@@ -296,69 +277,84 @@
         inverses[k] = inverse
         full[s:e, s:e] = (jnp.where(r <= c, done, 0.0) * root).T
         if e < order:
-            panel = nt(full[e:order, s:e], inverse, HIGHEST)
+            panel = nt3(split(full[e:order, s:e]), split(inverse))
             full[e:order, s:e] = panel
+            high, low = split(panel)
             for o in range(e, order, BLOCK):
-                full[o:order, o : o + BLOCK] = full[o:order, o : o + BLOCK] - nt(
-                    panel[o - e :], panel[o - e : o - e + BLOCK], HIGHEST
+                y = slice(o - e, o - e + BLOCK)
+                full[o:order, o : o + BLOCK] = full[o:order, o : o + BLOCK] - nt3(
+                    (high[o - e :], low[o - e :]), (high[y], low[y])
                 )
 
 
+def tile_inverse(first, second, between):
+    def product(left, right):
+        return jnp.dot(left, right, precision=lax.Precision.HIGHEST, preferred_element_type=jnp.float32)
+
+    corner = -product(second, product(between, first))
+    above = jnp.concatenate([first, jnp.zeros_like(first)], axis=1)
+    return split(jnp.concatenate([above, jnp.concatenate([corner, second], axis=1)], axis=0))
+
+
 PAIRS = tuple((i, j) for i in range(LEAD_TILES) for j in range(i + 1))
 
 
-def factorize_first(ids, lead, size, blocks):
-    order = LEAD_TILES * size
-
-    def kernel(place_ref, *refs):
-        *pieces, full, inverses, work = refs
-        for ref, inner, chunk in pair_pieces(pieces, place_ref[1]):
-            for number, (i, j) in enumerate(PAIRS):
-                tile = ref[inner, number].astype(jnp.float32)
-                thin = tile.shape[0]
-                start = pl.multiple_of(i * size + chunk * thin, thin)
-                full[pl.ds(start, thin), j * size : (j + 1) * size] = tile
-        eliminate(full, inverses, work, blocks)
+def collect(ids, chunks):
+    _, thin, size = chunks[0].shape
+    count = len(chunks)
+
+    def kernel(ids_ref, *refs):
+        *chunk_refs, out_ref, sems = refs
+        for i in range(LEAD_TILES):
+            first = PAIRS.index((i, 0))
+            steps = lax.rem(ids_ref[0] - i + count, count)
+
+            def copy(ref, i=i, first=first):
+                return pltpu.make_async_copy(ref.at[pl.ds(0, i + 1)], out_ref.at[pl.ds(first, i + 1)], sems.at[i])
+
+            for s in range(count):
+
+                @pl.when(steps == s)
+                def _():
+                    copy(chunk_refs[s]).start()
+
+        for i in range(LEAD_TILES):
+            first = PAIRS.index((i, 0))
+            pltpu.make_async_copy(
+                chunk_refs[0].at[pl.ds(0, i + 1)], out_ref.at[pl.ds(first, i + 1)], sems.at[i]
+            ).wait()
 
     return pl.pallas_call(
         kernel,
-        name="factorize_first",
-        out_shape=(
-            jax.ShapeDtypeStruct((order, order), jnp.float32),
-            jax.ShapeDtypeStruct((order // BLOCK, BLOCK, BLOCK), jnp.float32),
-        ),
-        in_specs=[smem()] + [vmem()] * len(lead),
-        out_specs=(vmem(),) * 2,
-        scratch_shapes=[pltpu.VMEM((BLOCK, BLOCK), jnp.float32)],
-        compiler_params=pltpu.CompilerParams(vmem_limit_bytes=VMEM_BYTES),
-    )(ids, *lead)
-
-
-def factorize_last(begun, begun_inverses, ids, size, blocks):
+        name="collect",
+        out_shape=jax.ShapeDtypeStruct((len(PAIRS), thin, size), chunks[0].dtype),
+        in_specs=[smem()] + [hbm()] * count,
+        out_specs=vmem(),
+        scratch_shapes=[pltpu.SemaphoreType.DMA((LEAD_TILES,))],
+    )(ids, *chunks)
+
+
+def factorize_first(ids, lead, size):
     order = LEAD_TILES * size
-
-    def kernel(ids_ref, begun_ref, begun_inv_ref, high_ref, low_ref, inv_high_ref, inv_low_ref, own_ref, full, inverses, work):
-        full[...] = begun_ref[...]
-        inverses[...] = begun_inv_ref[...]
-        eliminate(full, inverses, work, blocks)
-        half = size // BLOCK
-        for q in range(LEAD_TILES):
+    done = order - size
+    half = size // BLOCK
+
+    def kernel(ids_ref, *refs):
+        *pieces, high_ref, low_ref, ih_ref, il_ref, own_ref, rest_ref, full, inverses, work = refs
+        for ref, source in ring_pieces(pieces, lax.div(ids_ref[1], 2)):
+            for number, (i, j) in enumerate(PAIRS):
+                tile = ref[number].astype(jnp.float32)
+                thin = tile.shape[0]
+                start = pl.multiple_of(i * size + source * thin, thin)
+                full[pl.ds(start, thin), j * size : (j + 1) * size] = tile
+        eliminate(full, inverses, work, range(done // BLOCK))
+        for q in range(LEAD_TILES - 1):
             s = q * size
             full[s : s + BLOCK, s + BLOCK : s + size] = jnp.zeros((BLOCK, size - BLOCK), jnp.float32)
-            first, second = inverses[q * half], inverses[q * half + 1]
-            corner = -jnp.dot(
-                second,
-                jnp.dot(
-                    full[s + BLOCK : s + size, s : s + BLOCK], first,
-                    precision=HIGHEST, preferred_element_type=jnp.float32,
-                ),
-                precision=HIGHEST, preferred_element_type=jnp.float32,
+            ih_ref[q], il_ref[q] = tile_inverse(
+                inverses[q * half], inverses[q * half + 1], full[s + BLOCK : s + size, s : s + BLOCK]
             )
-            for (y, x, part) in ((0, 0, first), (0, 1, jnp.zeros_like(first)), (1, 0, corner), (1, 1, second)):
-                high, low = split(part)
-                inv_high_ref[q, y * BLOCK : (y + 1) * BLOCK, x * BLOCK : (x + 1) * BLOCK] = high
-                inv_low_ref[q, y * BLOCK : (y + 1) * BLOCK, x * BLOCK : (x + 1) * BLOCK] = low
-        for i, j in PAIRS:
+        for i, j in PAIRS[:-1]:
             tile = full[i * size : (i + 1) * size, j * size : (j + 1) * size]
             high, low = split(tile)
             high_ref[i * size : (i + 1) * size, j * size : (j + 1) * size] = high
@@ -368,21 +364,48 @@
             def _():
                 own_ref[...] = tile
 
-    wide = jax.ShapeDtypeStruct((order, order), jnp.bfloat16)
-    inv = jax.ShapeDtypeStruct((LEAD_TILES, size, size), jnp.bfloat16)
+        rest_ref[...] = full[done:order, done:order]
+
+    wide = jax.ShapeDtypeStruct((order, done), jnp.bfloat16)
+    inv = jax.ShapeDtypeStruct((LEAD_TILES - 1, size, size), jnp.bfloat16)
+    tile = jax.ShapeDtypeStruct((size, size), jnp.float32)
+    return pl.pallas_call(
+        kernel,
+        name="factorize_first",
+        out_shape=(wide, wide, inv, inv, tile, tile),
+        in_specs=[smem()] + [vmem()] * len(lead),
+        out_specs=(vmem(),) * 6,
+        scratch_shapes=[
+            pltpu.VMEM((order, order), jnp.float32),
+            pltpu.VMEM((done // BLOCK, BLOCK, BLOCK), jnp.float32),
+            pltpu.VMEM((BLOCK, BLOCK), jnp.float32),
+        ],
+        compiler_params=pltpu.CompilerParams(vmem_limit_bytes=VMEM_BYTES),
+    )(ids, *lead)
+
+
+def factorize_last(rest):
+    size = rest.shape[0]
+
+    def kernel(rest_ref, own_ref, ih_ref, il_ref, inverses, work):
+        own_ref[...] = rest_ref[...]
+        eliminate(own_ref, inverses, work, range(size // BLOCK))
+        own_ref[0:BLOCK, BLOCK:size] = jnp.zeros((BLOCK, size - BLOCK), jnp.float32)
+        ih_ref[...], il_ref[...] = tile_inverse(inverses[0], inverses[1], own_ref[BLOCK:size, 0:BLOCK])
+
+    inv = jax.ShapeDtypeStruct((size, size), jnp.bfloat16)
     return pl.pallas_call(
         kernel,
         name="factorize_last",
-        out_shape=(wide, wide, inv, inv, jax.ShapeDtypeStruct((size, size), jnp.float32)),
-        in_specs=[smem(), vmem(), vmem()],
-        out_specs=(vmem(),) * 5,
+        out_shape=(jax.ShapeDtypeStruct((size, size), jnp.float32), inv, inv),
+        in_specs=[vmem()],
+        out_specs=(vmem(),) * 3,
         scratch_shapes=[
-            pltpu.VMEM((order, order), jnp.float32),
-            pltpu.VMEM((order // BLOCK, BLOCK, BLOCK), jnp.float32),
+            pltpu.VMEM((size // BLOCK, BLOCK, BLOCK), jnp.float32),
             pltpu.VMEM((BLOCK, BLOCK), jnp.float32),
         ],
         compiler_params=pltpu.CompilerParams(vmem_limit_bytes=VMEM_BYTES),
-    )(ids, begun, begun_inverses)
+    )(rest)
 
 
 def solve(panels, factors):
@@ -391,14 +414,17 @@
     count = len(panels)
 
     def kernel(*refs):
-        panel_refs, (high_ref, low_ref, ih_ref, il_ref) = refs[:count], refs[count : count + 4]
-        *out_refs, xh, xl = refs[count + 4 :]
+        panel_refs = refs[:count]
+        high_ref, low_ref, ih_ref, il_ref, last_ih_ref, last_il_ref = refs[count : count + 6]
+        *out_refs, xh, xl = refs[count + 6 :]
         for q in range(LEAD_TILES):
             s, e = q * size, (q + 1) * size
             acc = jnp.concatenate([decode(ref[q]) for ref in panel_refs], axis=0)
             if q:
                 acc = acc - nt3((xh[:, 0:s], xl[:, 0:s]), (high_ref[s:e, 0:s], low_ref[s:e, 0:s]))
-            x = nt3(split(acc), (ih_ref[q], il_ref[q]))
+            last = q == LEAD_TILES - 1
+            inverse = (last_ih_ref[...], last_il_ref[...]) if last else (ih_ref[q], il_ref[q])
+            x = nt3(split(acc), inverse)
             xh[:, s:e], xl[:, s:e] = split(x)
             for number, ref in enumerate(out_refs):
                 ref[q] = encode(x[number * thin : (number + 1) * thin])
@@ -407,14 +433,14 @@
         kernel,
         name="solve",
         out_shape=(jax.ShapeDtypeStruct((LEAD_TILES, coded_rows, size), jnp.int16),) * count,
-        in_specs=[vmem()] * (count + 4),
+        in_specs=[vmem()] * (count + 6),
         out_specs=(vmem(),) * count,
         scratch_shapes=[pltpu.VMEM((count * thin, order), jnp.bfloat16)] * 2,
         compiler_params=pltpu.CompilerParams(vmem_limit_bytes=VMEM_BYTES),
     )(*panels, *factors)
 
 
-def finish(ids, rows, cols, own, extended, front):
+def finish(ids, rows, cols, own, last_own, extended, front):
     size = own.shape[0]
     order = LEAD_TILES * size
     tile_rows, tile_cols = front.shape[:2]
@@ -424,7 +450,7 @@
 
     def kernel(ids_ref, *refs):
         row_pieces, col_pieces = refs[:half], refs[half : 2 * half]
-        own_ref, ext_ref, front_ref, out_ref, xh, xl = refs[2 * half :]
+        own_ref, last_own_ref, ext_ref, front_ref, out_ref, xh, xl = refs[2 * half :]
         row, col = ids_ref[0], ids_ref[1]
 
         def put(a, b, tile):
@@ -463,6 +489,7 @@
             put(a, b, zero)
         in_panel = col < LEAD_TILES
         lead_row = row < LEAD_TILES
+        last_tile = LEAD_TILES - 1
         put_panel(1)
         put_panel(2)
 
@@ -481,7 +508,7 @@
         def _():
             @pl.when(lead_row)
             def _():
-                put(0, 0, own_ref[...])
+                put(0, 0, jnp.where((row == last_tile) & (col == last_tile), last_own_ref[...], own_ref[...]))
 
             @pl.when(jnp.logical_not(lead_row))
             def _():
@@ -500,11 +527,11 @@
         kernel,
         name="finish",
         out_shape=jax.ShapeDtypeStruct((tile_rows * size * tile_cols * parts, lanes), jnp.float32),
-        in_specs=[smem()] + [vmem()] * (2 * half + 3),
+        in_specs=[smem()] + [vmem()] * (2 * half + 4),
         out_specs=vmem(),
         scratch_shapes=[pltpu.VMEM((2 * tile_rows * size, order), jnp.bfloat16)] * 2,
         compiler_params=pltpu.CompilerParams(vmem_limit_bytes=VMEM_BYTES),
-    )(ids, *rows, *cols, own, extended, front)
+    )(ids, *rows, *cols, own, last_own, extended, front)
 
 
 SHIFTS = (1, 3, 2)
@@ -518,21 +545,28 @@
     return lax.ppermute(value, axis, [(i, target(i)) for i in range(lax.axis_size(axis))])
 
 
-def pair_gather(value, axis):
+def ring_gather(value, axis):
     ring = lax.axis_size(axis) // 2
-    partner = permute(value, axis, lambda i: i ^ 1)
-    pair = jnp.stack([value, partner])
-    shifted = [permute(pair, axis, lambda i: (i // 2 + shift) % ring * 2 + i % 2) for shift in SHIFTS]
-    return (pair, *shifted)
-
-
-def pair_pieces(pieces, place):
+    shifted = [permute(value, axis, lambda i: (i // 2 + shift) % ring * 2 + i % 2) for shift in SHIFTS]
+    return (value, *shifted)
+
+
+def ring_pieces(pieces, place):
     ring = len(SHIFTS) + 1
     for ref, shift in zip(pieces, (0,) + SHIFTS, strict=True):
-        source = lax.rem(lax.div(place, 2) + (ring - shift), ring) * 2
-        side = lax.rem(place, 2)
-        yield ref, 0, source + side
-        yield ref, 1, source + 1 - side
+        yield ref, lax.rem(place + (ring - shift), ring)
+
+
+def pair_gather(value, axis):
+    partner = permute(value, axis, lambda i: i ^ 1)
+    return ring_gather(jnp.stack([value, partner]), axis)
+
+
+def pair_pieces(pieces, place):
+    side = lax.rem(place, 2)
+    for ref, source in ring_pieces(pieces, lax.div(place, 2)):
+        yield ref, 0, 2 * source + side
+        yield ref, 1, 2 * source + 1 - side
 
 
 def per_device(front_matrix, contributions, target_front, target_row, target_col, live_count):
@@ -542,48 +576,36 @@
     front = front_matrix.reshape(tile_rows, size, tile_cols, size).transpose(0, 2, 1, 3)
     ids = jnp.stack([lax.axis_index("row"), lax.axis_index("col")]).astype(jnp.int32)
 
-    thin = size // n_col
-    chunk = exchange(front[0, 0].reshape(n_col, thin, size), "col")[:LEAD_TILES]
-
-    targets, bucket_of = plan(
+    ring = n_col // 2
+    thin = size // ring
+    chunks = jnp.repeat(front[0, 0].reshape(ring, thin, size), 2, axis=0)
+    chunk = exchange(chunks, "col")[:LEAD_TILES]
+    leading = [chunk]
+    for step in range(1, n_row):
+        leading.append(lax.ppermute(chunk, "row", [(i, (i + step) % n_row) for i in range(LEAD_TILES)]))
+
+    packed = pack(
+        contributions.reshape(slots, size, size),
         target_front.reshape(slots), target_row.reshape(slots), target_col.reshape(slots),
         live_count.reshape(1), n_front, n_row, n_col, tile_cols,
     )
-    packed = move(contributions.reshape(slots, size, size), bucket_of, targets.shape[0])
     received = exchange(packed, ("front", "row"))
 
-    capacity = targets.shape[0] // (n_front * n_row)
-    other = permute(targets, "front", lambda i: 1 - i)
-    front_index = lax.axis_index("front")
-    by_source = [jnp.where(front_index == source, targets, other) for source in range(n_front)]
-    aimed = lax.dynamic_index_in_dim(
-        jnp.stack(by_source).reshape(n_front, n_front, n_row, capacity), front_index, axis=1, keepdims=False
-    )
-    notes = aimed.transpose(1, 0, 2).reshape(n_row, 1, n_front * capacity).astype(jnp.bfloat16)
-    notes = jnp.pad(notes, ((0, 0), (0, 7), (0, size - n_front * capacity)))
-    flat = chunk.reshape(LEAD_TILES * thin, size)
-    sent = jnp.concatenate([jnp.broadcast_to(flat[None], (n_row,) + flat.shape), notes], axis=1)
-    got = exchange(sent, "row")
-    leading = got[:, : LEAD_TILES * thin].reshape(n_row, LEAD_TILES, thin, size)
-    arrived = got[:, LEAD_TILES * thin, : n_front * capacity].astype(jnp.int32)
-    arrived = arrived.reshape(n_row, n_front, capacity).transpose(1, 0, 2).reshape(targets.shape)
-
-    lower = jnp.concatenate([leading[i, : i + 1] for i in range(LEAD_TILES)], axis=0)
-    lead = pair_gather(lower, "col")
-    steps = LEAD_TILES * size // BLOCK
-    begun, inverses = factorize_first(ids, lead, size, range(FIRST_STEPS))
-    arrived, begun = lax.optimization_barrier((arrived, begun))
-
+    lead = ring_gather(collect(ids, leading), "col")
+    *factors, own, rest = factorize_first(ids, lead, size)
+    received, rest = lax.optimization_barrier((received, rest))
+
+    arrived = received[:, size, 0].astype(jnp.int32)
     extended, panel = assemble(received, arrived, front, n_col)
     mine = exchange(panel, "col")[:LEAD_TILES]
-    *factors, own = factorize_last(begun, inverses, ids, size, range(FIRST_STEPS, steps))
+    last_own, *last_inverse = factorize_last(rest)
     turned = lax.ppermute(
         mine, ("row", "col"), [(r * n_col + c, c * n_col + r) for r in range(n_row) for c in range(n_col)]
     )
-    solved, turned = solve((mine, turned), factors)
+    solved, turned = solve((mine, turned), (*factors, *last_inverse))
     rows = pair_gather(solved, "col")
     cols = pair_gather(turned, "row")
-    factor = finish(ids, rows, cols, own, extended, front)
+    factor = finish(ids, rows, cols, own, last_own, extended, front)
     return factor.reshape(1, tile_rows, 1, size, tile_cols, 1, size)
 
 

time: 239 us -> 225 us (0.941)
  waiting for transfers between devices: 95.1 us -> 71.9 us
  starting transfers between devices: 44.3 us -> 58.4 us
  Pallas kernels: 74.7 us -> 67.3 us
    ppermute x13 -> x11, waiting for transfers between devices: 87 us -> 23.2 us  [permute(): lax.ppermute(value, axis, [(i, target(i)) for i in range(lax.axis_size(ax...]
    ppermute x0 -> x7, waiting for transfers between devices: none -> 48.5 us  [per_device(): lax.ppermute(chunk, 'row', [(i, (i + step) % n_row) for i in range(LEAD_T...]
    ppermute x0 -> x7, starting transfers between devices: none -> 14.5 us  [per_device(): lax.ppermute(chunk, 'row', [(i, (i + step) % n_row) for i in range(LEAD_T...]
    all_to_all x3 -> x2, waiting for transfers between devices: 8.03 us -> 0.19 us  [exchange(): return lax.all_to_all(value, axis, split_axis=0, concat_axis=0, tiled=True)]
    pallas_call x4, Pallas kernels: 55.9 us -> 48.7 us  [the longest x1 31.4 us: factorize_first(): pl.pallas_call(kernel, name='factorize_first', out_shape=(wide, wide, inv...]
    all_to_all x3 -> x2, starting transfers between devices: 21.2 us -> 14.2 us  [exchange(): return lax.all_to_all(value, axis, split_axis=0, concat_axis=0, tiled=True)]
    ppermute x13 -> x11, starting transfers between devices: 22.5 us -> 29.1 us  [permute(): lax.ppermute(value, axis, [(i, target(i)) for i in range(lax.axis_size(ax...]
  transfers between devices with their start and end apart: 17 -> 21, of which waited for: 11 -> 12; matrix products, arithmetic and copies ran while one was open for 2% -> 1% of each run, Pallas kernels for 23% -> 22%
where the time goes in v5:
time: 225 us; the launch traced here: 222 us
  waiting for transfers between devices  71.9 us (32%)
  Pallas kernels  67.3 us (30%)
  starting transfers between devices  58.4 us (26%)
  blocking collectives  14.4 us (6%)
  other arithmetic  4.59 us (2%)
  local copies, waits for them, and re-layouts  4.52 us (2%)
    ppermute x7, waiting for transfers between devices, per_device(): lax.ppermute(chunk, 'row', [(i, (i + step) % n_row) for i in range(LEAD_T...  48.5 us
    pallas_call x1, Pallas kernels, factorize_first(): pl.pallas_call(kernel, name='factorize_first', out_shape=(wide, wide, inv...  31.4 us
    ppermute x11, starting transfers between devices, permute(): lax.ppermute(value, axis, [(i, target(i)) for i in range(lax.axis_size(ax...  29.1 us
    ppermute x11, waiting for transfers between devices, permute(): lax.ppermute(value, axis, [(i, target(i)) for i in range(lax.axis_size(ax...  23.2 us
    ppermute x7, starting transfers between devices, per_device(): lax.ppermute(chunk, 'row', [(i, (i + step) % n_row) for i in range(LEAD_T...  14.5 us
    all_to_all x1, blocking collectives, exchange(): return lax.all_to_all(value, axis, split_axis=0, concat_axis=0, tiled=True)  14.4 us
    all_to_all x2, starting transfers between devices, exchange(): return lax.all_to_all(value, axis, split_axis=0, concat_axis=0, tiled=True)  14.2 us
    pallas_call x1, Pallas kernels, factorize_last(): pl.pallas_call(kernel, name='factorize_last', out_shape=(jax.ShapeDtypeSt...  9.58 us
  transfers between devices with their start and end apart: 21, of which 12 were waited for; matrix products, arithmetic and copies ran while one was open for 1% of the time, Pallas kernels for 22%

profile of v5, /device:TPU:6, one launch (start us, length us, event | category | flops | bytes accessed | tf_op | source)
XLA Modules:
  0.0 222.1 jit_solution(4470509762578408402)
XLA Ops:
  0.0 0.9 slice.16
  0.9 0.7 broadcast_in_dim.3
  1.6 6.8 %all-to-all-start.1 = ((bf16[8,64,256]{2,1,0:T(8,128)(2,1)}), bf16[8,64,256]{2,1,0:T(8,128)(2,1)S(1)}, u32[]{:S(2)}, u32[]{:S(2)}) async-start(bf16[8,64,256]{2,1,0:T(8,128)(2,1)} %bitcast.10), calls=%async_computation.1 | async-start | bytes 524288 | tf_op jit(solution)/shard_map/all_to_all | solution.py:541
  9.1 5.3 %pack.1 = bf16[32,264,256]{2,1,0:T(8,128)(2,1)} custom-call(s32[32]{0:T(128)} %bitcast.27, s32[32]{0:T(128)} %bitcast.28, s32[32]{0:T(128)} %bitcast.29, s32[1]{0:T(128)} %bitcast.17.live_ref, bf16[32,256,256]{2,1,0:T(8,128)(2,1)} %bitcast.21), custom_call_target="tpu_custom_call" | custom-call | tf_op jit(solution)/shard_map/pack/pallas_call | solution.py:107
  14.3 0.2 all-to-all-done.1
  14.5 7.4 %all-to-all-start = ((bf16[32,264,256]{2,1,0:T(8,128)(2,1)}), bf16[32,264,256]{2,1,0:T(8,128)(2,1)}, u32[]{:S(2)}, u32[]{:S(2)}) async-start(bf16[32,264,256]{2,1,0:T(8,128)(2,1)} %pack.1), calls=%async_computation | async-start | bytes 8650752 | tf_op jit(solution)/shard_map/all_to_all | solution.py:541
  22.0 0.0 copy-start.3
  22.0 3.4 %collective-permute-start = (bf16[4,64,256]{2,1,0:T(8,128)(2,1)S(1)}, bf16[4,64,256]{2,1,0:T(8,128)(2,1)S(1)}, u32[]{:S(2)}, u32[]{:S(2)}) collective-permute-start(bf16[4,64,256]{2,1,0:T(8,128)(2,1)S(1)} %slice.17.refs_0_), channel_id=1, source_target_pairs={{0,8},{8,16},{16,24},{24,32},{1,9},{9,17},{17,25},{25,33},{2,10},{... | collective-permute-start | bytes 393224 | tf_op jit(solution)/shard_map/ppermute | solution.py:585
  25.4 3.4 %collective-permute-start.1 = (bf16[4,64,256]{2,1,0:T(8,128)(2,1)S(1)}, bf16[4,64,256]{2,1,0:T(8,128)(2,1)S(1)}, u32[]{:S(2)}, u32[]{:S(2)}) collective-permute-start(bf16[4,64,256]{2,1,0:T(8,128)(2,1)S(1)} %slice.17.refs_0_), channel_id=1, source_target_pairs={{0,16},{8,24},{16,32},{24,40},{1,17},{9,25},{17,33},{25,41},{2,18}... | collective-permute-start | bytes 393224 | tf_op jit(solution)/shard_map/ppermute | solution.py:585
  28.8 1.3 collective-permute-start.2
  30.1 1.3 collective-permute-start.3
  31.4 1.3 collective-permute-start.4
  32.7 41.8 %collective-permute-done.refs_1_ = bf16[4,64,256]{2,1,0:T(8,128)(2,1)S(1)} collective-permute-done((bf16[4,64,256]{2,1,0:T(8,128)(2,1)S(1)}, bf16[4,64,256]{2,1,0:T(8,128)(2,1)S(1)}, u32[]{:S(2)}, u32[]{:S(2)}) %collective-permute-start) | collective-permute-done | bytes 131104 | tf_op jit(solution)/shard_map/ppermute | solution.py:585
  74.5 1.9 collective-permute-start.5
  76.4 0.0 collective-permute-done.1.refs_2_
  76.4 0.0 copy-start.15
  76.4 1.9 collective-permute-start.6
  78.4 0.6 pad_add_fusion.2.ids_ref
  79.0 0.0 collective-permute-done.2.refs_3_
  79.0 1.5 collective-permute-done.3.refs_4_
  80.5 0.4 collective-permute-done.4.refs_5_
  80.9 3.3 %collective-permute-done.5.refs_6_ = bf16[4,64,256]{2,1,0:T(8,128)(2,1)S(1)} collective-permute-done((bf16[4,64,256]{2,1,0:T(8,128)(2,1)S(1)}, bf16[4,64,256]{2,1,0:T(8,128)(2,1)S(1)}, u32[]{:S(2)}, u32[]{:S(2)}) %collective-permute-start.5) | collective-permute-done | bytes 131104 | tf_op jit(solution)/shard_map/ppermute | solution.py:585
  84.2 1.5 collective-permute-done.6.refs_7_
  85.7 0.0 copy-done.3
  85.8 0.6 copy-done.20
  86.4 2.4 %collect.1.refs_0_ = bf16[10,64,256]{2,1,0:T(8,128)(2,1)} custom-call(s32[2]{0:T(128)} %pad_add_fusion.2.ids_ref, bf16[4,64,256]{2,1,0:T(8,128)(2,1)} %copy-done.3, bf16[4,64,256]{2,1,0:T(8,128)(2,1)} %copy-done.14, bf16[4,64,256]{2,1,0:T(8,128)(2,1)} %copy-done.15, bf16[4,64,256]{2,1,0:T(8,128)(2,1)} %copy-done.16, bf16[4,64,256]{2,1,0:T(8,128)(2,1)} %copy-done.17, ...), custom_call_target="tpu_custom_call" | custom-call | tf_op jit(solution)/shard_map/collect/pallas_call | solution.py:327
  88.8 0.8 collective-permute-start.7
  89.6 2.5 %collective-permute-start.8 = (bf16[10,64,256]{2,1,0:T(8,128)(2,1)}, bf16[10,64,256]{2,1,0:T(8,128)(2,1)S(1)}, u32[]{:S(2)}, u32[]{:S(2)}) collective-permute-start(bf16[10,64,256]{2,1,0:T(8,128)(2,1)} %collect.1.refs_0_), channel_id=1, source_target_pairs={{0,6},{1,7},{2,0},{3,1},{4,2},{5,3},{6,4},{7,5},{8,14},{9,15},{10,... | collective-permute-start | bytes 983048 | tf_op jit(solution)/shard_map/ppermute | solution.py:545
  92.2 1.3 collective-permute-start.9
  93.4 6.9 %collective-permute-done.7.refs_1_ = bf16[10,64,256]{2,1,0:T(8,128)(2,1)S(1)} collective-permute-done((bf16[10,64,256]{2,1,0:T(8,128)(2,1)}, bf16[10,64,256]{2,1,0:T(8,128)(2,1)S(1)}, u32[]{:S(2)}, u32[]{:S(2)}) %collective-permute-start.7) | collective-permute-done | bytes 327712 | tf_op jit(solution)/shard_map/ppermute | solution.py:545
  100.4 5.0 %collective-permute-done.8.refs_2_ = bf16[10,64,256]{2,1,0:T(8,128)(2,1)S(1)} collective-permute-done((bf16[10,64,256]{2,1,0:T(8,128)(2,1)}, bf16[10,64,256]{2,1,0:T(8,128)(2,1)S(1)}, u32[]{:S(2)}, u32[]{:S(2)}) %collective-permute-start.8) | collective-permute-done | bytes 327712 | tf_op jit(solution)/shard_map/ppermute | solution.py:545
  105.4 1.1 collective-permute-done.9.refs_3_
  106.5 0.0 copy-done.10
  106.5 0.7 copy-done.12
  107.2 31.4 %factorize_first.1 = (bf16[1024,768]{1,0:T(8,128)(2,1)}, bf16[1024,768]{1,0:T(8,128)(2,1)}, bf16[3,256,256]{2,1,0:T(8,128)(2,1)}, bf16[3,256,256]{2,1,0:T(8,128)...) custom-call(s32[2]{0:T(128)} %pad_add_fusion.2.ids_ref, bf16[10,64,256]{2,1,0:T(8,128)(2,1)} %collect.1.refs_0_, ...), custom_call_target="tpu_custom_call" | custom-call | tf_op jit(solution)/shard_map/factorize_first/pallas_call | solution.py:372
  138.6 0.0 all-to-all-done.received_ref
  138.6 2.1 convert_reduce_fusion.arrived_ref
  140.7 4.9 %assemble.1 = (f32[5,256,256]{2,1,0:T(8,128)}, s16[8,104,256]{2,1,0:T(8,128)(2,1)}) custom-call(s32[32]{0:T(128)} %convert_reduce_fusion.arrived_ref, bf16[32,264,256]{2,1,0:T(8,128)(2,1)} %all-to-all-done.received_ref, bf16[3,3,256,256]{3,2,1,0:T(8,128)(2,1)} %bitcast.19), custom_call_target="tpu_custom_call" | custom-call | tf_op jit(solution)/shard_map/assemble/pallas_call | solution.py:190
  145.6 14.4 %all_to_all.15 = s16[8,104,256]{2,1,0:T(8,128)(2,1)S(1)} all-to-all(s16[8,104,256]{2,1,0:T(8,128)(2,1)} %get-tuple-element.22), channel_id=1, replica_groups=mesh['front'=2,'row'=8,'col'=8] {'col'}, dimensions={0} | all-to-all | bytes 851968 | tf_op jit(solution)/shard_map/all_to_all | solution.py:541
  160.1 0.7 collective-permute-start.10
  160.8 9.6 %factorize_last.1 = (f32[256,256]{1,0:T(8,128)}, bf16[256,256]{1,0:T(8,128)(2,1)}, bf16[256,256]{1,0:T(8,128)(2,1)}) custom-call(f32[256,256]{1,0:T(8,128)} %get-tuple-element.27.rest_ref), custom_call_target="tpu_custom_call" | custom-call | tf_op jit(solution)/shard_map/factorize_last/pallas_call | solution.py:397
  170.3 0.0 collective-permute-done.10.refs_1_
  170.3 0.7 copy-done.13
  171.0 5.7 %solve.1 = (s16[4,104,256]{2,1,0:T(8,128)(2,1)}, s16[4,104,256]{2,1,0:T(8,128)(2,1)}) custom-call(s16[4,104,256]{2,1,0:T(8,128)(2,1)} %copy-done.2, s16[4,104,256]{2,1,0:T(8,128)(2,1)} %copy-done.13, bf16[1024,768]{1,0:T(8,128)(2,1)} %get-tuple-element.23.refs_2_, bf16[1024,768]{1,0:T(8,128)(2,1)} %get-tuple-element.24.refs_3_, ...), custom_call_target="tpu_custom_call" | custom-call | tf_op jit(solution)/shard_map/solve/pallas_call | solution.py:432
  176.7 2.8 %collective-permute-start.11 = (s16[4,104,256]{2,1,0:T(8,128)(2,1)}, s16[4,104,256]{2,1,0:T(8,128)(2,1)S(1)}, u32[]{:S(2)}, u32[]{:S(2)}) collective-permute-start(s16[4,104,256]{2,1,0:T(8,128)(2,1)} %get-tuple-element.30), channel_id=1, source_target_pairs={{0,1},{1,0},{2,3},{3,2},{4,5},{5,4},{6,7},{7,6},{8,9},{9,8},{10,11... | collective-permute-start | bytes 638984 | tf_op jit(solution)/shard_map/ppermute | solution.py:545
  179.6 4.0 %collective-permute-done.11 = s16[4,104,256]{2,1,0:T(8,128)(2,1)S(1)} collective-permute-done((s16[4,104,256]{2,1,0:T(8,128)(2,1)}, s16[4,104,256]{2,1,0:T(8,128)(2,1)S(1)}, u32[]{:S(2)}, u32[]{:S(2)}) %collective-permute-start.11) | collective-permute-done | bytes 213024 | tf_op jit(solution)/shard_map/ppermute | solution.py:545
  183.6 1.0 pad_add_fusion.refs_0_
  184.6 1.1 collective-permute-start.12
  185.7 3.5 %collective-permute-start.15 = (s16[4,104,256]{2,1,0:T(8,128)(2,1)}, s16[4,104,256]{2,1,0:T(8,128)(2,1)S(1)}, u32[]{:S(2)}, u32[]{:S(2)}) collective-permute-start(s16[4,104,256]{2,1,0:T(8,128)(2,1)} %get-tuple-element.31), channel_id=1, source_target_pairs={{0,8},{8,0},{16,24},{24,16},{32,40},{40,32},{48,56},{56,48},{1,9},... | collective-permute-start | bytes 638984 | tf_op jit(solution)/shard_map/ppermute | solution.py:545
  189.2 5.8 %collective-permute-start.13 = (s16[2,4,104,256]{3,2,1,0:T(8,128)(2,1)S(1)}, s16[2,4,104,256]{3,2,1,0:T(8,128)(2,1)S(1)}, u32[]{:S(2)}, u32[]{:S(2)}) collective-permute-start(s16[2,4,104,256]{3,2,1,0:T(8,128)(2,1)S(1)} %pad_add_fusion.refs_0_), channel_id=1, source_target_pairs={{0,6},{1,7},{2,0},{3,1},{4,2},{5,3},{6,4},{7,5},{8,14},{9,15},{10,... | collective-permute-start | bytes 1277960 | tf_op jit(solution)/shard_map/ppermute | solution.py:545
  194.9 1.4 collective-permute-start.14
  196.3 0.0 collective-permute-done.15
  196.3 1.0 pad_add_fusion.1.refs_4_
  197.3 0.3 collective-permute-start.16
  197.6 3.1 %collective-permute-start.17 = (s16[2,4,104,256]{3,2,1,0:T(8,128)(2,1)S(1)}, s16[2,4,104,256]{3,2,1,0:T(8,128)(2,1)S(1)}, u32[]{:S(2)}, u32[]{:S(2)}) collective-permute-start(s16[2,4,104,256]{3,2,1,0:T(8,128)(2,1)S(1)} %pad_add_fusion.1.refs_4_), channel_id=1, source_target_pairs={{0,48},{8,56},{16,0},{24,8},{32,16},{40,24},{48,32},{56,40},{1,49}... | collective-permute-start | bytes 1277960 | tf_op jit(solution)/shard_map/ppermute | solution.py:545
  200.8 0.0 collective-permute-done.12.refs_1_
  200.8 6.5 %collective-permute-start.18 = (s16[2,4,104,256]{3,2,1,0:T(8,128)(2,1)S(1)}, s16[2,4,104,256]{3,2,1,0:T(8,128)(2,1)S(1)}, u32[]{:S(2)}, u32[]{:S(2)}) collective-permute-start(s16[2,4,104,256]{3,2,1,0:T(8,128)(2,1)S(1)} %pad_add_fusion.1.refs_4_), channel_id=1, source_target_pairs={{0,32},{8,40},{16,48},{24,56},{32,0},{40,8},{48,16},{56,24},{1,33}... | collective-permute-start | bytes 1277960 | tf_op jit(solution)/shard_map/ppermute | solution.py:545
  207.2 0.0 collective-permute-done.13.refs_2_
  207.3 0.0 collective-permute-done.14.refs_3_
  207.3 0.3 collective-permute-done.16.refs_5_
  207.6 0.0 collective-permute-done.17.refs_6_
  207.6 5.8 %collective-permute-done.18.refs_7_ = s16[2,4,104,256]{3,2,1,0:T(8,128)(2,1)S(1)} collective-permute-done((s16[2,4,104,256]{3,2,1,0:T(8,128)(2,1)S(1)}, s16[2,4,104,256]{3,2,1,0:T(8,128)(2,1)S(1)}, u32[]{:S(2)}, u32[]{:S(2)}) %collective-permute-start.18) | collective-permute-done | bytes 426016 | tf_op jit(solution)/shard_map/ppermute | solution.py:545
  213.4 0.7 copy-done.9
  214.1 8.0 %finish.1 = f32[4608,128]{1,0:T(8,128)} custom-call(s32[2]{0:T(128)} %pad_add_fusion.2.ids_ref, s16[2,4,104,256]{3,2,1,0:T(8,128)(2,1)} %copy-done, s16[2,4,104,256]{3,2,1,0:T(8,128)(2,1)} %copy-done.4, s16[2,4,104,256]{3,2,1,0:T(8,128)(2,1)} %copy-done.5, s16[2,4,104,256]{3,2,1,0:T(8,128)(2,1)} %copy-done.6, s16[2,4,104,256]{3,2,1,0:T(8,128)(2,1)} %copy-done.1, ...), custom_call_target="tpu_custom_call" | custom-call | tf_op jit(solution)/shard_map/finish/pallas_call | solution.py:526
  (36 shorter events, 0.1 us)
Async XLA Ops:
  1.6 12.9 %all-to-all-start.1 = ((bf16[8,64,256]{2,1,0:T(8,128)(2,1)}), bf16[8,64,256]{2,1,0:T(8,128)(2,1)S(1)}, u32[]{:S(2)}, u32[]{:S(2)}) async-start(bf16[8,64,256]{2,1,0:T(8,128)(2,1)} %bitcast.10), calls=%async_computation.1 | async-start | bytes 524288 | tf_op jit(solution)/shard_map/all_to_all | solution.py:541
  14.5 124.1 %all-to-all-start = ((bf16[32,264,256]{2,1,0:T(8,128)(2,1)}), bf16[32,264,256]{2,1,0:T(8,128)(2,1)}, u32[]{:S(2)}, u32[]{:S(2)}) async-start(bf16[32,264,256]{2,1,0:T(8,128)(2,1)} %pack.1), calls=%async_computation | async-start | bytes 8650752 | tf_op jit(solution)/shard_map/all_to_all | solution.py:541
  22.0 63.7 %copy-start.3 = (bf16[4,64,256]{2,1,0:T(8,128)(2,1)}, bf16[4,64,256]{2,1,0:T(8,128)(2,1)S(1)}, u32[]{:S(2)}) copy-start(bf16[4,64,256]{2,1,0:T(8,128)(2,1)S(1)} %slice.17.refs_0_) | copy-start | bytes 393220
  22.0 52.5 %collective-permute-start = (bf16[4,64,256]{2,1,0:T(8,128)(2,1)S(1)}, bf16[4,64,256]{2,1,0:T(8,128)(2,1)S(1)}, u32[]{:S(2)}, u32[]{:S(2)}) collective-permute-start(bf16[4,64,256]{2,1,0:T(8,128)(2,1)S(1)} %slice.17.refs_0_), channel_id=1, source_target_pairs={{0,8},{8,16},{16,24},{24,32},{1,9},{9,17},{17,25},{25,33},{2,10},{... | collective-permute-start | bytes 393224 | tf_op jit(solution)/shard_map/ppermute | solution.py:585
  25.4 51.0 %collective-permute-start.1 = (bf16[4,64,256]{2,1,0:T(8,128)(2,1)S(1)}, bf16[4,64,256]{2,1,0:T(8,128)(2,1)S(1)}, u32[]{:S(2)}, u32[]{:S(2)}) collective-permute-start(bf16[4,64,256]{2,1,0:T(8,128)(2,1)S(1)} %slice.17.refs_0_), channel_id=1, source_target_pairs={{0,16},{8,24},{16,32},{24,40},{1,17},{9,25},{17,33},{25,41},{2,18}... | collective-permute-start | bytes 393224 | tf_op jit(solution)/shard_map/ppermute | solution.py:585
  28.8 50.2 %collective-permute-start.2 = (bf16[4,64,256]{2,1,0:T(8,128)(2,1)S(1)}, bf16[4,64,256]{2,1,0:T(8,128)(2,1)S(1)}, u32[]{:S(2)}, u32[]{:S(2)}) collective-permute-start(bf16[4,64,256]{2,1,0:T(8,128)(2,1)S(1)} %slice.17.refs_0_), channel_id=1, source_target_pairs={{0,24},{8,32},{16,40},{24,48},{1,25},{9,33},{17,41},{25,49},{2,26}... | collective-permute-start | bytes 393224 | tf_op jit(solution)/shard_map/ppermute | solution.py:585
  30.1 50.4 %collective-permute-start.3 = (bf16[4,64,256]{2,1,0:T(8,128)(2,1)S(1)}, bf16[4,64,256]{2,1,0:T(8,128)(2,1)S(1)}, u32[]{:S(2)}, u32[]{:S(2)}) collective-permute-start(bf16[4,64,256]{2,1,0:T(8,128)(2,1)S(1)} %slice.17.refs_0_), channel_id=1, source_target_pairs={{0,32},{8,40},{16,48},{24,56},{1,33},{9,41},{17,49},{25,57},{2,34}... | collective-permute-start | bytes 393224 | tf_op jit(solution)/shard_map/ppermute | solution.py:585
  31.4 49.5 %collective-permute-start.4 = (bf16[4,64,256]{2,1,0:T(8,128)(2,1)S(1)}, bf16[4,64,256]{2,1,0:T(8,128)(2,1)S(1)}, u32[]{:S(2)}, u32[]{:S(2)}) collective-permute-start(bf16[4,64,256]{2,1,0:T(8,128)(2,1)S(1)} %slice.17.refs_0_), channel_id=1, source_target_pairs={{0,40},{8,48},{16,56},{24,0},{1,41},{9,49},{17,57},{25,1},{2,42},{... | collective-permute-start | bytes 393224 | tf_op jit(solution)/shard_map/ppermute | solution.py:585
  74.5 11.2 %copy-start.14 = (bf16[4,64,256]{2,1,0:T(8,128)(2,1)}, bf16[4,64,256]{2,1,0:T(8,128)(2,1)S(1)}, u32[]{:S(2)}) copy-start(bf16[4,64,256]{2,1,0:T(8,128)(2,1)S(1)} %collective-permute-done.refs_1_) | copy-start | bytes 393220
  74.5 9.7 %collective-permute-start.5 = (bf16[4,64,256]{2,1,0:T(8,128)(2,1)S(1)}, bf16[4,64,256]{2,1,0:T(8,128)(2,1)S(1)}, u32[]{:S(2)}, u32[]{:S(2)}) collective-permute-start(bf16[4,64,256]{2,1,0:T(8,128)(2,1)S(1)} %slice.17.refs_0_), channel_id=1, source_target_pairs={{0,48},{8,56},{16,0},{24,8},{1,49},{9,57},{17,1},{25,9},{2,50},{10... | collective-permute-start | bytes 393224 | tf_op jit(solution)/shard_map/ppermute | solution.py:585
  76.4 9.3 %copy-start.15 = (bf16[4,64,256]{2,1,0:T(8,128)(2,1)}, bf16[4,64,256]{2,1,0:T(8,128)(2,1)S(1)}, u32[]{:S(2)}) copy-start(bf16[4,64,256]{2,1,0:T(8,128)(2,1)S(1)} %collective-permute-done.1.refs_2_) | copy-start | bytes 393220
  76.4 9.3 %collective-permute-start.6 = (bf16[4,64,256]{2,1,0:T(8,128)(2,1)S(1)}, bf16[4,64,256]{2,1,0:T(8,128)(2,1)S(1)}, u32[]{:S(2)}, u32[]{:S(2)}) collective-permute-start(bf16[4,64,256]{2,1,0:T(8,128)(2,1)S(1)} %slice.17.refs_0_), channel_id=1, source_target_pairs={{0,56},{8,0},{16,8},{24,16},{1,57},{9,1},{17,9},{25,17},{2,58},{10... | collective-permute-start | bytes 393224 | tf_op jit(solution)/shard_map/ppermute | solution.py:585
  79.0 6.7 %copy-start.16 = (bf16[4,64,256]{2,1,0:T(8,128)(2,1)}, bf16[4,64,256]{2,1,0:T(8,128)(2,1)S(1)}, u32[]{:S(2)}) copy-start(bf16[4,64,256]{2,1,0:T(8,128)(2,1)S(1)} %collective-permute-done.2.refs_3_) | copy-start | bytes 393220
  80.5 5.2 %copy-start.17 = (bf16[4,64,256]{2,1,0:T(8,128)(2,1)}, bf16[4,64,256]{2,1,0:T(8,128)(2,1)S(1)}, u32[]{:S(2)}) copy-start(bf16[4,64,256]{2,1,0:T(8,128)(2,1)S(1)} %collective-permute-done.3.refs_4_) | copy-start | bytes 393220
  80.9 4.9 %copy-start.18 = (bf16[4,64,256]{2,1,0:T(8,128)(2,1)}, bf16[4,64,256]{2,1,0:T(8,128)(2,1)S(1)}, u32[]{:S(2)}) copy-start(bf16[4,64,256]{2,1,0:T(8,128)(2,1)S(1)} %collective-permute-done.4.refs_5_) | copy-start | bytes 393220
  84.2 1.6 copy-start.19
  85.8 0.7 copy-start.20
  88.8 11.5 %collective-permute-start.7 = (bf16[10,64,256]{2,1,0:T(8,128)(2,1)}, bf16[10,64,256]{2,1,0:T(8,128)(2,1)S(1)}, u32[]{:S(2)}, u32[]{:S(2)}) collective-permute-start(bf16[10,64,256]{2,1,0:T(8,128)(2,1)} %collect.1.refs_0_), channel_id=1, source_target_pairs={{0,2},{1,3},{2,4},{3,5},{4,6},{5,7},{6,0},{7,1},{8,10},{9,11},{10,... | collective-permute-start | bytes 983048 | tf_op jit(solution)/shard_map/ppermute | solution.py:545
  89.6 15.7 %collective-permute-start.8 = (bf16[10,64,256]{2,1,0:T(8,128)(2,1)}, bf16[10,64,256]{2,1,0:T(8,128)(2,1)S(1)}, u32[]{:S(2)}, u32[]{:S(2)}) collective-permute-start(bf16[10,64,256]{2,1,0:T(8,128)(2,1)} %collect.1.refs_0_), channel_id=1, source_target_pairs={{0,6},{1,7},{2,0},{3,1},{4,2},{5,3},{6,4},{7,5},{8,14},{9,15},{10,... | collective-permute-start | bytes 983048 | tf_op jit(solution)/shard_map/ppermute | solution.py:545
  92.2 14.3 %collective-permute-start.9 = (bf16[10,64,256]{2,1,0:T(8,128)(2,1)}, bf16[10,64,256]{2,1,0:T(8,128)(2,1)S(1)}, u32[]{:S(2)}, u32[]{:S(2)}) collective-permute-start(bf16[10,64,256]{2,1,0:T(8,128)(2,1)} %collect.1.refs_0_), channel_id=1, source_target_pairs={{0,4},{1,5},{2,6},{3,7},{4,0},{5,1},{6,2},{7,3},{8,12},{9,13},{10,... | collective-permute-start | bytes 983048 | tf_op jit(solution)/shard_map/ppermute | solution.py:545
  100.4 6.1 %copy-start.10 = (bf16[10,64,256]{2,1,0:T(8,128)(2,1)}, bf16[10,64,256]{2,1,0:T(8,128)(2,1)S(1)}, u32[]{:S(2)}) copy-start(bf16[10,64,256]{2,1,0:T(8,128)(2,1)S(1)} %collective-permute-done.7.refs_1_) | copy-start | bytes 983044
  105.4 1.1 copy-start.11
  106.5 0.7 copy-start.12
  160.1 10.3 %copy-start.2 = (s16[4,104,256]{2,1,0:T(8,128)(2,1)}, s16[4,104,256]{2,1,0:T(8,128)(2,1)S(1)}, u32[]{:S(2)}) copy-start(s16[4,104,256]{2,1,0:T(8,128)(2,1)S(1)} %slice.18.refs_0_) | copy-start | bytes 638980
  160.1 10.3 %collective-permute-start.10 = (s16[4,104,256]{2,1,0:T(8,128)(2,1)S(1)}, s16[4,104,256]{2,1,0:T(8,128)(2,1)S(1)}, u32[]{:S(2)}, u32[]{:S(2)}) collective-permute-start(s16[4,104,256]{2,1,0:T(8,128)(2,1)S(1)} %slice.18.refs_0_), channel_id=1, source_target_pairs={{0,0},{1,8},{2,16},{3,24},{4,32},{5,40},{6,48},{7,56},{8,1},{9,9},... | collective-permute-start | bytes 638984 | tf_op jit(solution)/shard_map/ppermute | solution.py:602
  170.3 0.7 copy-start.13
  176.7 6.8 %collective-permute-start.11 = (s16[4,104,256]{2,1,0:T(8,128)(2,1)}, s16[4,104,256]{2,1,0:T(8,128)(2,1)S(1)}, u32[]{:S(2)}, u32[]{:S(2)}) collective-permute-start(s16[4,104,256]{2,1,0:T(8,128)(2,1)} %get-tuple-element.30), channel_id=1, source_target_pairs={{0,1},{1,0},{2,3},{3,2},{4,5},{5,4},{6,7},{7,6},{8,9},{9,8},{10,11... | collective-permute-start | bytes 638984 | tf_op jit(solution)/shard_map/ppermute | solution.py:545
  184.6 28.8 %copy-start = (s16[2,4,104,256]{3,2,1,0:T(8,128)(2,1)}, s16[2,4,104,256]{3,2,1,0:T(8,128)(2,1)S(1)}, u32[]{:S(2)}) copy-start(s16[2,4,104,256]{3,2,1,0:T(8,128)(2,1)S(1)} %pad_add_fusion.refs_0_) | copy-start | bytes 1277956
  184.6 16.2 %collective-permute-start.12 = (s16[2,4,104,256]{3,2,1,0:T(8,128)(2,1)S(1)}, s16[2,4,104,256]{3,2,1,0:T(8,128)(2,1)S(1)}, u32[]{:S(2)}, u32[]{:S(2)}) collective-permute-start(s16[2,4,104,256]{3,2,1,0:T(8,128)(2,1)S(1)} %pad_add_fusion.refs_0_), channel_id=1, source_target_pairs={{0,2},{1,3},{2,4},{3,5},{4,6},{5,7},{6,0},{7,1},{8,10},{9,11},{10,... | collective-permute-start | bytes 1277960 | tf_op jit(solution)/shard_map/ppermute | solution.py:545
  185.7 10.7 %collective-permute-start.15 = (s16[4,104,256]{2,1,0:T(8,128)(2,1)}, s16[4,104,256]{2,1,0:T(8,128)(2,1)S(1)}, u32[]{:S(2)}, u32[]{:S(2)}) collective-permute-start(s16[4,104,256]{2,1,0:T(8,128)(2,1)} %get-tuple-element.31), channel_id=1, source_target_pairs={{0,8},{8,0},{16,24},{24,16},{32,40},{40,32},{48,56},{56,48},{1,9},... | collective-permute-start | bytes 638984 | tf_op jit(solution)/shard_map/ppermute | solution.py:545
  189.2 18.1 %collective-permute-start.13 = (s16[2,4,104,256]{3,2,1,0:T(8,128)(2,1)S(1)}, s16[2,4,104,256]{3,2,1,0:T(8,128)(2,1)S(1)}, u32[]{:S(2)}, u32[]{:S(2)}) collective-permute-start(s16[2,4,104,256]{3,2,1,0:T(8,128)(2,1)S(1)} %pad_add_fusion.refs_0_), channel_id=1, source_target_pairs={{0,6},{1,7},{2,0},{3,1},{4,2},{5,3},{6,4},{7,5},{8,14},{9,15},{10,... | collective-permute-start | bytes 1277960 | tf_op jit(solution)/shard_map/ppermute | solution.py:545
  194.9 12.3 %collective-permute-start.14 = (s16[2,4,104,256]{3,2,1,0:T(8,128)(2,1)S(1)}, s16[2,4,104,256]{3,2,1,0:T(8,128)(2,1)S(1)}, u32[]{:S(2)}, u32[]{:S(2)}) collective-permute-start(s16[2,4,104,256]{3,2,1,0:T(8,128)(2,1)S(1)} %pad_add_fusion.refs_0_), channel_id=1, source_target_pairs={{0,4},{1,5},{2,6},{3,7},{4,0},{5,1},{6,2},{7,3},{8,12},{9,13},{10,... | collective-permute-start | bytes 1277960 | tf_op jit(solution)/shard_map/ppermute | solution.py:545
  197.3 16.1 %copy-start.1 = (s16[2,4,104,256]{3,2,1,0:T(8,128)(2,1)}, s16[2,4,104,256]{3,2,1,0:T(8,128)(2,1)S(1)}, u32[]{:S(2)}) copy-start(s16[2,4,104,256]{3,2,1,0:T(8,128)(2,1)S(1)} %pad_add_fusion.1.refs_4_) | copy-start | bytes 1277956
  197.3 10.3 %collective-permute-start.16 = (s16[2,4,104,256]{3,2,1,0:T(8,128)(2,1)S(1)}, s16[2,4,104,256]{3,2,1,0:T(8,128)(2,1)S(1)}, u32[]{:S(2)}, u32[]{:S(2)}) collective-permute-start(s16[2,4,104,256]{3,2,1,0:T(8,128)(2,1)S(1)} %pad_add_fusion.1.refs_4_), channel_id=1, source_target_pairs={{0,16},{8,24},{16,32},{24,40},{32,48},{40,56},{48,0},{56,8},{1,17}... | collective-permute-start | bytes 1277960 | tf_op jit(solution)/shard_map/ppermute | solution.py:545
  197.6 9.9 %collective-permute-start.17 = (s16[2,4,104,256]{3,2,1,0:T(8,128)(2,1)S(1)}, s16[2,4,104,256]{3,2,1,0:T(8,128)(2,1)S(1)}, u32[]{:S(2)}, u32[]{:S(2)}) collective-permute-start(s16[2,4,104,256]{3,2,1,0:T(8,128)(2,1)S(1)} %pad_add_fusion.1.refs_4_), channel_id=1, source_target_pairs={{0,48},{8,56},{16,0},{24,8},{32,16},{40,24},{48,32},{56,40},{1,49}... | collective-permute-start | bytes 1277960 | tf_op jit(solution)/shard_map/ppermute | solution.py:545
  200.8 12.6 %copy-start.4 = (s16[2,4,104,256]{3,2,1,0:T(8,128)(2,1)}, s16[2,4,104,256]{3,2,1,0:T(8,128)(2,1)S(1)}, u32[]{:S(2)}) copy-start(s16[2,4,104,256]{3,2,1,0:T(8,128)(2,1)S(1)} %collective-permute-done.12.refs_1_) | copy-start | bytes 1277956
  200.8 12.6 %collective-permute-start.18 = (s16[2,4,104,256]{3,2,1,0:T(8,128)(2,1)S(1)}, s16[2,4,104,256]{3,2,1,0:T(8,128)(2,1)S(1)}, u32[]{:S(2)}, u32[]{:S(2)}) collective-permute-start(s16[2,4,104,256]{3,2,1,0:T(8,128)(2,1)S(1)} %pad_add_fusion.1.refs_4_), channel_id=1, source_target_pairs={{0,32},{8,40},{16,48},{24,56},{32,0},{40,8},{48,16},{56,24},{1,33}... | collective-permute-start | bytes 1277960 | tf_op jit(solution)/shard_map/ppermute | solution.py:545
  207.3 6.1 %copy-start.5 = (s16[2,4,104,256]{3,2,1,0:T(8,128)(2,1)}, s16[2,4,104,256]{3,2,1,0:T(8,128)(2,1)S(1)}, u32[]{:S(2)}) copy-start(s16[2,4,104,256]{3,2,1,0:T(8,128)(2,1)S(1)} %collective-permute-done.13.refs_2_) | copy-start | bytes 1277956
  207.3 6.1 %copy-start.6 = (s16[2,4,104,256]{3,2,1,0:T(8,128)(2,1)}, s16[2,4,104,256]{3,2,1,0:T(8,128)(2,1)S(1)}, u32[]{:S(2)}) copy-start(s16[2,4,104,256]{3,2,1,0:T(8,128)(2,1)S(1)} %collective-permute-done.14.refs_3_) | copy-start | bytes 1277956
  207.5 5.8 %copy-start.7 = (s16[2,4,104,256]{3,2,1,0:T(8,128)(2,1)}, s16[2,4,104,256]{3,2,1,0:T(8,128)(2,1)S(1)}, u32[]{:S(2)}) copy-start(s16[2,4,104,256]{3,2,1,0:T(8,128)(2,1)S(1)} %collective-permute-done.16.refs_5_) | copy-start | bytes 1277956
  207.6 5.8 %copy-start.8 = (s16[2,4,104,256]{3,2,1,0:T(8,128)(2,1)}, s16[2,4,104,256]{3,2,1,0:T(8,128)(2,1)S(1)}, u32[]{:S(2)}) copy-start(s16[2,4,104,256]{3,2,1,0:T(8,128)(2,1)S(1)} %collective-permute-done.17.refs_6_) | copy-start | bytes 1277956
  213.4 0.8 copy-start.9

commit v6 on v5

--- a/solution.py
+++ b/solution.py
@@ -150,27 +150,38 @@
 EXTENDED = ((1, 0), (1, 1), (2, 0), (2, 1), (2, 2))
 
 
-def assemble(received, arrived, front, chunks):
+def assemble(received, front, chunks):
     total, _, size = received.shape
     thin = front.shape[0] * size // chunks
 
-    def kernel(arrived_ref, received_ref, front_ref, ext_ref, panel_ref, landed, column, sems):
+    def kernel(
+        received_ref, front_ref, ext_ref, panel_ref, landed, column, notes, numbers, arrived_ref, sems, note_sem
+    ):
+        note_copy = pltpu.make_async_copy(received_ref.at[:, pl.ds(size, NOTE_ROWS)], notes, note_sem)
+        note_copy.start()
+
         def copy(i):
             return pltpu.make_async_copy(received_ref.at[i, pl.ds(0, size)], landed.at[i], sems.at[i])
 
         def fetch(i, carry):
-            @pl.when(arrived_ref[i] >= 0)
+            @pl.when(arrived_ref[i, 0] >= 0)
             def _():
                 copy(i).start()
 
             return carry
 
-        lax.fori_loop(0, total, fetch, 0)
+        note_copy.wait()
+        for i in range(total):
+            numbers[i : i + 1, :] = notes[i, 0:1, 0 : numbers.shape[1]].astype(jnp.float32).astype(jnp.int32)
+        number_copy = pltpu.make_async_copy(numbers, arrived_ref, note_sem)
+        number_copy.start()
         for slot, (a, b) in enumerate(EXTENDED):
             ext_ref[slot] = front_ref[a, b].astype(jnp.float32)
+        number_copy.wait()
+        lax.fori_loop(0, total, fetch, 0)
 
         def add(i, carry):
-            target = arrived_ref[i]
+            target = arrived_ref[i, 0]
 
             @pl.when(target >= 0)
             def _():
@@ -194,15 +205,19 @@
             jax.ShapeDtypeStruct((len(EXTENDED), size, size), jnp.float32),
             jax.ShapeDtypeStruct((chunks, thin + SCALE_ROWS, size), jnp.int16),
         ),
-        in_specs=[smem(), hbm(), vmem()],
+        in_specs=[hbm(), vmem()],
         out_specs=(vmem(), vmem()),
         scratch_shapes=[
             pltpu.VMEM((total, size, size), jnp.bfloat16),
             pltpu.VMEM((3 * size, size), jnp.float32),
+            pltpu.VMEM((total, NOTE_ROWS, size), jnp.bfloat16),
+            pltpu.VMEM((total, 128), jnp.int32),
+            pltpu.SMEM((total, 128), jnp.int32),
             pltpu.SemaphoreType.DMA((total,)),
+            pltpu.SemaphoreType.DMA,
         ],
         compiler_params=pltpu.CompilerParams(vmem_limit_bytes=VMEM_BYTES),
-    )(arrived, received, front)
+    )(received, front)
 
 
 def pick_lane(value, lane):
@@ -299,39 +314,42 @@
 PAIRS = tuple((i, j) for i in range(LEAD_TILES) for j in range(i + 1))
 
 
-def collect(ids, chunks):
-    _, thin, size = chunks[0].shape
-    count = len(chunks)
+def collect(ids, pairs):
+    _, _, thin, size = pairs[0].shape
+    ring = len(pairs)
 
     def kernel(ids_ref, *refs):
-        *chunk_refs, out_ref, sems = refs
+        *pair_refs, out_ref, sems = refs
+        place, side = lax.div(ids_ref[0], 2), lax.rem(ids_ref[0], 2)
+        copies = []
         for i in range(LEAD_TILES):
             first = PAIRS.index((i, 0))
-            steps = lax.rem(ids_ref[0] - i + count, count)
-
-            def copy(ref, i=i, first=first):
-                return pltpu.make_async_copy(ref.at[pl.ds(0, i + 1)], out_ref.at[pl.ds(first, i + 1)], sems.at[i])
-
-            for s in range(count):
+            inner = lax.rem(side + i, 2)
+            steps = lax.rem(place - i // 2 + ring, ring)
+
+            def copy(ref, i=i, first=first, inner=inner):
+                return pltpu.make_async_copy(
+                    ref.at[inner, pl.ds(0, i + 1)], out_ref.at[pl.ds(first, i + 1)], sems.at[i]
+                )
+
+            for s in range(ring):
 
                 @pl.when(steps == s)
                 def _():
-                    copy(chunk_refs[s]).start()
-
-        for i in range(LEAD_TILES):
-            first = PAIRS.index((i, 0))
-            pltpu.make_async_copy(
-                chunk_refs[0].at[pl.ds(0, i + 1)], out_ref.at[pl.ds(first, i + 1)], sems.at[i]
-            ).wait()
+                    copy(pair_refs[s]).start()
+
+            copies.append(copy(pair_refs[0]))
+        for one in copies:
+            one.wait()
 
     return pl.pallas_call(
         kernel,
         name="collect",
-        out_shape=jax.ShapeDtypeStruct((len(PAIRS), thin, size), chunks[0].dtype),
-        in_specs=[smem()] + [hbm()] * count,
+        out_shape=jax.ShapeDtypeStruct((len(PAIRS), thin, size), pairs[0].dtype),
+        in_specs=[smem()] + [hbm()] * ring,
         out_specs=vmem(),
         scratch_shapes=[pltpu.SemaphoreType.DMA((LEAD_TILES,))],
-    )(ids, *chunks)
+    )(ids, *pairs)
 
 
 def factorize_first(ids, lead, size):
@@ -341,8 +359,9 @@
 
     def kernel(ids_ref, *refs):
         *pieces, high_ref, low_ref, ih_ref, il_ref, own_ref, rest_ref, full, inverses, work = refs
-        for ref, source in ring_pieces(pieces, lax.div(ids_ref[1], 2)):
-            for number, (i, j) in enumerate(PAIRS):
+        for ref, first, source in ring_pieces(pieces, lax.div(ids_ref[1], 2), len(PAIRS)):
+            for number in range(ref.shape[0]):
+                i, j = PAIRS[first + number]
                 tile = ref[number].astype(jnp.float32)
                 thin = tile.shape[0]
                 start = pl.multiple_of(i * size + source * thin, thin)
@@ -384,28 +403,47 @@
     )(ids, *lead)
 
 
-def factorize_last(rest):
+def factorize_next(rest):
+    def kernel(rest_ref, out_ref, inverses, work):
+        out_ref[...] = rest_ref[...]
+        eliminate(out_ref, inverses, work, range(1))
+
+    return pl.pallas_call(
+        kernel,
+        name="factorize_next",
+        out_shape=(
+            jax.ShapeDtypeStruct(rest.shape, jnp.float32),
+            jax.ShapeDtypeStruct((1, BLOCK, BLOCK), jnp.float32),
+        ),
+        in_specs=[vmem()],
+        out_specs=(vmem(),) * 2,
+        scratch_shapes=[pltpu.VMEM((BLOCK, BLOCK), jnp.float32)],
+        compiler_params=pltpu.CompilerParams(vmem_limit_bytes=VMEM_BYTES),
+    )(rest)
+
+
+def factorize_last(rest, first_inverse):
     size = rest.shape[0]
 
-    def kernel(rest_ref, own_ref, ih_ref, il_ref, inverses, work):
+    def kernel(rest_ref, first_ref, own_ref, ih_ref, il_ref, inverses, work):
         own_ref[...] = rest_ref[...]
-        eliminate(own_ref, inverses, work, range(size // BLOCK))
+        eliminate(own_ref, inverses, work, range(1, 2))
         own_ref[0:BLOCK, BLOCK:size] = jnp.zeros((BLOCK, size - BLOCK), jnp.float32)
-        ih_ref[...], il_ref[...] = tile_inverse(inverses[0], inverses[1], own_ref[BLOCK:size, 0:BLOCK])
+        ih_ref[...], il_ref[...] = tile_inverse(first_ref[0], inverses[1], own_ref[BLOCK:size, 0:BLOCK])
 
     inv = jax.ShapeDtypeStruct((size, size), jnp.bfloat16)
     return pl.pallas_call(
         kernel,
         name="factorize_last",
         out_shape=(jax.ShapeDtypeStruct((size, size), jnp.float32), inv, inv),
-        in_specs=[vmem()],
+        in_specs=[vmem()] * 2,
         out_specs=(vmem(),) * 3,
         scratch_shapes=[
             pltpu.VMEM((size // BLOCK, BLOCK, BLOCK), jnp.float32),
             pltpu.VMEM((BLOCK, BLOCK), jnp.float32),
         ],
         compiler_params=pltpu.CompilerParams(vmem_limit_bytes=VMEM_BYTES),
-    )(rest)
+    )(rest, first_inverse)
 
 
 def solve(panels, factors):
@@ -534,9 +572,6 @@
     )(ids, *rows, *cols, own, last_own, extended, front)
 
 
-SHIFTS = (1, 3, 2)
-
-
 def exchange(value, axis):
     return lax.all_to_all(value, axis, split_axis=0, concat_axis=0, tiled=True)
 
@@ -547,14 +582,19 @@
 
 def ring_gather(value, axis):
     ring = lax.axis_size(axis) // 2
-    shifted = [permute(value, axis, lambda i: (i // 2 + shift) % ring * 2 + i % 2) for shift in SHIFTS]
-    return (value, *shifted)
-
-
-def ring_pieces(pieces, place):
-    ring = len(SHIFTS) + 1
-    for ref, shift in zip(pieces, (0,) + SHIFTS, strict=True):
-        yield ref, lax.rem(place + (ring - shift), ring)
+    half = value.shape[0] // 2
+
+    def shift(array, steps):
+        return permute(array, axis, lambda i: (i // 2 + steps) % ring * 2 + i % 2)
+
+    before, after = shift(value, 1), shift(value, ring - 1)
+    return (value, before, after, shift(before[:half], 1), shift(after[half:], ring - 1))
+
+
+def ring_pieces(pieces, place, length):
+    ring = len(pieces) - 1
+    for ref, step, first in zip(pieces, (0, 1, 3, 2, 2), (0, 0, 0, 0, length // 2), strict=True):
+        yield ref, first, lax.rem(place + (ring - step), ring)
 
 
 def pair_gather(value, axis):
@@ -564,9 +604,9 @@
 
 def pair_pieces(pieces, place):
     side = lax.rem(place, 2)
-    for ref, source in ring_pieces(pieces, lax.div(place, 2)):
-        yield ref, 0, 2 * source + side
-        yield ref, 1, 2 * source + 1 - side
+    for ref, first, source in ring_pieces(pieces, lax.div(place, 2), 2):
+        for position in range(ref.shape[0]):
+            yield ref, position, 2 * source + (side if first + position == 0 else 1 - side)
 
 
 def per_device(front_matrix, contributions, target_front, target_row, target_col, live_count):
@@ -580,9 +620,12 @@
     thin = size // ring
     chunks = jnp.repeat(front[0, 0].reshape(ring, thin, size), 2, axis=0)
     chunk = exchange(chunks, "col")[:LEAD_TILES]
-    leading = [chunk]
-    for step in range(1, n_row):
-        leading.append(lax.ppermute(chunk, "row", [(i, (i + step) % n_row) for i in range(LEAD_TILES)]))
+    owners = range(LEAD_TILES)
+    partner = lax.ppermute(chunk, "row", [(i, i ^ 1) for i in owners])
+    pair = jnp.stack([chunk, partner])
+    leading = [pair]
+    for step in range(1, n_row // 2):
+        leading.append(lax.ppermute(pair, "row", [(i, (i + 2 * step) % n_row) for i in owners]))
 
     packed = pack(
         contributions.reshape(slots, size, size),
@@ -595,10 +638,10 @@
     *factors, own, rest = factorize_first(ids, lead, size)
     received, rest = lax.optimization_barrier((received, rest))
 
-    arrived = received[:, size, 0].astype(jnp.int32)
-    extended, panel = assemble(received, arrived, front, n_col)
+    extended, panel = assemble(received, front, n_col)
     mine = exchange(panel, "col")[:LEAD_TILES]
-    last_own, *last_inverse = factorize_last(rest)
+    rest, first_inverse = factorize_next(rest)
+    last_own, *last_inverse = factorize_last(rest, first_inverse)
     turned = lax.ppermute(
         mine, ("row", "col"), [(r * n_col + c, c * n_col + r) for r in range(n_row) for c in range(n_col)]
     )

time: 225 us -> 227 us (level)
  waiting for transfers between devices: 71.9 us -> 81.3 us
  starting transfers between devices: 58.4 us -> 50.9 us
  Pallas kernels: 67.3 us -> 70.7 us
    ppermute x7 -> x4, waiting for transfers between devices: 48.5 us -> 59.1 us  [the longest x1 50 us: per_device(): partner = lax.ppermute(chunk, 'row', [(i, i ^ 1) for i in owners])]
    ppermute x7 -> x4, starting transfers between devices: 14.5 us -> 7.73 us  [the longest x3 5.67 us: per_device(): lax.ppermute(pair, 'row', [(i, (i + 2 * step) % n_row) for i in owners])]
    pallas_call x0 -> x1, Pallas kernels: none -> 5.63 us  [factorize_next(): pl.pallas_call(kernel, name='factorize_next', out_shape=(jax.ShapeDtypeSt...]
    pallas_call x1, Pallas kernels: 9.58 us -> 5.55 us  [factorize_last(): pl.pallas_call(kernel, name='factorize_last', out_shape=(jax.ShapeDtypeSt...]
    ppermute x11 -> x14, waiting for transfers between devices: 23.2 us -> 22.1 us  [permute(): lax.ppermute(value, axis, [(i, target(i)) for i in range(lax.axis_size(ax...]
    ppermute x11 -> x14, starting transfers between devices: 29.1 us -> 28.3 us  [permute(): lax.ppermute(value, axis, [(i, target(i)) for i in range(lax.axis_size(ax...]
  transfers between devices with their start and end apart: 21 -> 21, of which waited for: 12 -> 11; matrix products, arithmetic and copies ran while one was open for 1% -> 1% of each run, Pallas kernels for 22% -> 22%
where the time goes in v6:
time: 227 us; the launch traced here: 224 us
  waiting for transfers between devices  81.3 us (36%)
  Pallas kernels  70.7 us (31%)
  starting transfers between devices  50.9 us (22%)
  blocking collectives  12.5 us (6%)
  local copies, waits for them, and re-layouts  5.21 us (2%)
  other arithmetic  2.51 us (1%)
    ppermute x1, waiting for transfers between devices, per_device(): partner = lax.ppermute(chunk, 'row', [(i, i ^ 1) for i in owners])  50 us
    pallas_call x1, Pallas kernels, factorize_first(): pl.pallas_call(kernel, name='factorize_first', out_shape=(wide, wide, inv...  31.4 us
    ppermute x14, starting transfers between devices, permute(): lax.ppermute(value, axis, [(i, target(i)) for i in range(lax.axis_size(ax...  28.3 us
    ppermute x14, waiting for transfers between devices, permute(): lax.ppermute(value, axis, [(i, target(i)) for i in range(lax.axis_size(ax...  22.1 us
    all_to_all x2, starting transfers between devices, exchange(): return lax.all_to_all(value, axis, split_axis=0, concat_axis=0, tiled=True)  14.2 us
    all_to_all x1, blocking collectives, exchange(): return lax.all_to_all(value, axis, split_axis=0, concat_axis=0, tiled=True)  12.5 us
    ppermute x3, waiting for transfers between devices, per_device(): lax.ppermute(pair, 'row', [(i, (i + 2 * step) % n_row) for i in owners])  9.08 us
    pallas_call x1, Pallas kernels, finish(): pl.pallas_call(kernel, name='finish', out_shape=jax.ShapeDtypeStruct((til...  8.04 us
  transfers between devices with their start and end apart: 21, of which 11 were waited for; matrix products, arithmetic and copies ran while one was open for 1% of the time, Pallas kernels for 22%

profile of v6, /device:TPU:6, one launch (start us, length us, event | category | flops | bytes accessed | tf_op | source)
XLA Modules:
  0.0 224.1 jit_solution(14977198561642383639)
XLA Ops:
  0.0 0.9 slice.36
  0.9 0.7 broadcast_in_dim.3
  1.6 6.8 %all-to-all-start.1 = ((bf16[8,64,256]{2,1,0:T(8,128)(2,1)}), bf16[8,64,256]{2,1,0:T(8,128)(2,1)S(1)}, u32[]{:S(2)}, u32[]{:S(2)}) async-start(bf16[8,64,256]{2,1,0:T(8,128)(2,1)} %bitcast.10), calls=%async_computation.1 | async-start | bytes 524288 | tf_op jit(solution)/shard_map/all_to_all | solution.py:576
  9.1 5.3 %pack.1 = bf16[32,264,256]{2,1,0:T(8,128)(2,1)} custom-call(s32[32]{0:T(128)} %bitcast.31, s32[32]{0:T(128)} %bitcast.32, s32[32]{0:T(128)} %bitcast.33, s32[1]{0:T(128)} %bitcast.20.live_ref, bf16[32,256,256]{2,1,0:T(8,128)(2,1)} %bitcast.24), custom_call_target="tpu_custom_call" | custom-call | tf_op jit(solution)/shard_map/pack/pallas_call | solution.py:107
  14.3 0.2 all-to-all-done.1
  14.5 7.4 %all-to-all-start = ((bf16[32,264,256]{2,1,0:T(8,128)(2,1)}), bf16[32,264,256]{2,1,0:T(8,128)(2,1)}, u32[]{:S(2)}, u32[]{:S(2)}) async-start(bf16[32,264,256]{2,1,0:T(8,128)(2,1)} %pack.1), calls=%async_computation | async-start | bytes 8650752 | tf_op jit(solution)/shard_map/all_to_all | solution.py:576
  22.0 2.1 collective-permute-start
  24.1 50.0 %collective-permute-done = bf16[4,64,256]{2,1,0:T(8,128)(2,1)S(1)} collective-permute-done((bf16[4,64,256]{2,1,0:T(8,128)(2,1)S(1)}, bf16[4,64,256]{2,1,0:T(8,128)(2,1)S(1)}, u32[]{:S(2)}, u32[]{:S(2)}) %collective-permute-start) | collective-permute-done | bytes 131104 | tf_op jit(solution)/shard_map/ppermute | solution.py:624
  74.1 0.0 copy-start.2
  74.1 2.4 %collective-permute-start.1 = (bf16[2,4,64,256]{3,2,1,0:T(8,128)(2,1)S(1)}, bf16[2,4,64,256]{3,2,1,0:T(8,128)(2,1)S(1)}, u32[]{:S(2)}, u32[]{:S(2)}) collective-permute-start(bf16[2,4,64,256]{3,2,1,0:T(8,128)(2,1)S(1)} %pad_maximum_fusion.refs_0_), channel_id=1, source_target_pairs={{0,16},{8,24},{16,32},{24,40},{1,17},{9,25},{17,33},{25,41},{2,18}... | collective-permute-start | bytes 786440 | tf_op jit(solution)/shard_map/ppermute | solution.py:628
  76.5 1.3 collective-permute-start.2
  77.9 1.9 collective-permute-start.3
  79.8 0.6 pad_add_fusion.2.ids_ref
  80.3 2.9 %collective-permute-done.1.refs_1_ = bf16[2,4,64,256]{3,2,1,0:T(8,128)(2,1)S(1)} collective-permute-done((bf16[2,4,64,256]{3,2,1,0:T(8,128)(2,1)S(1)}, bf16[2,4,64,256]{3,2,1,0:T(8,128)(2,1)S(1)}, u32[]{:S(2)}, u32[]{:S(2)}) %collective-permute-start.1) | collective-permute-done | bytes 262176 | tf_op jit(solution)/shard_map/ppermute | solution.py:628
  83.2 4.1 %collective-permute-done.2.refs_2_ = bf16[2,4,64,256]{3,2,1,0:T(8,128)(2,1)S(1)} collective-permute-done((bf16[2,4,64,256]{3,2,1,0:T(8,128)(2,1)S(1)}, bf16[2,4,64,256]{3,2,1,0:T(8,128)(2,1)S(1)}, u32[]{:S(2)}, u32[]{:S(2)}) %collective-permute-start.2) | collective-permute-done | bytes 262176 | tf_op jit(solution)/shard_map/ppermute | solution.py:628
  87.3 2.1 collective-permute-done.3.refs_3_
  89.4 0.0 copy-done.10
  89.5 0.7 copy-done.12
  90.2 2.4 %collect.1.refs_0_ = bf16[10,64,256]{2,1,0:T(8,128)(2,1)} custom-call(s32[2]{0:T(128)} %pad_add_fusion.2.ids_ref, bf16[2,4,64,256]{3,2,1,0:T(8,128)(2,1)} %copy-done.2, bf16[2,4,64,256]{3,2,1,0:T(8,128)(2,1)} %copy-done.10, bf16[2,4,64,256]{3,2,1,0:T(8,128)(2,1)} %copy-done.11, bf16[2,4,64,256]{3,2,1,0:T(8,128)(2,1)} %copy-done.12), custom_call_target="tpu_custom_call" | custom-call | tf_op jit(solution)/shard_map/collect/pallas_call | solution.py:345
  92.6 0.8 collective-permute-start.4
  93.4 2.5 %collective-permute-start.5 = (bf16[10,64,256]{2,1,0:T(8,128)(2,1)}, bf16[10,64,256]{2,1,0:T(8,128)(2,1)S(1)}, u32[]{:S(2)}, u32[]{:S(2)}) collective-permute-start(bf16[10,64,256]{2,1,0:T(8,128)(2,1)} %collect.1.refs_0_), channel_id=1, source_target_pairs={{0,6},{1,7},{2,0},{3,1},{4,2},{5,3},{6,4},{7,5},{8,14},{9,15},{10,... | collective-permute-start | bytes 983048 | tf_op jit(solution)/shard_map/ppermute | solution.py:580
  95.9 6.8 %collective-permute-done.4.refs_1_ = bf16[10,64,256]{2,1,0:T(8,128)(2,1)S(1)} collective-permute-done((bf16[10,64,256]{2,1,0:T(8,128)(2,1)}, bf16[10,64,256]{2,1,0:T(8,128)(2,1)S(1)}, u32[]{:S(2)}, u32[]{:S(2)}) %collective-permute-start.4) | collective-permute-done | bytes 327712 | tf_op jit(solution)/shard_map/ppermute | solution.py:580
  102.7 0.1 collective-permute-start.6
  102.8 0.0 collective-permute-done.5.refs_2_
  102.8 3.3 %collective-permute-start.7 = (bf16[5,64,256]{2,1,0:T(8,128)(2,1)S(1)}, bf16[5,64,256]{2,1,0:T(8,128)(2,1)S(1)}, u32[]{:S(2)}, u32[]{:S(2)}) collective-permute-start(bf16[5,64,256]{2,1,0:T(8,128)(2,1)S(1)} %slice.39), channel_id=1, source_target_pairs={{0,6},{1,7},{2,0},{3,1},{4,2},{5,3},{6,4},{7,5},{8,14},{9,15},{10,... | collective-permute-start | bytes 491528 | tf_op jit(solution)/shard_map/ppermute | solution.py:580
  106.1 3.2 %collective-permute-done.6.refs_3_ = bf16[5,64,256]{2,1,0:T(8,128)(2,1)S(1)} collective-permute-done((bf16[5,64,256]{2,1,0:T(8,128)(2,1)S(1)}, bf16[5,64,256]{2,1,0:T(8,128)(2,1)S(1)}, u32[]{:S(2)}, u32[]{:S(2)}) %collective-permute-start.6) | collective-permute-done | bytes 163872 | tf_op jit(solution)/shard_map/ppermute | solution.py:580
  109.3 0.0 collective-permute-done.7.refs_4_
  109.3 0.7 copy-done.18
  110.0 0.7 copy-done.19
  110.6 31.4 %factorize_first.1 = (bf16[1024,768]{1,0:T(8,128)(2,1)}, bf16[1024,768]{1,0:T(8,128)(2,1)}, bf16[3,256,256]{2,1,0:T(8,128)(2,1)}, bf16[3,256,256]{2,1,0:T(8,128)...) custom-call(s32[2]{0:T(128)} %pad_add_fusion.2.ids_ref, bf16[10,64,256]{2,1,0:T(8,128)(2,1)} %collect.1.refs_0_, ...), custom_call_target="tpu_custom_call" | custom-call | tf_op jit(solution)/shard_map/factorize_first/pallas_call | solution.py:391
  142.0 0.0 all-to-all-done.received_ref
  142.0 6.7 %assemble.1 = (f32[5,256,256]{2,1,0:T(8,128)}, s16[8,104,256]{2,1,0:T(8,128)(2,1)}) custom-call(bf16[32,264,256]{2,1,0:T(8,128)(2,1)} %all-to-all-done.received_ref, bf16[3,3,256,256]{3,2,1,0:T(8,128)(2,1)} %bitcast.22), custom_call_target="tpu_custom_call" | custom-call | tf_op jit(solution)/shard_map/assemble/pallas_call | solution.py:201
  148.7 12.5 %all_to_all.15 = s16[8,104,256]{2,1,0:T(8,128)(2,1)S(1)} all-to-all(s16[8,104,256]{2,1,0:T(8,128)(2,1)} %get-tuple-element.24), channel_id=1, replica_groups=mesh['front'=2,'row'=8,'col'=8] {'col'}, dimensions={0} | all-to-all | bytes 851968 | tf_op jit(solution)/shard_map/all_to_all | solution.py:576
  161.3 0.7 collective-permute-start.8
  162.0 5.6 %factorize_next.1 = (f32[256,256]{1,0:T(8,128)}, f32[1,128,128]{2,1,0:T(8,128)}) custom-call(f32[256,256]{1,0:T(8,128)} %get-tuple-element.29.rest_ref), custom_call_target="tpu_custom_call" | custom-call | tf_op jit(solution)/shard_map/factorize_next/pallas_call | solution.py:411
  167.6 5.6 %factorize_last.1 = (f32[256,256]{1,0:T(8,128)}, bf16[256,256]{1,0:T(8,128)(2,1)}, bf16[256,256]{1,0:T(8,128)(2,1)}) custom-call(f32[256,256]{1,0:T(8,128)} %get-tuple-element.30.rest_ref, f32[1,128,128]{2,1,0:T(8,128)} %get-tuple-element.31.first_ref), custom_call_target="tpu_custom_call" | custom-call | tf_op jit(solution)/shard_map/factorize_last/pallas_call | solution.py:435
  173.1 0.0 collective-permute-done.8.refs_1_
  173.2 0.7 copy-done.17
  173.8 5.7 %solve.1 = (s16[4,104,256]{2,1,0:T(8,128)(2,1)}, s16[4,104,256]{2,1,0:T(8,128)(2,1)}) custom-call(s16[4,104,256]{2,1,0:T(8,128)(2,1)} %copy-done.7, s16[4,104,256]{2,1,0:T(8,128)(2,1)} %copy-done.17, bf16[1024,768]{1,0:T(8,128)(2,1)} %get-tuple-element.25.refs_2_, bf16[1024,768]{1,0:T(8,128)(2,1)} %get-tuple-element.26.refs_3_, ...), custom_call_target="tpu_custom_call" | custom-call | tf_op jit(solution)/shard_map/solve/pallas_call | solution.py:470
  179.5 5.2 %collective-permute-start.9 = (s16[4,104,256]{2,1,0:T(8,128)(2,1)}, s16[4,104,256]{2,1,0:T(8,128)(2,1)S(1)}, u32[]{:S(2)}, u32[]{:S(2)}) collective-permute-start(s16[4,104,256]{2,1,0:T(8,128)(2,1)} %get-tuple-element.34), channel_id=1, source_target_pairs={{0,1},{1,0},{2,3},{3,2},{4,5},{5,4},{6,7},{7,6},{8,9},{9,8},{10,11... | collective-permute-start | bytes 638984 | tf_op jit(solution)/shard_map/ppermute | solution.py:580
  184.7 0.1 collective-permute-start.14
  184.8 4.0 %collective-permute-done.9 = s16[4,104,256]{2,1,0:T(8,128)(2,1)S(1)} collective-permute-done((s16[4,104,256]{2,1,0:T(8,128)(2,1)}, s16[4,104,256]{2,1,0:T(8,128)(2,1)S(1)}, u32[]{:S(2)}, u32[]{:S(2)}) %collective-permute-start.9) | collective-permute-done | bytes 213024 | tf_op jit(solution)/shard_map/ppermute | solution.py:580
  188.7 1.0 pad_add_fusion.refs_0_
  189.7 0.6 collective-permute-start.10
  190.4 5.4 %collective-permute-start.11 = (s16[2,4,104,256]{3,2,1,0:T(8,128)(2,1)S(1)}, s16[2,4,104,256]{3,2,1,0:T(8,128)(2,1)S(1)}, u32[]{:S(2)}, u32[]{:S(2)}) collective-permute-start(s16[2,4,104,256]{3,2,1,0:T(8,128)(2,1)S(1)} %pad_add_fusion.refs_0_), channel_id=1, source_target_pairs={{0,6},{1,7},{2,0},{3,1},{4,2},{5,3},{6,4},{7,5},{8,14},{9,15},{10,... | collective-permute-start | bytes 1277960 | tf_op jit(solution)/shard_map/ppermute | solution.py:580
  195.7 0.0 collective-permute-done.14
  195.7 1.0 pad_add_fusion.1.refs_5_
  196.7 1.0 collective-permute-start.15
  197.7 2.3 %collective-permute-start.16 = (s16[2,4,104,256]{3,2,1,0:T(8,128)(2,1)S(1)}, s16[2,4,104,256]{3,2,1,0:T(8,128)(2,1)S(1)}, u32[]{:S(2)}, u32[]{:S(2)}) collective-permute-start(s16[2,4,104,256]{3,2,1,0:T(8,128)(2,1)S(1)} %pad_add_fusion.1.refs_5_), channel_id=1, source_target_pairs={{0,48},{8,56},{16,0},{24,8},{32,16},{40,24},{48,32},{56,40},{1,49}... | collective-permute-start | bytes 1277960 | tf_op jit(solution)/shard_map/ppermute | solution.py:580
  200.0 3.6 %collective-permute-done.10.refs_1_ = s16[2,4,104,256]{3,2,1,0:T(8,128)(2,1)S(1)} collective-permute-done((s16[2,4,104,256]{3,2,1,0:T(8,128)(2,1)S(1)}, s16[2,4,104,256]{3,2,1,0:T(8,128)(2,1)S(1)}, u32[]{:S(2)}, u32[]{:S(2)}) %collective-permute-start.10) | collective-permute-done | bytes 426016 | tf_op jit(solution)/shard_map/ppermute | solution.py:580
  203.6 0.1 collective-permute-start.12
  203.7 0.0 collective-permute-done.11.refs_2_
  203.7 3.5 %collective-permute-start.13 = (s16[1,4,104,256]{3,2,1,0:T(8,128)(2,1)S(1)}, s16[1,4,104,256]{3,2,1,0:T(8,128)(2,1)S(1)}, u32[]{:S(2)}, u32[]{:S(2)}) collective-permute-start(s16[1,4,104,256]{3,2,1,0:T(8,128)(2,1)S(1)} %slice.42), channel_id=1, source_target_pairs={{0,6},{1,7},{2,0},{3,1},{4,2},{5,3},{6,4},{7,5},{8,14},{9,15},{10,... | collective-permute-start | bytes 638984 | tf_op jit(solution)/shard_map/ppermute | solution.py:580
  207.2 1.0 collective-permute-done.15.refs_6_
  208.2 0.1 collective-permute-start.17
  208.3 0.0 collective-permute-done.16.refs_7_
  208.3 3.4 %collective-permute-start.18 = (s16[1,4,104,256]{3,2,1,0:T(8,128)(2,1)S(1)}, s16[1,4,104,256]{3,2,1,0:T(8,128)(2,1)S(1)}, u32[]{:S(2)}, u32[]{:S(2)}) collective-permute-start(s16[1,4,104,256]{3,2,1,0:T(8,128)(2,1)S(1)} %slice.44), channel_id=1, source_target_pairs={{0,48},{8,56},{16,0},{24,8},{32,16},{40,24},{48,32},{56,40},{1,49}... | collective-permute-start | bytes 638984 | tf_op jit(solution)/shard_map/ppermute | solution.py:580
  211.7 0.0 collective-permute-done.12.refs_3_
  211.7 0.0 collective-permute-done.13.refs_4_
  211.7 3.6 %collective-permute-done.17.refs_8_ = s16[1,4,104,256]{3,2,1,0:T(8,128)(2,1)S(1)} collective-permute-done((s16[1,4,104,256]{3,2,1,0:T(8,128)(2,1)S(1)}, s16[1,4,104,256]{3,2,1,0:T(8,128)(2,1)S(1)}, u32[]{:S(2)}, u32[]{:S(2)}) %collective-permute-start.17) | collective-permute-done | bytes 213024 | tf_op jit(solution)/shard_map/ppermute | solution.py:580
  215.3 0.0 collective-permute-done.18.refs_9_
  215.4 0.6 copy-done.15
  216.0 0.1 copy-done.16
  216.1 8.0 %finish.1 = f32[4608,128]{1,0:T(8,128)} custom-call(s32[2]{0:T(128)} %pad_add_fusion.2.ids_ref, s16[2,4,104,256]{3,2,1,0:T(8,128)(2,1)} %copy-done, s16[2,4,104,256]{3,2,1,0:T(8,128)(2,1)} %copy-done.3, s16[2,4,104,256]{3,2,1,0:T(8,128)(2,1)} %copy-done.4, s16[1,4,104,256]{3,2,1,0:T(8,128)(2,1)} %copy-done.13, s16[1,4,104,256]{3,2,1,0:T(8,128)(2,1)} %copy-done.14, ...), custom_call_target="tpu_custom_call" | custom-call | tf_op jit(solution)/shard_map/finish/pallas_call | solution.py:564
  (41 shorter events, 0.2 us)
Async XLA Ops:
  1.6 12.9 %all-to-all-start.1 = ((bf16[8,64,256]{2,1,0:T(8,128)(2,1)}), bf16[8,64,256]{2,1,0:T(8,128)(2,1)S(1)}, u32[]{:S(2)}, u32[]{:S(2)}) async-start(bf16[8,64,256]{2,1,0:T(8,128)(2,1)} %bitcast.10), calls=%async_computation.1 | async-start | bytes 524288 | tf_op jit(solution)/shard_map/all_to_all | solution.py:576
  14.5 127.5 %all-to-all-start = ((bf16[32,264,256]{2,1,0:T(8,128)(2,1)}), bf16[32,264,256]{2,1,0:T(8,128)(2,1)}, u32[]{:S(2)}, u32[]{:S(2)}) async-start(bf16[32,264,256]{2,1,0:T(8,128)(2,1)} %pack.1), calls=%async_computation | async-start | bytes 8650752 | tf_op jit(solution)/shard_map/all_to_all | solution.py:576
  22.0 52.0 %collective-permute-start = (bf16[4,64,256]{2,1,0:T(8,128)(2,1)S(1)}, bf16[4,64,256]{2,1,0:T(8,128)(2,1)S(1)}, u32[]{:S(2)}, u32[]{:S(2)}) collective-permute-start(bf16[4,64,256]{2,1,0:T(8,128)(2,1)S(1)} %get-tuple-element.40), channel_id=1, source_target_pairs={{0,8},{8,0},{16,24},{24,16},{1,9},{9,1},{17,25},{25,17},{2,10},{10... | collective-permute-start | bytes 393224 | tf_op jit(solution)/shard_map/ppermute | solution.py:624
  74.1 15.4 %copy-start.2 = (bf16[2,4,64,256]{3,2,1,0:T(8,128)(2,1)}, bf16[2,4,64,256]{3,2,1,0:T(8,128)(2,1)S(1)}, u32[]{:S(2)}) copy-start(bf16[2,4,64,256]{3,2,1,0:T(8,128)(2,1)S(1)} %pad_maximum_fusion.refs_0_) | copy-start | bytes 786436
  74.1 9.1 %collective-permute-start.1 = (bf16[2,4,64,256]{3,2,1,0:T(8,128)(2,1)S(1)}, bf16[2,4,64,256]{3,2,1,0:T(8,128)(2,1)S(1)}, u32[]{:S(2)}, u32[]{:S(2)}) collective-permute-start(bf16[2,4,64,256]{3,2,1,0:T(8,128)(2,1)S(1)} %pad_maximum_fusion.refs_0_), channel_id=1, source_target_pairs={{0,16},{8,24},{16,32},{24,40},{1,17},{9,25},{17,33},{25,41},{2,18}... | collective-permute-start | bytes 786440 | tf_op jit(solution)/shard_map/ppermute | solution.py:628
  76.5 10.8 %collective-permute-start.2 = (bf16[2,4,64,256]{3,2,1,0:T(8,128)(2,1)S(1)}, bf16[2,4,64,256]{3,2,1,0:T(8,128)(2,1)S(1)}, u32[]{:S(2)}, u32[]{:S(2)}) collective-permute-start(bf16[2,4,64,256]{3,2,1,0:T(8,128)(2,1)S(1)} %pad_maximum_fusion.refs_0_), channel_id=1, source_target_pairs={{0,32},{8,40},{16,48},{24,56},{1,33},{9,41},{17,49},{25,57},{2,34}... | collective-permute-start | bytes 786440 | tf_op jit(solution)/shard_map/ppermute | solution.py:628
  77.9 11.6 %collective-permute-start.3 = (bf16[2,4,64,256]{3,2,1,0:T(8,128)(2,1)S(1)}, bf16[2,4,64,256]{3,2,1,0:T(8,128)(2,1)S(1)}, u32[]{:S(2)}, u32[]{:S(2)}) collective-permute-start(bf16[2,4,64,256]{3,2,1,0:T(8,128)(2,1)S(1)} %pad_maximum_fusion.refs_0_), channel_id=1, source_target_pairs={{0,48},{8,56},{16,0},{24,8},{1,49},{9,57},{17,1},{25,9},{2,50},{10... | collective-permute-start | bytes 786440 | tf_op jit(solution)/shard_map/ppermute | solution.py:628
  83.2 6.2 %copy-start.10 = (bf16[2,4,64,256]{3,2,1,0:T(8,128)(2,1)}, bf16[2,4,64,256]{3,2,1,0:T(8,128)(2,1)S(1)}, u32[]{:S(2)}) copy-start(bf16[2,4,64,256]{3,2,1,0:T(8,128)(2,1)S(1)} %collective-permute-done.1.refs_1_) | copy-start | bytes 786436
  87.3 2.1 copy-start.11
  89.4 0.7 copy-start.12
  92.6 10.1 %collective-permute-start.4 = (bf16[10,64,256]{2,1,0:T(8,128)(2,1)}, bf16[10,64,256]{2,1,0:T(8,128)(2,1)S(1)}, u32[]{:S(2)}, u32[]{:S(2)}) collective-permute-start(bf16[10,64,256]{2,1,0:T(8,128)(2,1)} %collect.1.refs_0_), channel_id=1, source_target_pairs={{0,2},{1,3},{2,4},{3,5},{4,6},{5,7},{6,0},{7,1},{8,10},{9,11},{10,... | collective-permute-start | bytes 983048 | tf_op jit(solution)/shard_map/ppermute | solution.py:580
  93.4 9.4 %collective-permute-start.5 = (bf16[10,64,256]{2,1,0:T(8,128)(2,1)}, bf16[10,64,256]{2,1,0:T(8,128)(2,1)S(1)}, u32[]{:S(2)}, u32[]{:S(2)}) collective-permute-start(bf16[10,64,256]{2,1,0:T(8,128)(2,1)} %collect.1.refs_0_), channel_id=1, source_target_pairs={{0,6},{1,7},{2,0},{3,1},{4,2},{5,3},{6,4},{7,5},{8,14},{9,15},{10,... | collective-permute-start | bytes 983048 | tf_op jit(solution)/shard_map/ppermute | solution.py:580
  102.7 6.6 %copy-start.8 = (bf16[10,64,256]{2,1,0:T(8,128)(2,1)}, bf16[10,64,256]{2,1,0:T(8,128)(2,1)S(1)}, u32[]{:S(2)}) copy-start(bf16[10,64,256]{2,1,0:T(8,128)(2,1)S(1)} %collective-permute-done.4.refs_1_) | copy-start | bytes 983044
  102.7 6.6 %collective-permute-start.6 = (bf16[5,64,256]{2,1,0:T(8,128)(2,1)S(1)}, bf16[5,64,256]{2,1,0:T(8,128)(2,1)S(1)}, u32[]{:S(2)}, u32[]{:S(2)}) collective-permute-start(bf16[5,64,256]{2,1,0:T(8,128)(2,1)S(1)} %slice.38), channel_id=1, source_target_pairs={{0,2},{1,3},{2,4},{3,5},{4,6},{5,7},{6,0},{7,1},{8,10},{9,11},{10,... | collective-permute-start | bytes 491528 | tf_op jit(solution)/shard_map/ppermute | solution.py:580
  102.8 6.5 %copy-start.9 = (bf16[10,64,256]{2,1,0:T(8,128)(2,1)}, bf16[10,64,256]{2,1,0:T(8,128)(2,1)S(1)}, u32[]{:S(2)}) copy-start(bf16[10,64,256]{2,1,0:T(8,128)(2,1)S(1)} %collective-permute-done.5.refs_2_) | copy-start | bytes 983044
  102.8 6.5 %collective-permute-start.7 = (bf16[5,64,256]{2,1,0:T(8,128)(2,1)S(1)}, bf16[5,64,256]{2,1,0:T(8,128)(2,1)S(1)}, u32[]{:S(2)}, u32[]{:S(2)}) collective-permute-start(bf16[5,64,256]{2,1,0:T(8,128)(2,1)S(1)} %slice.39), channel_id=1, source_target_pairs={{0,6},{1,7},{2,0},{3,1},{4,2},{5,3},{6,4},{7,5},{8,14},{9,15},{10,... | collective-permute-start | bytes 491528 | tf_op jit(solution)/shard_map/ppermute | solution.py:580
  109.3 0.7 copy-start.18
  110.0 0.7 copy-start.19
  161.3 11.9 %copy-start.7 = (s16[4,104,256]{2,1,0:T(8,128)(2,1)}, s16[4,104,256]{2,1,0:T(8,128)(2,1)S(1)}, u32[]{:S(2)}) copy-start(s16[4,104,256]{2,1,0:T(8,128)(2,1)S(1)} %slice.40.refs_0_) | copy-start | bytes 638980
  161.3 11.9 %collective-permute-start.8 = (s16[4,104,256]{2,1,0:T(8,128)(2,1)S(1)}, s16[4,104,256]{2,1,0:T(8,128)(2,1)S(1)}, u32[]{:S(2)}, u32[]{:S(2)}) collective-permute-start(s16[4,104,256]{2,1,0:T(8,128)(2,1)S(1)} %slice.40.refs_0_), channel_id=1, source_target_pairs={{0,0},{1,8},{2,16},{3,24},{4,32},{5,40},{6,48},{7,56},{8,1},{9,9},... | collective-permute-start | bytes 638984 | tf_op jit(solution)/shard_map/ppermute | solution.py:645
  173.1 0.7 copy-start.17
  179.5 9.2 %collective-permute-start.9 = (s16[4,104,256]{2,1,0:T(8,128)(2,1)}, s16[4,104,256]{2,1,0:T(8,128)(2,1)S(1)}, u32[]{:S(2)}, u32[]{:S(2)}) collective-permute-start(s16[4,104,256]{2,1,0:T(8,128)(2,1)} %get-tuple-element.34), channel_id=1, source_target_pairs={{0,1},{1,0},{2,3},{3,2},{4,5},{5,4},{6,7},{7,6},{8,9},{9,8},{10,11... | collective-permute-start | bytes 638984 | tf_op jit(solution)/shard_map/ppermute | solution.py:580
  184.7 11.0 %collective-permute-start.14 = (s16[4,104,256]{2,1,0:T(8,128)(2,1)}, s16[4,104,256]{2,1,0:T(8,128)(2,1)S(1)}, u32[]{:S(2)}, u32[]{:S(2)}) collective-permute-start(s16[4,104,256]{2,1,0:T(8,128)(2,1)} %get-tuple-element.35), channel_id=1, source_target_pairs={{0,8},{8,0},{16,24},{24,16},{32,40},{40,32},{48,56},{56,48},{1,9},... | collective-permute-start | bytes 638984 | tf_op jit(solution)/shard_map/ppermute | solution.py:580
  189.7 25.6 %copy-start = (s16[2,4,104,256]{3,2,1,0:T(8,128)(2,1)}, s16[2,4,104,256]{3,2,1,0:T(8,128)(2,1)S(1)}, u32[]{:S(2)}) copy-start(s16[2,4,104,256]{3,2,1,0:T(8,128)(2,1)S(1)} %pad_add_fusion.refs_0_) | copy-start | bytes 1277956
  189.7 13.8 %collective-permute-start.10 = (s16[2,4,104,256]{3,2,1,0:T(8,128)(2,1)S(1)}, s16[2,4,104,256]{3,2,1,0:T(8,128)(2,1)S(1)}, u32[]{:S(2)}, u32[]{:S(2)}) collective-permute-start(s16[2,4,104,256]{3,2,1,0:T(8,128)(2,1)S(1)} %pad_add_fusion.refs_0_), channel_id=1, source_target_pairs={{0,2},{1,3},{2,4},{3,5},{4,6},{5,7},{6,0},{7,1},{8,10},{9,11},{10,... | collective-permute-start | bytes 1277960 | tf_op jit(solution)/shard_map/ppermute | solution.py:580
  190.4 13.3 %collective-permute-start.11 = (s16[2,4,104,256]{3,2,1,0:T(8,128)(2,1)S(1)}, s16[2,4,104,256]{3,2,1,0:T(8,128)(2,1)S(1)}, u32[]{:S(2)}, u32[]{:S(2)}) collective-permute-start(s16[2,4,104,256]{3,2,1,0:T(8,128)(2,1)S(1)} %pad_add_fusion.refs_0_), channel_id=1, source_target_pairs={{0,6},{1,7},{2,0},{3,1},{4,2},{5,3},{6,4},{7,5},{8,14},{9,15},{10,... | collective-permute-start | bytes 1277960 | tf_op jit(solution)/shard_map/ppermute | solution.py:580
  196.7 18.7 %copy-start.1 = (s16[2,4,104,256]{3,2,1,0:T(8,128)(2,1)}, s16[2,4,104,256]{3,2,1,0:T(8,128)(2,1)S(1)}, u32[]{:S(2)}) copy-start(s16[2,4,104,256]{3,2,1,0:T(8,128)(2,1)S(1)} %pad_add_fusion.1.refs_5_) | copy-start | bytes 1277956
  196.7 11.5 %collective-permute-start.15 = (s16[2,4,104,256]{3,2,1,0:T(8,128)(2,1)S(1)}, s16[2,4,104,256]{3,2,1,0:T(8,128)(2,1)S(1)}, u32[]{:S(2)}, u32[]{:S(2)}) collective-permute-start(s16[2,4,104,256]{3,2,1,0:T(8,128)(2,1)S(1)} %pad_add_fusion.1.refs_5_), channel_id=1, source_target_pairs={{0,16},{8,24},{16,32},{24,40},{32,48},{40,56},{48,0},{56,8},{1,17}... | collective-permute-start | bytes 1277960 | tf_op jit(solution)/shard_map/ppermute | solution.py:580
  197.7 10.6 %collective-permute-start.16 = (s16[2,4,104,256]{3,2,1,0:T(8,128)(2,1)S(1)}, s16[2,4,104,256]{3,2,1,0:T(8,128)(2,1)S(1)}, u32[]{:S(2)}, u32[]{:S(2)}) collective-permute-start(s16[2,4,104,256]{3,2,1,0:T(8,128)(2,1)S(1)} %pad_add_fusion.1.refs_5_), channel_id=1, source_target_pairs={{0,48},{8,56},{16,0},{24,8},{32,16},{40,24},{48,32},{56,40},{1,49}... | collective-permute-start | bytes 1277960 | tf_op jit(solution)/shard_map/ppermute | solution.py:580
  203.6 11.8 %copy-start.3 = (s16[2,4,104,256]{3,2,1,0:T(8,128)(2,1)}, s16[2,4,104,256]{3,2,1,0:T(8,128)(2,1)S(1)}, u32[]{:S(2)}) copy-start(s16[2,4,104,256]{3,2,1,0:T(8,128)(2,1)S(1)} %collective-permute-done.10.refs_1_) | copy-start | bytes 1277956
  203.6 8.1 %collective-permute-start.12 = (s16[1,4,104,256]{3,2,1,0:T(8,128)(2,1)S(1)}, s16[1,4,104,256]{3,2,1,0:T(8,128)(2,1)S(1)}, u32[]{:S(2)}, u32[]{:S(2)}) collective-permute-start(s16[1,4,104,256]{3,2,1,0:T(8,128)(2,1)S(1)} %slice.41), channel_id=1, source_target_pairs={{0,2},{1,3},{2,4},{3,5},{4,6},{5,7},{6,0},{7,1},{8,10},{9,11},{10,... | collective-permute-start | bytes 638984 | tf_op jit(solution)/shard_map/ppermute | solution.py:580
  203.7 11.7 %copy-start.4 = (s16[2,4,104,256]{3,2,1,0:T(8,128)(2,1)}, s16[2,4,104,256]{3,2,1,0:T(8,128)(2,1)S(1)}, u32[]{:S(2)}) copy-start(s16[2,4,104,256]{3,2,1,0:T(8,128)(2,1)S(1)} %collective-permute-done.11.refs_2_) | copy-start | bytes 1277956
  203.7 8.0 %collective-permute-start.13 = (s16[1,4,104,256]{3,2,1,0:T(8,128)(2,1)S(1)}, s16[1,4,104,256]{3,2,1,0:T(8,128)(2,1)S(1)}, u32[]{:S(2)}, u32[]{:S(2)}) collective-permute-start(s16[1,4,104,256]{3,2,1,0:T(8,128)(2,1)S(1)} %slice.42), channel_id=1, source_target_pairs={{0,6},{1,7},{2,0},{3,1},{4,2},{5,3},{6,4},{7,5},{8,14},{9,15},{10,... | collective-permute-start | bytes 638984 | tf_op jit(solution)/shard_map/ppermute | solution.py:580
  208.2 7.2 %copy-start.5 = (s16[2,4,104,256]{3,2,1,0:T(8,128)(2,1)}, s16[2,4,104,256]{3,2,1,0:T(8,128)(2,1)S(1)}, u32[]{:S(2)}) copy-start(s16[2,4,104,256]{3,2,1,0:T(8,128)(2,1)S(1)} %collective-permute-done.15.refs_6_) | copy-start | bytes 1277956
  208.2 7.1 %collective-permute-start.17 = (s16[1,4,104,256]{3,2,1,0:T(8,128)(2,1)S(1)}, s16[1,4,104,256]{3,2,1,0:T(8,128)(2,1)S(1)}, u32[]{:S(2)}, u32[]{:S(2)}) collective-permute-start(s16[1,4,104,256]{3,2,1,0:T(8,128)(2,1)S(1)} %slice.43), channel_id=1, source_target_pairs={{0,16},{8,24},{16,32},{24,40},{32,48},{40,56},{48,0},{56,8},{1,17}... | collective-permute-start | bytes 638984 | tf_op jit(solution)/shard_map/ppermute | solution.py:580
  208.3 7.1 %copy-start.6 = (s16[2,4,104,256]{3,2,1,0:T(8,128)(2,1)}, s16[2,4,104,256]{3,2,1,0:T(8,128)(2,1)S(1)}, u32[]{:S(2)}) copy-start(s16[2,4,104,256]{3,2,1,0:T(8,128)(2,1)S(1)} %collective-permute-done.16.refs_7_) | copy-start | bytes 1277956
  208.3 7.0 %collective-permute-start.18 = (s16[1,4,104,256]{3,2,1,0:T(8,128)(2,1)S(1)}, s16[1,4,104,256]{3,2,1,0:T(8,128)(2,1)S(1)}, u32[]{:S(2)}, u32[]{:S(2)}) collective-permute-start(s16[1,4,104,256]{3,2,1,0:T(8,128)(2,1)S(1)} %slice.44), channel_id=1, source_target_pairs={{0,48},{8,56},{16,0},{24,8},{32,16},{40,24},{48,32},{56,40},{1,49}... | collective-permute-start | bytes 638984 | tf_op jit(solution)/shard_map/ppermute | solution.py:580
  211.7 3.7 %copy-start.13 = (s16[1,4,104,256]{3,2,1,0:T(8,128)(2,1)}, s16[1,4,104,256]{3,2,1,0:T(8,128)(2,1)S(1)}, u32[]{:S(2)}) copy-start(s16[1,4,104,256]{3,2,1,0:T(8,128)(2,1)S(1)} %collective-permute-done.12.refs_3_) | copy-start | bytes 638980
  211.7 3.7 %copy-start.14 = (s16[1,4,104,256]{3,2,1,0:T(8,128)(2,1)}, s16[1,4,104,256]{3,2,1,0:T(8,128)(2,1)S(1)}, u32[]{:S(2)}) copy-start(s16[1,4,104,256]{3,2,1,0:T(8,128)(2,1)S(1)} %collective-permute-done.13.refs_4_) | copy-start | bytes 638980
  215.3 0.7 copy-start.15
  215.3 0.8 copy-start.16

commit v7 on v6

--- a/solution.py
+++ b/solution.py
@@ -352,13 +352,43 @@
     )(ids, *pairs)
 
 
+FIRST_TILES = 2
+
+
+def columns_out(full, inverses, tiles, high_ref, low_ref, ih_ref, il_ref, rest_ref):
+    order = full.shape[0]
+    size = ih_ref.shape[1]
+    half = size // BLOCK
+    for q in range(tiles):
+        s, e = q * size, (q + 1) * size
+        full[s : s + BLOCK, s + BLOCK : e] = jnp.zeros((BLOCK, size - BLOCK), jnp.float32)
+        ih_ref[q], il_ref[q] = tile_inverse(inverses[q * half], inverses[q * half + 1], full[s + BLOCK : e, s : s + BLOCK])
+        if e < order:
+            high_ref[e:order, s:e], low_ref[e:order, s:e] = split(full[e:order, s:e])
+    done = tiles * size
+    rest_ref[...] = full[done:order, done:order]
+
+
+def columns_shapes(order, tiles, size):
+    wide = jax.ShapeDtypeStruct((order, tiles * size), jnp.bfloat16)
+    inv = jax.ShapeDtypeStruct((tiles, size, size), jnp.bfloat16)
+    left = order - tiles * size
+    return (wide, wide, inv, inv, jax.ShapeDtypeStruct((left, left), jnp.float32))
+
+
+def columns_scratch(order, tiles, size):
+    return [
+        pltpu.VMEM((order, order), jnp.float32),
+        pltpu.VMEM((tiles * size // BLOCK, BLOCK, BLOCK), jnp.float32),
+        pltpu.VMEM((BLOCK, BLOCK), jnp.float32),
+    ]
+
+
 def factorize_first(ids, lead, size):
     order = LEAD_TILES * size
-    done = order - size
-    half = size // BLOCK
 
     def kernel(ids_ref, *refs):
-        *pieces, high_ref, low_ref, ih_ref, il_ref, own_ref, rest_ref, full, inverses, work = refs
+        *pieces, high_ref, low_ref, ih_ref, il_ref, rest_ref, own_ref, full, inverses, work = refs
         for ref, first, source in ring_pieces(pieces, lax.div(ids_ref[1], 2), len(PAIRS)):
             for number in range(ref.shape[0]):
                 i, j = PAIRS[first + number]
@@ -366,41 +396,44 @@
                 thin = tile.shape[0]
                 start = pl.multiple_of(i * size + source * thin, thin)
                 full[pl.ds(start, thin), j * size : (j + 1) * size] = tile
-        eliminate(full, inverses, work, range(done // BLOCK))
-        for q in range(LEAD_TILES - 1):
-            s = q * size
-            full[s : s + BLOCK, s + BLOCK : s + size] = jnp.zeros((BLOCK, size - BLOCK), jnp.float32)
-            ih_ref[q], il_ref[q] = tile_inverse(
-                inverses[q * half], inverses[q * half + 1], full[s + BLOCK : s + size, s : s + BLOCK]
-            )
-        for i, j in PAIRS[:-1]:
-            tile = full[i * size : (i + 1) * size, j * size : (j + 1) * size]
-            high, low = split(tile)
-            high_ref[i * size : (i + 1) * size, j * size : (j + 1) * size] = high
-            low_ref[i * size : (i + 1) * size, j * size : (j + 1) * size] = low
-
-            @pl.when((ids_ref[0] == i) & (ids_ref[1] == j))
-            def _():
-                own_ref[...] = tile
-
-        rest_ref[...] = full[done:order, done:order]
-
-    wide = jax.ShapeDtypeStruct((order, done), jnp.bfloat16)
-    inv = jax.ShapeDtypeStruct((LEAD_TILES - 1, size, size), jnp.bfloat16)
-    tile = jax.ShapeDtypeStruct((size, size), jnp.float32)
+        eliminate(full, inverses, work, range(FIRST_TILES * size // BLOCK))
+        columns_out(full, inverses, FIRST_TILES, high_ref, low_ref, ih_ref, il_ref, rest_ref)
+        for i, j in PAIRS:
+            if j < FIRST_TILES:
+
+                @pl.when((ids_ref[0] == i) & (ids_ref[1] == j))
+                def _():
+                    own_ref[...] = full[i * size : (i + 1) * size, j * size : (j + 1) * size]
+
     return pl.pallas_call(
         kernel,
         name="factorize_first",
-        out_shape=(wide, wide, inv, inv, tile, tile),
+        out_shape=(*columns_shapes(order, FIRST_TILES, size), jax.ShapeDtypeStruct((size, size), jnp.float32)),
         in_specs=[smem()] + [vmem()] * len(lead),
         out_specs=(vmem(),) * 6,
-        scratch_shapes=[
-            pltpu.VMEM((order, order), jnp.float32),
-            pltpu.VMEM((done // BLOCK, BLOCK, BLOCK), jnp.float32),
-            pltpu.VMEM((BLOCK, BLOCK), jnp.float32),
-        ],
+        scratch_shapes=columns_scratch(order, FIRST_TILES, size),
         compiler_params=pltpu.CompilerParams(vmem_limit_bytes=VMEM_BYTES),
     )(ids, *lead)
+
+
+def factorize_second(rest, size):
+    order = rest.shape[0]
+
+    def kernel(rest_ref, high_ref, low_ref, ih_ref, il_ref, out_ref, column_ref, full, inverses, work):
+        full[...] = rest_ref[...]
+        eliminate(full, inverses, work, range(size // BLOCK))
+        columns_out(full, inverses, 1, high_ref, low_ref, ih_ref, il_ref, out_ref)
+        column_ref[...] = full[:, 0:size]
+
+    return pl.pallas_call(
+        kernel,
+        name="factorize_second",
+        out_shape=(*columns_shapes(order, 1, size), jax.ShapeDtypeStruct((order, size), jnp.float32)),
+        in_specs=[vmem()],
+        out_specs=(vmem(),) * 6,
+        scratch_shapes=columns_scratch(order, 1, size),
+        compiler_params=pltpu.CompilerParams(vmem_limit_bytes=VMEM_BYTES),
+    )(rest)
 
 
 def factorize_next(rest):
@@ -446,39 +479,49 @@
     )(rest, first_inverse)
 
 
-def solve(panels, factors):
+def solve(panels, first, second, last):
     _, coded_rows, size = panels[0].shape
     thin, order = coded_rows - SCALE_ROWS, LEAD_TILES * size
     count = len(panels)
+    inner = FIRST_TILES * size
 
     def kernel(*refs):
         panel_refs = refs[:count]
-        high_ref, low_ref, ih_ref, il_ref, last_ih_ref, last_il_ref = refs[count : count + 6]
-        *out_refs, xh, xl = refs[count + 6 :]
+        high1, low1, ih1, il1, high2, low2, ih2, il2, ih3, il3 = refs[count : count + 10]
+        *out_refs, xh, xl = refs[count + 10 :]
         for q in range(LEAD_TILES):
             s, e = q * size, (q + 1) * size
             acc = jnp.concatenate([decode(ref[q]) for ref in panel_refs], axis=0)
             if q:
-                acc = acc - nt3((xh[:, 0:s], xl[:, 0:s]), (high_ref[s:e, 0:s], low_ref[s:e, 0:s]))
-            last = q == LEAD_TILES - 1
-            inverse = (last_ih_ref[...], last_il_ref[...]) if last else (ih_ref[q], il_ref[q])
+                k = min(s, inner)
+                acc = acc - nt3((xh[:, 0:k], xl[:, 0:k]), (high1[s:e, 0:k], low1[s:e, 0:k]))
+            if s > inner:
+                y = slice(s - inner, e - inner)
+                acc = acc - nt3((xh[:, inner:s], xl[:, inner:s]), (high2[y, :], low2[y, :]))
+            if q < FIRST_TILES:
+                inverse = (ih1[q], il1[q])
+            elif q == FIRST_TILES:
+                inverse = (ih2[0], il2[0])
+            else:
+                inverse = (ih3[...], il3[...])
             x = nt3(split(acc), inverse)
-            xh[:, s:e], xl[:, s:e] = split(x)
-            for number, ref in enumerate(out_refs):
-                ref[q] = encode(x[number * thin : (number + 1) * thin])
+            if e < order:
+                xh[:, s:e], xl[:, s:e] = split(x)
+            for number in range(count):
+                out_refs[number // 2][number % 2, q] = encode(x[number * thin : (number + 1) * thin])
 
     return pl.pallas_call(
         kernel,
         name="solve",
-        out_shape=(jax.ShapeDtypeStruct((LEAD_TILES, coded_rows, size), jnp.int16),) * count,
-        in_specs=[vmem()] * (count + 6),
-        out_specs=(vmem(),) * count,
-        scratch_shapes=[pltpu.VMEM((count * thin, order), jnp.bfloat16)] * 2,
+        out_shape=(jax.ShapeDtypeStruct((2, LEAD_TILES, coded_rows, size), jnp.int16),) * (count // 2),
+        in_specs=[vmem()] * (count + 10),
+        out_specs=(vmem(),) * (count // 2),
+        scratch_shapes=[pltpu.VMEM((count * thin, order - size), jnp.bfloat16)] * 2,
         compiler_params=pltpu.CompilerParams(vmem_limit_bytes=VMEM_BYTES),
-    )(*panels, *factors)
-
-
-def finish(ids, rows, cols, own, last_own, extended, front):
+    )(*panels, *first, *second, *last)
+
+
+def finish(ids, rows, cols, own, column, last_own, extended, front):
     size = own.shape[0]
     order = LEAD_TILES * size
     tile_rows, tile_cols = front.shape[:2]
@@ -488,7 +531,7 @@
 
     def kernel(ids_ref, *refs):
         row_pieces, col_pieces = refs[:half], refs[half : 2 * half]
-        own_ref, last_own_ref, ext_ref, front_ref, out_ref, xh, xl = refs[2 * half :]
+        own_ref, column_ref, last_own_ref, ext_ref, front_ref, out_ref, xh, xl = refs[2 * half :]
         row, col = ids_ref[0], ids_ref[1]
 
         def put(a, b, tile):
@@ -546,7 +589,9 @@
         def _():
             @pl.when(lead_row)
             def _():
-                put(0, 0, jnp.where((row == last_tile) & (col == last_tile), last_own_ref[...], own_ref[...]))
+                start = pl.multiple_of(jnp.clip(row - FIRST_TILES, 0, 1) * size, size)
+                late = jnp.where(col == last_tile, last_own_ref[...], column_ref[pl.ds(start, size), :])
+                put(0, 0, jnp.where(col < FIRST_TILES, own_ref[...], late))
 
             @pl.when(jnp.logical_not(lead_row))
             def _():
@@ -565,11 +610,11 @@
         kernel,
         name="finish",
         out_shape=jax.ShapeDtypeStruct((tile_rows * size * tile_cols * parts, lanes), jnp.float32),
-        in_specs=[smem()] + [vmem()] * (2 * half + 4),
+        in_specs=[smem()] + [vmem()] * (2 * half + 5),
         out_specs=vmem(),
         scratch_shapes=[pltpu.VMEM((2 * tile_rows * size, order), jnp.bfloat16)] * 2,
         compiler_params=pltpu.CompilerParams(vmem_limit_bytes=VMEM_BYTES),
-    )(ids, *rows, *cols, own, last_own, extended, front)
+    )(ids, *rows, *cols, own, column, last_own, extended, front)
 
 
 def exchange(value, axis):
@@ -595,11 +640,6 @@
     ring = len(pieces) - 1
     for ref, step, first in zip(pieces, (0, 1, 3, 2, 2), (0, 0, 0, 0, length // 2), strict=True):
         yield ref, first, lax.rem(place + (ring - step), ring)
-
-
-def pair_gather(value, axis):
-    partner = permute(value, axis, lambda i: i ^ 1)
-    return ring_gather(jnp.stack([value, partner]), axis)
 
 
 def pair_pieces(pieces, place):
@@ -635,20 +675,23 @@
     received = exchange(packed, ("front", "row"))
 
     lead = ring_gather(collect(ids, leading), "col")
-    *factors, own, rest = factorize_first(ids, lead, size)
+    *first, rest, own = factorize_first(ids, lead, size)
     received, rest = lax.optimization_barrier((received, rest))
 
     extended, panel = assemble(received, front, n_col)
     mine = exchange(panel, "col")[:LEAD_TILES]
-    rest, first_inverse = factorize_next(rest)
-    last_own, *last_inverse = factorize_last(rest, first_inverse)
+    *second, rest, column = factorize_second(rest, size)
     turned = lax.ppermute(
         mine, ("row", "col"), [(r * n_col + c, c * n_col + r) for r in range(n_row) for c in range(n_col)]
     )
-    solved, turned = solve((mine, turned), (*factors, *last_inverse))
-    rows = pair_gather(solved, "col")
-    cols = pair_gather(turned, "row")
-    factor = finish(ids, rows, cols, own, last_own, extended, front)
+    beside = permute(mine, "col", lambda i: i ^ 1)
+    rest, first_inverse = factorize_next(rest)
+    turned_beside = permute(turned, "row", lambda i: i ^ 1)
+    last_own, *last = factorize_last(rest, first_inverse)
+    row_pair, col_pair = solve((mine, beside, turned, turned_beside), first, second, last)
+    rows = ring_gather(row_pair, "col")
+    cols = ring_gather(col_pair, "row")
+    factor = finish(ids, rows, cols, own, column, last_own, extended, front)
     return factor.reshape(1, tile_rows, 1, size, tile_cols, 1, size)
 
 

time: 227 us -> 232 us (1.022)
  starting transfers between devices: 50.9 us -> 59.3 us
  waiting for transfers between devices: 81.3 us -> 77.2 us
  Pallas kernels: 70.7 us -> 73.7 us
    ppermute x14, starting transfers between devices: 28.3 us -> 36.7 us  [permute(): lax.ppermute(value, axis, [(i, target(i)) for i in range(lax.axis_size(ax...]
    ppermute x14, waiting for transfers between devices: 22.1 us -> 18 us  [permute(): lax.ppermute(value, axis, [(i, target(i)) for i in range(lax.axis_size(ax...]
    pallas_call x2 -> x3, Pallas kernels: 37.1 us -> 39.7 us  [the longest x1 22.7 us: factorize_first(): pl.pallas_call(kernel, name='factorize_first', out_shape=(*columns_shapes...]
  transfers between devices with their start and end apart: 21 -> 21, of which waited for: 11 -> 10; matrix products, arithmetic and copies ran while one was open for 1% -> 0% of each run, Pallas kernels for 22% -> 23%
where the time goes in v7:
time: 232 us; the launch traced here: 230 us
  waiting for transfers between devices  77.2 us (33%)
  Pallas kernels  73.7 us (32%)
  starting transfers between devices  59.3 us (26%)
  blocking collectives  12.5 us (5%)
  local copies, waits for them, and re-layouts  5.2 us (2%)
    ppermute x1, waiting for transfers between devices, per_device(): partner = lax.ppermute(chunk, 'row', [(i, i ^ 1) for i in owners])  50 us
    ppermute x14, starting transfers between devices, permute(): lax.ppermute(value, axis, [(i, target(i)) for i in range(lax.axis_size(ax...  36.7 us
    pallas_call x1, Pallas kernels, factorize_first(): pl.pallas_call(kernel, name='factorize_first', out_shape=(*columns_shapes...  22.7 us
    ppermute x14, waiting for transfers between devices, permute(): lax.ppermute(value, axis, [(i, target(i)) for i in range(lax.axis_size(ax...  18 us
    all_to_all x2, starting transfers between devices, exchange(): return lax.all_to_all(value, axis, split_axis=0, concat_axis=0, tiled=True)  14.2 us
    all_to_all x1, blocking collectives, exchange(): return lax.all_to_all(value, axis, split_axis=0, concat_axis=0, tiled=True)  12.5 us
    pallas_call x1, Pallas kernels, factorize_second(): pl.pallas_call(kernel, name='factorize_second', out_shape=(*columns_shape...  10.7 us
    ppermute x3, waiting for transfers between devices, per_device(): lax.ppermute(pair, 'row', [(i, (i + 2 * step) % n_row) for i in owners])  9.05 us
  transfers between devices with their start and end apart: 21, of which 10 were waited for; matrix products, arithmetic and copies ran while one was open for 0% of the time, Pallas kernels for 23%

profile of v7, /device:TPU:6, one launch (start us, length us, event | category | flops | bytes accessed | tf_op | source)
XLA Modules:
  0.0 229.5 jit_solution(10826864510549098086)
XLA Ops:
  0.0 0.9 slice.36
  0.9 0.7 broadcast_in_dim.3
  1.6 6.8 %all-to-all-start.1 = ((bf16[8,64,256]{2,1,0:T(8,128)(2,1)}), bf16[8,64,256]{2,1,0:T(8,128)(2,1)S(1)}, u32[]{:S(2)}, u32[]{:S(2)}) async-start(bf16[8,64,256]{2,1,0:T(8,128)(2,1)} %bitcast.10), calls=%async_computation.1 | async-start | bytes 524288 | tf_op jit(solution)/shard_map/all_to_all | solution.py:621
  9.1 5.3 %pack.1 = bf16[32,264,256]{2,1,0:T(8,128)(2,1)} custom-call(s32[32]{0:T(128)} %bitcast.23, s32[32]{0:T(128)} %bitcast.24, s32[32]{0:T(128)} %bitcast.25, s32[1]{0:T(128)} %bitcast.16.live_ref, bf16[32,256,256]{2,1,0:T(8,128)(2,1)} %bitcast.20), custom_call_target="tpu_custom_call" | custom-call | tf_op jit(solution)/shard_map/pack/pallas_call | solution.py:107
  14.3 0.2 all-to-all-done.1
  14.5 7.4 %all-to-all-start = ((bf16[32,264,256]{2,1,0:T(8,128)(2,1)}), bf16[32,264,256]{2,1,0:T(8,128)(2,1)}, u32[]{:S(2)}, u32[]{:S(2)}) async-start(bf16[32,264,256]{2,1,0:T(8,128)(2,1)} %pack.1), calls=%async_computation | async-start | bytes 8650752 | tf_op jit(solution)/shard_map/all_to_all | solution.py:621
  22.0 2.1 collective-permute-start
  24.1 50.0 %collective-permute-done = bf16[4,64,256]{2,1,0:T(8,128)(2,1)S(1)} collective-permute-done((bf16[4,64,256]{2,1,0:T(8,128)(2,1)S(1)}, bf16[4,64,256]{2,1,0:T(8,128)(2,1)S(1)}, u32[]{:S(2)}, u32[]{:S(2)}) %collective-permute-start) | collective-permute-done | bytes 131104 | tf_op jit(solution)/shard_map/ppermute | solution.py:664
  74.1 0.0 copy-start
  74.1 2.4 %collective-permute-start.1 = (bf16[2,4,64,256]{3,2,1,0:T(8,128)(2,1)S(1)}, bf16[2,4,64,256]{3,2,1,0:T(8,128)(2,1)S(1)}, u32[]{:S(2)}, u32[]{:S(2)}) collective-permute-start(bf16[2,4,64,256]{3,2,1,0:T(8,128)(2,1)S(1)} %pad_maximum_fusion.refs_0_), channel_id=1, source_target_pairs={{0,16},{8,24},{16,32},{24,40},{1,17},{9,25},{17,33},{25,41},{2,18}... | collective-permute-start | bytes 786440 | tf_op jit(solution)/shard_map/ppermute | solution.py:668
  76.5 1.3 collective-permute-start.2
  77.9 1.9 collective-permute-start.3
  79.8 0.6 pad_add_fusion.ids_ref
  80.4 2.8 %collective-permute-done.1.refs_1_ = bf16[2,4,64,256]{3,2,1,0:T(8,128)(2,1)S(1)} collective-permute-done((bf16[2,4,64,256]{3,2,1,0:T(8,128)(2,1)S(1)}, bf16[2,4,64,256]{3,2,1,0:T(8,128)(2,1)S(1)}, u32[]{:S(2)}, u32[]{:S(2)}) %collective-permute-start.1) | collective-permute-done | bytes 262176 | tf_op jit(solution)/shard_map/ppermute | solution.py:668
  83.2 4.1 %collective-permute-done.2.refs_2_ = bf16[2,4,64,256]{3,2,1,0:T(8,128)(2,1)S(1)} collective-permute-done((bf16[2,4,64,256]{3,2,1,0:T(8,128)(2,1)S(1)}, bf16[2,4,64,256]{3,2,1,0:T(8,128)(2,1)S(1)}, u32[]{:S(2)}, u32[]{:S(2)}) %collective-permute-start.2) | collective-permute-done | bytes 262176 | tf_op jit(solution)/shard_map/ppermute | solution.py:668
  87.3 2.1 collective-permute-done.3.refs_3_
  89.4 0.0 copy-done.8
  89.5 0.7 copy-done.10
  90.2 2.4 %collect.1.refs_0_ = bf16[10,64,256]{2,1,0:T(8,128)(2,1)} custom-call(s32[2]{0:T(128)} %pad_add_fusion.ids_ref, bf16[2,4,64,256]{3,2,1,0:T(8,128)(2,1)} %copy-done, bf16[2,4,64,256]{3,2,1,0:T(8,128)(2,1)} %copy-done.8, bf16[2,4,64,256]{3,2,1,0:T(8,128)(2,1)} %copy-done.9, bf16[2,4,64,256]{3,2,1,0:T(8,128)(2,1)} %copy-done.10), custom_call_target="tpu_custom_call" | custom-call | tf_op jit(solution)/shard_map/collect/pallas_call | solution.py:345
  92.6 0.8 collective-permute-start.4
  93.4 2.5 %collective-permute-start.5 = (bf16[10,64,256]{2,1,0:T(8,128)(2,1)}, bf16[10,64,256]{2,1,0:T(8,128)(2,1)S(1)}, u32[]{:S(2)}, u32[]{:S(2)}) collective-permute-start(bf16[10,64,256]{2,1,0:T(8,128)(2,1)} %collect.1.refs_0_), channel_id=1, source_target_pairs={{0,6},{1,7},{2,0},{3,1},{4,2},{5,3},{6,4},{7,5},{8,14},{9,15},{10,... | collective-permute-start | bytes 983048 | tf_op jit(solution)/shard_map/ppermute | solution.py:625
  95.9 6.8 %collective-permute-done.4.refs_1_ = bf16[10,64,256]{2,1,0:T(8,128)(2,1)S(1)} collective-permute-done((bf16[10,64,256]{2,1,0:T(8,128)(2,1)}, bf16[10,64,256]{2,1,0:T(8,128)(2,1)S(1)}, u32[]{:S(2)}, u32[]{:S(2)}) %collective-permute-start.4) | collective-permute-done | bytes 327712 | tf_op jit(solution)/shard_map/ppermute | solution.py:625
  102.7 0.1 collective-permute-start.6
  102.8 0.0 collective-permute-done.5.refs_2_
  102.8 3.3 %collective-permute-start.7 = (bf16[5,64,256]{2,1,0:T(8,128)(2,1)S(1)}, bf16[5,64,256]{2,1,0:T(8,128)(2,1)S(1)}, u32[]{:S(2)}, u32[]{:S(2)}) collective-permute-start(bf16[5,64,256]{2,1,0:T(8,128)(2,1)S(1)} %slice.39), channel_id=1, source_target_pairs={{0,6},{1,7},{2,0},{3,1},{4,2},{5,3},{6,4},{7,5},{8,14},{9,15},{10,... | collective-permute-start | bytes 491528 | tf_op jit(solution)/shard_map/ppermute | solution.py:625
  106.1 3.2 %collective-permute-done.6.refs_3_ = bf16[5,64,256]{2,1,0:T(8,128)(2,1)S(1)} collective-permute-done((bf16[5,64,256]{2,1,0:T(8,128)(2,1)S(1)}, bf16[5,64,256]{2,1,0:T(8,128)(2,1)S(1)}, u32[]{:S(2)}, u32[]{:S(2)}) %collective-permute-start.6) | collective-permute-done | bytes 163872 | tf_op jit(solution)/shard_map/ppermute | solution.py:625
  109.3 0.0 collective-permute-done.7.refs_4_
  109.3 0.6 copy-done.18
  110.0 0.7 copy-done.19
  110.6 22.7 %factorize_first.1 = (bf16[1024,512]{1,0:T(8,128)(2,1)}, bf16[1024,512]{1,0:T(8,128)(2,1)}, bf16[2,256,256]{2,1,0:T(8,128)(2,1)}, bf16[2,256,256]{2,1,0:T(8,128)...) custom-call(s32[2]{0:T(128)} %pad_add_fusion.ids_ref, bf16[10,64,256]{2,1,0:T(8,128)(2,1)} %collect.1.refs_0_, ...), custom_call_target="tpu_custom_call" | custom-call | tf_op jit(solution)/shard_map/factorize_first/pallas_call | solution.py:408
  133.3 0.0 all-to-all-done.received_ref
  133.3 6.7 %assemble.1 = (f32[5,256,256]{2,1,0:T(8,128)}, s16[8,104,256]{2,1,0:T(8,128)(2,1)}) custom-call(bf16[32,264,256]{2,1,0:T(8,128)(2,1)} %all-to-all-done.received_ref, bf16[3,3,256,256]{3,2,1,0:T(8,128)(2,1)} %bitcast.18), custom_call_target="tpu_custom_call" | custom-call | tf_op jit(solution)/shard_map/assemble/pallas_call | solution.py:201
  140.0 12.5 %all_to_all.15 = s16[8,104,256]{2,1,0:T(8,128)(2,1)S(1)} all-to-all(s16[8,104,256]{2,1,0:T(8,128)(2,1)} %get-tuple-element.30), channel_id=1, replica_groups=mesh['front'=2,'row'=8,'col'=8] {'col'}, dimensions={0} | all-to-all | bytes 851968 | tf_op jit(solution)/shard_map/all_to_all | solution.py:621
  152.6 0.7 collective-permute-start.9
  153.2 5.3 %collective-permute-start.8 = (s16[4,104,256]{2,1,0:T(8,128)(2,1)S(1)}, s16[4,104,256]{2,1,0:T(8,128)(2,1)S(1)}, u32[]{:S(2)}, u32[]{:S(2)}) collective-permute-start(s16[4,104,256]{2,1,0:T(8,128)(2,1)S(1)} %slice.40.refs_0_), channel_id=1, source_target_pairs={{0,1},{1,0},{2,3},{3,2},{4,5},{5,4},{6,7},{7,6},{8,9},{9,8},{10,11... | collective-permute-start | bytes 638984 | tf_op jit(solution)/shard_map/ppermute | solution.py:625
  158.5 0.0 collective-permute-done.9.refs_2_
  158.5 8.1 %collective-permute-start.10 = (s16[4,104,256]{2,1,0:T(8,128)(2,1)S(1)}, s16[4,104,256]{2,1,0:T(8,128)(2,1)S(1)}, u32[]{:S(2)}, u32[]{:S(2)}) collective-permute-start(s16[4,104,256]{2,1,0:T(8,128)(2,1)S(1)} %collective-permute-done.9.refs_2_), channel_id=1, source_target_pairs={{0,8},{8,0},{16,24},{24,16},{32,40},{40,32},{48,56},{56,48},{1,9},... | collective-permute-start | bytes 638984 | tf_op jit(solution)/shard_map/ppermute | solution.py:625
  166.6 10.7 %factorize_second.1 = (bf16[512,256]{1,0:T(8,128)(2,1)}, bf16[512,256]{1,0:T(8,128)(2,1)}, bf16[1,256,256]{2,1,0:T(8,128)(2,1)}, bf16[1,256,256]{2,1,0:T(8,128)(...) custom-call(f32[512,512]{1,0:T(8,128)} %get-tuple-element.35.rest_ref), custom_call_target="tpu_custom_call" | custom-call | tf_op jit(solution)/shard_map/factorize_second/pallas_call | solution.py:428
  177.3 5.6 %factorize_next.1 = (f32[256,256]{1,0:T(8,128)}, f32[1,128,128]{2,1,0:T(8,128)}) custom-call(f32[256,256]{1,0:T(8,128)} %get-tuple-element.40.rest_ref), custom_call_target="tpu_custom_call" | custom-call | tf_op jit(solution)/shard_map/factorize_next/pallas_call | solution.py:444
  182.9 5.6 %factorize_last.1 = (f32[256,256]{1,0:T(8,128)}, bf16[256,256]{1,0:T(8,128)(2,1)}, bf16[256,256]{1,0:T(8,128)(2,1)}) custom-call(f32[256,256]{1,0:T(8,128)} %get-tuple-element.41.rest_ref, f32[1,128,128]{2,1,0:T(8,128)} %get-tuple-element.42.first_ref), custom_call_target="tpu_custom_call" | custom-call | tf_op jit(solution)/shard_map/factorize_last/pallas_call | solution.py:468
  188.5 0.0 collective-permute-done.8.refs_1_
  188.5 0.0 collective-permute-done.10.refs_3_
  188.5 0.6 copy-done.15
  189.2 0.1 copy-done.16
  189.3 6.3 %solve.1 = (s16[2,4,104,256]{3,2,1,0:T(8,128)(2,1)}, s16[2,4,104,256]{3,2,1,0:T(8,128)(2,1)}) custom-call(s16[4,104,256]{2,1,0:T(8,128)(2,1)} %copy-done.5, s16[4,104,256]{2,1,0:T(8,128)(2,1)} %copy-done.15, s16[4,104,256]{2,1,0:T(8,128)(2,1)} %copy-done.13, s16[4,104,256]{2,1,0:T(8,128)(2,1)} %copy-done.16, bf16[1024,512]{1,0:T(8,128)(2,1)} %get-tuple-element.31.refs_4_, ...), custom_call_target="tpu_custom_call" | custom-call | tf_op jit(solution)/shard_map/solve/pallas_call | solution.py:513
  195.6 1.4 collective-permute-start.11
  197.0 3.9 %collective-permute-start.12 = (s16[2,4,104,256]{3,2,1,0:T(8,128)(2,1)}, s16[2,4,104,256]{3,2,1,0:T(8,128)(2,1)S(1)}, u32[]{:S(2)}, u32[]{:S(2)}) collective-permute-start(s16[2,4,104,256]{3,2,1,0:T(8,128)(2,1)} %get-tuple-element.45.refs_0_), channel_id=1, source_target_pairs={{0,6},{1,7},{2,0},{3,1},{4,2},{5,3},{6,4},{7,5},{8,14},{9,15},{10,... | collective-permute-start | bytes 1277960 | tf_op jit(solution)/shard_map/ppermute | solution.py:625
  200.9 0.0 collective-permute-start.15
  200.9 4.3 %collective-permute-start.16 = (s16[2,4,104,256]{3,2,1,0:T(8,128)(2,1)}, s16[2,4,104,256]{3,2,1,0:T(8,128)(2,1)S(1)}, u32[]{:S(2)}, u32[]{:S(2)}) collective-permute-start(s16[2,4,104,256]{3,2,1,0:T(8,128)(2,1)} %get-tuple-element.46.refs_5_), channel_id=1, source_target_pairs={{0,48},{8,56},{16,0},{24,8},{32,16},{40,24},{48,32},{56,40},{1,49}... | collective-permute-start | bytes 1277960 | tf_op jit(solution)/shard_map/ppermute | solution.py:625
  205.2 4.2 %collective-permute-done.11.refs_1_ = s16[2,4,104,256]{3,2,1,0:T(8,128)(2,1)S(1)} collective-permute-done((s16[2,4,104,256]{3,2,1,0:T(8,128)(2,1)}, s16[2,4,104,256]{3,2,1,0:T(8,128)(2,1)S(1)}, u32[]{:S(2)}, u32[]{:S(2)}) %collective-permute-start.11) | collective-permute-done | bytes 426016 | tf_op jit(solution)/shard_map/ppermute | solution.py:625
  209.4 0.1 collective-permute-start.13
  209.5 0.0 collective-permute-done.12.refs_2_
  209.6 3.3 %collective-permute-start.14 = (s16[1,4,104,256]{3,2,1,0:T(8,128)(2,1)S(1)}, s16[1,4,104,256]{3,2,1,0:T(8,128)(2,1)S(1)}, u32[]{:S(2)}, u32[]{:S(2)}) collective-permute-start(s16[1,4,104,256]{3,2,1,0:T(8,128)(2,1)S(1)} %slice.42), channel_id=1, source_target_pairs={{0,6},{1,7},{2,0},{3,1},{4,2},{5,3},{6,4},{7,5},{8,14},{9,15},{10,... | collective-permute-start | bytes 638984 | tf_op jit(solution)/shard_map/ppermute | solution.py:625
  212.8 0.0 collective-permute-done.15.refs_6_
  212.8 0.1 collective-permute-start.17
  213.0 0.0 collective-permute-done.16.refs_7_
  213.0 3.6 %collective-permute-start.18 = (s16[1,4,104,256]{3,2,1,0:T(8,128)(2,1)S(1)}, s16[1,4,104,256]{3,2,1,0:T(8,128)(2,1)S(1)}, u32[]{:S(2)}, u32[]{:S(2)}) collective-permute-start(s16[1,4,104,256]{3,2,1,0:T(8,128)(2,1)S(1)} %slice.44), channel_id=1, source_target_pairs={{0,48},{8,56},{16,0},{24,8},{32,16},{40,24},{48,32},{56,40},{1,49}... | collective-permute-start | bytes 638984 | tf_op jit(solution)/shard_map/ppermute | solution.py:625
  216.6 0.0 collective-permute-done.13.refs_3_
  216.6 0.0 collective-permute-done.14.refs_4_
  216.6 3.7 %collective-permute-done.17.refs_8_ = s16[1,4,104,256]{3,2,1,0:T(8,128)(2,1)S(1)} collective-permute-done((s16[1,4,104,256]{3,2,1,0:T(8,128)(2,1)S(1)}, s16[1,4,104,256]{3,2,1,0:T(8,128)(2,1)S(1)}, u32[]{:S(2)}, u32[]{:S(2)}) %collective-permute-start.17) | collective-permute-done | bytes 213024 | tf_op jit(solution)/shard_map/ppermute | solution.py:625
  220.3 0.1 collective-permute-done.18.refs_9_
  220.5 0.5 copy-done.14
  221.0 0.1 copy-done.17
  221.1 8.4 %finish.1 = f32[4608,128]{1,0:T(8,128)} custom-call(s32[2]{0:T(128)} %pad_add_fusion.ids_ref, s16[2,4,104,256]{3,2,1,0:T(8,128)(2,1)} %get-tuple-element.45.refs_0_, s16[2,4,104,256]{3,2,1,0:T(8,128)(2,1)} %copy-done.1, s16[2,4,104,256]{3,2,1,0:T(8,128)(2,1)} %copy-done.2, s16[1,4,104,256]{3,2,1,0:T(8,128)(2,1)} %copy-done.11, ...), custom_call_target="tpu_custom_call" | custom-call | tf_op jit(solution)/shard_map/finish/pallas_call | solution.py:609
  (40 shorter events, 0.2 us)
Async XLA Ops:
  1.6 12.9 %all-to-all-start.1 = ((bf16[8,64,256]{2,1,0:T(8,128)(2,1)}), bf16[8,64,256]{2,1,0:T(8,128)(2,1)S(1)}, u32[]{:S(2)}, u32[]{:S(2)}) async-start(bf16[8,64,256]{2,1,0:T(8,128)(2,1)} %bitcast.10), calls=%async_computation.1 | async-start | bytes 524288 | tf_op jit(solution)/shard_map/all_to_all | solution.py:621
  14.5 118.8 %all-to-all-start = ((bf16[32,264,256]{2,1,0:T(8,128)(2,1)}), bf16[32,264,256]{2,1,0:T(8,128)(2,1)}, u32[]{:S(2)}, u32[]{:S(2)}) async-start(bf16[32,264,256]{2,1,0:T(8,128)(2,1)} %pack.1), calls=%async_computation | async-start | bytes 8650752 | tf_op jit(solution)/shard_map/all_to_all | solution.py:621
  22.0 52.0 %collective-permute-start = (bf16[4,64,256]{2,1,0:T(8,128)(2,1)S(1)}, bf16[4,64,256]{2,1,0:T(8,128)(2,1)S(1)}, u32[]{:S(2)}, u32[]{:S(2)}) collective-permute-start(bf16[4,64,256]{2,1,0:T(8,128)(2,1)S(1)} %get-tuple-element.52), channel_id=1, source_target_pairs={{0,8},{8,0},{16,24},{24,16},{1,9},{9,1},{17,25},{25,17},{2,10},{10... | collective-permute-start | bytes 393224 | tf_op jit(solution)/shard_map/ppermute | solution.py:664
  74.1 15.4 %copy-start = (bf16[2,4,64,256]{3,2,1,0:T(8,128)(2,1)}, bf16[2,4,64,256]{3,2,1,0:T(8,128)(2,1)S(1)}, u32[]{:S(2)}) copy-start(bf16[2,4,64,256]{3,2,1,0:T(8,128)(2,1)S(1)} %pad_maximum_fusion.refs_0_) | copy-start | bytes 786436
  74.1 9.1 %collective-permute-start.1 = (bf16[2,4,64,256]{3,2,1,0:T(8,128)(2,1)S(1)}, bf16[2,4,64,256]{3,2,1,0:T(8,128)(2,1)S(1)}, u32[]{:S(2)}, u32[]{:S(2)}) collective-permute-start(bf16[2,4,64,256]{3,2,1,0:T(8,128)(2,1)S(1)} %pad_maximum_fusion.refs_0_), channel_id=1, source_target_pairs={{0,16},{8,24},{16,32},{24,40},{1,17},{9,25},{17,33},{25,41},{2,18}... | collective-permute-start | bytes 786440 | tf_op jit(solution)/shard_map/ppermute | solution.py:668
  76.5 10.8 %collective-permute-start.2 = (bf16[2,4,64,256]{3,2,1,0:T(8,128)(2,1)S(1)}, bf16[2,4,64,256]{3,2,1,0:T(8,128)(2,1)S(1)}, u32[]{:S(2)}, u32[]{:S(2)}) collective-permute-start(bf16[2,4,64,256]{3,2,1,0:T(8,128)(2,1)S(1)} %pad_maximum_fusion.refs_0_), channel_id=1, source_target_pairs={{0,32},{8,40},{16,48},{24,56},{1,33},{9,41},{17,49},{25,57},{2,34}... | collective-permute-start | bytes 786440 | tf_op jit(solution)/shard_map/ppermute | solution.py:668
  77.9 11.6 %collective-permute-start.3 = (bf16[2,4,64,256]{3,2,1,0:T(8,128)(2,1)S(1)}, bf16[2,4,64,256]{3,2,1,0:T(8,128)(2,1)S(1)}, u32[]{:S(2)}, u32[]{:S(2)}) collective-permute-start(bf16[2,4,64,256]{3,2,1,0:T(8,128)(2,1)S(1)} %pad_maximum_fusion.refs_0_), channel_id=1, source_target_pairs={{0,48},{8,56},{16,0},{24,8},{1,49},{9,57},{17,1},{25,9},{2,50},{10... | collective-permute-start | bytes 786440 | tf_op jit(solution)/shard_map/ppermute | solution.py:668
  83.2 6.2 %copy-start.8 = (bf16[2,4,64,256]{3,2,1,0:T(8,128)(2,1)}, bf16[2,4,64,256]{3,2,1,0:T(8,128)(2,1)S(1)}, u32[]{:S(2)}) copy-start(bf16[2,4,64,256]{3,2,1,0:T(8,128)(2,1)S(1)} %collective-permute-done.1.refs_1_) | copy-start | bytes 786436
  87.3 2.1 copy-start.9
  89.4 0.7 copy-start.10
  92.6 10.1 %collective-permute-start.4 = (bf16[10,64,256]{2,1,0:T(8,128)(2,1)}, bf16[10,64,256]{2,1,0:T(8,128)(2,1)S(1)}, u32[]{:S(2)}, u32[]{:S(2)}) collective-permute-start(bf16[10,64,256]{2,1,0:T(8,128)(2,1)} %collect.1.refs_0_), channel_id=1, source_target_pairs={{0,2},{1,3},{2,4},{3,5},{4,6},{5,7},{6,0},{7,1},{8,10},{9,11},{10,... | collective-permute-start | bytes 983048 | tf_op jit(solution)/shard_map/ppermute | solution.py:625
  93.4 9.4 %collective-permute-start.5 = (bf16[10,64,256]{2,1,0:T(8,128)(2,1)}, bf16[10,64,256]{2,1,0:T(8,128)(2,1)S(1)}, u32[]{:S(2)}, u32[]{:S(2)}) collective-permute-start(bf16[10,64,256]{2,1,0:T(8,128)(2,1)} %collect.1.refs_0_), channel_id=1, source_target_pairs={{0,6},{1,7},{2,0},{3,1},{4,2},{5,3},{6,4},{7,5},{8,14},{9,15},{10,... | collective-permute-start | bytes 983048 | tf_op jit(solution)/shard_map/ppermute | solution.py:625
  102.7 6.6 %copy-start.6 = (bf16[10,64,256]{2,1,0:T(8,128)(2,1)}, bf16[10,64,256]{2,1,0:T(8,128)(2,1)S(1)}, u32[]{:S(2)}) copy-start(bf16[10,64,256]{2,1,0:T(8,128)(2,1)S(1)} %collective-permute-done.4.refs_1_) | copy-start | bytes 983044
  102.7 6.6 %collective-permute-start.6 = (bf16[5,64,256]{2,1,0:T(8,128)(2,1)S(1)}, bf16[5,64,256]{2,1,0:T(8,128)(2,1)S(1)}, u32[]{:S(2)}, u32[]{:S(2)}) collective-permute-start(bf16[5,64,256]{2,1,0:T(8,128)(2,1)S(1)} %slice.38), channel_id=1, source_target_pairs={{0,2},{1,3},{2,4},{3,5},{4,6},{5,7},{6,0},{7,1},{8,10},{9,11},{10,... | collective-permute-start | bytes 491528 | tf_op jit(solution)/shard_map/ppermute | solution.py:625
  102.8 6.5 %copy-start.7 = (bf16[10,64,256]{2,1,0:T(8,128)(2,1)}, bf16[10,64,256]{2,1,0:T(8,128)(2,1)S(1)}, u32[]{:S(2)}) copy-start(bf16[10,64,256]{2,1,0:T(8,128)(2,1)S(1)} %collective-permute-done.5.refs_2_) | copy-start | bytes 983044
  102.8 6.5 %collective-permute-start.7 = (bf16[5,64,256]{2,1,0:T(8,128)(2,1)S(1)}, bf16[5,64,256]{2,1,0:T(8,128)(2,1)S(1)}, u32[]{:S(2)}, u32[]{:S(2)}) collective-permute-start(bf16[5,64,256]{2,1,0:T(8,128)(2,1)S(1)} %slice.39), channel_id=1, source_target_pairs={{0,6},{1,7},{2,0},{3,1},{4,2},{5,3},{6,4},{7,5},{8,14},{9,15},{10,... | collective-permute-start | bytes 491528 | tf_op jit(solution)/shard_map/ppermute | solution.py:625
  109.3 0.7 copy-start.18
  110.0 0.7 copy-start.19
  152.5 36.0 %copy-start.5 = (s16[4,104,256]{2,1,0:T(8,128)(2,1)}, s16[4,104,256]{2,1,0:T(8,128)(2,1)S(1)}, u32[]{:S(2)}) copy-start(s16[4,104,256]{2,1,0:T(8,128)(2,1)S(1)} %slice.40.refs_0_) | copy-start | bytes 638980
  152.6 6.0 %collective-permute-start.9 = (s16[4,104,256]{2,1,0:T(8,128)(2,1)S(1)}, s16[4,104,256]{2,1,0:T(8,128)(2,1)S(1)}, u32[]{:S(2)}, u32[]{:S(2)}) collective-permute-start(s16[4,104,256]{2,1,0:T(8,128)(2,1)S(1)} %slice.40.refs_0_), channel_id=1, source_target_pairs={{0,0},{1,8},{2,16},{3,24},{4,32},{5,40},{6,48},{7,56},{8,1},{9,9},... | collective-permute-start | bytes 638984 | tf_op jit(solution)/shard_map/ppermute | solution.py:684
  153.2 35.3 %collective-permute-start.8 = (s16[4,104,256]{2,1,0:T(8,128)(2,1)S(1)}, s16[4,104,256]{2,1,0:T(8,128)(2,1)S(1)}, u32[]{:S(2)}, u32[]{:S(2)}) collective-permute-start(s16[4,104,256]{2,1,0:T(8,128)(2,1)S(1)} %slice.40.refs_0_), channel_id=1, source_target_pairs={{0,1},{1,0},{2,3},{3,2},{4,5},{5,4},{6,7},{7,6},{8,9},{9,8},{10,11... | collective-permute-start | bytes 638984 | tf_op jit(solution)/shard_map/ppermute | solution.py:625
  158.5 30.0 %copy-start.13 = (s16[4,104,256]{2,1,0:T(8,128)(2,1)}, s16[4,104,256]{2,1,0:T(8,128)(2,1)S(1)}, u32[]{:S(2)}) copy-start(s16[4,104,256]{2,1,0:T(8,128)(2,1)S(1)} %collective-permute-done.9.refs_2_) | copy-start | bytes 638980
  158.5 30.0 %collective-permute-start.10 = (s16[4,104,256]{2,1,0:T(8,128)(2,1)S(1)}, s16[4,104,256]{2,1,0:T(8,128)(2,1)S(1)}, u32[]{:S(2)}, u32[]{:S(2)}) collective-permute-start(s16[4,104,256]{2,1,0:T(8,128)(2,1)S(1)} %collective-permute-done.9.refs_2_), channel_id=1, source_target_pairs={{0,8},{8,0},{16,24},{24,16},{32,40},{40,32},{48,56},{56,48},{1,9},... | collective-permute-start | bytes 638984 | tf_op jit(solution)/shard_map/ppermute | solution.py:625
  188.5 0.7 copy-start.15
  188.5 0.7 copy-start.16
  195.6 13.8 %collective-permute-start.11 = (s16[2,4,104,256]{3,2,1,0:T(8,128)(2,1)}, s16[2,4,104,256]{3,2,1,0:T(8,128)(2,1)S(1)}, u32[]{:S(2)}, u32[]{:S(2)}) collective-permute-start(s16[2,4,104,256]{3,2,1,0:T(8,128)(2,1)} %get-tuple-element.45.refs_0_), channel_id=1, source_target_pairs={{0,2},{1,3},{2,4},{3,5},{4,6},{5,7},{6,0},{7,1},{8,10},{9,11},{10,... | collective-permute-start | bytes 1277960 | tf_op jit(solution)/shard_map/ppermute | solution.py:625
  197.0 12.5 %collective-permute-start.12 = (s16[2,4,104,256]{3,2,1,0:T(8,128)(2,1)}, s16[2,4,104,256]{3,2,1,0:T(8,128)(2,1)S(1)}, u32[]{:S(2)}, u32[]{:S(2)}) collective-permute-start(s16[2,4,104,256]{3,2,1,0:T(8,128)(2,1)} %get-tuple-element.45.refs_0_), channel_id=1, source_target_pairs={{0,6},{1,7},{2,0},{3,1},{4,2},{5,3},{6,4},{7,5},{8,14},{9,15},{10,... | collective-permute-start | bytes 1277960 | tf_op jit(solution)/shard_map/ppermute | solution.py:625
  200.9 12.0 %collective-permute-start.15 = (s16[2,4,104,256]{3,2,1,0:T(8,128)(2,1)}, s16[2,4,104,256]{3,2,1,0:T(8,128)(2,1)S(1)}, u32[]{:S(2)}, u32[]{:S(2)}) collective-permute-start(s16[2,4,104,256]{3,2,1,0:T(8,128)(2,1)} %get-tuple-element.46.refs_5_), channel_id=1, source_target_pairs={{0,16},{8,24},{16,32},{24,40},{32,48},{40,56},{48,0},{56,8},{1,17}... | collective-permute-start | bytes 1277960 | tf_op jit(solution)/shard_map/ppermute | solution.py:625
  200.9 12.1 %collective-permute-start.16 = (s16[2,4,104,256]{3,2,1,0:T(8,128)(2,1)}, s16[2,4,104,256]{3,2,1,0:T(8,128)(2,1)S(1)}, u32[]{:S(2)}, u32[]{:S(2)}) collective-permute-start(s16[2,4,104,256]{3,2,1,0:T(8,128)(2,1)} %get-tuple-element.46.refs_5_), channel_id=1, source_target_pairs={{0,48},{8,56},{16,0},{24,8},{32,16},{40,24},{48,32},{56,40},{1,49}... | collective-permute-start | bytes 1277960 | tf_op jit(solution)/shard_map/ppermute | solution.py:625
  209.4 11.0 %copy-start.1 = (s16[2,4,104,256]{3,2,1,0:T(8,128)(2,1)}, s16[2,4,104,256]{3,2,1,0:T(8,128)(2,1)S(1)}, u32[]{:S(2)}) copy-start(s16[2,4,104,256]{3,2,1,0:T(8,128)(2,1)S(1)} %collective-permute-done.11.refs_1_) | copy-start | bytes 1277956
  209.4 7.1 %collective-permute-start.13 = (s16[1,4,104,256]{3,2,1,0:T(8,128)(2,1)S(1)}, s16[1,4,104,256]{3,2,1,0:T(8,128)(2,1)S(1)}, u32[]{:S(2)}, u32[]{:S(2)}) collective-permute-start(s16[1,4,104,256]{3,2,1,0:T(8,128)(2,1)S(1)} %slice.41), channel_id=1, source_target_pairs={{0,2},{1,3},{2,4},{3,5},{4,6},{5,7},{6,0},{7,1},{8,10},{9,11},{10,... | collective-permute-start | bytes 638984 | tf_op jit(solution)/shard_map/ppermute | solution.py:625
  209.5 10.9 %copy-start.2 = (s16[2,4,104,256]{3,2,1,0:T(8,128)(2,1)}, s16[2,4,104,256]{3,2,1,0:T(8,128)(2,1)S(1)}, u32[]{:S(2)}) copy-start(s16[2,4,104,256]{3,2,1,0:T(8,128)(2,1)S(1)} %collective-permute-done.12.refs_2_) | copy-start | bytes 1277956
  209.6 7.0 %collective-permute-start.14 = (s16[1,4,104,256]{3,2,1,0:T(8,128)(2,1)S(1)}, s16[1,4,104,256]{3,2,1,0:T(8,128)(2,1)S(1)}, u32[]{:S(2)}, u32[]{:S(2)}) collective-permute-start(s16[1,4,104,256]{3,2,1,0:T(8,128)(2,1)S(1)} %slice.42), channel_id=1, source_target_pairs={{0,6},{1,7},{2,0},{3,1},{4,2},{5,3},{6,4},{7,5},{8,14},{9,15},{10,... | collective-permute-start | bytes 638984 | tf_op jit(solution)/shard_map/ppermute | solution.py:625
  212.8 7.6 %copy-start.3 = (s16[2,4,104,256]{3,2,1,0:T(8,128)(2,1)}, s16[2,4,104,256]{3,2,1,0:T(8,128)(2,1)S(1)}, u32[]{:S(2)}) copy-start(s16[2,4,104,256]{3,2,1,0:T(8,128)(2,1)S(1)} %collective-permute-done.15.refs_6_) | copy-start | bytes 1277956
  212.8 7.4 %collective-permute-start.17 = (s16[1,4,104,256]{3,2,1,0:T(8,128)(2,1)S(1)}, s16[1,4,104,256]{3,2,1,0:T(8,128)(2,1)S(1)}, u32[]{:S(2)}, u32[]{:S(2)}) collective-permute-start(s16[1,4,104,256]{3,2,1,0:T(8,128)(2,1)S(1)} %slice.43), channel_id=1, source_target_pairs={{0,16},{8,24},{16,32},{24,40},{32,48},{40,56},{48,0},{56,8},{1,17}... | collective-permute-start | bytes 638984 | tf_op jit(solution)/shard_map/ppermute | solution.py:625
  213.0 7.4 %copy-start.4 = (s16[2,4,104,256]{3,2,1,0:T(8,128)(2,1)}, s16[2,4,104,256]{3,2,1,0:T(8,128)(2,1)S(1)}, u32[]{:S(2)}) copy-start(s16[2,4,104,256]{3,2,1,0:T(8,128)(2,1)S(1)} %collective-permute-done.16.refs_7_) | copy-start | bytes 1277956
  213.0 7.4 %collective-permute-start.18 = (s16[1,4,104,256]{3,2,1,0:T(8,128)(2,1)S(1)}, s16[1,4,104,256]{3,2,1,0:T(8,128)(2,1)S(1)}, u32[]{:S(2)}, u32[]{:S(2)}) collective-permute-start(s16[1,4,104,256]{3,2,1,0:T(8,128)(2,1)S(1)} %slice.44), channel_id=1, source_target_pairs={{0,48},{8,56},{16,0},{24,8},{32,16},{40,24},{48,32},{56,40},{1,49}... | collective-permute-start | bytes 638984 | tf_op jit(solution)/shard_map/ppermute | solution.py:625
  216.6 3.9 %copy-start.11 = (s16[1,4,104,256]{3,2,1,0:T(8,128)(2,1)}, s16[1,4,104,256]{3,2,1,0:T(8,128)(2,1)S(1)}, u32[]{:S(2)}) copy-start(s16[1,4,104,256]{3,2,1,0:T(8,128)(2,1)S(1)} %collective-permute-done.13.refs_3_) | copy-start | bytes 638980
  216.6 3.9 %copy-start.12 = (s16[1,4,104,256]{3,2,1,0:T(8,128)(2,1)}, s16[1,4,104,256]{3,2,1,0:T(8,128)(2,1)S(1)}, u32[]{:S(2)}) copy-start(s16[1,4,104,256]{3,2,1,0:T(8,128)(2,1)S(1)} %collective-permute-done.14.refs_4_) | copy-start | bytes 638980
  220.3 0.7 copy-start.14
  220.4 0.7 copy-start.17

commit v8 on v7

--- a/solution.py
+++ b/solution.py
@@ -163,13 +163,8 @@
         def copy(i):
             return pltpu.make_async_copy(received_ref.at[i, pl.ds(0, size)], landed.at[i], sems.at[i])
 
-        def fetch(i, carry):
-            @pl.when(arrived_ref[i, 0] >= 0)
-            def _():
-                copy(i).start()
-
-            return carry
-
+        for i in range(total):
+            copy(i).start()
         note_copy.wait()
         for i in range(total):
             numbers[i : i + 1, :] = notes[i, 0:1, 0 : numbers.shape[1]].astype(jnp.float32).astype(jnp.int32)
@@ -178,14 +173,13 @@
         for slot, (a, b) in enumerate(EXTENDED):
             ext_ref[slot] = front_ref[a, b].astype(jnp.float32)
         number_copy.wait()
-        lax.fori_loop(0, total, fetch, 0)
 
         def add(i, carry):
             target = arrived_ref[i, 0]
+            copy(i).wait()
 
             @pl.when(target >= 0)
             def _():
-                copy(i).wait()
                 slot = jnp.where(target >= 6, target - 4, target - 3)
                 ext_ref[slot] = ext_ref[slot] + landed[i].astype(jnp.float32)
 
@@ -379,7 +373,7 @@
 def columns_scratch(order, tiles, size):
     return [
         pltpu.VMEM((order, order), jnp.float32),
-        pltpu.VMEM((tiles * size // BLOCK, BLOCK, BLOCK), jnp.float32),
+        pltpu.VMEM((tiles * size // BLOCK + 1, BLOCK, BLOCK), jnp.float32),
         pltpu.VMEM((BLOCK, BLOCK), jnp.float32),
     ]
 
@@ -388,7 +382,7 @@
     order = LEAD_TILES * size
 
     def kernel(ids_ref, *refs):
-        *pieces, high_ref, low_ref, ih_ref, il_ref, rest_ref, own_ref, full, inverses, work = refs
+        *pieces, high_ref, low_ref, ih_ref, il_ref, rest_ref, own_ref, begun_ref, full, inverses, work = refs
         for ref, first, source in ring_pieces(pieces, lax.div(ids_ref[1], 2), len(PAIRS)):
             for number in range(ref.shape[0]):
                 i, j = PAIRS[first + number]
@@ -396,7 +390,9 @@
                 thin = tile.shape[0]
                 start = pl.multiple_of(i * size + source * thin, thin)
                 full[pl.ds(start, thin), j * size : (j + 1) * size] = tile
-        eliminate(full, inverses, work, range(FIRST_TILES * size // BLOCK))
+        steps = FIRST_TILES * size // BLOCK
+        eliminate(full, inverses, work, range(steps + 1))
+        begun_ref[...] = inverses[steps]
         columns_out(full, inverses, FIRST_TILES, high_ref, low_ref, ih_ref, il_ref, rest_ref)
         for i, j in PAIRS:
             if j < FIRST_TILES:
@@ -408,20 +404,25 @@
     return pl.pallas_call(
         kernel,
         name="factorize_first",
-        out_shape=(*columns_shapes(order, FIRST_TILES, size), jax.ShapeDtypeStruct((size, size), jnp.float32)),
+        out_shape=(
+            *columns_shapes(order, FIRST_TILES, size),
+            jax.ShapeDtypeStruct((size, size), jnp.float32),
+            jax.ShapeDtypeStruct((BLOCK, BLOCK), jnp.float32),
+        ),
         in_specs=[smem()] + [vmem()] * len(lead),
-        out_specs=(vmem(),) * 6,
+        out_specs=(vmem(),) * 7,
         scratch_shapes=columns_scratch(order, FIRST_TILES, size),
         compiler_params=pltpu.CompilerParams(vmem_limit_bytes=VMEM_BYTES),
     )(ids, *lead)
 
 
-def factorize_second(rest, size):
+def factorize_second(rest, begun, size):
     order = rest.shape[0]
 
-    def kernel(rest_ref, high_ref, low_ref, ih_ref, il_ref, out_ref, column_ref, full, inverses, work):
+    def kernel(rest_ref, begun_ref, high_ref, low_ref, ih_ref, il_ref, out_ref, column_ref, full, inverses, work):
         full[...] = rest_ref[...]
-        eliminate(full, inverses, work, range(size // BLOCK))
+        inverses[0] = begun_ref[...]
+        eliminate(full, inverses, work, range(1, size // BLOCK))
         columns_out(full, inverses, 1, high_ref, low_ref, ih_ref, il_ref, out_ref)
         column_ref[...] = full[:, 0:size]
 
@@ -429,11 +430,11 @@
         kernel,
         name="factorize_second",
         out_shape=(*columns_shapes(order, 1, size), jax.ShapeDtypeStruct((order, size), jnp.float32)),
-        in_specs=[vmem()],
+        in_specs=[vmem()] * 2,
         out_specs=(vmem(),) * 6,
         scratch_shapes=columns_scratch(order, 1, size),
         compiler_params=pltpu.CompilerParams(vmem_limit_bytes=VMEM_BYTES),
-    )(rest)
+    )(rest, begun)
 
 
 def factorize_next(rest):
@@ -521,17 +522,20 @@
     )(*panels, *first, *second, *last)
 
 
-def finish(ids, rows, cols, own, column, last_own, extended, front):
+def finish(ids, rows, cols, own, column, last_own, extended, corner, tile_rows, tile_cols):
     size = own.shape[0]
     order = LEAD_TILES * size
-    tile_rows, tile_cols = front.shape[:2]
     lanes = 128
     parts = size // lanes
     half = len(rows)
 
     def kernel(ids_ref, *refs):
-        row_pieces, col_pieces = refs[:half], refs[half : 2 * half]
-        own_ref, column_ref, last_own_ref, ext_ref, front_ref, out_ref, xh, xl = refs[2 * half :]
+        own_ref, column_ref, last_own_ref, ext_ref, corner_ref, out_ref, xh, xl = refs[2 * half : 2 * half + 8]
+        landed, sems = refs[2 * half + 8 : -1], refs[-1]
+        copies = [pltpu.make_async_copy(refs[n], landed[n], sems.at[n]) for n in range(2 * half)]
+        for copy in copies:
+            copy.start()
+        row_pieces, col_pieces = landed[:half], landed[half:]
         row, col = ids_ref[0], ids_ref[1]
 
         def put(a, b, tile):
@@ -539,8 +543,13 @@
                 start = (a * size * tile_cols + b) * parts + part
                 out_ref[pl.ds(start, size, stride=tile_cols * parts), :] = tile[:, part * lanes : (part + 1) * lanes]
 
+        zero = jnp.zeros((size, size), jnp.float32)
+        for a, b in ((0, 1), (0, 2), (1, 2)):
+            put(a, b, zero)
         for pieces, place, first in ((row_pieces, col, 0), (col_pieces, row, tile_rows * size)):
             for ref, inner, chunk in pair_pieces(pieces, place):
+                if inner == 0:
+                    copies[next(n for n in range(2 * half) if landed[n] is ref)].wait()
                 for q in range(LEAD_TILES):
                     value = decode(ref[inner, q])
                     thin = value.shape[0]
@@ -565,9 +574,6 @@
                     low = xl[a * size : (a + 1) * size, q * size : (q + 1) * size].astype(jnp.float32)
                     put(a, 0, high + low)
 
-        zero = jnp.zeros((size, size), jnp.float32)
-        for a, b in ((0, 1), (0, 2), (1, 2)):
-            put(a, b, zero)
         in_panel = col < LEAD_TILES
         lead_row = row < LEAD_TILES
         last_tile = LEAD_TILES - 1
@@ -599,7 +605,7 @@
 
             @pl.when(jnp.logical_not(in_panel))
             def _():
-                update(0, 0, front_ref[0, 0].astype(jnp.float32))
+                update(0, 0, corner_ref[...].astype(jnp.float32))
 
             update(1, 1, ext_ref[1])
             update(2, 2, ext_ref[4])
@@ -610,11 +616,15 @@
         kernel,
         name="finish",
         out_shape=jax.ShapeDtypeStruct((tile_rows * size * tile_cols * parts, lanes), jnp.float32),
-        in_specs=[smem()] + [vmem()] * (2 * half + 5),
+        in_specs=[smem()] + [hbm()] * (2 * half) + [vmem()] * 5,
         out_specs=vmem(),
-        scratch_shapes=[pltpu.VMEM((2 * tile_rows * size, order), jnp.bfloat16)] * 2,
+        scratch_shapes=[
+            *[pltpu.VMEM((2 * tile_rows * size, order), jnp.bfloat16)] * 2,
+            *[pltpu.VMEM(piece.shape, piece.dtype) for piece in (*rows, *cols)],
+            pltpu.SemaphoreType.DMA((2 * half,)),
+        ],
         compiler_params=pltpu.CompilerParams(vmem_limit_bytes=VMEM_BYTES),
-    )(ids, *rows, *cols, own, column, last_own, extended, front)
+    )(ids, *rows, *cols, own, column, last_own, extended, corner)
 
 
 def exchange(value, axis):
@@ -675,12 +685,12 @@
     received = exchange(packed, ("front", "row"))
 
     lead = ring_gather(collect(ids, leading), "col")
-    *first, rest, own = factorize_first(ids, lead, size)
+    *first, rest, own, begun = factorize_first(ids, lead, size)
     received, rest = lax.optimization_barrier((received, rest))
 
     extended, panel = assemble(received, front, n_col)
     mine = exchange(panel, "col")[:LEAD_TILES]
-    *second, rest, column = factorize_second(rest, size)
+    *second, rest, column = factorize_second(rest, begun, size)
     turned = lax.ppermute(
         mine, ("row", "col"), [(r * n_col + c, c * n_col + r) for r in range(n_row) for c in range(n_col)]
     )
@@ -691,7 +701,7 @@
     row_pair, col_pair = solve((mine, beside, turned, turned_beside), first, second, last)
     rows = ring_gather(row_pair, "col")
     cols = ring_gather(col_pair, "row")
-    factor = finish(ids, rows, cols, own, column, last_own, extended, front)
+    factor = finish(ids, rows, cols, own, column, last_own, extended, front[0, 0], tile_rows, tile_cols)
     return factor.reshape(1, tile_rows, 1, size, tile_cols, 1, size)
 
 

time: 232 us -> 234 us (level)
    pallas_call x1, Pallas kernels: 22.7 us -> 26.9 us  [factorize_first(): pl.pallas_call(kernel, name='factorize_first', out_shape=(*columns_shapes...]
    pallas_call x1, Pallas kernels: 10.7 us -> 6.57 us  [factorize_second(): pl.pallas_call(kernel, name='factorize_second', out_shape=(*columns_shape...]
where the time goes in v8:
time: 234 us; the launch traced here: 231 us
  waiting for transfers between devices  77.3 us (33%)
  Pallas kernels  74.2 us (32%)
  starting transfers between devices  59.2 us (25%)
  blocking collectives  12.5 us (5%)
  local copies, waits for them, and re-layouts  5.85 us (2%)
    ppermute x1, waiting for transfers between devices, per_device(): partner = lax.ppermute(chunk, 'row', [(i, i ^ 1) for i in owners])  50 us
    ppermute x14, starting transfers between devices, permute(): lax.ppermute(value, axis, [(i, target(i)) for i in range(lax.axis_size(ax...  36.6 us
    pallas_call x1, Pallas kernels, factorize_first(): pl.pallas_call(kernel, name='factorize_first', out_shape=(*columns_shapes...  26.9 us
    ppermute x14, waiting for transfers between devices, permute(): lax.ppermute(value, axis, [(i, target(i)) for i in range(lax.axis_size(ax...  18.2 us
    all_to_all x2, starting transfers between devices, exchange(): return lax.all_to_all(value, axis, split_axis=0, concat_axis=0, tiled=True)  14.2 us
    all_to_all x1, blocking collectives, exchange(): return lax.all_to_all(value, axis, split_axis=0, concat_axis=0, tiled=True)  12.5 us
    ppermute x3, waiting for transfers between devices, per_device(): lax.ppermute(pair, 'row', [(i, (i + 2 * step) % n_row) for i in owners])  8.98 us
    pallas_call x1, Pallas kernels, finish(): pl.pallas_call(kernel, name='finish', out_shape=jax.ShapeDtypeStruct((til...  8.66 us
  transfers between devices with their start and end apart: 21, of which 10 were waited for; matrix products, arithmetic and copies ran while one was open for 0% of the time, Pallas kernels for 23%

profile of v8, /device:TPU:6, one launch (start us, length us, event | category | flops | bytes accessed | tf_op | source)
XLA Modules:
  0.0 230.9 jit_solution(3518920337708062082)
XLA Ops:
  0.0 1.6 slice_bitcast_fusion.1
  1.6 0.7 broadcast_in_dim.3
  2.3 6.8 %all-to-all-start.1 = ((bf16[8,64,256]{2,1,0:T(8,128)(2,1)}), bf16[8,64,256]{2,1,0:T(8,128)(2,1)S(1)}, u32[]{:S(2)}, u32[]{:S(2)}) async-start(bf16[8,64,256]{2,1,0:T(8,128)(2,1)} %bitcast.10), calls=%async_computation.1 | async-start | bytes 524288 | tf_op jit(solution)/shard_map/all_to_all | solution.py:631
  9.7 5.3 %pack.1 = bf16[32,264,256]{2,1,0:T(8,128)(2,1)} custom-call(s32[32]{0:T(128)} %bitcast.24, s32[32]{0:T(128)} %bitcast.25, s32[32]{0:T(128)} %bitcast.26, s32[1]{0:T(128)} %bitcast.18.live_ref, bf16[32,256,256]{2,1,0:T(8,128)(2,1)} %bitcast.19), custom_call_target="tpu_custom_call" | custom-call | tf_op jit(solution)/shard_map/pack/pallas_call | solution.py:107
  15.0 0.2 all-to-all-done.1
  15.2 7.4 %all-to-all-start = ((bf16[32,264,256]{2,1,0:T(8,128)(2,1)}), bf16[32,264,256]{2,1,0:T(8,128)(2,1)}, u32[]{:S(2)}, u32[]{:S(2)}) async-start(bf16[32,264,256]{2,1,0:T(8,128)(2,1)} %pack.1), calls=%async_computation | async-start | bytes 8650752 | tf_op jit(solution)/shard_map/all_to_all | solution.py:631
  22.7 2.1 collective-permute-start
  24.7 50.0 %collective-permute-done = bf16[4,64,256]{2,1,0:T(8,128)(2,1)S(1)} collective-permute-done((bf16[4,64,256]{2,1,0:T(8,128)(2,1)S(1)}, bf16[4,64,256]{2,1,0:T(8,128)(2,1)S(1)}, u32[]{:S(2)}, u32[]{:S(2)}) %collective-permute-start) | collective-permute-done | bytes 131104 | tf_op jit(solution)/shard_map/ppermute | solution.py:674
  74.7 0.0 copy-start
  74.7 2.4 %collective-permute-start.1 = (bf16[2,4,64,256]{3,2,1,0:T(8,128)(2,1)S(1)}, bf16[2,4,64,256]{3,2,1,0:T(8,128)(2,1)S(1)}, u32[]{:S(2)}, u32[]{:S(2)}) collective-permute-start(bf16[2,4,64,256]{3,2,1,0:T(8,128)(2,1)S(1)} %pad_maximum_fusion.refs_0_), channel_id=1, source_target_pairs={{0,16},{8,24},{16,32},{24,40},{1,17},{9,25},{17,33},{25,41},{2,18}... | collective-permute-start | bytes 786440 | tf_op jit(solution)/shard_map/ppermute | solution.py:678
  77.2 1.3 collective-permute-start.2
  78.5 1.9 collective-permute-start.3
  80.4 0.7 pad_add_fusion.ids_ref
  81.1 2.7 %collective-permute-done.1.refs_1_ = bf16[2,4,64,256]{3,2,1,0:T(8,128)(2,1)S(1)} collective-permute-done((bf16[2,4,64,256]{3,2,1,0:T(8,128)(2,1)S(1)}, bf16[2,4,64,256]{3,2,1,0:T(8,128)(2,1)S(1)}, u32[]{:S(2)}, u32[]{:S(2)}) %collective-permute-start.1) | collective-permute-done | bytes 262176 | tf_op jit(solution)/shard_map/ppermute | solution.py:678
  83.9 4.1 %collective-permute-done.2.refs_2_ = bf16[2,4,64,256]{3,2,1,0:T(8,128)(2,1)S(1)} collective-permute-done((bf16[2,4,64,256]{3,2,1,0:T(8,128)(2,1)S(1)}, bf16[2,4,64,256]{3,2,1,0:T(8,128)(2,1)S(1)}, u32[]{:S(2)}, u32[]{:S(2)}) %collective-permute-start.2) | collective-permute-done | bytes 262176 | tf_op jit(solution)/shard_map/ppermute | solution.py:678
  88.0 2.1 collective-permute-done.3.refs_3_
  90.1 0.0 copy-done.8
  90.1 0.7 copy-done.10
  90.8 2.4 %collect.1.refs_0_ = bf16[10,64,256]{2,1,0:T(8,128)(2,1)} custom-call(s32[2]{0:T(128)} %pad_add_fusion.ids_ref, bf16[2,4,64,256]{3,2,1,0:T(8,128)(2,1)} %copy-done, bf16[2,4,64,256]{3,2,1,0:T(8,128)(2,1)} %copy-done.8, bf16[2,4,64,256]{3,2,1,0:T(8,128)(2,1)} %copy-done.9, bf16[2,4,64,256]{3,2,1,0:T(8,128)(2,1)} %copy-done.10), custom_call_target="tpu_custom_call" | custom-call | tf_op jit(solution)/shard_map/collect/pallas_call | solution.py:339
  93.3 0.8 collective-permute-start.4
  94.1 2.5 %collective-permute-start.5 = (bf16[10,64,256]{2,1,0:T(8,128)(2,1)}, bf16[10,64,256]{2,1,0:T(8,128)(2,1)S(1)}, u32[]{:S(2)}, u32[]{:S(2)}) collective-permute-start(bf16[10,64,256]{2,1,0:T(8,128)(2,1)} %collect.1.refs_0_), channel_id=1, source_target_pairs={{0,6},{1,7},{2,0},{3,1},{4,2},{5,3},{6,4},{7,5},{8,14},{9,15},{10,... | collective-permute-start | bytes 983048 | tf_op jit(solution)/shard_map/ppermute | solution.py:635
  96.6 6.8 %collective-permute-done.4.refs_1_ = bf16[10,64,256]{2,1,0:T(8,128)(2,1)S(1)} collective-permute-done((bf16[10,64,256]{2,1,0:T(8,128)(2,1)}, bf16[10,64,256]{2,1,0:T(8,128)(2,1)S(1)}, u32[]{:S(2)}, u32[]{:S(2)}) %collective-permute-start.4) | collective-permute-done | bytes 327712 | tf_op jit(solution)/shard_map/ppermute | solution.py:635
  103.3 0.1 collective-permute-start.6
  103.4 0.0 collective-permute-done.5.refs_2_
  103.5 3.3 %collective-permute-start.7 = (bf16[5,64,256]{2,1,0:T(8,128)(2,1)S(1)}, bf16[5,64,256]{2,1,0:T(8,128)(2,1)S(1)}, u32[]{:S(2)}, u32[]{:S(2)}) collective-permute-start(bf16[5,64,256]{2,1,0:T(8,128)(2,1)S(1)} %slice.40), channel_id=1, source_target_pairs={{0,6},{1,7},{2,0},{3,1},{4,2},{5,3},{6,4},{7,5},{8,14},{9,15},{10,... | collective-permute-start | bytes 491528 | tf_op jit(solution)/shard_map/ppermute | solution.py:635
  106.7 3.2 %collective-permute-done.6.refs_3_ = bf16[5,64,256]{2,1,0:T(8,128)(2,1)S(1)} collective-permute-done((bf16[5,64,256]{2,1,0:T(8,128)(2,1)S(1)}, bf16[5,64,256]{2,1,0:T(8,128)(2,1)S(1)}, u32[]{:S(2)}, u32[]{:S(2)}) %collective-permute-start.6) | collective-permute-done | bytes 163872 | tf_op jit(solution)/shard_map/ppermute | solution.py:635
  109.9 0.0 collective-permute-done.7.refs_4_
  110.0 0.6 copy-done.18
  110.6 0.7 copy-done.19
  111.3 26.9 %factorize_first.1 = (bf16[1024,512]{1,0:T(8,128)(2,1)}, bf16[1024,512]{1,0:T(8,128)(2,1)}, bf16[2,256,256]{2,1,0:T(8,128)(2,1)}, bf16[2,256,256]{2,1,0:T(8,128)...) custom-call(s32[2]{0:T(128)} %pad_add_fusion.ids_ref, bf16[10,64,256]{2,1,0:T(8,128)(2,1)} %collect.1.refs_0_, ...), custom_call_target="tpu_custom_call" | custom-call | tf_op jit(solution)/shard_map/factorize_first/pallas_call | solution.py:404
  138.1 0.0 all-to-all-done.received_ref
  138.1 6.9 %assemble.1 = (f32[5,256,256]{2,1,0:T(8,128)}, s16[8,104,256]{2,1,0:T(8,128)(2,1)}) custom-call(bf16[32,264,256]{2,1,0:T(8,128)(2,1)} %all-to-all-done.received_ref, bf16[3,3,256,256]{3,2,1,0:T(8,128)(2,1)} %bitcast.21), custom_call_target="tpu_custom_call" | custom-call | tf_op jit(solution)/shard_map/assemble/pallas_call | solution.py:195
  145.1 12.5 %all_to_all.15 = s16[8,104,256]{2,1,0:T(8,128)(2,1)S(1)} all-to-all(s16[8,104,256]{2,1,0:T(8,128)(2,1)} %get-tuple-element.31), channel_id=1, replica_groups=mesh['front'=2,'row'=8,'col'=8] {'col'}, dimensions={0} | all-to-all | bytes 851968 | tf_op jit(solution)/shard_map/all_to_all | solution.py:631
  157.6 0.7 collective-permute-start.9
  158.3 5.4 %collective-permute-start.8 = (s16[4,104,256]{2,1,0:T(8,128)(2,1)S(1)}, s16[4,104,256]{2,1,0:T(8,128)(2,1)S(1)}, u32[]{:S(2)}, u32[]{:S(2)}) collective-permute-start(s16[4,104,256]{2,1,0:T(8,128)(2,1)S(1)} %slice.41.refs_0_), channel_id=1, source_target_pairs={{0,1},{1,0},{2,3},{3,2},{4,5},{5,4},{6,7},{7,6},{8,9},{9,8},{10,11... | collective-permute-start | bytes 638984 | tf_op jit(solution)/shard_map/ppermute | solution.py:635
  163.6 0.0 collective-permute-done.9.refs_2_
  163.6 8.1 %collective-permute-start.10 = (s16[4,104,256]{2,1,0:T(8,128)(2,1)S(1)}, s16[4,104,256]{2,1,0:T(8,128)(2,1)S(1)}, u32[]{:S(2)}, u32[]{:S(2)}) collective-permute-start(s16[4,104,256]{2,1,0:T(8,128)(2,1)S(1)} %collective-permute-done.9.refs_2_), channel_id=1, source_target_pairs={{0,8},{8,0},{16,24},{24,16},{32,40},{40,32},{48,56},{56,48},{1,9},... | collective-permute-start | bytes 638984 | tf_op jit(solution)/shard_map/ppermute | solution.py:635
  171.7 6.6 %factorize_second.1 = (bf16[512,256]{1,0:T(8,128)(2,1)}, bf16[512,256]{1,0:T(8,128)(2,1)}, bf16[1,256,256]{2,1,0:T(8,128)(2,1)}, bf16[1,256,256]{2,1,0:T(8,128)(...) custom-call(f32[512,512]{1,0:T(8,128)} %get-tuple-element.36.rest_ref, f32[128,128]{1,0:T(8,128)} %get-tuple-element.37.begun_ref), custom_call_target="tpu_custom_call" | custom-call | tf_op jit(solution)/shard_map/factorize_second/pallas_call | solution.py:429
  178.3 5.6 %factorize_next.1 = (f32[256,256]{1,0:T(8,128)}, f32[1,128,128]{2,1,0:T(8,128)}) custom-call(f32[256,256]{1,0:T(8,128)} %get-tuple-element.42.rest_ref), custom_call_target="tpu_custom_call" | custom-call | tf_op jit(solution)/shard_map/factorize_next/pallas_call | solution.py:445
  183.9 5.6 %factorize_last.1 = (f32[256,256]{1,0:T(8,128)}, bf16[256,256]{1,0:T(8,128)(2,1)}, bf16[256,256]{1,0:T(8,128)(2,1)}) custom-call(f32[256,256]{1,0:T(8,128)} %get-tuple-element.43.rest_ref, f32[1,128,128]{2,1,0:T(8,128)} %get-tuple-element.44.first_ref), custom_call_target="tpu_custom_call" | custom-call | tf_op jit(solution)/shard_map/factorize_last/pallas_call | solution.py:469
  189.5 0.0 collective-permute-done.8.refs_1_
  189.5 0.0 collective-permute-done.10.refs_3_
  189.5 0.6 copy-done.15
  190.2 0.1 copy-done.17
  190.3 6.3 %solve.1 = (s16[2,4,104,256]{3,2,1,0:T(8,128)(2,1)}, s16[2,4,104,256]{3,2,1,0:T(8,128)(2,1)}) custom-call(s16[4,104,256]{2,1,0:T(8,128)(2,1)} %copy-done.5, s16[4,104,256]{2,1,0:T(8,128)(2,1)} %copy-done.15, s16[4,104,256]{2,1,0:T(8,128)(2,1)} %copy-done.13, s16[4,104,256]{2,1,0:T(8,128)(2,1)} %copy-done.17, bf16[1024,512]{1,0:T(8,128)(2,1)} %get-tuple-element.32.refs_4_, ...), custom_call_target="tpu_custom_call" | custom-call | tf_op jit(solution)/shard_map/solve/pallas_call | solution.py:514
  196.6 1.6 collective-permute-start.11
  198.2 3.7 %collective-permute-start.12 = (s16[2,4,104,256]{3,2,1,0:T(8,128)(2,1)}, s16[2,4,104,256]{3,2,1,0:T(8,128)(2,1)S(1)}, u32[]{:S(2)}, u32[]{:S(2)}) collective-permute-start(s16[2,4,104,256]{3,2,1,0:T(8,128)(2,1)} %get-tuple-element.47.refs_0_), channel_id=1, source_target_pairs={{0,6},{1,7},{2,0},{3,1},{4,2},{5,3},{6,4},{7,5},{8,14},{9,15},{10,... | collective-permute-start | bytes 1277960 | tf_op jit(solution)/shard_map/ppermute | solution.py:635
  201.9 0.0 collective-permute-start.15
  201.9 4.2 %collective-permute-start.16 = (s16[2,4,104,256]{3,2,1,0:T(8,128)(2,1)}, s16[2,4,104,256]{3,2,1,0:T(8,128)(2,1)S(1)}, u32[]{:S(2)}, u32[]{:S(2)}) collective-permute-start(s16[2,4,104,256]{3,2,1,0:T(8,128)(2,1)} %get-tuple-element.48.refs_5_), channel_id=1, source_target_pairs={{0,48},{8,56},{16,0},{24,8},{32,16},{40,24},{48,32},{56,40},{1,49}... | collective-permute-start | bytes 1277960 | tf_op jit(solution)/shard_map/ppermute | solution.py:635
  206.0 4.4 %collective-permute-done.11.refs_1_ = s16[2,4,104,256]{3,2,1,0:T(8,128)(2,1)S(1)} collective-permute-done((s16[2,4,104,256]{3,2,1,0:T(8,128)(2,1)}, s16[2,4,104,256]{3,2,1,0:T(8,128)(2,1)S(1)}, u32[]{:S(2)}, u32[]{:S(2)}) %collective-permute-start.11) | collective-permute-done | bytes 426016 | tf_op jit(solution)/shard_map/ppermute | solution.py:635
  210.4 0.1 collective-permute-start.13
  210.5 0.0 collective-permute-done.12.refs_2_
  210.5 3.3 %collective-permute-start.14 = (s16[1,4,104,256]{3,2,1,0:T(8,128)(2,1)S(1)}, s16[1,4,104,256]{3,2,1,0:T(8,128)(2,1)S(1)}, u32[]{:S(2)}, u32[]{:S(2)}) collective-permute-start(s16[1,4,104,256]{3,2,1,0:T(8,128)(2,1)S(1)} %slice.43), channel_id=1, source_target_pairs={{0,6},{1,7},{2,0},{3,1},{4,2},{5,3},{6,4},{7,5},{8,14},{9,15},{10,... | collective-permute-start | bytes 638984 | tf_op jit(solution)/shard_map/ppermute | solution.py:635
  213.8 0.0 collective-permute-done.15.refs_6_
  213.8 0.1 collective-permute-start.17
  213.9 0.0 collective-permute-done.16.refs_7_
  214.0 3.6 %collective-permute-start.18 = (s16[1,4,104,256]{3,2,1,0:T(8,128)(2,1)S(1)}, s16[1,4,104,256]{3,2,1,0:T(8,128)(2,1)S(1)}, u32[]{:S(2)}, u32[]{:S(2)}) collective-permute-start(s16[1,4,104,256]{3,2,1,0:T(8,128)(2,1)S(1)} %slice.45), channel_id=1, source_target_pairs={{0,48},{8,56},{16,0},{24,8},{32,16},{40,24},{48,32},{56,40},{1,49}... | collective-permute-start | bytes 638984 | tf_op jit(solution)/shard_map/ppermute | solution.py:635
  217.5 0.0 collective-permute-done.13.refs_3_
  217.6 0.0 collective-permute-done.14.refs_4_
  217.6 3.7 %collective-permute-done.17.refs_8_ = s16[1,4,104,256]{3,2,1,0:T(8,128)(2,1)S(1)} collective-permute-done((s16[1,4,104,256]{3,2,1,0:T(8,128)(2,1)S(1)}, s16[1,4,104,256]{3,2,1,0:T(8,128)(2,1)S(1)}, u32[]{:S(2)}, u32[]{:S(2)}) %collective-permute-start.17) | collective-permute-done | bytes 213024 | tf_op jit(solution)/shard_map/ppermute | solution.py:635
  221.2 0.1 collective-permute-done.18.refs_9_
  221.4 0.5 copy-done.14
  221.9 0.1 copy-done.16
  222.1 8.7 %finish.1 = f32[4608,128]{1,0:T(8,128)} custom-call(s32[2]{0:T(128)} %pad_add_fusion.ids_ref, s16[2,4,104,256]{3,2,1,0:T(8,128)(2,1)} %get-tuple-element.47.refs_0_, s16[2,4,104,256]{3,2,1,0:T(8,128)(2,1)} %copy-done.1, s16[2,4,104,256]{3,2,1,0:T(8,128)(2,1)} %copy-done.2, s16[1,4,104,256]{3,2,1,0:T(8,128)(2,1)} %copy-done.11, ...), custom_call_target="tpu_custom_call" | custom-call | tf_op jit(solution)/shard_map/finish/pallas_call | solution.py:615
  (40 shorter events, 0.2 us)
Async XLA Ops:
  2.3 12.9 %all-to-all-start.1 = ((bf16[8,64,256]{2,1,0:T(8,128)(2,1)}), bf16[8,64,256]{2,1,0:T(8,128)(2,1)S(1)}, u32[]{:S(2)}, u32[]{:S(2)}) async-start(bf16[8,64,256]{2,1,0:T(8,128)(2,1)} %bitcast.10), calls=%async_computation.1 | async-start | bytes 524288 | tf_op jit(solution)/shard_map/all_to_all | solution.py:631
  15.2 123.0 %all-to-all-start = ((bf16[32,264,256]{2,1,0:T(8,128)(2,1)}), bf16[32,264,256]{2,1,0:T(8,128)(2,1)}, u32[]{:S(2)}, u32[]{:S(2)}) async-start(bf16[32,264,256]{2,1,0:T(8,128)(2,1)} %pack.1), calls=%async_computation | async-start | bytes 8650752 | tf_op jit(solution)/shard_map/all_to_all | solution.py:631
  22.7 52.0 %collective-permute-start = (bf16[4,64,256]{2,1,0:T(8,128)(2,1)S(1)}, bf16[4,64,256]{2,1,0:T(8,128)(2,1)S(1)}, u32[]{:S(2)}, u32[]{:S(2)}) collective-permute-start(bf16[4,64,256]{2,1,0:T(8,128)(2,1)S(1)} %get-tuple-element.56), channel_id=1, source_target_pairs={{0,8},{8,0},{16,24},{24,16},{1,9},{9,1},{17,25},{25,17},{2,10},{10... | collective-permute-start | bytes 393224 | tf_op jit(solution)/shard_map/ppermute | solution.py:674
  74.7 15.4 %copy-start = (bf16[2,4,64,256]{3,2,1,0:T(8,128)(2,1)}, bf16[2,4,64,256]{3,2,1,0:T(8,128)(2,1)S(1)}, u32[]{:S(2)}) copy-start(bf16[2,4,64,256]{3,2,1,0:T(8,128)(2,1)S(1)} %pad_maximum_fusion.refs_0_) | copy-start | bytes 786436
  74.7 9.1 %collective-permute-start.1 = (bf16[2,4,64,256]{3,2,1,0:T(8,128)(2,1)S(1)}, bf16[2,4,64,256]{3,2,1,0:T(8,128)(2,1)S(1)}, u32[]{:S(2)}, u32[]{:S(2)}) collective-permute-start(bf16[2,4,64,256]{3,2,1,0:T(8,128)(2,1)S(1)} %pad_maximum_fusion.refs_0_), channel_id=1, source_target_pairs={{0,16},{8,24},{16,32},{24,40},{1,17},{9,25},{17,33},{25,41},{2,18}... | collective-permute-start | bytes 786440 | tf_op jit(solution)/shard_map/ppermute | solution.py:678
  77.2 10.8 %collective-permute-start.2 = (bf16[2,4,64,256]{3,2,1,0:T(8,128)(2,1)S(1)}, bf16[2,4,64,256]{3,2,1,0:T(8,128)(2,1)S(1)}, u32[]{:S(2)}, u32[]{:S(2)}) collective-permute-start(bf16[2,4,64,256]{3,2,1,0:T(8,128)(2,1)S(1)} %pad_maximum_fusion.refs_0_), channel_id=1, source_target_pairs={{0,32},{8,40},{16,48},{24,56},{1,33},{9,41},{17,49},{25,57},{2,34}... | collective-permute-start | bytes 786440 | tf_op jit(solution)/shard_map/ppermute | solution.py:678
  78.5 11.6 %collective-permute-start.3 = (bf16[2,4,64,256]{3,2,1,0:T(8,128)(2,1)S(1)}, bf16[2,4,64,256]{3,2,1,0:T(8,128)(2,1)S(1)}, u32[]{:S(2)}, u32[]{:S(2)}) collective-permute-start(bf16[2,4,64,256]{3,2,1,0:T(8,128)(2,1)S(1)} %pad_maximum_fusion.refs_0_), channel_id=1, source_target_pairs={{0,48},{8,56},{16,0},{24,8},{1,49},{9,57},{17,1},{25,9},{2,50},{10... | collective-permute-start | bytes 786440 | tf_op jit(solution)/shard_map/ppermute | solution.py:678
  83.9 6.2 %copy-start.8 = (bf16[2,4,64,256]{3,2,1,0:T(8,128)(2,1)}, bf16[2,4,64,256]{3,2,1,0:T(8,128)(2,1)S(1)}, u32[]{:S(2)}) copy-start(bf16[2,4,64,256]{3,2,1,0:T(8,128)(2,1)S(1)} %collective-permute-done.1.refs_1_) | copy-start | bytes 786436
  88.0 2.1 copy-start.9
  90.1 0.7 copy-start.10
  93.3 10.1 %collective-permute-start.4 = (bf16[10,64,256]{2,1,0:T(8,128)(2,1)}, bf16[10,64,256]{2,1,0:T(8,128)(2,1)S(1)}, u32[]{:S(2)}, u32[]{:S(2)}) collective-permute-start(bf16[10,64,256]{2,1,0:T(8,128)(2,1)} %collect.1.refs_0_), channel_id=1, source_target_pairs={{0,2},{1,3},{2,4},{3,5},{4,6},{5,7},{6,0},{7,1},{8,10},{9,11},{10,... | collective-permute-start | bytes 983048 | tf_op jit(solution)/shard_map/ppermute | solution.py:635
  94.1 9.4 %collective-permute-start.5 = (bf16[10,64,256]{2,1,0:T(8,128)(2,1)}, bf16[10,64,256]{2,1,0:T(8,128)(2,1)S(1)}, u32[]{:S(2)}, u32[]{:S(2)}) collective-permute-start(bf16[10,64,256]{2,1,0:T(8,128)(2,1)} %collect.1.refs_0_), channel_id=1, source_target_pairs={{0,6},{1,7},{2,0},{3,1},{4,2},{5,3},{6,4},{7,5},{8,14},{9,15},{10,... | collective-permute-start | bytes 983048 | tf_op jit(solution)/shard_map/ppermute | solution.py:635
  103.3 6.6 %copy-start.6 = (bf16[10,64,256]{2,1,0:T(8,128)(2,1)}, bf16[10,64,256]{2,1,0:T(8,128)(2,1)S(1)}, u32[]{:S(2)}) copy-start(bf16[10,64,256]{2,1,0:T(8,128)(2,1)S(1)} %collective-permute-done.4.refs_1_) | copy-start | bytes 983044
  103.3 6.6 %collective-permute-start.6 = (bf16[5,64,256]{2,1,0:T(8,128)(2,1)S(1)}, bf16[5,64,256]{2,1,0:T(8,128)(2,1)S(1)}, u32[]{:S(2)}, u32[]{:S(2)}) collective-permute-start(bf16[5,64,256]{2,1,0:T(8,128)(2,1)S(1)} %slice.39), channel_id=1, source_target_pairs={{0,2},{1,3},{2,4},{3,5},{4,6},{5,7},{6,0},{7,1},{8,10},{9,11},{10,... | collective-permute-start | bytes 491528 | tf_op jit(solution)/shard_map/ppermute | solution.py:635
  103.4 6.5 %copy-start.7 = (bf16[10,64,256]{2,1,0:T(8,128)(2,1)}, bf16[10,64,256]{2,1,0:T(8,128)(2,1)S(1)}, u32[]{:S(2)}) copy-start(bf16[10,64,256]{2,1,0:T(8,128)(2,1)S(1)} %collective-permute-done.5.refs_2_) | copy-start | bytes 983044
  103.5 6.5 %collective-permute-start.7 = (bf16[5,64,256]{2,1,0:T(8,128)(2,1)S(1)}, bf16[5,64,256]{2,1,0:T(8,128)(2,1)S(1)}, u32[]{:S(2)}, u32[]{:S(2)}) collective-permute-start(bf16[5,64,256]{2,1,0:T(8,128)(2,1)S(1)} %slice.40), channel_id=1, source_target_pairs={{0,6},{1,7},{2,0},{3,1},{4,2},{5,3},{6,4},{7,5},{8,14},{9,15},{10,... | collective-permute-start | bytes 491528 | tf_op jit(solution)/shard_map/ppermute | solution.py:635
  109.9 0.7 copy-start.18
  110.6 0.7 copy-start.19
  157.6 31.9 %copy-start.5 = (s16[4,104,256]{2,1,0:T(8,128)(2,1)}, s16[4,104,256]{2,1,0:T(8,128)(2,1)S(1)}, u32[]{:S(2)}) copy-start(s16[4,104,256]{2,1,0:T(8,128)(2,1)S(1)} %slice.41.refs_0_) | copy-start | bytes 638980
  157.6 6.1 %collective-permute-start.9 = (s16[4,104,256]{2,1,0:T(8,128)(2,1)S(1)}, s16[4,104,256]{2,1,0:T(8,128)(2,1)S(1)}, u32[]{:S(2)}, u32[]{:S(2)}) collective-permute-start(s16[4,104,256]{2,1,0:T(8,128)(2,1)S(1)} %slice.41.refs_0_), channel_id=1, source_target_pairs={{0,0},{1,8},{2,16},{3,24},{4,32},{5,40},{6,48},{7,56},{8,1},{9,9},... | collective-permute-start | bytes 638984 | tf_op jit(solution)/shard_map/ppermute | solution.py:694
  158.3 31.2 %collective-permute-start.8 = (s16[4,104,256]{2,1,0:T(8,128)(2,1)S(1)}, s16[4,104,256]{2,1,0:T(8,128)(2,1)S(1)}, u32[]{:S(2)}, u32[]{:S(2)}) collective-permute-start(s16[4,104,256]{2,1,0:T(8,128)(2,1)S(1)} %slice.41.refs_0_), channel_id=1, source_target_pairs={{0,1},{1,0},{2,3},{3,2},{4,5},{5,4},{6,7},{7,6},{8,9},{9,8},{10,11... | collective-permute-start | bytes 638984 | tf_op jit(solution)/shard_map/ppermute | solution.py:635
  163.6 25.9 %copy-start.13 = (s16[4,104,256]{2,1,0:T(8,128)(2,1)}, s16[4,104,256]{2,1,0:T(8,128)(2,1)S(1)}, u32[]{:S(2)}) copy-start(s16[4,104,256]{2,1,0:T(8,128)(2,1)S(1)} %collective-permute-done.9.refs_2_) | copy-start | bytes 638980
  163.6 25.8 %collective-permute-start.10 = (s16[4,104,256]{2,1,0:T(8,128)(2,1)S(1)}, s16[4,104,256]{2,1,0:T(8,128)(2,1)S(1)}, u32[]{:S(2)}, u32[]{:S(2)}) collective-permute-start(s16[4,104,256]{2,1,0:T(8,128)(2,1)S(1)} %collective-permute-done.9.refs_2_), channel_id=1, source_target_pairs={{0,8},{8,0},{16,24},{24,16},{32,40},{40,32},{48,56},{56,48},{1,9},... | collective-permute-start | bytes 638984 | tf_op jit(solution)/shard_map/ppermute | solution.py:635
  189.5 0.7 copy-start.15
  189.5 0.8 copy-start.17
  196.6 13.8 %collective-permute-start.11 = (s16[2,4,104,256]{3,2,1,0:T(8,128)(2,1)}, s16[2,4,104,256]{3,2,1,0:T(8,128)(2,1)S(1)}, u32[]{:S(2)}, u32[]{:S(2)}) collective-permute-start(s16[2,4,104,256]{3,2,1,0:T(8,128)(2,1)} %get-tuple-element.47.refs_0_), channel_id=1, source_target_pairs={{0,2},{1,3},{2,4},{3,5},{4,6},{5,7},{6,0},{7,1},{8,10},{9,11},{10,... | collective-permute-start | bytes 1277960 | tf_op jit(solution)/shard_map/ppermute | solution.py:635
  198.2 12.3 %collective-permute-start.12 = (s16[2,4,104,256]{3,2,1,0:T(8,128)(2,1)}, s16[2,4,104,256]{3,2,1,0:T(8,128)(2,1)S(1)}, u32[]{:S(2)}, u32[]{:S(2)}) collective-permute-start(s16[2,4,104,256]{3,2,1,0:T(8,128)(2,1)} %get-tuple-element.47.refs_0_), channel_id=1, source_target_pairs={{0,6},{1,7},{2,0},{3,1},{4,2},{5,3},{6,4},{7,5},{8,14},{9,15},{10,... | collective-permute-start | bytes 1277960 | tf_op jit(solution)/shard_map/ppermute | solution.py:635
  201.9 12.0 %collective-permute-start.15 = (s16[2,4,104,256]{3,2,1,0:T(8,128)(2,1)}, s16[2,4,104,256]{3,2,1,0:T(8,128)(2,1)S(1)}, u32[]{:S(2)}, u32[]{:S(2)}) collective-permute-start(s16[2,4,104,256]{3,2,1,0:T(8,128)(2,1)} %get-tuple-element.48.refs_5_), channel_id=1, source_target_pairs={{0,16},{8,24},{16,32},{24,40},{32,48},{40,56},{48,0},{56,8},{1,17}... | collective-permute-start | bytes 1277960 | tf_op jit(solution)/shard_map/ppermute | solution.py:635
  201.9 12.1 %collective-permute-start.16 = (s16[2,4,104,256]{3,2,1,0:T(8,128)(2,1)}, s16[2,4,104,256]{3,2,1,0:T(8,128)(2,1)S(1)}, u32[]{:S(2)}, u32[]{:S(2)}) collective-permute-start(s16[2,4,104,256]{3,2,1,0:T(8,128)(2,1)} %get-tuple-element.48.refs_5_), channel_id=1, source_target_pairs={{0,48},{8,56},{16,0},{24,8},{32,16},{40,24},{48,32},{56,40},{1,49}... | collective-permute-start | bytes 1277960 | tf_op jit(solution)/shard_map/ppermute | solution.py:635
  210.4 11.0 %copy-start.1 = (s16[2,4,104,256]{3,2,1,0:T(8,128)(2,1)}, s16[2,4,104,256]{3,2,1,0:T(8,128)(2,1)S(1)}, u32[]{:S(2)}) copy-start(s16[2,4,104,256]{3,2,1,0:T(8,128)(2,1)S(1)} %collective-permute-done.11.refs_1_) | copy-start | bytes 1277956
  210.4 7.1 %collective-permute-start.13 = (s16[1,4,104,256]{3,2,1,0:T(8,128)(2,1)S(1)}, s16[1,4,104,256]{3,2,1,0:T(8,128)(2,1)S(1)}, u32[]{:S(2)}, u32[]{:S(2)}) collective-permute-start(s16[1,4,104,256]{3,2,1,0:T(8,128)(2,1)S(1)} %slice.42), channel_id=1, source_target_pairs={{0,2},{1,3},{2,4},{3,5},{4,6},{5,7},{6,0},{7,1},{8,10},{9,11},{10,... | collective-permute-start | bytes 638984 | tf_op jit(solution)/shard_map/ppermute | solution.py:635
  210.5 10.9 %copy-start.2 = (s16[2,4,104,256]{3,2,1,0:T(8,128)(2,1)}, s16[2,4,104,256]{3,2,1,0:T(8,128)(2,1)S(1)}, u32[]{:S(2)}) copy-start(s16[2,4,104,256]{3,2,1,0:T(8,128)(2,1)S(1)} %collective-permute-done.12.refs_2_) | copy-start | bytes 1277956
  210.5 7.0 %collective-permute-start.14 = (s16[1,4,104,256]{3,2,1,0:T(8,128)(2,1)S(1)}, s16[1,4,104,256]{3,2,1,0:T(8,128)(2,1)S(1)}, u32[]{:S(2)}, u32[]{:S(2)}) collective-permute-start(s16[1,4,104,256]{3,2,1,0:T(8,128)(2,1)S(1)} %slice.43), channel_id=1, source_target_pairs={{0,6},{1,7},{2,0},{3,1},{4,2},{5,3},{6,4},{7,5},{8,14},{9,15},{10,... | collective-permute-start | bytes 638984 | tf_op jit(solution)/shard_map/ppermute | solution.py:635
  213.8 7.6 %copy-start.3 = (s16[2,4,104,256]{3,2,1,0:T(8,128)(2,1)}, s16[2,4,104,256]{3,2,1,0:T(8,128)(2,1)S(1)}, u32[]{:S(2)}) copy-start(s16[2,4,104,256]{3,2,1,0:T(8,128)(2,1)S(1)} %collective-permute-done.15.refs_6_) | copy-start | bytes 1277956
  213.8 7.4 %collective-permute-start.17 = (s16[1,4,104,256]{3,2,1,0:T(8,128)(2,1)S(1)}, s16[1,4,104,256]{3,2,1,0:T(8,128)(2,1)S(1)}, u32[]{:S(2)}, u32[]{:S(2)}) collective-permute-start(s16[1,4,104,256]{3,2,1,0:T(8,128)(2,1)S(1)} %slice.44), channel_id=1, source_target_pairs={{0,16},{8,24},{16,32},{24,40},{32,48},{40,56},{48,0},{56,8},{1,17}... | collective-permute-start | bytes 638984 | tf_op jit(solution)/shard_map/ppermute | solution.py:635
  213.9 7.5 %copy-start.4 = (s16[2,4,104,256]{3,2,1,0:T(8,128)(2,1)}, s16[2,4,104,256]{3,2,1,0:T(8,128)(2,1)S(1)}, u32[]{:S(2)}) copy-start(s16[2,4,104,256]{3,2,1,0:T(8,128)(2,1)S(1)} %collective-permute-done.16.refs_7_) | copy-start | bytes 1277956
  214.0 7.4 %collective-permute-start.18 = (s16[1,4,104,256]{3,2,1,0:T(8,128)(2,1)S(1)}, s16[1,4,104,256]{3,2,1,0:T(8,128)(2,1)S(1)}, u32[]{:S(2)}, u32[]{:S(2)}) collective-permute-start(s16[1,4,104,256]{3,2,1,0:T(8,128)(2,1)S(1)} %slice.45), channel_id=1, source_target_pairs={{0,48},{8,56},{16,0},{24,8},{32,16},{40,24},{48,32},{56,40},{1,49}... | collective-permute-start | bytes 638984 | tf_op jit(solution)/shard_map/ppermute | solution.py:635
  217.5 3.9 %copy-start.11 = (s16[1,4,104,256]{3,2,1,0:T(8,128)(2,1)}, s16[1,4,104,256]{3,2,1,0:T(8,128)(2,1)S(1)}, u32[]{:S(2)}) copy-start(s16[1,4,104,256]{3,2,1,0:T(8,128)(2,1)S(1)} %collective-permute-done.13.refs_3_) | copy-start | bytes 638980
  217.6 3.9 %copy-start.12 = (s16[1,4,104,256]{3,2,1,0:T(8,128)(2,1)}, s16[1,4,104,256]{3,2,1,0:T(8,128)(2,1)S(1)}, u32[]{:S(2)}) copy-start(s16[1,4,104,256]{3,2,1,0:T(8,128)(2,1)S(1)} %collective-permute-done.14.refs_4_) | copy-start | bytes 638980
  221.2 0.7 copy-start.14
  221.4 0.7 copy-start.16

commit v9 on v8

--- a/solution.py
+++ b/solution.py
@@ -11,6 +11,7 @@
 HALF = 64
 RUN = 32
 STRIP = 8
+LANES = 128
 VMEM_BYTES = 56 * 1024 * 1024
 
 
@@ -127,24 +128,27 @@
 SCALE_STEPS = 64
 
 
+def picked(n):
+    shape = (n, LANES)
+    return lax.broadcasted_iota(jnp.int32, shape, 0) == lax.broadcasted_iota(jnp.int32, shape, 1)
+
+
 def encode(values):
     n, m = values.shape
     top = jnp.max(jnp.abs(values), axis=1, keepdims=True)
     code = jnp.floor(jnp.log2(jnp.maximum(top, 2.0**-110)) * SCALE_STEPS) + 1.0
     coded = jnp.round(values * jnp.exp2(15.0 - 1e-3 - code / SCALE_STEPS))
-    picked = lax.broadcasted_iota(jnp.int32, (n, m), 0) == lax.broadcasted_iota(jnp.int32, (n, m), 1)
-    line = jnp.sum(jnp.where(picked, code, 0.0), axis=0, keepdims=True)
-    lines = jnp.broadcast_to(line, (SCALE_ROWS, m))
+    line = jnp.sum(jnp.where(picked(n), code, 0.0), axis=0, keepdims=True)
+    lines = jnp.broadcast_to(jnp.concatenate([line] * (m // LANES), axis=1), (SCALE_ROWS, m))
     return jnp.concatenate([coded, lines], axis=0).astype(jnp.int32).astype(jnp.int16)
 
 
 def decode(coded):
     wide = coded.astype(jnp.int32).astype(jnp.float32)
-    n, m = wide.shape[0] - SCALE_ROWS, wide.shape[1]
-    values, line = wide[:n], wide[n : n + 1]
-    picked = lax.broadcasted_iota(jnp.int32, (n, m), 0) == lax.broadcasted_iota(jnp.int32, (n, m), 1)
-    code = jnp.sum(jnp.where(picked, jnp.broadcast_to(line, (n, m)), 0.0), axis=1, keepdims=True)
-    return values * jnp.exp2(code / SCALE_STEPS - 15.0 + 1e-3)
+    n = wide.shape[0] - SCALE_ROWS
+    scales = jnp.exp2(wide[n : n + 1, 0:LANES] / SCALE_STEPS - 15.0 + 1e-3)
+    scale = jnp.sum(jnp.where(picked(n), jnp.broadcast_to(scales, (n, LANES)), 0.0), axis=1, keepdims=True)
+    return wide[:n] * scale
 
 
 EXTENDED = ((1, 0), (1, 1), (2, 0), (2, 1), (2, 2))
@@ -163,8 +167,13 @@
         def copy(i):
             return pltpu.make_async_copy(received_ref.at[i, pl.ds(0, size)], landed.at[i], sems.at[i])
 
-        for i in range(total):
-            copy(i).start()
+        def fetch(i, carry):
+            @pl.when(arrived_ref[i, 0] >= 0)
+            def _():
+                copy(i).start()
+
+            return carry
+
         note_copy.wait()
         for i in range(total):
             numbers[i : i + 1, :] = notes[i, 0:1, 0 : numbers.shape[1]].astype(jnp.float32).astype(jnp.int32)
@@ -173,13 +182,14 @@
         for slot, (a, b) in enumerate(EXTENDED):
             ext_ref[slot] = front_ref[a, b].astype(jnp.float32)
         number_copy.wait()
+        lax.fori_loop(0, total, fetch, 0)
 
         def add(i, carry):
             target = arrived_ref[i, 0]
-            copy(i).wait()
 
             @pl.when(target >= 0)
             def _():
+                copy(i).wait()
                 slot = jnp.where(target >= 6, target - 4, target - 3)
                 ext_ref[slot] = ext_ref[slot] + landed[i].astype(jnp.float32)
 
@@ -530,12 +540,8 @@
     half = len(rows)
 
     def kernel(ids_ref, *refs):
-        own_ref, column_ref, last_own_ref, ext_ref, corner_ref, out_ref, xh, xl = refs[2 * half : 2 * half + 8]
-        landed, sems = refs[2 * half + 8 : -1], refs[-1]
-        copies = [pltpu.make_async_copy(refs[n], landed[n], sems.at[n]) for n in range(2 * half)]
-        for copy in copies:
-            copy.start()
-        row_pieces, col_pieces = landed[:half], landed[half:]
+        row_pieces, col_pieces = refs[:half], refs[half : 2 * half]
+        own_ref, column_ref, last_own_ref, ext_ref, corner_ref, out_ref, xh, xl = refs[2 * half :]
         row, col = ids_ref[0], ids_ref[1]
 
         def put(a, b, tile):
@@ -543,13 +549,8 @@
                 start = (a * size * tile_cols + b) * parts + part
                 out_ref[pl.ds(start, size, stride=tile_cols * parts), :] = tile[:, part * lanes : (part + 1) * lanes]
 
-        zero = jnp.zeros((size, size), jnp.float32)
-        for a, b in ((0, 1), (0, 2), (1, 2)):
-            put(a, b, zero)
         for pieces, place, first in ((row_pieces, col, 0), (col_pieces, row, tile_rows * size)):
             for ref, inner, chunk in pair_pieces(pieces, place):
-                if inner == 0:
-                    copies[next(n for n in range(2 * half) if landed[n] is ref)].wait()
                 for q in range(LEAD_TILES):
                     value = decode(ref[inner, q])
                     thin = value.shape[0]
@@ -574,6 +575,9 @@
                     low = xl[a * size : (a + 1) * size, q * size : (q + 1) * size].astype(jnp.float32)
                     put(a, 0, high + low)
 
+        zero = jnp.zeros((size, size), jnp.float32)
+        for a, b in ((0, 1), (0, 2), (1, 2)):
+            put(a, b, zero)
         in_panel = col < LEAD_TILES
         lead_row = row < LEAD_TILES
         last_tile = LEAD_TILES - 1
@@ -616,13 +620,9 @@
         kernel,
         name="finish",
         out_shape=jax.ShapeDtypeStruct((tile_rows * size * tile_cols * parts, lanes), jnp.float32),
-        in_specs=[smem()] + [hbm()] * (2 * half) + [vmem()] * 5,
+        in_specs=[smem()] + [vmem()] * (2 * half + 5),
         out_specs=vmem(),
-        scratch_shapes=[
-            *[pltpu.VMEM((2 * tile_rows * size, order), jnp.bfloat16)] * 2,
-            *[pltpu.VMEM(piece.shape, piece.dtype) for piece in (*rows, *cols)],
-            pltpu.SemaphoreType.DMA((2 * half,)),
-        ],
+        scratch_shapes=[pltpu.VMEM((2 * tile_rows * size, order), jnp.bfloat16)] * 2,
         compiler_params=pltpu.CompilerParams(vmem_limit_bytes=VMEM_BYTES),
     )(ids, *rows, *cols, own, column, last_own, extended, corner)
 

time: 234 us -> 232 us (level)
  no operation moved by 1% of the time
where the time goes in v9:
time: 232 us; the launch traced here: 229 us
  waiting for transfers between devices  77.2 us (33%)
  Pallas kernels  72.8 us (31%)
  starting transfers between devices  59.3 us (26%)
  blocking collectives  12.5 us (5%)
  local copies, waits for them, and re-layouts  5.84 us (3%)
    ppermute x1, waiting for transfers between devices, per_device(): partner = lax.ppermute(chunk, 'row', [(i, i ^ 1) for i in owners])  50 us
    ppermute x14, starting transfers between devices, permute(): lax.ppermute(value, axis, [(i, target(i)) for i in range(lax.axis_size(ax...  36.7 us
    pallas_call x1, Pallas kernels, factorize_first(): pl.pallas_call(kernel, name='factorize_first', out_shape=(*columns_shapes...  26.9 us
    ppermute x14, waiting for transfers between devices, permute(): lax.ppermute(value, axis, [(i, target(i)) for i in range(lax.axis_size(ax...  18 us
    all_to_all x2, starting transfers between devices, exchange(): return lax.all_to_all(value, axis, split_axis=0, concat_axis=0, tiled=True)  14.2 us
    all_to_all x1, blocking collectives, exchange(): return lax.all_to_all(value, axis, split_axis=0, concat_axis=0, tiled=True)  12.5 us
    ppermute x3, waiting for transfers between devices, per_device(): lax.ppermute(pair, 'row', [(i, (i + 2 * step) % n_row) for i in owners])  8.98 us
    pallas_call x1, Pallas kernels, finish(): pl.pallas_call(kernel, name='finish', out_shape=jax.ShapeDtypeStruct((til...  7.45 us
  transfers between devices with their start and end apart: 21, of which 10 were waited for; matrix products, arithmetic and copies ran while one was open for 0% of the time, Pallas kernels for 23%

profile of v9, /device:TPU:6, one launch (start us, length us, event | category | flops | bytes accessed | tf_op | source)
XLA Modules:
  0.0 229.3 jit_solution(16715944762940262494)
XLA Ops:
  0.0 1.6 slice_bitcast_fusion.1
  1.6 0.7 broadcast_in_dim.3
  2.3 6.8 %all-to-all-start.1 = ((bf16[8,64,256]{2,1,0:T(8,128)(2,1)}), bf16[8,64,256]{2,1,0:T(8,128)(2,1)S(1)}, u32[]{:S(2)}, u32[]{:S(2)}) async-start(bf16[8,64,256]{2,1,0:T(8,128)(2,1)} %bitcast.10), calls=%async_computation.1 | async-start | bytes 524288 | tf_op jit(solution)/shard_map/all_to_all | solution.py:631
  9.7 5.3 %pack.1 = bf16[32,264,256]{2,1,0:T(8,128)(2,1)} custom-call(s32[32]{0:T(128)} %bitcast.24, s32[32]{0:T(128)} %bitcast.25, s32[32]{0:T(128)} %bitcast.26, s32[1]{0:T(128)} %bitcast.18.live_ref, bf16[32,256,256]{2,1,0:T(8,128)(2,1)} %bitcast.19), custom_call_target="tpu_custom_call" | custom-call | tf_op jit(solution)/shard_map/pack/pallas_call | solution.py:108
  15.0 0.2 all-to-all-done.1
  15.2 7.4 %all-to-all-start = ((bf16[32,264,256]{2,1,0:T(8,128)(2,1)}), bf16[32,264,256]{2,1,0:T(8,128)(2,1)}, u32[]{:S(2)}, u32[]{:S(2)}) async-start(bf16[32,264,256]{2,1,0:T(8,128)(2,1)} %pack.1), calls=%async_computation | async-start | bytes 8650752 | tf_op jit(solution)/shard_map/all_to_all | solution.py:631
  22.7 2.1 collective-permute-start
  24.7 50.0 %collective-permute-done = bf16[4,64,256]{2,1,0:T(8,128)(2,1)S(1)} collective-permute-done((bf16[4,64,256]{2,1,0:T(8,128)(2,1)S(1)}, bf16[4,64,256]{2,1,0:T(8,128)(2,1)S(1)}, u32[]{:S(2)}, u32[]{:S(2)}) %collective-permute-start) | collective-permute-done | bytes 131104 | tf_op jit(solution)/shard_map/ppermute | solution.py:674
  74.7 0.0 copy-start
  74.7 2.4 %collective-permute-start.1 = (bf16[2,4,64,256]{3,2,1,0:T(8,128)(2,1)S(1)}, bf16[2,4,64,256]{3,2,1,0:T(8,128)(2,1)S(1)}, u32[]{:S(2)}, u32[]{:S(2)}) collective-permute-start(bf16[2,4,64,256]{3,2,1,0:T(8,128)(2,1)S(1)} %pad_maximum_fusion.refs_0_), channel_id=1, source_target_pairs={{0,16},{8,24},{16,32},{24,40},{1,17},{9,25},{17,33},{25,41},{2,18}... | collective-permute-start | bytes 786440 | tf_op jit(solution)/shard_map/ppermute | solution.py:678
  77.2 1.3 collective-permute-start.2
  78.5 1.9 collective-permute-start.3
  80.4 0.7 pad_add_fusion.ids_ref
  81.1 2.7 %collective-permute-done.1.refs_1_ = bf16[2,4,64,256]{3,2,1,0:T(8,128)(2,1)S(1)} collective-permute-done((bf16[2,4,64,256]{3,2,1,0:T(8,128)(2,1)S(1)}, bf16[2,4,64,256]{3,2,1,0:T(8,128)(2,1)S(1)}, u32[]{:S(2)}, u32[]{:S(2)}) %collective-permute-start.1) | collective-permute-done | bytes 262176 | tf_op jit(solution)/shard_map/ppermute | solution.py:678
  83.9 4.1 %collective-permute-done.2.refs_2_ = bf16[2,4,64,256]{3,2,1,0:T(8,128)(2,1)S(1)} collective-permute-done((bf16[2,4,64,256]{3,2,1,0:T(8,128)(2,1)S(1)}, bf16[2,4,64,256]{3,2,1,0:T(8,128)(2,1)S(1)}, u32[]{:S(2)}, u32[]{:S(2)}) %collective-permute-start.2) | collective-permute-done | bytes 262176 | tf_op jit(solution)/shard_map/ppermute | solution.py:678
  88.0 2.1 collective-permute-done.3.refs_3_
  90.1 0.0 copy-done.8
  90.1 0.7 copy-done.10
  90.8 2.4 %collect.1.refs_0_ = bf16[10,64,256]{2,1,0:T(8,128)(2,1)} custom-call(s32[2]{0:T(128)} %pad_add_fusion.ids_ref, bf16[2,4,64,256]{3,2,1,0:T(8,128)(2,1)} %copy-done, bf16[2,4,64,256]{3,2,1,0:T(8,128)(2,1)} %copy-done.8, bf16[2,4,64,256]{3,2,1,0:T(8,128)(2,1)} %copy-done.9, bf16[2,4,64,256]{3,2,1,0:T(8,128)(2,1)} %copy-done.10), custom_call_target="tpu_custom_call" | custom-call | tf_op jit(solution)/shard_map/collect/pallas_call | solution.py:349
  93.3 0.8 collective-permute-start.4
  94.1 2.5 %collective-permute-start.5 = (bf16[10,64,256]{2,1,0:T(8,128)(2,1)}, bf16[10,64,256]{2,1,0:T(8,128)(2,1)S(1)}, u32[]{:S(2)}, u32[]{:S(2)}) collective-permute-start(bf16[10,64,256]{2,1,0:T(8,128)(2,1)} %collect.1.refs_0_), channel_id=1, source_target_pairs={{0,6},{1,7},{2,0},{3,1},{4,2},{5,3},{6,4},{7,5},{8,14},{9,15},{10,... | collective-permute-start | bytes 983048 | tf_op jit(solution)/shard_map/ppermute | solution.py:635
  96.6 6.8 %collective-permute-done.4.refs_1_ = bf16[10,64,256]{2,1,0:T(8,128)(2,1)S(1)} collective-permute-done((bf16[10,64,256]{2,1,0:T(8,128)(2,1)}, bf16[10,64,256]{2,1,0:T(8,128)(2,1)S(1)}, u32[]{:S(2)}, u32[]{:S(2)}) %collective-permute-start.4) | collective-permute-done | bytes 327712 | tf_op jit(solution)/shard_map/ppermute | solution.py:635
  103.3 0.1 collective-permute-start.6
  103.4 0.0 collective-permute-done.5.refs_2_
  103.5 3.3 %collective-permute-start.7 = (bf16[5,64,256]{2,1,0:T(8,128)(2,1)S(1)}, bf16[5,64,256]{2,1,0:T(8,128)(2,1)S(1)}, u32[]{:S(2)}, u32[]{:S(2)}) collective-permute-start(bf16[5,64,256]{2,1,0:T(8,128)(2,1)S(1)} %slice.40), channel_id=1, source_target_pairs={{0,6},{1,7},{2,0},{3,1},{4,2},{5,3},{6,4},{7,5},{8,14},{9,15},{10,... | collective-permute-start | bytes 491528 | tf_op jit(solution)/shard_map/ppermute | solution.py:635
  106.7 3.2 %collective-permute-done.6.refs_3_ = bf16[5,64,256]{2,1,0:T(8,128)(2,1)S(1)} collective-permute-done((bf16[5,64,256]{2,1,0:T(8,128)(2,1)S(1)}, bf16[5,64,256]{2,1,0:T(8,128)(2,1)S(1)}, u32[]{:S(2)}, u32[]{:S(2)}) %collective-permute-start.6) | collective-permute-done | bytes 163872 | tf_op jit(solution)/shard_map/ppermute | solution.py:635
  109.9 0.0 collective-permute-done.7.refs_4_
  110.0 0.6 copy-done.18
  110.6 0.7 copy-done.19
  111.3 26.9 %factorize_first.1 = (bf16[1024,512]{1,0:T(8,128)(2,1)}, bf16[1024,512]{1,0:T(8,128)(2,1)}, bf16[2,256,256]{2,1,0:T(8,128)(2,1)}, bf16[2,256,256]{2,1,0:T(8,128)...) custom-call(s32[2]{0:T(128)} %pad_add_fusion.ids_ref, bf16[10,64,256]{2,1,0:T(8,128)(2,1)} %collect.1.refs_0_, ...), custom_call_target="tpu_custom_call" | custom-call | tf_op jit(solution)/shard_map/factorize_first/pallas_call | solution.py:414
  138.1 0.0 all-to-all-done.received_ref
  138.1 6.7 %assemble.1 = (f32[5,256,256]{2,1,0:T(8,128)}, s16[8,104,256]{2,1,0:T(8,128)(2,1)}) custom-call(bf16[32,264,256]{2,1,0:T(8,128)(2,1)} %all-to-all-done.received_ref, bf16[3,3,256,256]{3,2,1,0:T(8,128)(2,1)} %bitcast.21), custom_call_target="tpu_custom_call" | custom-call | tf_op jit(solution)/shard_map/assemble/pallas_call | solution.py:205
  144.8 12.5 %all_to_all.15 = s16[8,104,256]{2,1,0:T(8,128)(2,1)S(1)} all-to-all(s16[8,104,256]{2,1,0:T(8,128)(2,1)} %get-tuple-element.31), channel_id=1, replica_groups=mesh['front'=2,'row'=8,'col'=8] {'col'}, dimensions={0} | all-to-all | bytes 851968 | tf_op jit(solution)/shard_map/all_to_all | solution.py:631
  157.4 0.7 collective-permute-start.9
  158.1 5.3 %collective-permute-start.8 = (s16[4,104,256]{2,1,0:T(8,128)(2,1)S(1)}, s16[4,104,256]{2,1,0:T(8,128)(2,1)S(1)}, u32[]{:S(2)}, u32[]{:S(2)}) collective-permute-start(s16[4,104,256]{2,1,0:T(8,128)(2,1)S(1)} %slice.41.refs_0_), channel_id=1, source_target_pairs={{0,1},{1,0},{2,3},{3,2},{4,5},{5,4},{6,7},{7,6},{8,9},{9,8},{10,11... | collective-permute-start | bytes 638984 | tf_op jit(solution)/shard_map/ppermute | solution.py:635
  163.4 0.0 collective-permute-done.9.refs_2_
  163.4 8.1 %collective-permute-start.10 = (s16[4,104,256]{2,1,0:T(8,128)(2,1)S(1)}, s16[4,104,256]{2,1,0:T(8,128)(2,1)S(1)}, u32[]{:S(2)}, u32[]{:S(2)}) collective-permute-start(s16[4,104,256]{2,1,0:T(8,128)(2,1)S(1)} %collective-permute-done.9.refs_2_), channel_id=1, source_target_pairs={{0,8},{8,0},{16,24},{24,16},{32,40},{40,32},{48,56},{56,48},{1,9},... | collective-permute-start | bytes 638984 | tf_op jit(solution)/shard_map/ppermute | solution.py:635
  171.4 6.6 %factorize_second.1 = (bf16[512,256]{1,0:T(8,128)(2,1)}, bf16[512,256]{1,0:T(8,128)(2,1)}, bf16[1,256,256]{2,1,0:T(8,128)(2,1)}, bf16[1,256,256]{2,1,0:T(8,128)(...) custom-call(f32[512,512]{1,0:T(8,128)} %get-tuple-element.36.rest_ref, f32[128,128]{1,0:T(8,128)} %get-tuple-element.37.begun_ref), custom_call_target="tpu_custom_call" | custom-call | tf_op jit(solution)/shard_map/factorize_second/pallas_call | solution.py:439
  178.0 5.6 %factorize_next.1 = (f32[256,256]{1,0:T(8,128)}, f32[1,128,128]{2,1,0:T(8,128)}) custom-call(f32[256,256]{1,0:T(8,128)} %get-tuple-element.42.rest_ref), custom_call_target="tpu_custom_call" | custom-call | tf_op jit(solution)/shard_map/factorize_next/pallas_call | solution.py:455
  183.6 5.6 %factorize_last.1 = (f32[256,256]{1,0:T(8,128)}, bf16[256,256]{1,0:T(8,128)(2,1)}, bf16[256,256]{1,0:T(8,128)(2,1)}) custom-call(f32[256,256]{1,0:T(8,128)} %get-tuple-element.43.rest_ref, f32[1,128,128]{2,1,0:T(8,128)} %get-tuple-element.44.first_ref), custom_call_target="tpu_custom_call" | custom-call | tf_op jit(solution)/shard_map/factorize_last/pallas_call | solution.py:479
  189.2 0.0 collective-permute-done.8.refs_1_
  189.2 0.0 collective-permute-done.10.refs_3_
  189.2 0.6 copy-done.15
  189.9 0.1 copy-done.17
  190.0 6.3 %solve.1 = (s16[2,4,104,256]{3,2,1,0:T(8,128)(2,1)}, s16[2,4,104,256]{3,2,1,0:T(8,128)(2,1)}) custom-call(s16[4,104,256]{2,1,0:T(8,128)(2,1)} %copy-done.5, s16[4,104,256]{2,1,0:T(8,128)(2,1)} %copy-done.15, s16[4,104,256]{2,1,0:T(8,128)(2,1)} %copy-done.13, s16[4,104,256]{2,1,0:T(8,128)(2,1)} %copy-done.17, bf16[1024,512]{1,0:T(8,128)(2,1)} %get-tuple-element.32.refs_4_, ...), custom_call_target="tpu_custom_call" | custom-call | tf_op jit(solution)/shard_map/solve/pallas_call | solution.py:524
  196.3 1.4 collective-permute-start.11
  197.7 3.9 %collective-permute-start.12 = (s16[2,4,104,256]{3,2,1,0:T(8,128)(2,1)}, s16[2,4,104,256]{3,2,1,0:T(8,128)(2,1)S(1)}, u32[]{:S(2)}, u32[]{:S(2)}) collective-permute-start(s16[2,4,104,256]{3,2,1,0:T(8,128)(2,1)} %get-tuple-element.47.refs_0_), channel_id=1, source_target_pairs={{0,6},{1,7},{2,0},{3,1},{4,2},{5,3},{6,4},{7,5},{8,14},{9,15},{10,... | collective-permute-start | bytes 1277960 | tf_op jit(solution)/shard_map/ppermute | solution.py:635
  201.6 0.0 collective-permute-start.15
  201.6 4.3 %collective-permute-start.16 = (s16[2,4,104,256]{3,2,1,0:T(8,128)(2,1)}, s16[2,4,104,256]{3,2,1,0:T(8,128)(2,1)S(1)}, u32[]{:S(2)}, u32[]{:S(2)}) collective-permute-start(s16[2,4,104,256]{3,2,1,0:T(8,128)(2,1)} %get-tuple-element.48.refs_5_), channel_id=1, source_target_pairs={{0,48},{8,56},{16,0},{24,8},{32,16},{40,24},{48,32},{56,40},{1,49}... | collective-permute-start | bytes 1277960 | tf_op jit(solution)/shard_map/ppermute | solution.py:635
  205.9 4.2 %collective-permute-done.11.refs_1_ = s16[2,4,104,256]{3,2,1,0:T(8,128)(2,1)S(1)} collective-permute-done((s16[2,4,104,256]{3,2,1,0:T(8,128)(2,1)}, s16[2,4,104,256]{3,2,1,0:T(8,128)(2,1)S(1)}, u32[]{:S(2)}, u32[]{:S(2)}) %collective-permute-start.11) | collective-permute-done | bytes 426016 | tf_op jit(solution)/shard_map/ppermute | solution.py:635
  210.1 0.1 collective-permute-start.13
  210.2 0.0 collective-permute-done.12.refs_2_
  210.3 3.3 %collective-permute-start.14 = (s16[1,4,104,256]{3,2,1,0:T(8,128)(2,1)S(1)}, s16[1,4,104,256]{3,2,1,0:T(8,128)(2,1)S(1)}, u32[]{:S(2)}, u32[]{:S(2)}) collective-permute-start(s16[1,4,104,256]{3,2,1,0:T(8,128)(2,1)S(1)} %slice.43), channel_id=1, source_target_pairs={{0,6},{1,7},{2,0},{3,1},{4,2},{5,3},{6,4},{7,5},{8,14},{9,15},{10,... | collective-permute-start | bytes 638984 | tf_op jit(solution)/shard_map/ppermute | solution.py:635
  213.5 0.0 collective-permute-done.15.refs_6_
  213.6 0.1 collective-permute-start.17
  213.7 0.0 collective-permute-done.16.refs_7_
  213.7 3.5 %collective-permute-start.18 = (s16[1,4,104,256]{3,2,1,0:T(8,128)(2,1)S(1)}, s16[1,4,104,256]{3,2,1,0:T(8,128)(2,1)S(1)}, u32[]{:S(2)}, u32[]{:S(2)}) collective-permute-start(s16[1,4,104,256]{3,2,1,0:T(8,128)(2,1)S(1)} %slice.45), channel_id=1, source_target_pairs={{0,48},{8,56},{16,0},{24,8},{32,16},{40,24},{48,32},{56,40},{1,49}... | collective-permute-start | bytes 638984 | tf_op jit(solution)/shard_map/ppermute | solution.py:635
  217.3 0.0 collective-permute-done.13.refs_3_
  217.3 0.0 collective-permute-done.14.refs_4_
  217.3 3.7 %collective-permute-done.17.refs_8_ = s16[1,4,104,256]{3,2,1,0:T(8,128)(2,1)S(1)} collective-permute-done((s16[1,4,104,256]{3,2,1,0:T(8,128)(2,1)S(1)}, s16[1,4,104,256]{3,2,1,0:T(8,128)(2,1)S(1)}, u32[]{:S(2)}, u32[]{:S(2)}) %collective-permute-start.17) | collective-permute-done | bytes 213024 | tf_op jit(solution)/shard_map/ppermute | solution.py:635
  221.0 0.2 collective-permute-done.18.refs_9_
  221.2 0.5 copy-done.14
  221.7 0.1 copy-done.16
  221.8 7.5 %finish.1 = f32[4608,128]{1,0:T(8,128)} custom-call(s32[2]{0:T(128)} %pad_add_fusion.ids_ref, s16[2,4,104,256]{3,2,1,0:T(8,128)(2,1)} %get-tuple-element.47.refs_0_, s16[2,4,104,256]{3,2,1,0:T(8,128)(2,1)} %copy-done.1, s16[2,4,104,256]{3,2,1,0:T(8,128)(2,1)} %copy-done.2, s16[1,4,104,256]{3,2,1,0:T(8,128)(2,1)} %copy-done.11, ...), custom_call_target="tpu_custom_call" | custom-call | tf_op jit(solution)/shard_map/finish/pallas_call | solution.py:619
  (40 shorter events, 0.2 us)
Async XLA Ops:
  2.3 12.9 %all-to-all-start.1 = ((bf16[8,64,256]{2,1,0:T(8,128)(2,1)}), bf16[8,64,256]{2,1,0:T(8,128)(2,1)S(1)}, u32[]{:S(2)}, u32[]{:S(2)}) async-start(bf16[8,64,256]{2,1,0:T(8,128)(2,1)} %bitcast.10), calls=%async_computation.1 | async-start | bytes 524288 | tf_op jit(solution)/shard_map/all_to_all | solution.py:631
  15.2 123.0 %all-to-all-start = ((bf16[32,264,256]{2,1,0:T(8,128)(2,1)}), bf16[32,264,256]{2,1,0:T(8,128)(2,1)}, u32[]{:S(2)}, u32[]{:S(2)}) async-start(bf16[32,264,256]{2,1,0:T(8,128)(2,1)} %pack.1), calls=%async_computation | async-start | bytes 8650752 | tf_op jit(solution)/shard_map/all_to_all | solution.py:631
  22.7 52.0 %collective-permute-start = (bf16[4,64,256]{2,1,0:T(8,128)(2,1)S(1)}, bf16[4,64,256]{2,1,0:T(8,128)(2,1)S(1)}, u32[]{:S(2)}, u32[]{:S(2)}) collective-permute-start(bf16[4,64,256]{2,1,0:T(8,128)(2,1)S(1)} %get-tuple-element.56), channel_id=1, source_target_pairs={{0,8},{8,0},{16,24},{24,16},{1,9},{9,1},{17,25},{25,17},{2,10},{10... | collective-permute-start | bytes 393224 | tf_op jit(solution)/shard_map/ppermute | solution.py:674
  74.7 15.4 %copy-start = (bf16[2,4,64,256]{3,2,1,0:T(8,128)(2,1)}, bf16[2,4,64,256]{3,2,1,0:T(8,128)(2,1)S(1)}, u32[]{:S(2)}) copy-start(bf16[2,4,64,256]{3,2,1,0:T(8,128)(2,1)S(1)} %pad_maximum_fusion.refs_0_) | copy-start | bytes 786436
  74.7 9.1 %collective-permute-start.1 = (bf16[2,4,64,256]{3,2,1,0:T(8,128)(2,1)S(1)}, bf16[2,4,64,256]{3,2,1,0:T(8,128)(2,1)S(1)}, u32[]{:S(2)}, u32[]{:S(2)}) collective-permute-start(bf16[2,4,64,256]{3,2,1,0:T(8,128)(2,1)S(1)} %pad_maximum_fusion.refs_0_), channel_id=1, source_target_pairs={{0,16},{8,24},{16,32},{24,40},{1,17},{9,25},{17,33},{25,41},{2,18}... | collective-permute-start | bytes 786440 | tf_op jit(solution)/shard_map/ppermute | solution.py:678
  77.2 10.8 %collective-permute-start.2 = (bf16[2,4,64,256]{3,2,1,0:T(8,128)(2,1)S(1)}, bf16[2,4,64,256]{3,2,1,0:T(8,128)(2,1)S(1)}, u32[]{:S(2)}, u32[]{:S(2)}) collective-permute-start(bf16[2,4,64,256]{3,2,1,0:T(8,128)(2,1)S(1)} %pad_maximum_fusion.refs_0_), channel_id=1, source_target_pairs={{0,32},{8,40},{16,48},{24,56},{1,33},{9,41},{17,49},{25,57},{2,34}... | collective-permute-start | bytes 786440 | tf_op jit(solution)/shard_map/ppermute | solution.py:678
  78.5 11.6 %collective-permute-start.3 = (bf16[2,4,64,256]{3,2,1,0:T(8,128)(2,1)S(1)}, bf16[2,4,64,256]{3,2,1,0:T(8,128)(2,1)S(1)}, u32[]{:S(2)}, u32[]{:S(2)}) collective-permute-start(bf16[2,4,64,256]{3,2,1,0:T(8,128)(2,1)S(1)} %pad_maximum_fusion.refs_0_), channel_id=1, source_target_pairs={{0,48},{8,56},{16,0},{24,8},{1,49},{9,57},{17,1},{25,9},{2,50},{10... | collective-permute-start | bytes 786440 | tf_op jit(solution)/shard_map/ppermute | solution.py:678
  83.9 6.2 %copy-start.8 = (bf16[2,4,64,256]{3,2,1,0:T(8,128)(2,1)}, bf16[2,4,64,256]{3,2,1,0:T(8,128)(2,1)S(1)}, u32[]{:S(2)}) copy-start(bf16[2,4,64,256]{3,2,1,0:T(8,128)(2,1)S(1)} %collective-permute-done.1.refs_1_) | copy-start | bytes 786436
  88.0 2.1 copy-start.9
  90.1 0.7 copy-start.10
  93.3 10.1 %collective-permute-start.4 = (bf16[10,64,256]{2,1,0:T(8,128)(2,1)}, bf16[10,64,256]{2,1,0:T(8,128)(2,1)S(1)}, u32[]{:S(2)}, u32[]{:S(2)}) collective-permute-start(bf16[10,64,256]{2,1,0:T(8,128)(2,1)} %collect.1.refs_0_), channel_id=1, source_target_pairs={{0,2},{1,3},{2,4},{3,5},{4,6},{5,7},{6,0},{7,1},{8,10},{9,11},{10,... | collective-permute-start | bytes 983048 | tf_op jit(solution)/shard_map/ppermute | solution.py:635
  94.1 9.4 %collective-permute-start.5 = (bf16[10,64,256]{2,1,0:T(8,128)(2,1)}, bf16[10,64,256]{2,1,0:T(8,128)(2,1)S(1)}, u32[]{:S(2)}, u32[]{:S(2)}) collective-permute-start(bf16[10,64,256]{2,1,0:T(8,128)(2,1)} %collect.1.refs_0_), channel_id=1, source_target_pairs={{0,6},{1,7},{2,0},{3,1},{4,2},{5,3},{6,4},{7,5},{8,14},{9,15},{10,... | collective-permute-start | bytes 983048 | tf_op jit(solution)/shard_map/ppermute | solution.py:635
  103.3 6.6 %copy-start.6 = (bf16[10,64,256]{2,1,0:T(8,128)(2,1)}, bf16[10,64,256]{2,1,0:T(8,128)(2,1)S(1)}, u32[]{:S(2)}) copy-start(bf16[10,64,256]{2,1,0:T(8,128)(2,1)S(1)} %collective-permute-done.4.refs_1_) | copy-start | bytes 983044
  103.3 6.6 %collective-permute-start.6 = (bf16[5,64,256]{2,1,0:T(8,128)(2,1)S(1)}, bf16[5,64,256]{2,1,0:T(8,128)(2,1)S(1)}, u32[]{:S(2)}, u32[]{:S(2)}) collective-permute-start(bf16[5,64,256]{2,1,0:T(8,128)(2,1)S(1)} %slice.39), channel_id=1, source_target_pairs={{0,2},{1,3},{2,4},{3,5},{4,6},{5,7},{6,0},{7,1},{8,10},{9,11},{10,... | collective-permute-start | bytes 491528 | tf_op jit(solution)/shard_map/ppermute | solution.py:635
  103.4 6.5 %copy-start.7 = (bf16[10,64,256]{2,1,0:T(8,128)(2,1)}, bf16[10,64,256]{2,1,0:T(8,128)(2,1)S(1)}, u32[]{:S(2)}) copy-start(bf16[10,64,256]{2,1,0:T(8,128)(2,1)S(1)} %collective-permute-done.5.refs_2_) | copy-start | bytes 983044
  103.5 6.5 %collective-permute-start.7 = (bf16[5,64,256]{2,1,0:T(8,128)(2,1)S(1)}, bf16[5,64,256]{2,1,0:T(8,128)(2,1)S(1)}, u32[]{:S(2)}, u32[]{:S(2)}) collective-permute-start(bf16[5,64,256]{2,1,0:T(8,128)(2,1)S(1)} %slice.40), channel_id=1, source_target_pairs={{0,6},{1,7},{2,0},{3,1},{4,2},{5,3},{6,4},{7,5},{8,14},{9,15},{10,... | collective-permute-start | bytes 491528 | tf_op jit(solution)/shard_map/ppermute | solution.py:635
  109.9 0.7 copy-start.18
  110.6 0.7 copy-start.19
  157.4 31.8 %copy-start.5 = (s16[4,104,256]{2,1,0:T(8,128)(2,1)}, s16[4,104,256]{2,1,0:T(8,128)(2,1)S(1)}, u32[]{:S(2)}) copy-start(s16[4,104,256]{2,1,0:T(8,128)(2,1)S(1)} %slice.41.refs_0_) | copy-start | bytes 638980
  157.4 6.0 %collective-permute-start.9 = (s16[4,104,256]{2,1,0:T(8,128)(2,1)S(1)}, s16[4,104,256]{2,1,0:T(8,128)(2,1)S(1)}, u32[]{:S(2)}, u32[]{:S(2)}) collective-permute-start(s16[4,104,256]{2,1,0:T(8,128)(2,1)S(1)} %slice.41.refs_0_), channel_id=1, source_target_pairs={{0,0},{1,8},{2,16},{3,24},{4,32},{5,40},{6,48},{7,56},{8,1},{9,9},... | collective-permute-start | bytes 638984 | tf_op jit(solution)/shard_map/ppermute | solution.py:694
  158.1 31.1 %collective-permute-start.8 = (s16[4,104,256]{2,1,0:T(8,128)(2,1)S(1)}, s16[4,104,256]{2,1,0:T(8,128)(2,1)S(1)}, u32[]{:S(2)}, u32[]{:S(2)}) collective-permute-start(s16[4,104,256]{2,1,0:T(8,128)(2,1)S(1)} %slice.41.refs_0_), channel_id=1, source_target_pairs={{0,1},{1,0},{2,3},{3,2},{4,5},{5,4},{6,7},{7,6},{8,9},{9,8},{10,11... | collective-permute-start | bytes 638984 | tf_op jit(solution)/shard_map/ppermute | solution.py:635
  163.4 25.9 %copy-start.13 = (s16[4,104,256]{2,1,0:T(8,128)(2,1)}, s16[4,104,256]{2,1,0:T(8,128)(2,1)S(1)}, u32[]{:S(2)}) copy-start(s16[4,104,256]{2,1,0:T(8,128)(2,1)S(1)} %collective-permute-done.9.refs_2_) | copy-start | bytes 638980
  163.4 25.8 %collective-permute-start.10 = (s16[4,104,256]{2,1,0:T(8,128)(2,1)S(1)}, s16[4,104,256]{2,1,0:T(8,128)(2,1)S(1)}, u32[]{:S(2)}, u32[]{:S(2)}) collective-permute-start(s16[4,104,256]{2,1,0:T(8,128)(2,1)S(1)} %collective-permute-done.9.refs_2_), channel_id=1, source_target_pairs={{0,8},{8,0},{16,24},{24,16},{32,40},{40,32},{48,56},{56,48},{1,9},... | collective-permute-start | bytes 638984 | tf_op jit(solution)/shard_map/ppermute | solution.py:635
  189.2 0.7 copy-start.15
  189.2 0.8 copy-start.17
  196.3 13.8 %collective-permute-start.11 = (s16[2,4,104,256]{3,2,1,0:T(8,128)(2,1)}, s16[2,4,104,256]{3,2,1,0:T(8,128)(2,1)S(1)}, u32[]{:S(2)}, u32[]{:S(2)}) collective-permute-start(s16[2,4,104,256]{3,2,1,0:T(8,128)(2,1)} %get-tuple-element.47.refs_0_), channel_id=1, source_target_pairs={{0,2},{1,3},{2,4},{3,5},{4,6},{5,7},{6,0},{7,1},{8,10},{9,11},{10,... | collective-permute-start | bytes 1277960 | tf_op jit(solution)/shard_map/ppermute | solution.py:635
  197.7 12.5 %collective-permute-start.12 = (s16[2,4,104,256]{3,2,1,0:T(8,128)(2,1)}, s16[2,4,104,256]{3,2,1,0:T(8,128)(2,1)S(1)}, u32[]{:S(2)}, u32[]{:S(2)}) collective-permute-start(s16[2,4,104,256]{3,2,1,0:T(8,128)(2,1)} %get-tuple-element.47.refs_0_), channel_id=1, source_target_pairs={{0,6},{1,7},{2,0},{3,1},{4,2},{5,3},{6,4},{7,5},{8,14},{9,15},{10,... | collective-permute-start | bytes 1277960 | tf_op jit(solution)/shard_map/ppermute | solution.py:635
  201.6 12.0 %collective-permute-start.15 = (s16[2,4,104,256]{3,2,1,0:T(8,128)(2,1)}, s16[2,4,104,256]{3,2,1,0:T(8,128)(2,1)S(1)}, u32[]{:S(2)}, u32[]{:S(2)}) collective-permute-start(s16[2,4,104,256]{3,2,1,0:T(8,128)(2,1)} %get-tuple-element.48.refs_5_), channel_id=1, source_target_pairs={{0,16},{8,24},{16,32},{24,40},{32,48},{40,56},{48,0},{56,8},{1,17}... | collective-permute-start | bytes 1277960 | tf_op jit(solution)/shard_map/ppermute | solution.py:635
  201.6 12.1 %collective-permute-start.16 = (s16[2,4,104,256]{3,2,1,0:T(8,128)(2,1)}, s16[2,4,104,256]{3,2,1,0:T(8,128)(2,1)S(1)}, u32[]{:S(2)}, u32[]{:S(2)}) collective-permute-start(s16[2,4,104,256]{3,2,1,0:T(8,128)(2,1)} %get-tuple-element.48.refs_5_), channel_id=1, source_target_pairs={{0,48},{8,56},{16,0},{24,8},{32,16},{40,24},{48,32},{56,40},{1,49}... | collective-permute-start | bytes 1277960 | tf_op jit(solution)/shard_map/ppermute | solution.py:635
  210.1 11.0 %copy-start.1 = (s16[2,4,104,256]{3,2,1,0:T(8,128)(2,1)}, s16[2,4,104,256]{3,2,1,0:T(8,128)(2,1)S(1)}, u32[]{:S(2)}) copy-start(s16[2,4,104,256]{3,2,1,0:T(8,128)(2,1)S(1)} %collective-permute-done.11.refs_1_) | copy-start | bytes 1277956
  210.1 7.1 %collective-permute-start.13 = (s16[1,4,104,256]{3,2,1,0:T(8,128)(2,1)S(1)}, s16[1,4,104,256]{3,2,1,0:T(8,128)(2,1)S(1)}, u32[]{:S(2)}, u32[]{:S(2)}) collective-permute-start(s16[1,4,104,256]{3,2,1,0:T(8,128)(2,1)S(1)} %slice.42), channel_id=1, source_target_pairs={{0,2},{1,3},{2,4},{3,5},{4,6},{5,7},{6,0},{7,1},{8,10},{9,11},{10,... | collective-permute-start | bytes 638984 | tf_op jit(solution)/shard_map/ppermute | solution.py:635
  210.2 10.9 %copy-start.2 = (s16[2,4,104,256]{3,2,1,0:T(8,128)(2,1)}, s16[2,4,104,256]{3,2,1,0:T(8,128)(2,1)S(1)}, u32[]{:S(2)}) copy-start(s16[2,4,104,256]{3,2,1,0:T(8,128)(2,1)S(1)} %collective-permute-done.12.refs_2_) | copy-start | bytes 1277956
  210.3 7.0 %collective-permute-start.14 = (s16[1,4,104,256]{3,2,1,0:T(8,128)(2,1)S(1)}, s16[1,4,104,256]{3,2,1,0:T(8,128)(2,1)S(1)}, u32[]{:S(2)}, u32[]{:S(2)}) collective-permute-start(s16[1,4,104,256]{3,2,1,0:T(8,128)(2,1)S(1)} %slice.43), channel_id=1, source_target_pairs={{0,6},{1,7},{2,0},{3,1},{4,2},{5,3},{6,4},{7,5},{8,14},{9,15},{10,... | collective-permute-start | bytes 638984 | tf_op jit(solution)/shard_map/ppermute | solution.py:635
  213.5 7.6 %copy-start.3 = (s16[2,4,104,256]{3,2,1,0:T(8,128)(2,1)}, s16[2,4,104,256]{3,2,1,0:T(8,128)(2,1)S(1)}, u32[]{:S(2)}) copy-start(s16[2,4,104,256]{3,2,1,0:T(8,128)(2,1)S(1)} %collective-permute-done.15.refs_6_) | copy-start | bytes 1277956
  213.6 7.4 %collective-permute-start.17 = (s16[1,4,104,256]{3,2,1,0:T(8,128)(2,1)S(1)}, s16[1,4,104,256]{3,2,1,0:T(8,128)(2,1)S(1)}, u32[]{:S(2)}, u32[]{:S(2)}) collective-permute-start(s16[1,4,104,256]{3,2,1,0:T(8,128)(2,1)S(1)} %slice.44), channel_id=1, source_target_pairs={{0,16},{8,24},{16,32},{24,40},{32,48},{40,56},{48,0},{56,8},{1,17}... | collective-permute-start | bytes 638984 | tf_op jit(solution)/shard_map/ppermute | solution.py:635
  213.7 7.4 %copy-start.4 = (s16[2,4,104,256]{3,2,1,0:T(8,128)(2,1)}, s16[2,4,104,256]{3,2,1,0:T(8,128)(2,1)S(1)}, u32[]{:S(2)}) copy-start(s16[2,4,104,256]{3,2,1,0:T(8,128)(2,1)S(1)} %collective-permute-done.16.refs_7_) | copy-start | bytes 1277956
  213.7 7.4 %collective-permute-start.18 = (s16[1,4,104,256]{3,2,1,0:T(8,128)(2,1)S(1)}, s16[1,4,104,256]{3,2,1,0:T(8,128)(2,1)S(1)}, u32[]{:S(2)}, u32[]{:S(2)}) collective-permute-start(s16[1,4,104,256]{3,2,1,0:T(8,128)(2,1)S(1)} %slice.45), channel_id=1, source_target_pairs={{0,48},{8,56},{16,0},{24,8},{32,16},{40,24},{48,32},{56,40},{1,49}... | collective-permute-start | bytes 638984 | tf_op jit(solution)/shard_map/ppermute | solution.py:635
  217.3 3.9 %copy-start.11 = (s16[1,4,104,256]{3,2,1,0:T(8,128)(2,1)}, s16[1,4,104,256]{3,2,1,0:T(8,128)(2,1)S(1)}, u32[]{:S(2)}) copy-start(s16[1,4,104,256]{3,2,1,0:T(8,128)(2,1)S(1)} %collective-permute-done.13.refs_3_) | copy-start | bytes 638980
  217.3 3.9 %copy-start.12 = (s16[1,4,104,256]{3,2,1,0:T(8,128)(2,1)}, s16[1,4,104,256]{3,2,1,0:T(8,128)(2,1)S(1)}, u32[]{:S(2)}) copy-start(s16[1,4,104,256]{3,2,1,0:T(8,128)(2,1)S(1)} %collective-permute-done.14.refs_4_) | copy-start | bytes 638980
  221.0 0.7 copy-start.14
  221.1 0.7 copy-start.16
